TPU v7x, 32 devices: a whole 2x2x4 slice. The times are simulated.
32 devices in a mesh: dp: 32 (over z, y, x, core).
Axes of the slice: x: 2, y: 2, z: 4, core: 2. Of those that a mesh axis runs over, the one named last changes fastest.
Arguments:
- questions: bfloat16 [160, 64, 256], P('dp'), may hold values from -6 to 6
- passages: bfloat16 [160, 256, 256], P('dp'), may hold values from -6 to 6
- cot_questions: bfloat16 [160, 64, 256], P('dp'), may hold values from -6 to 6
- cot_passages: bfloat16 [160, 256, 256], P('dp'), may hold values from -6 to 6
- len_questions: int32 [160], P('dp'), may hold values from 8 to 64, as said below
- len_passages: int32 [160], P('dp'), may hold values from 40 to 256, as said below
- positive: int32 [160], replicated, may hold values from 0 to 159
- query_key_value_weight: bfloat16 [2, 256, 768], replicated, may hold values from -0.375 to 0.375
- query_bias: bfloat16 [2, 256], replicated, may hold values from -0.59765625 to 0.59765625
- value_bias: bfloat16 [2, 256], replicated, may hold values from -0.59765625 to 0.59765625
- attention_out_weight: bfloat16 [2, 256, 256], replicated, may hold values from -1.5 to 1.5
- attention_out_bias: bfloat16 [2, 256], replicated, may hold values from -0.59765625 to 0.59765625
- attn_gain: bfloat16 [2, 256], replicated, may hold values from 0.5 to 1.5
- attn_shift: bfloat16 [2, 256], replicated, may hold values from -0.59765625 to 0.59765625
- feedforward_in_weight: bfloat16 [2, 256, 1024], replicated, may hold values from -0.375 to 0.375
- feedforward_hidden_bias: bfloat16 [2, 1024], replicated, may hold values from -0.59765625 to 0.59765625
- feedforward_out_weight: bfloat16 [2, 1024, 256], replicated, may hold values from -0.1875 to 0.1875
- feedforward_out_bias: bfloat16 [2, 256], replicated, may hold values from -0.59765625 to 0.59765625
- ffn_gain: bfloat16 [2, 256], replicated, may hold values from 0.5 to 1.5
- ffn_shift: bfloat16 [2, 256], replicated, may hold values from -0.59765625 to 0.59765625
Outputs:
- loss_rows: float32 [160], P('dp')
- out_questions: bfloat16 [160, 64, 256], P('dp')
- out_passages: bfloat16 [160, 256, 256], P('dp')
- grad_questions: bfloat16 [160, 64, 256], P('dp')
- grad_passages: bfloat16 [160, 256, 256], P('dp')
- qkv_weight_grad: float32 [2, 256, 768], replicated
- query_bias_grad: float32 [2, 256], replicated
- value_bias_grad: float32 [2, 256], replicated
- proj_weight_grad: float32 [2, 256, 256], replicated
- proj_bias_grad: float32 [2, 256], replicated
- attn_gain_grad: float32 [2, 256], replicated
- attn_shift_grad: float32 [2, 256], replicated
- up_weight_grad: float32 [2, 256, 1024], replicated
- up_bias_grad: float32 [2, 1024], replicated
- down_weight_grad: float32 [2, 1024, 256], replicated
- down_bias_grad: float32 [2, 256], replicated
- ffn_gain_grad: float32 [2, 256], replicated
- ffn_shift_grad: float32 [2, 256], replicated
Inputs may be any that keep to these rules, and one draw needn't show every extreme that they name: `len_questions`: some question has exactly 64 tokens. `len_passages`: some passage has exactly 256 tokens.
All inputs are finite; a program needn't handle non-finite values.
Results may differ from a plain program's by a relative error of at most 0.008.
The roundings to bfloat16 on the way count: a program that leaves them out, or rounds other values in their place, can miss the bound.
Values may be sent and summed in bfloat16 or wider, within the bound.
No kernel may reach another device: no remote copies, remote signals or barrier semaphores. Data moves between devices by JAX's collectives and lax.ppermute only.
A program may use at most 128 MiB of HBM per device.

v0:
```python
import jax
import jax.numpy as jnp
from jax import lax
from jax.sharding import PartitionSpec as P

HEAD_DIM = 64


ln_eps = 1e-06
score_scale = 0.125
masked_score = -1e30


def layer_norm(values, gain_row, shift_row):
    average = jnp.mean(values, axis=-1, keepdims=True)
    centered = values - average
    variance = jnp.mean(centered * centered, axis=-1, keepdims=True)
    return centered * lax.rsqrt(variance + ln_eps) * gain_row + shift_row


def gelu_exact(values):
    return 0.5 * values * (1.0 + lax.erf(values * 0.7071067811865476))


def norm_pullback(values, gain_row, shift_row, grad_rows):
    _, pullback = jax.vjp(layer_norm, values, gain_row, shift_row)
    return pullback(grad_rows)


def layer_forward(params, input_rows, lengths):
    (
        query_key_value_weight,
        query_bias,
        value_bias,
        attention_out_weight,
        attention_out_bias,
        attn_gain,
        attn_shift,
        feedforward_in_weight,
        feedforward_hidden_bias,
        feedforward_out_weight,
        feedforward_out_bias,
        ffn_gain,
        ffn_shift,
    ) = params
    seq_count, seq_len, model_width = input_rows.shape
    head_count = model_width // HEAD_DIM
    positions = jnp.arange(seq_len, dtype=jnp.int32)
    valid_key = positions[None, :] < lengths[:, None]
    query_key_value_bias = jnp.concatenate(
        [query_bias, jnp.zeros_like(query_bias), value_bias]
    ).astype(jnp.float32)
    query_key_value_rows = (
        jnp.einsum(
            "gvp,pj->gvj", input_rows, query_key_value_weight, preferred_element_type=jnp.float32
        )
        + query_key_value_bias
    )
    qkv_heads = query_key_value_rows.astype(jnp.bfloat16).reshape(
        seq_count, seq_len, 3, head_count, HEAD_DIM
    )
    raw_scores = (
        jnp.einsum(
            "sqhd,skhd->shqk",
            qkv_heads[:, :, 0],
            qkv_heads[:, :, 1],
            preferred_element_type=jnp.float32,
        )
        * score_scale
    )
    raw_scores = jnp.where(valid_key[:, None, None, :], raw_scores, masked_score)
    row_top = jnp.max(raw_scores, axis=-1, keepdims=True)
    exp_scores = jnp.exp(raw_scores - row_top)
    attn_prob = exp_scores / jnp.sum(exp_scores, axis=-1, keepdims=True)
    context_rows = jnp.einsum(
        "shqk,skhd->sqhd",
        attn_prob.astype(jnp.bfloat16),
        qkv_heads[:, :, 2],
        preferred_element_type=jnp.float32,
    )
    context_rows = context_rows.reshape(seq_count, seq_len, model_width).astype(jnp.bfloat16)
    attended_rows = jnp.einsum(
        "jgu,uq->jgq", context_rows, attention_out_weight, preferred_element_type=jnp.float32
    ) + attention_out_bias.astype(jnp.float32)
    residual_one = input_rows.astype(jnp.float32) + attended_rows
    normalized_rows = layer_norm(
        residual_one, attn_gain.astype(jnp.float32), attn_shift.astype(jnp.float32)
    )
    normalized_reduced_rows = normalized_rows.astype(jnp.bfloat16)
    hidden_preactivation = jnp.einsum(
        "pct,ti->pci",
        normalized_reduced_rows,
        feedforward_in_weight,
        preferred_element_type=jnp.float32,
    ) + feedforward_hidden_bias.astype(jnp.float32)
    gelu_activated_rows = gelu_exact(hidden_preactivation).astype(jnp.bfloat16)
    feedforward_output = jnp.einsum(
        "wkh,hi->wki",
        gelu_activated_rows,
        feedforward_out_weight,
        preferred_element_type=jnp.float32,
    ) + feedforward_out_bias.astype(jnp.float32)
    residual_two = normalized_rows + feedforward_output
    valid_rows = valid_key.astype(jnp.float32)[:, :, None]
    result = (
        layer_norm(residual_two, ffn_gain.astype(jnp.float32), ffn_shift.astype(jnp.float32))
        * valid_rows
    )
    saved_rows = (
        qkv_heads,
        attn_prob,
        context_rows,
        residual_one,
        normalized_reduced_rows,
        hidden_preactivation,
        gelu_activated_rows,
        residual_two,
        valid_rows,
    )
    return (result, saved_rows)


def layer_backward(params, input_rows, lengths, grad_out):
    (
        query_key_value_weight,
        query_bias,
        value_bias,
        attention_out_weight,
        attention_out_bias,
        attn_gain,
        attn_shift,
        feedforward_in_weight,
        feedforward_hidden_bias,
        feedforward_out_weight,
        feedforward_out_bias,
        ffn_gain,
        ffn_shift,
    ) = params
    _, saved_rows = layer_forward(params, input_rows, lengths)
    (
        qkv_heads,
        attn_prob,
        context_rows,
        residual_one,
        normalized_reduced_rows,
        hidden_preactivation,
        gelu_activated_rows,
        residual_two,
        valid_rows,
    ) = saved_rows
    seq_count, seq_len, model_width = input_rows.shape
    head_count = model_width // HEAD_DIM
    grad_result = grad_out * valid_rows
    grad_two, ffn_gain_grad, ffn_shift_grad = norm_pullback(
        residual_two, ffn_gain.astype(jnp.float32), ffn_shift.astype(jnp.float32), grad_result
    )
    feedforward_gradient = grad_two.astype(jnp.bfloat16)
    down_weight_grad = jnp.einsum(
        "inu,inm->um", gelu_activated_rows, feedforward_gradient, preferred_element_type=jnp.float32
    )
    down_bias_grad = jnp.sum(feedforward_gradient.astype(jnp.float32), axis=(0, 1))
    activation_gradient = jnp.einsum(
        "tjx,ux->tju",
        feedforward_gradient,
        feedforward_out_weight,
        preferred_element_type=jnp.float32,
    )
    _, gelu_pull = jax.vjp(gelu_exact, hidden_preactivation)
    preactivation_gradient = gelu_pull(activation_gradient)[0].astype(jnp.bfloat16)
    up_weight_grad = jnp.einsum(
        "hir,him->rm",
        normalized_reduced_rows,
        preactivation_gradient,
        preferred_element_type=jnp.float32,
    )
    up_bias_grad = jnp.sum(preactivation_gradient.astype(jnp.float32), axis=(0, 1))
    grad_normed = grad_two + jnp.einsum(
        "hzn,rn->hzr",
        preactivation_gradient,
        feedforward_in_weight,
        preferred_element_type=jnp.float32,
    )
    grad_one, attn_gain_grad, attn_shift_grad = norm_pullback(
        residual_one, attn_gain.astype(jnp.float32), attn_shift.astype(jnp.float32), grad_normed
    )
    attention_gradient = grad_one.astype(jnp.bfloat16)
    proj_weight_grad = jnp.einsum(
        "upb,uph->bh", context_rows, attention_gradient, preferred_element_type=jnp.float32
    )
    proj_bias_grad = jnp.sum(attention_gradient.astype(jnp.float32), axis=(0, 1))
    grad_context = jnp.einsum(
        "rbv,av->rba", attention_gradient, attention_out_weight, preferred_element_type=jnp.float32
    )
    grad_context = grad_context.astype(jnp.bfloat16).reshape(
        seq_count, seq_len, head_count, HEAD_DIM
    )
    query_rows = qkv_heads[:, :, 0]
    key_rows = qkv_heads[:, :, 1]
    value_rows = qkv_heads[:, :, 2]
    grad_prob = jnp.einsum(
        "sqhd,skhd->shqk", grad_context, value_rows, preferred_element_type=jnp.float32
    )
    grad_values = jnp.einsum(
        "shqk,sqhd->skhd",
        attn_prob.astype(jnp.bfloat16),
        grad_context,
        preferred_element_type=jnp.float32,
    )
    prob_dot = jnp.sum(attn_prob * grad_prob, axis=-1, keepdims=True)
    grad_raw = (attn_prob * (grad_prob - prob_dot)).astype(jnp.bfloat16)
    grad_queries = (
        jnp.einsum("shqk,skhd->sqhd", grad_raw, key_rows, preferred_element_type=jnp.float32)
        * score_scale
    )
    grad_keys = (
        jnp.einsum("shqk,sqhd->skhd", grad_raw, query_rows, preferred_element_type=jnp.float32)
        * score_scale
    )
    projected_gradient = jnp.stack([grad_queries, grad_keys, grad_values], axis=2)
    projected_gradient = projected_gradient.reshape(seq_count, seq_len, 3 * model_width).astype(
        jnp.bfloat16
    )
    qkv_weight_grad = jnp.einsum(
        "qjb,qjc->bc", input_rows, projected_gradient, preferred_element_type=jnp.float32
    )
    bias_sums = jnp.sum(projected_gradient.astype(jnp.float32), axis=(0, 1))
    query_bias_grad = bias_sums[:model_width]
    value_bias_grad = bias_sums[2 * model_width :]
    grad_inputs = grad_one + jnp.einsum(
        "ncf,yf->ncy",
        projected_gradient,
        query_key_value_weight,
        preferred_element_type=jnp.float32,
    )
    weight_grads = (
        qkv_weight_grad,
        query_bias_grad,
        value_bias_grad,
        proj_weight_grad,
        proj_bias_grad,
        attn_gain_grad,
        attn_shift_grad,
        up_weight_grad,
        up_bias_grad,
        down_weight_grad,
        down_bias_grad,
        ffn_gain_grad,
        ffn_shift_grad,
    )
    return (grad_inputs.astype(jnp.bfloat16), weight_grads)


def pack_flat(arrays):
    flat_grads = jnp.concatenate([member.reshape(-1) for member in arrays])
    return flat_grads


def unpack_flat(flat_grads, templates):
    pieces = []
    offset = 0
    for template in templates:
        entries = template.size
        pieces.append(flat_grads[offset : offset + entries].reshape(template.shape))
        offset = offset + entries
    return tuple(pieces)


def body(
    questions,
    passages,
    cot_questions,
    cot_passages,
    len_questions,
    len_passages,
    positive,
    query_key_value_weight,
    query_bias,
    value_bias,
    attention_out_weight,
    attention_out_bias,
    attn_gain,
    attn_shift,
    feedforward_in_weight,
    feedforward_hidden_bias,
    feedforward_out_weight,
    feedforward_out_bias,
    ffn_gain,
    ffn_shift,
):
    weights = (
        query_key_value_weight,
        query_bias,
        value_bias,
        attention_out_weight,
        attention_out_bias,
        attn_gain,
        attn_shift,
        feedforward_in_weight,
        feedforward_hidden_bias,
        feedforward_out_weight,
        feedforward_out_bias,
        ffn_gain,
        ffn_shift,
    )
    question_params = tuple((member[0] for member in weights))
    passage_params = tuple((member[1] for member in weights))
    local_count = questions.shape[0]
    question_out, _ = layer_forward(question_params, questions, len_questions)
    passage_out, _ = layer_forward(passage_params, passages, len_passages)
    question_low = question_out.astype(jnp.bfloat16)
    passage_low = passage_out.astype(jnp.bfloat16)
    question_cls = question_low[:, 0]
    passage_cls = passage_low[:, 0]
    all_passage_cls = lax.all_gather(passage_cls, "dp", axis=0, tiled=True)
    first_row = lax.axis_index("dp") * local_count
    logits = (
        jnp.einsum("qd,pd->qp", question_cls, all_passage_cls, preferred_element_type=jnp.float32)
        * score_scale
    )
    own_positive = lax.dynamic_slice_in_dim(positive, first_row, local_count)
    columns = jnp.arange(logits.shape[1], dtype=jnp.int32)
    positive_hot = (columns[None, :] == own_positive[:, None]).astype(jnp.float32)
    row_top = jnp.max(logits, axis=1, keepdims=True)
    log_total = row_top + jnp.log(jnp.sum(jnp.exp(logits - row_top), axis=1, keepdims=True))
    loss_rows = log_total[:, 0] - jnp.sum(logits * positive_hot, axis=1)
    grad_logits = (jnp.exp(logits - log_total) - positive_hot).astype(jnp.bfloat16)
    grad_cls_q = (
        jnp.einsum("qp,pd->qd", grad_logits, all_passage_cls, preferred_element_type=jnp.float32)
        * score_scale
    )
    grad_cls_p = lax.psum_scatter(
        jnp.einsum("qp,qd->pd", grad_logits, question_cls, preferred_element_type=jnp.float32)
        * score_scale,
        "dp",
        scatter_dimension=0,
        tiled=True,
    )
    grad_out_q = cot_questions.astype(jnp.float32).at[:, 0].add(grad_cls_q)
    grad_out_p = cot_passages.astype(jnp.float32).at[:, 0].add(grad_cls_p)
    grad_in_q, question_grads = layer_backward(
        question_params, questions, len_questions, grad_out_q
    )
    grad_in_p, passage_grads = layer_backward(passage_params, passages, len_passages, grad_out_p)
    stacked = tuple(
        (
            jnp.stack([question_part, passage_part])
            for question_part, passage_part in zip(question_grads, passage_grads)
        )
    )
    shares = lax.psum_scatter(pack_flat(stacked), "dp", scatter_dimension=0, tiled=True)
    summed = unpack_flat(lax.all_gather(shares, "dp", axis=0, tiled=True), stacked)
    return (loss_rows, question_low, passage_low, grad_in_q, grad_in_p) + summed


def solution(mesh):
    return jax.shard_map(
        body,
        mesh=mesh,
        in_specs=(
            P("dp", None, None),
            P("dp", None, None),
            P("dp", None, None),
            P("dp", None, None),
            P("dp"),
            P("dp"),
            P(),
            P(),
            P(),
            P(),
            P(),
            P(),
            P(),
            P(),
            P(),
            P(),
            P(),
            P(),
            P(),
            P(),
        ),
        out_specs=(
            P("dp"),
            P("dp", None, None),
            P("dp", None, None),
            P("dp", None, None),
            P("dp", None, None),
            P(),
            P(),
            P(),
            P(),
            P(),
            P(),
            P(),
            P(),
            P(),
            P(),
            P(),
            P(),
            P(),
        ),
        check_vma=False,
    )
```

profile of v0, /device:TPU:0, one launch (start us, length us, event | category | flops | bytes accessed | tf_op | source)
XLA Modules:
  0.0 641.5 jit_solution(1127631216348365106)
XLA Ops:
  8.1 1.4 fusion.14
  13.1 1.6 multiply_convert_fusion.3
  16.3 2.0 add_convert_fusion.1
  18.3 2.7 copy.89
  21.9 2.0 fusion.100
  24.7 1.7 copy-done.3
  27.8 3.8 multiply_convert_fusion.1
  35.1 43.6 %all-gather = bf16[160,1,256]{2,1,0:T(2,128)(2,1)S(1)} all-gather(bf16[5,1,256]{2,1,0:T(2,128)(2,1)S(1)} %slice.361), channel_id=2, replica_groups=mesh['dp'=32] {'dp'}, dimensions={0}, use_global_device_ids=true | all-gather | bytes 84480 | tf_op jit(solution)/shard_map/all_gather | solution.py:314
  83.6 1.6 multiply_reduce_fusion.9
  87.6 2.9 convert_reduce_fusion.4
  90.5 1.6 convolution_bitcast_fusion.4
  96.6 1.9 reshape.635
  98.5 1.5 multiply_reduce_fusion.8
  102.2 1.5 convolution_bitcast_fusion.2
  104.0 1.7 copy.99
  105.7 2.0 convert_element_type.419
  107.8 1.3 convolution_bitcast_fusion.5
  109.1 2.3 convert_element_type.421
  111.5 87.6 %all-reduce.9.cloned.1.call-done = f32[160,256]{1,0:T(8,128)} async-done(((f32[160,256]{1,0:T(8,128)}), f32[160,256]{1,0:T(8,128)}) %all-reduce.9.cloned.1.call-update) | async-done | bytes 163856
  200.6 1.4 scatter-add.9
  202.0 2.1 multiply_reduce_fusion.1
  206.6 5.5 convert_reduce_fusion
  213.4 1.4 multiply_reduce_fusion.2
  223.4 1.9 convolution_bitcast_fusion.1
  227.5 1.5 convert_reduce_fusion.1
  229.3 1.7 copy.103
  234.0 3.0 copy.105
  237.0 2.4 reshape.638
  239.5 2.8 constant_dynamic-update-slice_fusion.9
  242.6 2.4 copy.138
  245.1 1.3 constant_dynamic-update-slice_fusion.8
  246.4 1.3 constant_dynamic-update-slice_fusion.7
  248.6 1.3 constant_dynamic-update-slice_fusion.5
  251.2 1.3 constant_dynamic-update-slice_fusion.3
  252.5 18.1 %dynamic-update-slice.14 = f32[1579008]{0:T(1024)} dynamic-update-slice(f32[1579008]{0:T(1024)} %constant_dynamic-update-slice_fusion.3, f32[524288]{0:T(1024)S(1)} %bitcast.289, s32[]{} %constant.140) | dynamic-update-slice | bytes 4194308
  270.6 1.3 bitcast_dynamic-update-slice_fusion
  271.9 18.8 %dynamic-update-slice.16 = f32[1579008]{0:T(1024)} dynamic-update-slice(f32[1579008]{0:T(1024)} %bitcast_dynamic-update-slice_fusion, f32[524288]{0:T(1024)} %bitcast.290, s32[]{} %constant.142) | dynamic-update-slice | bytes 4194308
  290.7 1.3 constant_dynamic-update-slice_fusion.2
  294.7 159.1 %all-reduce.11.cloned.1.call-done = f32[1579008]{0:T(1024)} async-done(((f32[1579008]{0:T(1024)}), f32[1579008]{0:T(1024)}) %all-reduce.11.cloned.1.call-update) | async-done | bytes 6316048
  453.7 2.8 broadcast.298
  456.6 1.9 dynamic-slice_dynamic-update-slice_fusion
  460.9 3.2 fusion.11
  464.0 152.2 %all-reduce.7.cloned.1.call-done = f32[1579008]{0:T(1024)} async-done(((f32[1579008]{0:T(1024)}), f32[1579008]{0:T(1024)}) %all-reduce.7.cloned.1.call-update) | async-done | bytes 6316048
  616.3 3.8 fusion.96
  620.1 2.7 reshape.653
  622.8 1.6 reshape.655
  624.4 1.4 slice-done
  625.8 1.4 reshape.651
  (362 shorter events, 60.5 us)
Async XLA Ops:
  7.2 191.9 %all-reduce.9.cloned.1.call-start = ((), (), s32[]{:S(2)}) async-start(), calls=%async_computation.1 | async-start | bytes 327680
  10.6 5.0 copy-start.53
  13.0 18.6 %copy-start.64 = (f32[1,256]{1,0:T(1,128)}, f32[1,256]{1,0:T(1,128)S(1)}, u32[]{:S(2)}) copy-start(f32[1,256]{1,0:T(1,128)S(1)} %get-tuple-element.108) | copy-start | bytes 3076
  13.1 18.5 %copy-start.74 = (f32[1,256]{1,0:T(1,128)}, f32[1,256]{1,0:T(1,128)S(1)}, u32[]{:S(2)}) copy-start(f32[1,256]{1,0:T(1,128)S(1)} %get-tuple-element.110) | copy-start | bytes 3076
  13.1 14.2 %copy-start.89 = (f32[1,1024]{1,0:T(1,128)}, f32[1,1024]{1,0:T(1,128)S(1)}, u32[]{:S(2)}) copy-start(f32[1,1024]{1,0:T(1,128)S(1)} %get-tuple-element.100) | copy-start | bytes 12292
  15.2 3.0 copy-start.48
  15.4 2.8 copy-start.61
  15.4 2.8 copy-start.54
  15.5 18.2 %copy-start.66 = (f32[1,256]{1,0:T(1,128)}, f32[1,256]{1,0:T(1,128)S(1)}, u32[]{:S(2)}) copy-start(f32[1,256]{1,0:T(1,128)S(1)} %get-tuple-element.102) | copy-start | bytes 3076
  16.2 4.7 copy-start.37
  20.9 3.1 copy-start.1
  21.9 11.7 %copy-start.44 = (f32[5,256]{1,0:T(8,128)}, f32[5,256]{1,0:T(8,128)S(1)}, u32[]{:S(2)}) copy-start(f32[5,256]{1,0:T(8,128)S(1)} %get-tuple-element.117) | copy-start | bytes 15364
  27.3 4.3 copy-start.49
  27.3 4.3 copy-start.42
  27.8 3.8 copy-start.98
  33.2 45.9 %copy-start.105 = (s32[160]{0:T(256)S(1)}, s32[160]{0:T(256)}, u32[]{:S(2)}) copy-start(s32[160]{0:T(256)} %param.30) | copy-start | bytes 1924
  80.8 372.9 %all-reduce.11.cloned.1.call-start = ((), (), s32[]{:S(2)}) async-start(), calls=%async_computation.2 | async-start | bytes 12632064
  83.5 4.1 copy-start.99
  87.6 2.9 copy-start.38
  87.6 2.9 copy-start.5
  87.6 2.9 copy-start.58
  87.6 2.9 copy-start.70
  87.6 2.9 copy-start.81
  87.6 2.9 copy-start.94
  90.5 2.6 copy-start.60
  92.1 2.7 copy-start.15
  93.1 5.4 copy-start.32
  96.6 3.4 copy-start.73
  104.0 3.8 copy-start.41
  107.7 96.4 %copy-start.12 = (bf16[5,64,768]{2,1,0:T(8,128)(2,1)}, bf16[5,64,768]{2,1,0:T(8,128)(2,1)S(1)}, u32[]{:S(2)}) copy-start(bf16[5,64,768]{2,1,0:T(8,128)(2,1)S(1)} %convert_element_type.419) | copy-start | bytes 1474564
  107.8 94.3 %copy-start.45 = (f32[5,256]{1,0:T(8,128)S(1)}, f32[5,256]{1,0:T(8,128)}, u32[]{:S(2)}) copy-start(f32[5,256]{1,0:T(8,128)} %copy-done.44) | copy-start | bytes 15364
  107.8 94.3 %copy-start.47 = (f32[5,256]{1,0:T(8,128)S(1)}, f32[5,256]{1,0:T(8,128)}, u32[]{:S(2)}) copy-start(f32[5,256]{1,0:T(8,128)} %copy-done.46) | copy-start | bytes 15364
  107.8 94.2 %copy-start.67 = (f32[1,256]{1,0:T(1,128)S(1)}, f32[1,256]{1,0:T(1,128)}, u32[]{:S(2)}) copy-start(f32[1,256]{1,0:T(1,128)} %copy-done.66) | copy-start | bytes 3076
  109.1 95.1 %copy-start.52 = (f32[5,256]{1,0:T(8,128)S(1)}, f32[5,256]{1,0:T(8,128)}, u32[]{:S(2)}) copy-start(f32[5,256]{1,0:T(8,128)} %copy-done.51) | copy-start | bytes 15364
  206.6 5.5 copy-start.43
  206.6 5.5 copy-start.65
  206.6 5.5 copy-start.75
  206.6 6.8 %copy-start.104 = (bf16[2,256,1024]{2,1,0:T(8,128)(2,1)S(1)}, bf16[2,256,1024]{2,1,0:T(8,128)(2,1)}, u32[]{:S(2)}) copy-start(bf16[2,256,1024]{2,1,0:T(8,128)(2,1)} %param.38) | copy-start | bytes 3145732
  212.1 5.7 slice-start.2
  213.4 4.5 slice-start.3
  239.5 2.8 copy-start.79
  239.5 2.9 copy-start.92
  239.5 2.9 copy-start.91
  239.5 2.9 copy-start.23
  239.5 2.9 copy-start.25
  242.6 5.1 copy-start.10
  242.6 9.9 %copy-start.88 = (f32[1024]{0:T(1024)S(1)}, f32[1024]{0:T(1024)}, u32[]{:S(2)}) copy-start(f32[1024]{0:T(1024)} %get-tuple-element.145) | copy-start | bytes 12292
  294.6 321.7 %all-reduce.7.cloned.1.call-start = ((), (), s32[]{:S(2)}) async-start(), calls=%async_computation | async-start | bytes 12632064
  (69 other events, 106.4 us)
Sparse Core Ops, SparseCore 0:
  81.0 118.0 all-reduce.8
  294.7 158.9 all-reduce.10
  459.5 156.7 all-reduce.6
where the time goes:
time: 646 us; the launch traced here: 642 us
  waiting for transfers between devices  399 us (62%)
  local copies, waits for them, and re-layouts  113 us (17%)
  matrix products  45.7 us (7%)
  blocking collectives  43.6 us (7%)
  other arithmetic  24.6 us (4%)
  between operations  15.5 us (2%)
    unnamed x6, waiting for transfers between devices  399 us
    unnamed x251, local copies, waits for them, and re-layouts  73.1 us
    all_gather x1, blocking collectives, body(): all_passage_cls = lax.all_gather(passage_cls, 'dp', axis=0, tiled=True)  43.6 us
  transfers between devices with their start and end apart: 3, of which 3 were waited for; matrix products, arithmetic and copies ran while one was open for 5% of the time, Pallas kernels for 0%

commit v1 on v0

v1 whole, which is shorter than its diff:
```python
import functools

import jax
import jax.numpy as jnp
from jax import lax
from jax.experimental import pallas as pl
from jax.experimental.pallas import tpu as pltpu
from jax.sharding import PartitionSpec as P

HEAD_DIM = 64
WIDTH = 256
HEADS = WIDTH // HEAD_DIM
HIDDEN = 1024
BLOCKS = HIDDEN // WIDTH
PAD = 8
VECTOR_ROWS = 16
GROUP_ROWS = 13 * WIDTH
ln_eps = 1e-06
score_scale = 0.125
masked_score = -1e30
f32 = jnp.float32
bf16 = jnp.bfloat16

QUERY_BIAS, VALUE_BIAS, PROJ_BIAS, ATTN_GAIN, ATTN_SHIFT, DOWN_BIAS, FFN_GAIN, FFN_SHIFT = range(8)
UP_BIAS = 8


def dot(a, b):
    return lax.dot_general(a, b, (((1,), (0,)), ((), ())), preferred_element_type=f32)


def dot_nt(a, b):
    return lax.dot_general(a, b, (((1,), (1,)), ((), ())), preferred_element_type=f32)


def dot_tn(a, b):
    return lax.dot_general(a, b, (((0,), (0,)), ((), ())), preferred_element_type=f32)


def row_loop(rows, chunk, step):
    def body(index, carry):
        step(pl.multiple_of(index * chunk, chunk))
        return carry

    lax.fori_loop(0, rows // chunk, body, 0)


def vector(ref, which):
    return ref[...].astype(f32)[which : which + 1]


def lane_head(rows):
    return lax.broadcasted_iota(jnp.int32, (rows, WIDTH), 1) // HEAD_DIM


def stack_heads(values):
    head = lane_head(values.shape[0])
    wide = values.astype(f32)
    return jnp.concatenate(
        [jnp.where(head == h, wide, 0.0).astype(bf16) for h in range(HEADS)], axis=0
    )


def pick_heads(stacked, rows):
    head = lane_head(rows)
    result = stacked[:rows]
    for h in range(1, HEADS):
        result = jnp.where(head == h, stacked[h * rows : (h + 1) * rows], result)
    return result


def forward_kernel(
    which, seqs, length,
    len_ref, x_ref, wqkv_ref, qb_ref, vb_ref, wo_ref, ob_ref, g1_ref, b1_ref,
    w1_ref, hb_ref, w2_ref, fb_ref, g2_ref, b2_ref,
    out_ref, cls_ref, qkv_ref, p_ref, ctx_ref, n1_ref, r1_ref, nb_ref, gp_ref, act_ref, n2_ref, r2_ref,
    wide_ref, score_ref, prob_ref,
):
    rows = seqs * length
    step = pl.program_id(0)
    x = x_ref[...]
    qkv_ref[:, :WIDTH] = (dot(x, wqkv_ref[:, :WIDTH]) + vector(qb_ref, which)).astype(bf16)
    qkv_ref[:, WIDTH : 2 * WIDTH] = dot(x, wqkv_ref[:, WIDTH : 2 * WIDTH]).astype(bf16)
    qkv_ref[:, 2 * WIDTH :] = (dot(x, wqkv_ref[:, 2 * WIDTH :]) + vector(vb_ref, which)).astype(bf16)
    stack_rows = HEADS * length
    for s in range(seqs):
        span = slice(s * length, (s + 1) * length)
        size = len_ref[step * seqs + s]
        queries = stack_heads(qkv_ref[span, :WIDTH])
        score_ref[...] = dot_nt(queries, qkv_ref[span, WIDTH : 2 * WIDTH])

        def softmax(row):
            part = score_ref[pl.ds(row, 32), :] * score_scale
            key = lax.broadcasted_iota(jnp.int32, part.shape, 1)
            part = jnp.where(key < size, part, masked_score)
            part = jnp.exp(part - jnp.max(part, axis=1, keepdims=True))
            prob = part * (1.0 / jnp.sum(part, axis=1, keepdims=True))
            p_ref[pl.ds(s * stack_rows + row, 32), :] = prob
            prob_ref[pl.ds(row, 32), :] = prob.astype(bf16)

        row_loop(stack_rows, 32, softmax)
        context = dot(prob_ref[...], qkv_ref[span, 2 * WIDTH :])
        ctx_ref[span, :] = pick_heads(context, length).astype(bf16)
    n2_ref[...] = dot(ctx_ref[...], wo_ref[...])
    ob, g1, b1 = vector(ob_ref, which), vector(g1_ref, which), vector(b1_ref, which)

    def first_norm(row):
        here = pl.ds(row, 32)
        value = x_ref[here, :].astype(f32) + (n2_ref[here, :] + ob)
        centered = value - jnp.mean(value, axis=1, keepdims=True)
        inverse = lax.rsqrt(jnp.mean(centered * centered, axis=1, keepdims=True) + ln_eps)
        unit = centered * inverse
        n1_ref[here, :] = unit
        r1_ref[here, :] = inverse
        nb_ref[here, :] = (unit * g1 + b1).astype(bf16)

    row_loop(rows, 32, first_norm)
    wide_ref[...] = dot(nb_ref[...], w1_ref[...])
    hb = vector(hb_ref, which)

    def gelu(row):
        here = pl.ds(row, 16)
        for j in range(BLOCKS):
            lanes = slice(j * WIDTH, (j + 1) * WIDTH)
            value = wide_ref[here, lanes] + hb[:, lanes]
            cumulative = 0.5 + 0.5 * lax.erf(value * 0.7071067811865476)
            density = jnp.exp(value * value * -0.5) * 0.3989422804014327
            act_ref[here, lanes] = (value * cumulative).astype(bf16)
            gp_ref[here, lanes] = cumulative + value * density

    row_loop(rows, 16, gelu)
    n2_ref[...] = dot(act_ref[...], w2_ref[...])
    fb, g2, b2 = vector(fb_ref, which), vector(g2_ref, which), vector(b2_ref, which)

    for s in range(seqs):
        size = len_ref[step * seqs + s]

        def second_norm(row):
            here = pl.ds(s * length + row, 32)
            value = (n1_ref[here, :] * g1 + b1) + (n2_ref[here, :] + fb)
            centered = value - jnp.mean(value, axis=1, keepdims=True)
            inverse = lax.rsqrt(jnp.mean(centered * centered, axis=1, keepdims=True) + ln_eps)
            unit = centered * inverse
            n2_ref[here, :] = unit
            r2_ref[here, :] = inverse
            position = row + lax.broadcasted_iota(jnp.int32, (32, WIDTH), 0)
            out_ref[here, :] = jnp.where(position < size, unit * g2 + b2, 0.0).astype(bf16)

        row_loop(length, 32, second_norm)
        cls_ref[pl.ds(step * seqs + s, 1), :] = out_ref[s * length : s * length + 16, :].astype(f32)[:1]


def add_row(vec_ref, row, values):
    vec_ref[row : row + 1, :] = vec_ref[row : row + 1, :] + jnp.sum(values, axis=0, keepdims=True)


def ffn_phase(which, seqs, length, first, len_ref, cls_ref, cot_ref, n2_ref, r2_ref, gp_ref, w2_ref, g2_ref, two_ref, gffn_ref, gpre_ref, vec_ref, wide_ref):
    g2 = vector(g2_ref, which)
    for s in range(seqs):
        size = len_ref[first + s]
        cls_row = cls_ref[pl.ds(first + s, 1), :]

        def norm_back(row):
            here = pl.ds(s * length + row, 32)
            position = row + lax.broadcasted_iota(jnp.int32, (32, WIDTH), 0)
            grad = cot_ref[here, :].astype(f32) + jnp.where(position == 0, cls_row, 0.0)
            grad = jnp.where(position < size, grad, 0.0)
            unit = n2_ref[here, :]
            scaled = grad * g2
            first_mean = jnp.mean(scaled, axis=1, keepdims=True)
            second_mean = jnp.mean(scaled * unit, axis=1, keepdims=True)
            two = r2_ref[here, :] * (scaled - first_mean - unit * second_mean)
            low = two.astype(bf16)
            two_ref[here, :] = two
            gffn_ref[here, :] = low
            add_row(vec_ref, FFN_GAIN, grad * unit)
            add_row(vec_ref, FFN_SHIFT, grad)
            add_row(vec_ref, DOWN_BIAS, low.astype(f32))

        row_loop(length, 32, norm_back)
    wide_ref[...] = dot_nt(gffn_ref[...], w2_ref[...])

    def gelu_back(row):
        here = pl.ds(row, 16)
        for j in range(BLOCKS):
            lanes = slice(j * WIDTH, (j + 1) * WIDTH)
            low = (wide_ref[here, lanes] * gp_ref[here, lanes]).astype(bf16)
            gpre_ref[here, lanes] = low
            add_row(vec_ref, UP_BIAS + j, low.astype(f32))

    row_loop(seqs * length, 16, gelu_back)


def attn_norm_phase(which, rows, gpre_ref, w1_ref, two_ref, n1_ref, r1_ref, g1_ref, wo_ref, one_ref, gatt_ref, dctx_ref, vec_ref):
    one_ref[...] = dot_nt(gpre_ref[...], w1_ref[...])
    g1 = vector(g1_ref, which)

    def norm_back(row):
        here = pl.ds(row, 32)
        grad = two_ref[here, :] + one_ref[here, :]
        unit = n1_ref[here, :]
        scaled = grad * g1
        first_mean = jnp.mean(scaled, axis=1, keepdims=True)
        second_mean = jnp.mean(scaled * unit, axis=1, keepdims=True)
        one = r1_ref[here, :] * (scaled - first_mean - unit * second_mean)
        low = one.astype(bf16)
        one_ref[here, :] = one
        gatt_ref[here, :] = low
        add_row(vec_ref, ATTN_GAIN, grad * unit)
        add_row(vec_ref, ATTN_SHIFT, grad)
        add_row(vec_ref, PROJ_BIAS, low.astype(f32))

    row_loop(rows, 32, norm_back)
    dctx_ref[...] = dot_nt(gatt_ref[...], wo_ref[...]).astype(bf16)


def attn_core_phase(seqs, length, dctx_ref, qkv_ref, p_ref, gqkv_ref, vec_ref, dp_ref, ds_ref, pb_ref):
    stack_rows = HEADS * length
    for s in range(seqs):
        span = slice(s * length, (s + 1) * length)
        context = stack_heads(dctx_ref[span, :])
        dp_ref[...] = dot_nt(context, qkv_ref[span, 2 * WIDTH :])

        def softmax_back(row):
            prob = p_ref[pl.ds(s * stack_rows + row, 32), :]
            grad = dp_ref[pl.ds(row, 32), :]
            inner = jnp.sum(prob * grad, axis=1, keepdims=True)
            ds_ref[pl.ds(row, 32), :] = (prob * (grad - inner)).astype(bf16)
            pb_ref[pl.ds(row, 32), :] = prob.astype(bf16)

        row_loop(stack_rows, 32, softmax_back)
        queries = stack_heads(qkv_ref[span, :WIDTH])
        grad_q = (pick_heads(dot(ds_ref[...], qkv_ref[span, WIDTH : 2 * WIDTH]), length) * score_scale).astype(bf16)
        gqkv_ref[span, :WIDTH] = grad_q
        add_row(vec_ref, QUERY_BIAS, grad_q.astype(f32))
        gqkv_ref[span, WIDTH : 2 * WIDTH] = (dot_tn(ds_ref[...], queries) * score_scale).astype(bf16)
        grad_v = dot_tn(pb_ref[...], context).astype(bf16)
        gqkv_ref[span, 2 * WIDTH :] = grad_v
        add_row(vec_ref, VALUE_BIAS, grad_v.astype(f32))


def first_step(vec_ref):
    @pl.when(pl.program_id(0) == 0)
    def _():
        vec_ref[...] = jnp.zeros_like(vec_ref)


def ffn_kernel(which, length, len_ref, cls_ref, cot_ref, n2_ref, r2_ref, gp_ref, w2_ref, g2_ref, two_ref, gffn_ref, gpre_ref, vec_ref, wide_ref):
    first_step(vec_ref)
    ffn_phase(which, 1, length, pl.program_id(0), len_ref, cls_ref, cot_ref, n2_ref, r2_ref, gp_ref, w2_ref, g2_ref, two_ref, gffn_ref, gpre_ref, vec_ref, wide_ref)


def ffn_weight_kernel(act_ref, gffn_ref, nb_ref, gpre_ref, up_ref, down_ref):
    down_ref[...] = dot_tn(act_ref[...], gffn_ref[...]).astype(bf16)
    up_ref[...] = dot_tn(nb_ref[...], gpre_ref[...]).astype(bf16)


def attn_norm_kernel(which, length, gpre_ref, w1_ref, two_ref, n1_ref, r1_ref, g1_ref, wo_ref, ctx_ref, one_ref, dctx_ref, vec_ref, proj_ref, gatt_ref, acc_ref):
    first_step(vec_ref)
    first_step(acc_ref)
    attn_norm_phase(which, length, gpre_ref, w1_ref, two_ref, n1_ref, r1_ref, g1_ref, wo_ref, one_ref, gatt_ref, dctx_ref, vec_ref)
    acc_ref[...] += dot_tn(ctx_ref[...], gatt_ref[...])

    @pl.when(pl.program_id(0) == pl.num_programs(0) - 1)
    def _():
        proj_ref[...] = acc_ref[...].astype(bf16)


def attn_core_kernel(length, dctx_ref, qkv_ref, p_ref, x_ref, wqkv_ref, one_ref, gx_ref, vec_ref, dw_ref, gqkv_ref, dp_ref, ds_ref, pb_ref, acc_ref):
    first_step(vec_ref)
    first_step(acc_ref)
    attn_core_phase(1, length, dctx_ref, qkv_ref, p_ref, gqkv_ref, vec_ref, dp_ref, ds_ref, pb_ref)
    gx_ref[...] = (one_ref[...] + dot_nt(gqkv_ref[...], wqkv_ref[...])).astype(bf16)
    for j in range(3):
        acc_ref[j * WIDTH : (j + 1) * WIDTH, :] += dot_tn(x_ref[...], gqkv_ref[:, j * WIDTH : (j + 1) * WIDTH])

    @pl.when(pl.program_id(0) == pl.num_programs(0) - 1)
    def _():
        dw_ref[...] = acc_ref[...].astype(bf16)


def question_back_kernel(
    which, seqs, length,
    len_ref, cls_ref, cot_ref, x_ref, qkv_ref, p_ref, ctx_ref, n1_ref, r1_ref, nb_ref, gp_ref, act_ref, n2_ref, r2_ref,
    wqkv_ref, wo_ref, g1_ref, w1_ref, w2_ref, g2_ref,
    gx_ref, pack_ref,
    two_ref, gffn_ref, gpre_ref, vec_ref, wide_ref, one_ref, gatt_ref, dctx_ref, gqkv_ref, dp_ref, ds_ref, pb_ref,
):
    rows = seqs * length
    vec_ref[...] = jnp.zeros_like(vec_ref)
    ffn_phase(which, seqs, length, 0, len_ref, cls_ref, cot_ref, n2_ref, r2_ref, gp_ref, w2_ref, g2_ref, two_ref, gffn_ref, gpre_ref, vec_ref, wide_ref)
    for j in range(BLOCKS):
        lanes = slice(j * WIDTH, (j + 1) * WIDTH)
        pack_ref[(4 + j) * WIDTH : (5 + j) * WIDTH, :] = dot_tn(nb_ref[...], gpre_ref[:, lanes]).astype(bf16)
        pack_ref[(8 + j) * WIDTH : (9 + j) * WIDTH, :] = dot_tn(act_ref[:, lanes], gffn_ref[...]).astype(bf16)
    attn_norm_phase(which, rows, gpre_ref, w1_ref, two_ref, n1_ref, r1_ref, g1_ref, wo_ref, one_ref, gatt_ref, dctx_ref, vec_ref)
    pack_ref[3 * WIDTH : 4 * WIDTH, :] = dot_tn(ctx_ref[...], gatt_ref[...]).astype(bf16)
    attn_core_phase(seqs, length, dctx_ref, qkv_ref, p_ref, gqkv_ref, vec_ref, dp_ref, ds_ref, pb_ref)
    for j in range(3):
        lanes = slice(j * WIDTH, (j + 1) * WIDTH)
        pack_ref[j * WIDTH : (j + 1) * WIDTH, :] = dot_tn(x_ref[...], gqkv_ref[:, lanes]).astype(bf16)
    gx_ref[...] = (one_ref[...] + dot_nt(gqkv_ref[...], wqkv_ref[...])).astype(bf16)
    pack_ref[12 * WIDTH :, :] = jnp.zeros((WIDTH, WIDTH), bf16)
    pack_ref[12 * WIDTH : 12 * WIDTH + VECTOR_ROWS, :] = vec_ref[...].astype(bf16)


def loss_kernel(local, me_ref, all_ref, hot_ref, own_hot_ref, loss_ref, gq_ref, gp_ref, q_ref, p_ref):
    count = all_ref.shape[0]
    me = me_ref[0]
    wide = all_ref[...].astype(f32)
    q_ref[...] = wide[:, :PAD].reshape(count * PAD, WIDTH).astype(bf16)
    p_ref[...] = wide[:, PAD:].reshape(count * PAD, WIDTH).astype(bf16)
    own_q = all_ref[me][:PAD]
    own_p = all_ref[me][PAD:]
    logits = dot_nt(own_q, p_ref[...]) * score_scale
    column = lax.broadcasted_iota(jnp.int32, logits.shape, 1)
    logits = jnp.where(column % PAD < local, logits, masked_score)
    top = jnp.max(logits, axis=1, keepdims=True)
    total = top + jnp.log(jnp.sum(jnp.exp(logits - top), axis=1, keepdims=True))
    hot = (column == own_hot_ref[...]).astype(f32)
    loss_ref[...] = jnp.broadcast_to(total - jnp.sum(logits * hot, axis=1, keepdims=True), loss_ref.shape)
    grad = (jnp.exp(logits - total) - hot).astype(bf16)
    gq_ref[...] = dot(grad, p_ref[...]) * score_scale
    gp_ref[...] = jnp.zeros_like(gp_ref)
    block = 256 if count * PAD % 256 == 0 else count * PAD

    def part(index, carry):
        start = pl.multiple_of(index * block, block)
        queries = q_ref[pl.ds(start, block), :]
        scores = dot_nt(p_ref[...], queries) * score_scale
        row = lax.broadcasted_iota(jnp.int32, scores.shape, 0)
        scores = jnp.where(row % PAD < local, scores, masked_score)
        peak = jnp.max(scores, axis=0, keepdims=True)
        sums = peak + jnp.log(jnp.sum(jnp.exp(scores - peak), axis=0, keepdims=True))
        own = dot_nt(own_p, queries) * score_scale
        own_row = lax.broadcasted_iota(jnp.int32, own.shape, 0)
        own_lane = lax.broadcasted_iota(jnp.int32, own.shape, 1)
        own_hits = (own_row + me * PAD == hot_ref[:, pl.ds(start, block)]).astype(f32)
        own_grad = jnp.where(own_lane % PAD < local, jnp.exp(own - sums) - own_hits, 0.0)
        gp_ref[...] += dot(own_grad.astype(bf16), queries) * score_scale
        return carry

    lax.fori_loop(0, count * PAD // block, part, 0)


def unpack_kernel(q_ref, p_ref, qkv_ref, proj_ref, up_ref, down_ref, vec_ref):
    for which, ref in enumerate((q_ref, p_ref)):
        for j in range(3):
            qkv_ref[which, :, j * WIDTH : (j + 1) * WIDTH] = ref[j * WIDTH : (j + 1) * WIDTH, :].astype(f32)
        proj_ref[which] = ref[3 * WIDTH : 4 * WIDTH, :].astype(f32)
        for j in range(BLOCKS):
            up_ref[which, :, j * WIDTH : (j + 1) * WIDTH] = ref[(4 + j) * WIDTH : (5 + j) * WIDTH, :].astype(f32)
        down_ref[which] = ref[8 * WIDTH : 12 * WIDTH, :].astype(f32)
        vec_ref[which] = ref[12 * WIDTH : 12 * WIDTH + VECTOR_ROWS, :].astype(f32)


def smem():
    return pl.BlockSpec(memory_space=pltpu.SMEM)


def whole(shape):
    return pl.BlockSpec(shape, lambda i: (0,) * len(shape))


def rows_of(rows, columns):
    return pl.BlockSpec((rows, columns), lambda i: (i, 0))


def part_of(which, shape):
    return pl.BlockSpec((None,) + shape, lambda i: (which, 0, 0))


def params():
    return pltpu.CompilerParams(vmem_limit_bytes=56 * 1024 * 1024)


def shape(dims, kind):
    return jax.ShapeDtypeStruct(dims, kind)


def cost(flops, moved):
    return pl.CostEstimate(flops=flops, bytes_accessed=moved, transcendentals=0)


def pair(columns):
    return whole((2, columns))


def forward(which, steps, seqs, length, lengths, x, weights):
    wqkv, qb, vb, wo, ob, g1, b1, w1, hb, w2, fb, g2, b2 = weights
    rows = seqs * length
    total = steps * rows
    stack = HEADS * length
    kinds = [
        (WIDTH, bf16), (3 * WIDTH, bf16), (WIDTH, bf16), (WIDTH, f32), (1, f32), (WIDTH, bf16),
        (HIDDEN, f32), (HIDDEN, bf16), (WIDTH, f32), (1, f32),
    ]
    out_shape = [shape((total, c), k) for c, k in kinds]
    out_specs = [rows_of(rows, c) for c, _ in kinds]
    out_shape[1:1] = [shape((PAD, WIDTH), f32)]
    out_specs[1:1] = [whole((PAD, WIDTH))]
    out_shape[3:3] = [shape((steps * seqs * stack, length), f32)]
    out_specs[3:3] = [rows_of(seqs * stack, length)]
    return pl.pallas_call(
        functools.partial(forward_kernel, which, seqs, length),
        out_shape=out_shape,
        grid=(steps,),
        in_specs=[
            smem(), rows_of(rows, WIDTH), part_of(which, (WIDTH, 3 * WIDTH)), pair(WIDTH), pair(WIDTH),
            part_of(which, (WIDTH, WIDTH)), pair(WIDTH), pair(WIDTH), pair(WIDTH),
            part_of(which, (WIDTH, HIDDEN)), pair(HIDDEN), part_of(which, (HIDDEN, WIDTH)),
            pair(WIDTH), pair(WIDTH), pair(WIDTH),
        ],
        out_specs=out_specs,
        scratch_shapes=[
            pltpu.VMEM((rows, HIDDEN), f32),
            pltpu.VMEM((stack, length), f32),
            pltpu.VMEM((stack, length), bf16),
        ],
        compiler_params=params(),
        cost_estimate=cost(total * 2 * 800000, total * 12000),
        name="forward",
    )(lengths, x, wqkv, qb, vb, wo, ob, g1, b1, w1, hb, w2, fb, g2, b2)


def question_backward(which, seqs, length, lengths, cls_grad, cot, x, saved, weights):
    wqkv, qb, vb, wo, ob, g1, b1, w1, hb, w2, fb, g2, b2 = weights
    _, _, qkv, p, ctx, n1, r1, nb, gp, act, n2, r2 = saved
    rows = seqs * length
    stack = HEADS * length
    return pl.pallas_call(
        functools.partial(question_back_kernel, which, seqs, length),
        out_shape=[shape((rows, WIDTH), bf16), shape((GROUP_ROWS, WIDTH), bf16)],
        grid=(1,),
        in_specs=[
            smem(), whole((PAD, WIDTH)), rows_of(rows, WIDTH), rows_of(rows, WIDTH), rows_of(rows, 3 * WIDTH),
            rows_of(seqs * stack, length), rows_of(rows, WIDTH), rows_of(rows, WIDTH), rows_of(rows, 1),
            rows_of(rows, WIDTH), rows_of(rows, HIDDEN), rows_of(rows, HIDDEN), rows_of(rows, WIDTH), rows_of(rows, 1),
            part_of(which, (WIDTH, 3 * WIDTH)), part_of(which, (WIDTH, WIDTH)), pair(WIDTH),
            part_of(which, (WIDTH, HIDDEN)), part_of(which, (HIDDEN, WIDTH)), pair(WIDTH),
        ],
        out_specs=[rows_of(rows, WIDTH), rows_of(GROUP_ROWS, WIDTH)],
        scratch_shapes=[
            pltpu.VMEM((rows, WIDTH), f32), pltpu.VMEM((rows, WIDTH), bf16), pltpu.VMEM((rows, HIDDEN), bf16),
            pltpu.VMEM((VECTOR_ROWS, WIDTH), f32), pltpu.VMEM((rows, HIDDEN), f32), pltpu.VMEM((rows, WIDTH), f32),
            pltpu.VMEM((rows, WIDTH), bf16), pltpu.VMEM((rows, WIDTH), bf16), pltpu.VMEM((rows, 3 * WIDTH), bf16),
            pltpu.VMEM((stack, length), f32), pltpu.VMEM((stack, length), bf16), pltpu.VMEM((stack, length), bf16),
        ],
        compiler_params=params(),
        cost_estimate=cost(rows * 4 * 800000, rows * 12000),
        name="question_back",
    )(lengths, cls_grad, cot, x, qkv, p, ctx, n1, r1, nb, gp, act, n2, r2, wqkv, wo, g1, w1, w2, g2)


def passage_backward(which, steps, length, lengths, cls_grad, cot, x, saved, weights):
    wqkv, qb, vb, wo, ob, g1, b1, w1, hb, w2, fb, g2, b2 = weights
    _, _, qkv, p, ctx, n1, r1, nb, gp, act, n2, r2 = saved
    rows = length
    total = steps * rows
    stack = HEADS * length
    vec = shape((VECTOR_ROWS, WIDTH), f32)
    vec_spec = whole((VECTOR_ROWS, WIDTH))
    two, gffn, gpre, vec_a = pl.pallas_call(
        functools.partial(ffn_kernel, which, length),
        out_shape=[shape((total, WIDTH), f32), shape((total, WIDTH), bf16), shape((total, HIDDEN), bf16), vec],
        grid=(steps,),
        in_specs=[
            smem(), whole((PAD, WIDTH)), rows_of(rows, WIDTH), rows_of(rows, WIDTH), rows_of(rows, 1),
            rows_of(rows, HIDDEN), part_of(which, (HIDDEN, WIDTH)), pair(WIDTH),
        ],
        out_specs=[rows_of(rows, WIDTH), rows_of(rows, WIDTH), rows_of(rows, HIDDEN), vec_spec],
        scratch_shapes=[pltpu.VMEM((rows, HIDDEN), f32)],
        compiler_params=params(),
        cost_estimate=cost(total * 2 * 600000, total * 8000),
        name="ffn_back",
    )(lengths, cls_grad, cot, n2, r2, gp, w2, g2)
    up, down = pl.pallas_call(
        ffn_weight_kernel,
        out_shape=[shape((HIDDEN, WIDTH), bf16), shape((HIDDEN, WIDTH), bf16)],
        grid=(BLOCKS,),
        in_specs=[
            pl.BlockSpec((total, WIDTH), lambda i: (0, i)), whole((total, WIDTH)), whole((total, WIDTH)),
            pl.BlockSpec((total, WIDTH), lambda i: (0, i)),
        ],
        out_specs=[rows_of(WIDTH, WIDTH), rows_of(WIDTH, WIDTH)],
        compiler_params=params(),
        cost_estimate=cost(total * 2 * 600000, total * 6000),
        name="ffn_weights",
    )(act, gffn, nb, gpre)
    one, dctx, vec_b, proj = pl.pallas_call(
        functools.partial(attn_norm_kernel, which, length),
        out_shape=[shape((total, WIDTH), f32), shape((total, WIDTH), bf16), vec, shape((WIDTH, WIDTH), bf16)],
        grid=(steps,),
        in_specs=[
            rows_of(rows, HIDDEN), part_of(which, (WIDTH, HIDDEN)), rows_of(rows, WIDTH), rows_of(rows, WIDTH),
            rows_of(rows, 1), pair(WIDTH), part_of(which, (WIDTH, WIDTH)), rows_of(rows, WIDTH),
        ],
        out_specs=[rows_of(rows, WIDTH), rows_of(rows, WIDTH), vec_spec, whole((WIDTH, WIDTH))],
        scratch_shapes=[pltpu.VMEM((rows, WIDTH), bf16), pltpu.VMEM((WIDTH, WIDTH), f32)],
        compiler_params=params(),
        cost_estimate=cost(total * 2 * 600000, total * 8000),
        name="attn_norm_back",
    )(gpre, w1, two, n1, r1, g1, wo, ctx)
    gx, vec_c, dqkv = pl.pallas_call(
        functools.partial(attn_core_kernel, length),
        out_shape=[shape((total, WIDTH), bf16), vec, shape((3 * WIDTH, WIDTH), bf16)],
        grid=(steps,),
        in_specs=[
            rows_of(rows, WIDTH), rows_of(rows, 3 * WIDTH), rows_of(stack, length), rows_of(rows, WIDTH),
            part_of(which, (WIDTH, 3 * WIDTH)), rows_of(rows, WIDTH),
        ],
        out_specs=[rows_of(rows, WIDTH), vec_spec, whole((3 * WIDTH, WIDTH))],
        scratch_shapes=[
            pltpu.VMEM((rows, 3 * WIDTH), bf16), pltpu.VMEM((stack, length), f32), pltpu.VMEM((stack, length), bf16),
            pltpu.VMEM((stack, length), bf16), pltpu.VMEM((3 * WIDTH, WIDTH), f32),
        ],
        compiler_params=params(),
        cost_estimate=cost(total * 2 * 1000000, total * 10000),
        name="attn_core_back",
    )(dctx, qkv, p, x, wqkv, one)
    vecs = jnp.pad((vec_a + vec_b + vec_c).astype(bf16), ((0, WIDTH - VECTOR_ROWS), (0, 0)))
    return gx, jnp.concatenate([dqkv, proj, up, down, vecs])


def stages(count):
    masks = []
    bit = 1
    while bit < count:
        masks.append(bit)
        bit = bit * 2
    groups = [masks[:1]]
    rest = masks[1:]
    while rest:
        groups.append(rest[:2])
        rest = rest[2:]
    return [group for group in groups if group]


def partner_send(values, mask, count):
    return lax.ppermute(values, "dp", [(i, i ^ mask) for i in range(count)])


def combos(group):
    return [index * group[0] for index in range(1, 2 ** len(group))]


def reduce_scatter(buffer, count, me):
    for group in stages(count):
        radix = 2 ** len(group)
        digit = (me // group[0]) % radix
        split = buffer.reshape((radix, buffer.shape[0] // radix) + buffer.shape[1:])
        received = []
        for step, mask in enumerate(combos(group), start=1):
            outgoing = lax.dynamic_index_in_dim(split, digit ^ step, 0, keepdims=False)
            received.append(partner_send(outgoing, mask, count))
        total = lax.dynamic_index_in_dim(split, digit, 0, keepdims=False).astype(f32)
        for piece in received:
            total = total + piece.astype(f32)
        buffer = total.astype(bf16)
    return buffer


def gather_back(buffer, count, me):
    for group in reversed(stages(count)):
        radix = 2 ** len(group)
        digit = (me // group[0]) % radix
        joined = jnp.zeros((radix,) + buffer.shape, buffer.dtype)
        pieces = [buffer]
        for mask in combos(group):
            pieces.append(partner_send(buffer, mask, count))
        for step, piece in enumerate(pieces):
            joined = lax.dynamic_update_index_in_dim(joined, piece, digit ^ step, 0)
        buffer = joined.reshape((radix * buffer.shape[0],) + buffer.shape[1:])
    return buffer


def body(questions, passages, cot_questions, cot_passages, len_questions, len_passages, positive, *weights):
    local = questions.shape[0]
    question_length = questions.shape[1]
    passage_length = passages.shape[1]
    count = positive.shape[0] // local
    me = lax.axis_index("dp")
    x_q = questions.reshape(-1, WIDTH)
    x_p = passages.reshape(-1, WIDTH)
    saved_p = forward(1, local, 1, passage_length, len_passages, x_p, weights)
    saved_q = forward(0, 1, local, question_length, len_questions, x_q, weights)
    own_cls = jnp.concatenate([saved_q[1], saved_p[1]]).astype(bf16)
    all_cls = lax.all_to_all(
        jnp.broadcast_to(own_cls[None], (count,) + own_cls.shape), "dp", 0, 0, tiled=True
    )
    slots = positive // local * PAD + positive % local
    slots = jnp.pad(slots.reshape(count, local), ((0, 0), (0, PAD - local)), constant_values=-1)
    own_slots = lax.dynamic_slice_in_dim(slots, me, 1, axis=0).reshape(PAD, 1)
    loss, grad_cls_q, grad_cls_p = pl.pallas_call(
        functools.partial(loss_kernel, local),
        out_shape=[shape((PAD, 128), f32), shape((PAD, WIDTH), f32), shape((PAD, WIDTH), f32)],
        grid=(1,),
        in_specs=[smem(), whole((count, 2 * PAD, WIDTH)), whole((1, count * PAD)), whole((PAD, 1))],
        out_specs=[whole((PAD, 128)), whole((PAD, WIDTH)), whole((PAD, WIDTH))],
        scratch_shapes=[pltpu.VMEM((count * PAD, WIDTH), bf16), pltpu.VMEM((count * PAD, WIDTH), bf16)],
        compiler_params=params(),
        name="loss",
    )(me.reshape(1), all_cls, slots.reshape(1, -1), own_slots)
    loss_rows = loss[:local, 0]
    grad_q, pack_q = question_backward(
        0, local, question_length, len_questions, grad_cls_q, cot_questions.reshape(-1, WIDTH), x_q, saved_q, weights
    )
    sum_q = gather_back(reduce_scatter(pack_q, count, me), count, me)
    grad_p, pack_p = passage_backward(
        1, local, passage_length, len_passages, grad_cls_p, cot_passages.reshape(-1, WIDTH), x_p, saved_p, weights
    )
    sum_p = gather_back(reduce_scatter(pack_p, count, me), count, me)
    d_qkv, d_proj, d_up, d_down, vecs = pl.pallas_call(
        unpack_kernel,
        out_shape=[
            shape((2, WIDTH, 3 * WIDTH), f32), shape((2, WIDTH, WIDTH), f32), shape((2, WIDTH, HIDDEN), f32),
            shape((2, HIDDEN, WIDTH), f32), shape((2, VECTOR_ROWS, WIDTH), f32),
        ],
        grid=(1,),
        in_specs=[whole((GROUP_ROWS, WIDTH)), whole((GROUP_ROWS, WIDTH))],
        out_specs=[
            whole((2, WIDTH, 3 * WIDTH)), whole((2, WIDTH, WIDTH)), whole((2, WIDTH, HIDDEN)),
            whole((2, HIDDEN, WIDTH)), whole((2, VECTOR_ROWS, WIDTH)),
        ],
        compiler_params=params(),
        name="unpack",
    )(sum_q, sum_p)
    return (
        loss_rows, saved_q[0].reshape(questions.shape), saved_p[0].reshape(passages.shape),
        grad_q.reshape(questions.shape), grad_p.reshape(passages.shape),
        d_qkv, vecs[:, QUERY_BIAS], vecs[:, VALUE_BIAS], d_proj, vecs[:, PROJ_BIAS], vecs[:, ATTN_GAIN],
        vecs[:, ATTN_SHIFT], d_up, vecs[:, UP_BIAS : UP_BIAS + BLOCKS].reshape(2, HIDDEN), d_down,
        vecs[:, DOWN_BIAS], vecs[:, FFN_GAIN], vecs[:, FFN_SHIFT],
    )


def solution(mesh):
    split = P("dp", None, None)
    return jax.shard_map(
        body,
        mesh=mesh,
        in_specs=(split, split, split, split, P("dp"), P("dp")) + (P(),) * 14,
        out_specs=(P("dp"), split, split, split, split) + (P(),) * 13,
        check_vma=False,
    )
```

time: 646 us -> 248 us (0.38)
  waiting for transfers between devices: 399 us -> 34.2 us
  Pallas kernels: 0 us -> 148 us
  local copies, waits for them, and re-layouts: 113 us -> 17.9 us
  matrix products: 45.7 us -> 0 us
  blocking collectives: 43.6 us -> 0 us
  starting transfers between devices: 0.12 us -> 39.8 us
  other arithmetic: 24.6 us -> 5.86 us
  between operations: 15.5 us -> 1.09 us
    unnamed x6 -> x0, waiting for transfers between devices: 399 us -> none
    pallas_call x0 -> x9, Pallas kernels: none -> 148 us  [the longest x2 75.2 us: forward(): pl.pallas_call(functools.partial(forward_kernel, which, seqs, length), ou...]
    unnamed x251 -> x32, local copies, waits for them, and re-layouts: 73.1 us -> 11.1 us
    dot_general x38 -> x0, matrix products: 45.3 us -> none  [the longest x2 8.33 us: layer_backward(): jnp.einsum('tjx,ux->tju', feedforward_gradient, feedforward_out_weight, p...]
    all_gather x1 -> x0, blocking collectives: 43.6 us -> none  [body(): all_passage_cls = lax.all_gather(passage_cls, 'dp', axis=0, tiled=True)]
    ppermute x0 -> x28, starting transfers between devices: none -> 32.3 us  [partner_send(): return lax.ppermute(values, 'dp', [(i, i ^ mask) for i in range(count)])]
    ppermute x0 -> x28, waiting for transfers between devices: none -> 25.3 us  [partner_send(): return lax.ppermute(values, 'dp', [(i, i ^ mask) for i in range(count)])]
    reduce_sum x17 -> x0, other arithmetic: 12.6 us -> none  [the longest x2 3.74 us: layer_norm(): return centered * lax.rsqrt(variance + ln_eps) * gain_row + shift_row]
  transfers between devices with their start and end apart: 3 -> 29, of which waited for: 3 -> 13; matrix products, arithmetic and copies ran while one was open for 5% -> 4% of each run, Pallas kernels for 0% -> 21%
where the time goes in v1:
time: 248 us; the launch traced here: 247 us
  Pallas kernels  148 us (60%)
  starting transfers between devices  39.8 us (16%)
  waiting for transfers between devices  34.2 us (14%)
  local copies, waits for them, and re-layouts  17.9 us (7%)
  other arithmetic  5.86 us (2%)
    pallas_call x2, Pallas kernels, forward(): pl.pallas_call(functools.partial(forward_kernel, which, seqs, length), ou...  75.2 us
    ppermute x28, starting transfers between devices, partner_send(): return lax.ppermute(values, 'dp', [(i, i ^ mask) for i in range(count)])  32.3 us
    ppermute x28, waiting for transfers between devices, partner_send(): return lax.ppermute(values, 'dp', [(i, i ^ mask) for i in range(count)])  25.3 us
    pallas_call x1, Pallas kernels, passage_backward(): pl.pallas_call(functools.partial(attn_core_kernel, length), out_shape=[sh...  23.5 us
    pallas_call x1, Pallas kernels, question_backward(): pl.pallas_call(functools.partial(question_back_kernel, which, seqs, lengt...  14.2 us
    pallas_call x1, Pallas kernels, passage_backward(): pl.pallas_call(functools.partial(ffn_kernel, which, length), out_shape=[s...  11.6 us
    pallas_call x1, Pallas kernels, passage_backward(): pl.pallas_call(functools.partial(attn_norm_kernel, which, length), out_sh...  11.2 us
    unnamed x32, local copies, waits for them, and re-layouts  11.1 us
  transfers between devices with their start and end apart: 29, of which 13 were waited for; matrix products, arithmetic and copies ran while one was open for 4% of the time, Pallas kernels for 21%

profile of v1, /device:TPU:0, one launch (start us, length us, event | category | flops | bytes accessed | tf_op | source)
XLA Modules:
  0.0 247.2 jit_solution(14436729791548349437)
XLA Ops:
  0.7 58.0 %forward.3 = (bf16[1280,256]{1,0:T(8,128)(2,1)}, f32[8,256]{1,0:T(8,128)}, bf16[1280,768]{1,0:T(8,128)(2,1)}, f32[5120,256]{1,0:T(8,128)}, bf16[1280,256]{1,0:T(...) custom-call(s32[5]{0:T(128)} %len_ref.7, ...), custom_call_target="tpu_custom_call" | custom-call | flops 2048000000 | bytes 15360000 | tf_op jit(solution)/shard_map/forward/pallas_call | solution.py:404
  59.3 17.2 %forward.2 = (bf16[320,256]{1,0:T(8,128)(2,1)}, f32[8,256]{1,0:T(8,128)}, bf16[320,768]{1,0:T(8,128)(2,1)}, f32[1280,64]{1,0:T(8,128)}, bf16[320,256]{1,0:T(8,12...) custom-call(s32[5]{0:T(128)} %len_ref.6, ...), custom_call_target="tpu_custom_call" | custom-call | flops 512000000 | bytes 3840000 | tf_op jit(solution)/shard_map/forward/pallas_call | solution.py:404
  78.0 7.5 %all-to-all-start = ((bf16[32,16,256]{2,1,0:T(8,128)(2,1)}), bf16[32,16,256]{2,1,0:T(8,128)(2,1)S(1)}, u32[]{:S(2)}, u32[]{:S(2)}) async-start(bf16[32,16,256]{2,1,0:T(8,128)(2,1)} %broadcast_in_dim.69), calls=%async_computation | async-start | bytes 524288 | tf_op jit(solution)/shard_map/all_to_all | solution.py:588
  87.0 8.9 %all-to-all-done.all_ref = bf16[32,16,256]{2,1,0:T(8,128)(2,1)S(1)} async-done(((bf16[32,16,256]{2,1,0:T(8,128)(2,1)}), bf16[32,16,256]{2,1,0:T(8,128)(2,1)S(1)}, u32[]{:S(2)}, u32[]{:S(2)}) %all-to-all-start) | async-done | bytes 262176 | tf_op jit(solution)/shard_map/all_to_all | solution.py:588
  96.6 2.4 loss.1
  99.0 14.2 %question_back.1 = (bf16[320,256]{1,0:T(8,128)(2,1)}, bf16[3328,256]{1,0:T(8,128)(2,1)}) custom-call(s32[5]{0:T(128)} %len_ref.6, f32[8,256]{1,0:T(8,128)} %get-tuple-element.70.cls_ref, bf16[320,256]{1,0:T(8,128)(2,1)} %bitcast.173, bf16[320,256]{1,0:T(8,128)(2,1)} %bitcast.172, bf16[320,768]{1,0:T(8,128)(2,1)} %get-tuple-element.71.qkv_ref, ...), custom_call_target="tpu_custom_call" | custom-call | flops 1024000000 | bytes 3840000 | tf_op jit(solution)/shard_map/question_back/pallas_call | solution.py:431
  113.1 1.2 dynamic-slice_bitcast_fusion.1
  114.4 11.6 %ffn_back.1 = (f32[1280,256]{1,0:T(8,128)}, bf16[1280,256]{1,0:T(8,128)(2,1)}, bf16[1280,1024]{1,0:T(8,128)(2,1)}, f32[16,256]{1,0:T(8,128)}) custom-call(s32[5]{0:T(128)} %len_ref.7, f32[8,256]{1,0:T(8,128)} %get-tuple-element.82.cls_ref, bf16[1280,256]{1,0:T(8,128)(2,1)} %bitcast.168, f32[1280,256]{1,0:T(8,128)} %get-tuple-element.83.n2_ref, ...), custom_call_target="tpu_custom_call" | custom-call | flops 1536000000 | bytes 10240000 | tf_op jit(solution)/shard_map/ffn_back/pallas_call | solution.py:463
  126.0 11.2 %attn_norm_back.1 = (f32[1280,256]{1,0:T(8,128)}, bf16[1280,256]{1,0:T(8,128)(2,1)}, f32[16,256]{1,0:T(8,128)}, bf16[256,256]{1,0:T(8,128)(2,1)}) custom-call(bf16[1280,1024]{1,0:T(8,128)(2,1)} %get-tuple-element.86.gpre_ref, bf16[2,256,1024]{2,1,0:T(8,128)(2,1)} %w1_ref.7, f32[1280,256]{1,0:T(8,128)} %get-tuple-element.87.two_ref, ...), custom_call_target="tpu_custom_call" | custom-call | flops 1536000000 | bytes 10240000 | tf_op jit(solution)/shard_map/attn_norm_back/pallas_call | solution.py:490
  137.2 23.5 %attn_core_back.1 = (bf16[1280,256]{1,0:T(8,128)(2,1)}, f32[16,256]{1,0:T(8,128)}, bf16[768,256]{1,0:T(8,128)(2,1)}) custom-call(bf16[1280,256]{1,0:T(8,128)(2,1)} %get-tuple-element.91.dctx_ref, bf16[1280,768]{1,0:T(8,128)(2,1)} %get-tuple-element.92.qkv_ref, f32[5120,256]{1,0:T(8,128)} %get-tuple-element.93.p_ref, bf16[1280,256]{1,0:T(8,128)(2,1)} %bitcast.170, ...), custom_call_target="tpu_custom_call" | custom-call | flops 2560000000 | bytes 12800000 | tf_op jit(solution)/shard_map/attn_core_back/pallas_call | solution.py:504
  160.7 1.0 constant_dynamic-update-slice_fusion.3
  161.7 5.6 %ffn_weights.1 = (bf16[1024,256]{1,0:T(8,128)(2,1)}, bf16[1024,256]{1,0:T(8,128)(2,1)}) custom-call(bf16[1280,1024]{1,0:T(8,128)(2,1)} %get-tuple-element.99.act_ref, bf16[1280,256]{1,0:T(8,128)(2,1)} %get-tuple-element.100.gffn_ref, bf16[1280,256]{1,0:T(8,128)(2,1)} %get-tuple-element.101.nb_ref, bf16[1280,1024]{1,0:T(8,128)(2,1)} %get-tuple-element.86.gpre_ref), custom_call_target="tpu_custom_call" | custom-call | flops 1536000000 | bytes 7680000 | tf_op jit(solution)/shard_map/ffn_weights/pallas_call | solution.py:477
  167.4 1.1 constant_dynamic-update-slice_fusion.1
  168.5 1.1 constant_dynamic-update-slice_fusion
  170.2 1.6 fusion.1
  173.1 1.3 collective-permute-start.2
  174.4 1.8 collective-permute-start.3
  176.2 1.4 fusion
  178.1 1.3 collective-permute-start.16
  179.4 1.5 collective-permute-done.1
  180.9 1.2 collective-permute-start.17
  182.7 3.4 %collective-permute-done.2 = bf16[416,256]{1,0:T(8,128)(2,1)} collective-permute-done((bf16[416,256]{1,0:T(8,128)(2,1)}, bf16[416,256]{1,0:T(8,128)(2,1)}, u32[]{:S(2)}, u32[]{:S(2)}) %collective-permute-start.2) | collective-permute-done | bytes 213024 | tf_op jit(solution)/shard_map/ppermute | solution.py:540
  186.1 3.9 %collective-permute-done.15 = bf16[416,256]{1,0:T(8,128)(2,1)S(1)} collective-permute-done((bf16[416,256]{1,0:T(8,128)(2,1)S(1)}, bf16[416,256]{1,0:T(8,128)(2,1)S(1)}, u32[]{:S(2)}, u32[]{:S(2)}) %collective-permute-start.15) | collective-permute-done | bytes 213024 | tf_op jit(solution)/shard_map/ppermute | solution.py:540
  190.0 4.3 %collective-permute-done.16 = bf16[416,256]{1,0:T(8,128)(2,1)S(1)} collective-permute-done((bf16[416,256]{1,0:T(8,128)(2,1)S(1)}, bf16[416,256]{1,0:T(8,128)(2,1)S(1)}, u32[]{:S(2)}, u32[]{:S(2)}) %collective-permute-start.16) | collective-permute-done | bytes 213024 | tf_op jit(solution)/shard_map/ppermute | solution.py:540
  194.3 1.3 fusion.4
  196.4 1.1 collective-permute-start.19
  197.5 2.6 %collective-permute-start.20 = (bf16[104,256]{1,0:T(8,128)(2,1)S(1)}, bf16[104,256]{1,0:T(8,128)(2,1)S(1)}, u32[]{:S(2)}, u32[]{:S(2)}) collective-permute-start(bf16[104,256]{1,0:T(8,128)(2,1)S(1)} %get-tuple-element.123), channel_id=1, source_target_pairs={{0,24},{1,25},{2,26},{3,27},{4,28},{5,29},{6,30},{7,31},{8,16},{9,... | collective-permute-start | bytes 159752 | tf_op jit(solution)/shard_map/ppermute | solution.py:540
  200.2 1.8 collective-permute-start.5
  202.0 2.6 %collective-permute-start.6 = (bf16[104,256]{1,0:T(8,128)(2,1)S(1)}, bf16[104,256]{1,0:T(8,128)(2,1)S(1)}, u32[]{:S(2)}, u32[]{:S(2)}) collective-permute-start(bf16[104,256]{1,0:T(8,128)(2,1)S(1)} %get-tuple-element.126), channel_id=1, source_target_pairs={{0,24},{1,25},{2,26},{3,27},{4,28},{5,29},{6,30},{7,31},{8,16},{9,... | collective-permute-start | bytes 159752 | tf_op jit(solution)/shard_map/ppermute | solution.py:540
  205.2 1.7 collective-permute-start.22
  206.9 2.3 collective-permute-start.23
  209.2 1.2 collective-permute-start.7
  210.4 1.3 collective-permute-start.8
  211.7 2.0 collective-permute-start.9
  213.7 1.5 collective-permute-start.24
  216.0 1.3 collective-permute-start.26
  217.6 1.5 collective-permute-start.10
  220.0 2.0 collective-permute-done.24
  222.0 1.6 collective-permute-start.12
  223.6 1.7 collective-permute-done.25
  225.3 1.8 collective-permute-done.26
  227.2 1.0 collective-permute-done.10
  228.2 1.7 collective-permute-done.11
  229.9 1.8 collective-permute-done.12
  232.3 1.9 collective-permute-done.13
  234.2 1.2 copy-done
  235.4 4.8 %unpack.1 = (f32[2,256,768]{2,1,0:T(8,128)}, f32[2,256,256]{2,1,0:T(8,128)}, f32[2,256,1024]{2,1,0:T(8,128)}, f32[2,1024,256]{2,1,0:T(8,128)}, f32[2,16,256]{2,1,0:T(8,128)}) custom-call(bf16[3328,256]{1,0:T(8,128)(2,1)} %bitcast.142, bf16[3328,256]{1,0:T(8,128)(2,1)} %bitcast.143), custom_call_target="tpu_custom_call" | custom-call | tf_op jit(solution)/shard_map/unpack/pallas_call | solution.py:613
  240.2 1.0 fusion.18
  (100 shorter events, 17.3 us)
Async XLA Ops:
  59.3 26.2 %copy-start.8 = (s32[160]{0:T(256)S(1)}, s32[160]{0:T(256)}, u32[]{:S(2)}) copy-start(s32[160]{0:T(256)} %param.26) | copy-start | bytes 1924
  78.0 17.9 %all-to-all-start = ((bf16[32,16,256]{2,1,0:T(8,128)(2,1)}), bf16[32,16,256]{2,1,0:T(8,128)(2,1)S(1)}, u32[]{:S(2)}, u32[]{:S(2)}) async-start(bf16[32,16,256]{2,1,0:T(8,128)(2,1)} %broadcast_in_dim.69), calls=%async_computation | async-start | bytes 524288 | tf_op jit(solution)/shard_map/all_to_all | solution.py:588
  95.9 0.7 copy-start.2
  114.3 55.9 %collective-permute-start = (bf16[1664,256]{1,0:T(8,128)(2,1)S(1)}, bf16[1664,256]{1,0:T(8,128)(2,1)}, u32[]{:S(2)}, u32[]{:S(2)}) collective-permute-start(bf16[1664,256]{1,0:T(8,128)(2,1)S(1)} %dynamic-slice_bitcast_fusion.1), channel_id=1, source_target_pairs={{0,1},{1,0},{2,3},{3,2},{4,5},{5,4},{6,7},{7,6},{8,9},{9,8},{10,11... | collective-permute-start | bytes 2555912 | tf_op jit(solution)/shard_map/ppermute | solution.py:540
  137.2 24.5 %copy-start.3 = (bf16[256,256]{1,0:T(8,128)(2,1)S(1)}, bf16[256,256]{1,0:T(8,128)(2,1)}, u32[]{:S(2)}) copy-start(bf16[256,256]{1,0:T(8,128)(2,1)} %get-tuple-element.98) | copy-start | bytes 393220
  167.4 2.2 copy-start.4
  167.4 2.2 copy-start.5
  167.4 2.2 copy-start.6
  169.7 6.5 %collective-permute-start.14 = (bf16[1664,256]{1,0:T(8,128)(2,1)S(1)}, bf16[1664,256]{1,0:T(8,128)(2,1)}, u32[]{:S(2)}, u32[]{:S(2)}) collective-permute-start(bf16[1664,256]{1,0:T(8,128)(2,1)S(1)} %dynamic-slice_bitcast_fusion), channel_id=1, source_target_pairs={{0,1},{1,0},{2,3},{3,2},{4,5},{5,4},{6,7},{7,6},{8,9},{9,8},{10,11... | collective-permute-start | bytes 2555912 | tf_op jit(solution)/shard_map/ppermute | solution.py:540
  172.7 8.2 %collective-permute-start.1 = (bf16[416,256]{1,0:T(8,128)(2,1)S(1)}, bf16[416,256]{1,0:T(8,128)(2,1)}, u32[]{:S(2)}, u32[]{:S(2)}) collective-permute-start(bf16[416,256]{1,0:T(8,128)(2,1)S(1)} %get-tuple-element.119), channel_id=1, source_target_pairs={{0,2},{1,3},{2,0},{3,1},{4,6},{5,7},{6,4},{7,5},{8,10},{9,11},{10,... | collective-permute-start | bytes 638984 | tf_op jit(solution)/shard_map/ppermute | solution.py:540
  173.1 13.0 %collective-permute-start.2 = (bf16[416,256]{1,0:T(8,128)(2,1)}, bf16[416,256]{1,0:T(8,128)(2,1)}, u32[]{:S(2)}, u32[]{:S(2)}) collective-permute-start(bf16[416,256]{1,0:T(8,128)(2,1)} %get-tuple-element.121), channel_id=1, source_target_pairs={{0,4},{1,5},{2,6},{3,7},{4,0},{5,1},{6,2},{7,3},{8,12},{9,13},{10,... | collective-permute-start | bytes 638984 | tf_op jit(solution)/shard_map/ppermute | solution.py:540
  174.4 7.7 %copy-start.7 = (f32[8,128]{1,0:T(8,128)S(1)}, f32[8,128]{1,0:T(8,128)}, u32[]{:S(2)}) copy-start(f32[8,128]{1,0:T(8,128)} %get-tuple-element.67) | copy-start | bytes 12292
  174.4 11.6 %collective-permute-start.3 = (bf16[416,256]{1,0:T(8,128)(2,1)}, bf16[416,256]{1,0:T(8,128)(2,1)}, u32[]{:S(2)}, u32[]{:S(2)}) collective-permute-start(bf16[416,256]{1,0:T(8,128)(2,1)} %get-tuple-element.120), channel_id=1, source_target_pairs={{0,6},{1,7},{2,4},{3,5},{4,2},{5,3},{6,0},{7,1},{8,14},{9,15},{10,... | collective-permute-start | bytes 638984 | tf_op jit(solution)/shard_map/ppermute | solution.py:540
  177.6 12.4 %collective-permute-start.15 = (bf16[416,256]{1,0:T(8,128)(2,1)S(1)}, bf16[416,256]{1,0:T(8,128)(2,1)S(1)}, u32[]{:S(2)}, u32[]{:S(2)}) collective-permute-start(bf16[416,256]{1,0:T(8,128)(2,1)S(1)} %get-tuple-element.116), channel_id=1, source_target_pairs={{0,2},{1,3},{2,0},{3,1},{4,6},{5,7},{6,4},{7,5},{8,10},{9,11},{10,... | collective-permute-start | bytes 638984 | tf_op jit(solution)/shard_map/ppermute | solution.py:540
  178.1 16.2 %collective-permute-start.16 = (bf16[416,256]{1,0:T(8,128)(2,1)S(1)}, bf16[416,256]{1,0:T(8,128)(2,1)S(1)}, u32[]{:S(2)}, u32[]{:S(2)}) collective-permute-start(bf16[416,256]{1,0:T(8,128)(2,1)S(1)} %get-tuple-element.118), channel_id=1, source_target_pairs={{0,4},{1,5},{2,6},{3,7},{4,0},{5,1},{6,2},{7,3},{8,12},{9,13},{10,... | collective-permute-start | bytes 638984 | tf_op jit(solution)/shard_map/ppermute | solution.py:540
  180.9 13.4 %collective-permute-start.17 = (bf16[416,256]{1,0:T(8,128)(2,1)S(1)}, bf16[416,256]{1,0:T(8,128)(2,1)S(1)}, u32[]{:S(2)}, u32[]{:S(2)}) collective-permute-start(bf16[416,256]{1,0:T(8,128)(2,1)S(1)} %get-tuple-element.117), channel_id=1, source_target_pairs={{0,6},{1,7},{2,4},{3,5},{4,2},{5,3},{6,0},{7,1},{8,14},{9,15},{10,... | collective-permute-start | bytes 638984 | tf_op jit(solution)/shard_map/ppermute | solution.py:540
  195.7 6.3 %collective-permute-start.18 = (bf16[104,256]{1,0:T(8,128)(2,1)S(1)}, bf16[104,256]{1,0:T(8,128)(2,1)S(1)}, u32[]{:S(2)}, u32[]{:S(2)}) collective-permute-start(bf16[104,256]{1,0:T(8,128)(2,1)S(1)} %get-tuple-element.122), channel_id=1, source_target_pairs={{0,8},{1,9},{2,10},{3,11},{4,12},{5,13},{6,14},{7,15},{8,0},{9,1},... | collective-permute-start | bytes 159752 | tf_op jit(solution)/shard_map/ppermute | solution.py:540
  196.4 8.2 %collective-permute-start.19 = (bf16[104,256]{1,0:T(8,128)(2,1)S(1)}, bf16[104,256]{1,0:T(8,128)(2,1)S(1)}, u32[]{:S(2)}, u32[]{:S(2)}) collective-permute-start(bf16[104,256]{1,0:T(8,128)(2,1)S(1)} %get-tuple-element.124), channel_id=1, source_target_pairs={{0,16},{1,17},{2,18},{3,19},{4,20},{5,21},{6,22},{7,23},{8,24},{9,... | collective-permute-start | bytes 159752 | tf_op jit(solution)/shard_map/ppermute | solution.py:540
  197.5 7.1 %collective-permute-start.20 = (bf16[104,256]{1,0:T(8,128)(2,1)S(1)}, bf16[104,256]{1,0:T(8,128)(2,1)S(1)}, u32[]{:S(2)}, u32[]{:S(2)}) collective-permute-start(bf16[104,256]{1,0:T(8,128)(2,1)S(1)} %get-tuple-element.123), channel_id=1, source_target_pairs={{0,24},{1,25},{2,26},{3,27},{4,28},{5,29},{6,30},{7,31},{8,16},{9,... | collective-permute-start | bytes 159752 | tf_op jit(solution)/shard_map/ppermute | solution.py:540
  200.1 6.7 %collective-permute-start.4 = (bf16[104,256]{1,0:T(8,128)(2,1)S(1)}, bf16[104,256]{1,0:T(8,128)(2,1)S(1)}, u32[]{:S(2)}, u32[]{:S(2)}) collective-permute-start(bf16[104,256]{1,0:T(8,128)(2,1)S(1)} %get-tuple-element.125), channel_id=1, source_target_pairs={{0,8},{1,9},{2,10},{3,11},{4,12},{5,13},{6,14},{7,15},{8,0},{9,1},... | collective-permute-start | bytes 159752 | tf_op jit(solution)/shard_map/ppermute | solution.py:540
  200.2 8.9 %collective-permute-start.5 = (bf16[104,256]{1,0:T(8,128)(2,1)S(1)}, bf16[104,256]{1,0:T(8,128)(2,1)S(1)}, u32[]{:S(2)}, u32[]{:S(2)}) collective-permute-start(bf16[104,256]{1,0:T(8,128)(2,1)S(1)} %get-tuple-element.127), channel_id=1, source_target_pairs={{0,16},{1,17},{2,18},{3,19},{4,20},{5,21},{6,22},{7,23},{8,24},{9,... | collective-permute-start | bytes 159752 | tf_op jit(solution)/shard_map/ppermute | solution.py:540
  202.0 7.1 %collective-permute-start.6 = (bf16[104,256]{1,0:T(8,128)(2,1)S(1)}, bf16[104,256]{1,0:T(8,128)(2,1)S(1)}, u32[]{:S(2)}, u32[]{:S(2)}) collective-permute-start(bf16[104,256]{1,0:T(8,128)(2,1)S(1)} %get-tuple-element.126), channel_id=1, source_target_pairs={{0,24},{1,25},{2,26},{3,27},{4,28},{5,29},{6,30},{7,31},{8,16},{9,... | collective-permute-start | bytes 159752 | tf_op jit(solution)/shard_map/ppermute | solution.py:540
  204.7 7.0 %collective-permute-start.21 = (bf16[104,256]{1,0:T(8,128)(2,1)S(1)}, bf16[104,256]{1,0:T(8,128)(2,1)S(1)}, u32[]{:S(2)}, u32[]{:S(2)}) collective-permute-start(bf16[104,256]{1,0:T(8,128)(2,1)S(1)} %get-tuple-element.113), channel_id=1, source_target_pairs={{0,8},{1,9},{2,10},{3,11},{4,12},{5,13},{6,14},{7,15},{8,0},{9,1},... | collective-permute-start | bytes 159752 | tf_op jit(solution)/shard_map/ppermute | solution.py:540
  205.2 8.5 %collective-permute-start.22 = (bf16[104,256]{1,0:T(8,128)(2,1)S(1)}, bf16[104,256]{1,0:T(8,128)(2,1)S(1)}, u32[]{:S(2)}, u32[]{:S(2)}) collective-permute-start(bf16[104,256]{1,0:T(8,128)(2,1)S(1)} %get-tuple-element.113), channel_id=1, source_target_pairs={{0,16},{1,17},{2,18},{3,19},{4,20},{5,21},{6,22},{7,23},{8,24},{9,... | collective-permute-start | bytes 159752 | tf_op jit(solution)/shard_map/ppermute | solution.py:540
  206.9 6.8 %collective-permute-start.23 = (bf16[104,256]{1,0:T(8,128)(2,1)S(1)}, bf16[104,256]{1,0:T(8,128)(2,1)S(1)}, u32[]{:S(2)}, u32[]{:S(2)}) collective-permute-start(bf16[104,256]{1,0:T(8,128)(2,1)S(1)} %get-tuple-element.113), channel_id=1, source_target_pairs={{0,24},{1,25},{2,26},{3,27},{4,28},{5,29},{6,30},{7,31},{8,16},{9,... | collective-permute-start | bytes 159752 | tf_op jit(solution)/shard_map/ppermute | solution.py:540
  209.2 6.7 %collective-permute-start.7 = (bf16[104,256]{1,0:T(8,128)(2,1)S(1)}, bf16[104,256]{1,0:T(8,128)(2,1)S(1)}, u32[]{:S(2)}, u32[]{:S(2)}) collective-permute-start(bf16[104,256]{1,0:T(8,128)(2,1)S(1)} %get-tuple-element.115), channel_id=1, source_target_pairs={{0,8},{1,9},{2,10},{3,11},{4,12},{5,13},{6,14},{7,15},{8,0},{9,1},... | collective-permute-start | bytes 159752 | tf_op jit(solution)/shard_map/ppermute | solution.py:540
  210.4 6.9 %collective-permute-start.8 = (bf16[104,256]{1,0:T(8,128)(2,1)S(1)}, bf16[104,256]{1,0:T(8,128)(2,1)S(1)}, u32[]{:S(2)}, u32[]{:S(2)}) collective-permute-start(bf16[104,256]{1,0:T(8,128)(2,1)S(1)} %get-tuple-element.115), channel_id=1, source_target_pairs={{0,16},{1,17},{2,18},{3,19},{4,20},{5,21},{6,22},{7,23},{8,24},{9,... | collective-permute-start | bytes 159752 | tf_op jit(solution)/shard_map/ppermute | solution.py:540
  211.7 5.9 %collective-permute-start.9 = (bf16[104,256]{1,0:T(8,128)(2,1)S(1)}, bf16[104,256]{1,0:T(8,128)(2,1)S(1)}, u32[]{:S(2)}, u32[]{:S(2)}) collective-permute-start(bf16[104,256]{1,0:T(8,128)(2,1)S(1)} %get-tuple-element.115), channel_id=1, source_target_pairs={{0,24},{1,25},{2,26},{3,27},{4,28},{5,29},{6,30},{7,31},{8,16},{9,... | collective-permute-start | bytes 159752 | tf_op jit(solution)/shard_map/ppermute | solution.py:540
  213.7 8.3 %collective-permute-start.24 = (bf16[416,256]{1,0:T(8,128)(2,1)S(1)}, bf16[416,256]{1,0:T(8,128)(2,1)S(1)}, u32[]{:S(2)}, u32[]{:S(2)}) collective-permute-start(bf16[416,256]{1,0:T(8,128)(2,1)S(1)} %bitcast.164), channel_id=1, source_target_pairs={{0,2},{1,3},{2,0},{3,1},{4,6},{5,7},{6,4},{7,5},{8,10},{9,11},{10,... | collective-permute-start | bytes 638984 | tf_op jit(solution)/shard_map/ppermute | solution.py:540
  215.3 10.0 %collective-permute-start.25 = (bf16[416,256]{1,0:T(8,128)(2,1)S(1)}, bf16[416,256]{1,0:T(8,128)(2,1)S(1)}, u32[]{:S(2)}, u32[]{:S(2)}) collective-permute-start(bf16[416,256]{1,0:T(8,128)(2,1)S(1)} %bitcast.165), channel_id=1, source_target_pairs={{0,4},{1,5},{2,6},{3,7},{4,0},{5,1},{6,2},{7,3},{8,12},{9,13},{10,... | collective-permute-start | bytes 638984 | tf_op jit(solution)/shard_map/ppermute | solution.py:540
  216.0 11.1 %collective-permute-start.26 = (bf16[416,256]{1,0:T(8,128)(2,1)S(1)}, bf16[416,256]{1,0:T(8,128)(2,1)S(1)}, u32[]{:S(2)}, u32[]{:S(2)}) collective-permute-start(bf16[416,256]{1,0:T(8,128)(2,1)S(1)} %bitcast.166), channel_id=1, source_target_pairs={{0,6},{1,7},{2,4},{3,5},{4,2},{5,3},{6,0},{7,1},{8,14},{9,15},{10,... | collective-permute-start | bytes 638984 | tf_op jit(solution)/shard_map/ppermute | solution.py:540
  217.6 10.5 %collective-permute-start.10 = (bf16[416,256]{1,0:T(8,128)(2,1)S(1)}, bf16[416,256]{1,0:T(8,128)(2,1)S(1)}, u32[]{:S(2)}, u32[]{:S(2)}) collective-permute-start(bf16[416,256]{1,0:T(8,128)(2,1)S(1)} %bitcast.160), channel_id=1, source_target_pairs={{0,2},{1,3},{2,0},{3,1},{4,6},{5,7},{6,4},{7,5},{8,10},{9,11},{10,... | collective-permute-start | bytes 638984 | tf_op jit(solution)/shard_map/ppermute | solution.py:540
  219.2 10.7 %collective-permute-start.11 = (bf16[416,256]{1,0:T(8,128)(2,1)S(1)}, bf16[416,256]{1,0:T(8,128)(2,1)S(1)}, u32[]{:S(2)}, u32[]{:S(2)}) collective-permute-start(bf16[416,256]{1,0:T(8,128)(2,1)S(1)} %bitcast.161), channel_id=1, source_target_pairs={{0,4},{1,5},{2,6},{3,7},{4,0},{5,1},{6,2},{7,3},{8,12},{9,13},{10,... | collective-permute-start | bytes 638984 | tf_op jit(solution)/shard_map/ppermute | solution.py:540
  222.0 9.7 %collective-permute-start.12 = (bf16[416,256]{1,0:T(8,128)(2,1)S(1)}, bf16[416,256]{1,0:T(8,128)(2,1)S(1)}, u32[]{:S(2)}, u32[]{:S(2)}) collective-permute-start(bf16[416,256]{1,0:T(8,128)(2,1)S(1)} %bitcast.163), channel_id=1, source_target_pairs={{0,6},{1,7},{2,4},{3,5},{4,2},{5,3},{6,0},{7,1},{8,14},{9,15},{10,... | collective-permute-start | bytes 638984 | tf_op jit(solution)/shard_map/ppermute | solution.py:540
  227.1 5.1 %collective-permute-start.27 = (bf16[1664,256]{1,0:T(8,128)(2,1)S(1)}, bf16[1664,256]{1,0:T(8,128)(2,1)S(1)}, u32[]{:S(2)}, u32[]{:S(2)}) collective-permute-start(bf16[1664,256]{1,0:T(8,128)(2,1)S(1)} %bitcast.146), channel_id=1, source_target_pairs={{0,1},{1,0},{2,3},{3,2},{4,5},{5,4},{6,7},{7,6},{8,9},{9,8},{10,11... | collective-permute-start | bytes 2555912 | tf_op jit(solution)/shard_map/ppermute | solution.py:540
  231.7 2.4 collective-permute-start.13
  232.2 2.0 copy-start.1
  234.2 1.2 copy-start

commit v2 on v1

--- a/solution.py
+++ b/solution.py
@@ -15,6 +15,9 @@
 PAD = 8
 VECTOR_ROWS = 16
 GROUP_ROWS = 13 * WIDTH
+SOFT = 128
+NORM = 64
+GELU = 32
 ln_eps = 1e-06
 score_scale = 0.125
 masked_score = -1e30
@@ -42,7 +45,7 @@
         step(pl.multiple_of(index * chunk, chunk))
         return carry
 
-    lax.fori_loop(0, rows // chunk, body, 0)
+    lax.fori_loop(0, rows // chunk, body, 0, unroll=rows // chunk)
 
 
 def vector(ref, which):
@@ -90,22 +93,22 @@
         score_ref[...] = dot_nt(queries, qkv_ref[span, WIDTH : 2 * WIDTH])
 
         def softmax(row):
-            part = score_ref[pl.ds(row, 32), :] * score_scale
+            part = score_ref[pl.ds(row, SOFT), :] * score_scale
             key = lax.broadcasted_iota(jnp.int32, part.shape, 1)
             part = jnp.where(key < size, part, masked_score)
             part = jnp.exp(part - jnp.max(part, axis=1, keepdims=True))
             prob = part * (1.0 / jnp.sum(part, axis=1, keepdims=True))
-            p_ref[pl.ds(s * stack_rows + row, 32), :] = prob
-            prob_ref[pl.ds(row, 32), :] = prob.astype(bf16)
-
-        row_loop(stack_rows, 32, softmax)
+            p_ref[pl.ds(s * stack_rows + row, SOFT), :] = prob
+            prob_ref[pl.ds(row, SOFT), :] = prob.astype(bf16)
+
+        row_loop(stack_rows, SOFT, softmax)
         context = dot(prob_ref[...], qkv_ref[span, 2 * WIDTH :])
         ctx_ref[span, :] = pick_heads(context, length).astype(bf16)
     n2_ref[...] = dot(ctx_ref[...], wo_ref[...])
     ob, g1, b1 = vector(ob_ref, which), vector(g1_ref, which), vector(b1_ref, which)
 
     def first_norm(row):
-        here = pl.ds(row, 32)
+        here = pl.ds(row, NORM)
         value = x_ref[here, :].astype(f32) + (n2_ref[here, :] + ob)
         centered = value - jnp.mean(value, axis=1, keepdims=True)
         inverse = lax.rsqrt(jnp.mean(centered * centered, axis=1, keepdims=True) + ln_eps)
@@ -114,12 +117,12 @@
         r1_ref[here, :] = inverse
         nb_ref[here, :] = (unit * g1 + b1).astype(bf16)
 
-    row_loop(rows, 32, first_norm)
+    row_loop(rows, NORM, first_norm)
     wide_ref[...] = dot(nb_ref[...], w1_ref[...])
     hb = vector(hb_ref, which)
 
     def gelu(row):
-        here = pl.ds(row, 16)
+        here = pl.ds(row, GELU)
         for j in range(BLOCKS):
             lanes = slice(j * WIDTH, (j + 1) * WIDTH)
             value = wide_ref[here, lanes] + hb[:, lanes]
@@ -128,7 +131,7 @@
             act_ref[here, lanes] = (value * cumulative).astype(bf16)
             gp_ref[here, lanes] = cumulative + value * density
 
-    row_loop(rows, 16, gelu)
+    row_loop(rows, GELU, gelu)
     n2_ref[...] = dot(act_ref[...], w2_ref[...])
     fb, g2, b2 = vector(fb_ref, which), vector(g2_ref, which), vector(b2_ref, which)
 
@@ -136,17 +139,17 @@
         size = len_ref[step * seqs + s]
 
         def second_norm(row):
-            here = pl.ds(s * length + row, 32)
+            here = pl.ds(s * length + row, NORM)
             value = (n1_ref[here, :] * g1 + b1) + (n2_ref[here, :] + fb)
             centered = value - jnp.mean(value, axis=1, keepdims=True)
             inverse = lax.rsqrt(jnp.mean(centered * centered, axis=1, keepdims=True) + ln_eps)
             unit = centered * inverse
             n2_ref[here, :] = unit
             r2_ref[here, :] = inverse
-            position = row + lax.broadcasted_iota(jnp.int32, (32, WIDTH), 0)
+            position = row + lax.broadcasted_iota(jnp.int32, (NORM, WIDTH), 0)
             out_ref[here, :] = jnp.where(position < size, unit * g2 + b2, 0.0).astype(bf16)
 
-        row_loop(length, 32, second_norm)
+        row_loop(length, NORM, second_norm)
         cls_ref[pl.ds(step * seqs + s, 1), :] = out_ref[s * length : s * length + 16, :].astype(f32)[:1]
 
 
@@ -161,8 +164,8 @@
         cls_row = cls_ref[pl.ds(first + s, 1), :]
 
         def norm_back(row):
-            here = pl.ds(s * length + row, 32)
-            position = row + lax.broadcasted_iota(jnp.int32, (32, WIDTH), 0)
+            here = pl.ds(s * length + row, NORM)
+            position = row + lax.broadcasted_iota(jnp.int32, (NORM, WIDTH), 0)
             grad = cot_ref[here, :].astype(f32) + jnp.where(position == 0, cls_row, 0.0)
             grad = jnp.where(position < size, grad, 0.0)
             unit = n2_ref[here, :]
@@ -177,18 +180,18 @@
             add_row(vec_ref, FFN_SHIFT, grad)
             add_row(vec_ref, DOWN_BIAS, low.astype(f32))
 
-        row_loop(length, 32, norm_back)
+        row_loop(length, NORM, norm_back)
     wide_ref[...] = dot_nt(gffn_ref[...], w2_ref[...])
 
     def gelu_back(row):
-        here = pl.ds(row, 16)
+        here = pl.ds(row, GELU)
         for j in range(BLOCKS):
             lanes = slice(j * WIDTH, (j + 1) * WIDTH)
             low = (wide_ref[here, lanes] * gp_ref[here, lanes]).astype(bf16)
             gpre_ref[here, lanes] = low
             add_row(vec_ref, UP_BIAS + j, low.astype(f32))
 
-    row_loop(seqs * length, 16, gelu_back)
+    row_loop(seqs * length, GELU, gelu_back)
 
 
 def attn_norm_phase(which, rows, gpre_ref, w1_ref, two_ref, n1_ref, r1_ref, g1_ref, wo_ref, one_ref, gatt_ref, dctx_ref, vec_ref):
@@ -196,7 +199,7 @@
     g1 = vector(g1_ref, which)
 
     def norm_back(row):
-        here = pl.ds(row, 32)
+        here = pl.ds(row, NORM)
         grad = two_ref[here, :] + one_ref[here, :]
         unit = n1_ref[here, :]
         scaled = grad * g1
@@ -210,7 +213,7 @@
         add_row(vec_ref, ATTN_SHIFT, grad)
         add_row(vec_ref, PROJ_BIAS, low.astype(f32))
 
-    row_loop(rows, 32, norm_back)
+    row_loop(rows, NORM, norm_back)
     dctx_ref[...] = dot_nt(gatt_ref[...], wo_ref[...]).astype(bf16)
 
 
@@ -222,13 +225,13 @@
         dp_ref[...] = dot_nt(context, qkv_ref[span, 2 * WIDTH :])
 
         def softmax_back(row):
-            prob = p_ref[pl.ds(s * stack_rows + row, 32), :]
-            grad = dp_ref[pl.ds(row, 32), :]
+            prob = p_ref[pl.ds(s * stack_rows + row, SOFT), :]
+            grad = dp_ref[pl.ds(row, SOFT), :]
             inner = jnp.sum(prob * grad, axis=1, keepdims=True)
-            ds_ref[pl.ds(row, 32), :] = (prob * (grad - inner)).astype(bf16)
-            pb_ref[pl.ds(row, 32), :] = prob.astype(bf16)
-
-        row_loop(stack_rows, 32, softmax_back)
+            ds_ref[pl.ds(row, SOFT), :] = (prob * (grad - inner)).astype(bf16)
+            pb_ref[pl.ds(row, SOFT), :] = prob.astype(bf16)
+
+        row_loop(stack_rows, SOFT, softmax_back)
         queries = stack_heads(qkv_ref[span, :WIDTH])
         grad_q = (pick_heads(dot(ds_ref[...], qkv_ref[span, WIDTH : 2 * WIDTH]), length) * score_scale).astype(bf16)
         gqkv_ref[span, :WIDTH] = grad_q
@@ -250,9 +253,19 @@
     ffn_phase(which, 1, length, pl.program_id(0), len_ref, cls_ref, cot_ref, n2_ref, r2_ref, gp_ref, w2_ref, g2_ref, two_ref, gffn_ref, gpre_ref, vec_ref, wide_ref)
 
 
-def ffn_weight_kernel(act_ref, gffn_ref, nb_ref, gpre_ref, up_ref, down_ref):
-    down_ref[...] = dot_tn(act_ref[...], gffn_ref[...]).astype(bf16)
-    up_ref[...] = dot_tn(nb_ref[...], gpre_ref[...]).astype(bf16)
+def pack_kernel(act_ref, gffn_ref, nb_ref, gpre_ref, dqkv_ref, proj_ref, va_ref, vb_ref, vc_ref, pack_ref):
+    j = pl.program_id(0)
+    up_rows = pl.ds(pl.multiple_of((4 + j) * WIDTH, WIDTH), WIDTH)
+    down_rows = pl.ds(pl.multiple_of((8 + j) * WIDTH, WIDTH), WIDTH)
+    pack_ref[down_rows, :] = dot_tn(act_ref[...], gffn_ref[...]).astype(bf16)
+    pack_ref[up_rows, :] = dot_tn(nb_ref[...], gpre_ref[...]).astype(bf16)
+
+    @pl.when(j == 0)
+    def _():
+        pack_ref[: 3 * WIDTH, :] = dqkv_ref[...]
+        pack_ref[3 * WIDTH : 4 * WIDTH, :] = proj_ref[...]
+        pack_ref[12 * WIDTH :, :] = jnp.zeros((WIDTH, WIDTH), bf16)
+        pack_ref[12 * WIDTH : 12 * WIDTH + VECTOR_ROWS, :] = (va_ref[...] + vb_ref[...] + vc_ref[...]).astype(bf16)
 
 
 def attn_norm_kernel(which, length, gpre_ref, w1_ref, two_ref, n1_ref, r1_ref, g1_ref, wo_ref, ctx_ref, one_ref, dctx_ref, vec_ref, proj_ref, gatt_ref, acc_ref):
@@ -343,7 +356,11 @@
     lax.fori_loop(0, count * PAD // block, part, 0)
 
 
-def unpack_kernel(q_ref, p_ref, qkv_ref, proj_ref, up_ref, down_ref, vec_ref):
+VECTOR_OUTS = (QUERY_BIAS, VALUE_BIAS, PROJ_BIAS, ATTN_GAIN, ATTN_SHIFT, DOWN_BIAS, FFN_GAIN, FFN_SHIFT)
+
+
+def unpack_kernel(q_ref, p_ref, qkv_ref, proj_ref, up_ref, down_ref, up_bias_ref, *vector_refs):
+    tails = []
     for which, ref in enumerate((q_ref, p_ref)):
         for j in range(3):
             qkv_ref[which, :, j * WIDTH : (j + 1) * WIDTH] = ref[j * WIDTH : (j + 1) * WIDTH, :].astype(f32)
@@ -351,7 +368,13 @@
         for j in range(BLOCKS):
             up_ref[which, :, j * WIDTH : (j + 1) * WIDTH] = ref[(4 + j) * WIDTH : (5 + j) * WIDTH, :].astype(f32)
         down_ref[which] = ref[8 * WIDTH : 12 * WIDTH, :].astype(f32)
-        vec_ref[which] = ref[12 * WIDTH : 12 * WIDTH + VECTOR_ROWS, :].astype(f32)
+        tails.append(ref[12 * WIDTH : 12 * WIDTH + VECTOR_ROWS, :].astype(f32))
+    for row, ref in zip(VECTOR_OUTS, vector_refs):
+        for which in range(2):
+            ref[which : which + 1, :] = tails[which][row : row + 1]
+    for j in range(BLOCKS):
+        for which in range(2):
+            up_bias_ref[which : which + 1, j * WIDTH : (j + 1) * WIDTH] = tails[which][UP_BIAS + j : UP_BIAS + j + 1]
 
 
 def smem():
@@ -371,7 +394,7 @@
 
 
 def params():
-    return pltpu.CompilerParams(vmem_limit_bytes=56 * 1024 * 1024)
+    return pltpu.CompilerParams(vmem_limit_bytes=24 * 1024 * 1024)
 
 
 def shape(dims, kind):
@@ -474,19 +497,6 @@
         cost_estimate=cost(total * 2 * 600000, total * 8000),
         name="ffn_back",
     )(lengths, cls_grad, cot, n2, r2, gp, w2, g2)
-    up, down = pl.pallas_call(
-        ffn_weight_kernel,
-        out_shape=[shape((HIDDEN, WIDTH), bf16), shape((HIDDEN, WIDTH), bf16)],
-        grid=(BLOCKS,),
-        in_specs=[
-            pl.BlockSpec((total, WIDTH), lambda i: (0, i)), whole((total, WIDTH)), whole((total, WIDTH)),
-            pl.BlockSpec((total, WIDTH), lambda i: (0, i)),
-        ],
-        out_specs=[rows_of(WIDTH, WIDTH), rows_of(WIDTH, WIDTH)],
-        compiler_params=params(),
-        cost_estimate=cost(total * 2 * 600000, total * 6000),
-        name="ffn_weights",
-    )(act, gffn, nb, gpre)
     one, dctx, vec_b, proj = pl.pallas_call(
         functools.partial(attn_norm_kernel, which, length),
         out_shape=[shape((total, WIDTH), f32), shape((total, WIDTH), bf16), vec, shape((WIDTH, WIDTH), bf16)],
@@ -518,8 +528,21 @@
         cost_estimate=cost(total * 2 * 1000000, total * 10000),
         name="attn_core_back",
     )(dctx, qkv, p, x, wqkv, one)
-    vecs = jnp.pad((vec_a + vec_b + vec_c).astype(bf16), ((0, WIDTH - VECTOR_ROWS), (0, 0)))
-    return gx, jnp.concatenate([dqkv, proj, up, down, vecs])
+    pack = pl.pallas_call(
+        pack_kernel,
+        out_shape=shape((GROUP_ROWS, WIDTH), bf16),
+        grid=(BLOCKS,),
+        in_specs=[
+            pl.BlockSpec((total, WIDTH), lambda i: (0, i)), whole((total, WIDTH)), whole((total, WIDTH)),
+            pl.BlockSpec((total, WIDTH), lambda i: (0, i)), whole((3 * WIDTH, WIDTH)), whole((WIDTH, WIDTH)),
+            vec_spec, vec_spec, vec_spec,
+        ],
+        out_specs=whole((GROUP_ROWS, WIDTH)),
+        compiler_params=params(),
+        cost_estimate=cost(total * 2 * 600000, total * 6000),
+        name="ffn_weights",
+    )(act, gffn, nb, gpre, dqkv, proj, vec_a, vec_b, vec_c)
+    return gx, pack
 
 
 def stages(count):
@@ -610,27 +633,22 @@
         1, local, passage_length, len_passages, grad_cls_p, cot_passages.reshape(-1, WIDTH), x_p, saved_p, weights
     )
     sum_p = gather_back(reduce_scatter(pack_p, count, me), count, me)
-    d_qkv, d_proj, d_up, d_down, vecs = pl.pallas_call(
+    dims = [(2, WIDTH, 3 * WIDTH), (2, WIDTH, WIDTH), (2, WIDTH, HIDDEN), (2, HIDDEN, WIDTH), (2, HIDDEN)]
+    dims += [(2, WIDTH)] * len(VECTOR_OUTS)
+    d_qkv, d_proj, d_up, d_down, up_bias, query_bias, value_bias, proj_bias, gain_a, shift_a, down_bias, gain_f, shift_f = pl.pallas_call(
         unpack_kernel,
-        out_shape=[
-            shape((2, WIDTH, 3 * WIDTH), f32), shape((2, WIDTH, WIDTH), f32), shape((2, WIDTH, HIDDEN), f32),
-            shape((2, HIDDEN, WIDTH), f32), shape((2, VECTOR_ROWS, WIDTH), f32),
-        ],
+        out_shape=[shape(d, f32) for d in dims],
         grid=(1,),
         in_specs=[whole((GROUP_ROWS, WIDTH)), whole((GROUP_ROWS, WIDTH))],
-        out_specs=[
-            whole((2, WIDTH, 3 * WIDTH)), whole((2, WIDTH, WIDTH)), whole((2, WIDTH, HIDDEN)),
-            whole((2, HIDDEN, WIDTH)), whole((2, VECTOR_ROWS, WIDTH)),
-        ],
+        out_specs=[whole(d) for d in dims],
         compiler_params=params(),
         name="unpack",
     )(sum_q, sum_p)
     return (
         loss_rows, saved_q[0].reshape(questions.shape), saved_p[0].reshape(passages.shape),
         grad_q.reshape(questions.shape), grad_p.reshape(passages.shape),
-        d_qkv, vecs[:, QUERY_BIAS], vecs[:, VALUE_BIAS], d_proj, vecs[:, PROJ_BIAS], vecs[:, ATTN_GAIN],
-        vecs[:, ATTN_SHIFT], d_up, vecs[:, UP_BIAS : UP_BIAS + BLOCKS].reshape(2, HIDDEN), d_down,
-        vecs[:, DOWN_BIAS], vecs[:, FFN_GAIN], vecs[:, FFN_SHIFT],
+        d_qkv, query_bias, value_bias, d_proj, proj_bias, gain_a, shift_a, d_up, up_bias, d_down,
+        down_bias, gain_f, shift_f,
     )
 
 

time: 248 us -> 173 us (0.70)
  Pallas kernels: 148 us -> 42.9 us
  local copies, waits for them, and re-layouts: 17.9 us -> 49.8 us
    pallas_call x2, Pallas kernels: 75.2 us -> 16.3 us  [forward(): pl.pallas_call(functools.partial(forward_kernel, which, seqs, length), ou...]
    unnamed x32 -> x152, local copies, waits for them, and re-layouts: 11.1 us -> 44.4 us
    pallas_call x1, Pallas kernels: 23.5 us -> 7 us  [passage_backward(): pl.pallas_call(functools.partial(attn_core_kernel, length), out_shape=[sh...]
    pallas_call x1, Pallas kernels: 14.2 us -> 5.55 us  [question_backward(): pl.pallas_call(functools.partial(question_back_kernel, which, seqs, lengt...]
    pallas_call x1, Pallas kernels: 11.6 us -> 3.52 us  [passage_backward(): pl.pallas_call(functools.partial(ffn_kernel, which, length), out_shape=[s...]
    pallas_call x1, Pallas kernels: 11.2 us -> 3.69 us  [passage_backward(): pl.pallas_call(functools.partial(attn_norm_kernel, which, length), out_sh...]
    pallas_call x2, Pallas kernels: 10.4 us -> 5.99 us  [the longest x1 3 us: passage_backward(): pl.pallas_call(pack_kernel, out_shape=shape((GROUP_ROWS, WIDTH), bf16), g...]
  transfers between devices with their start and end apart: 29 -> 29, of which waited for: 13 -> 13; matrix products, arithmetic and copies ran while one was open for 4% -> 4% of each run, Pallas kernels for 21% -> 10%
where the time goes in v2:
time: 173 us; the launch traced here: 172 us
  local copies, waits for them, and re-layouts  49.8 us (29%)
  Pallas kernels  42.9 us (25%)
  starting transfers between devices  39.1 us (23%)
  waiting for transfers between devices  34.8 us (20%)
  other arithmetic  4.07 us (2%)
    unnamed x152, local copies, waits for them, and re-layouts  44.4 us
    ppermute x28, starting transfers between devices, partner_send(): return lax.ppermute(values, 'dp', [(i, i ^ mask) for i in range(count)])  31.6 us
    ppermute x28, waiting for transfers between devices, partner_send(): return lax.ppermute(values, 'dp', [(i, i ^ mask) for i in range(count)])  24.7 us
    pallas_call x2, Pallas kernels, forward(): pl.pallas_call(functools.partial(forward_kernel, which, seqs, length), ou...  16.3 us
    all_to_all x1, waiting for transfers between devices, body(): lax.all_to_all(jnp.broadcast_to(own_cls[None], (count,) + own_cls.shape),...  10.1 us
    all_to_all x1, starting transfers between devices, body(): lax.all_to_all(jnp.broadcast_to(own_cls[None], (count,) + own_cls.shape),...  7.5 us
    pallas_call x1, Pallas kernels, passage_backward(): pl.pallas_call(functools.partial(attn_core_kernel, length), out_shape=[sh...  7 us
    pallas_call x1, Pallas kernels, question_backward(): pl.pallas_call(functools.partial(question_back_kernel, which, seqs, lengt...  5.55 us
  transfers between devices with their start and end apart: 29, of which 13 were waited for; matrix products, arithmetic and copies ran while one was open for 4% of the time, Pallas kernels for 10%

profile of v2, /device:TPU:0, one launch (start us, length us, event | category | flops | bytes accessed | tf_op | source)
XLA Modules:
  0.0 172.1 jit_solution(8673533467072557703)
XLA Ops:
  0.7 1.2 copy-done
  1.9 1.2 copy-done.2
  3.1 1.1 copy-done.4
  13.1 12.4 %forward.3 = (bf16[1280,256]{1,0:T(8,128)(2,1)}, f32[8,256]{1,0:T(8,128)S(1)}, bf16[1280,768]{1,0:T(8,128)(2,1)S(1)}, f32[5120,256]{1,0:T(8,128)S(1)}, bf16[1280...) custom-call(s32[5]{0:T(128)S(1)} %copy-done.68, ...), custom_call_target="tpu_custom_call" | custom-call | flops 2048000000 | bytes 15360000 | tf_op jit(solution)/shard_map/forward/pallas_call | solution.py:427
  25.5 2.4 %copy-done.6 = f32[5120,256]{1,0:T(8,128)} copy-done((f32[5120,256]{1,0:T(8,128)}, f32[5120,256]{1,0:T(8,128)S(1)}, u32[]{:S(2)}) %copy-start.6) | copy-done | bytes 5242904
  27.9 2.3 %copy-done.7 = f32[1280,1024]{1,0:T(8,128)} copy-done((f32[1280,1024]{1,0:T(8,128)}, f32[1280,1024]{1,0:T(8,128)S(1)}, u32[]{:S(2)}) %copy-start.7) | copy-done | bytes 5242904
  30.2 1.5 copy-done.8
  31.7 1.3 copy-done.12
  35.6 4.0 %forward.2 = (bf16[320,256]{1,0:T(8,128)(2,1)}, f32[8,256]{1,0:T(8,128)S(1)}, bf16[320,768]{1,0:T(8,128)(2,1)S(1)}, f32[1280,64]{1,0:T(8,128)S(1)}, bf16[320,256...) custom-call(s32[5]{0:T(128)S(1)} %copy-done.59, ...), custom_call_target="tpu_custom_call" | custom-call | flops 512000000 | bytes 3840000 | tf_op jit(solution)/shard_map/forward/pallas_call | solution.py:427
  48.0 7.5 %all-to-all-start = ((bf16[32,16,256]{2,1,0:T(8,128)(2,1)}), bf16[32,16,256]{2,1,0:T(8,128)(2,1)S(1)}, u32[]{:S(2)}, u32[]{:S(2)}) async-start(bf16[32,16,256]{2,1,0:T(8,128)(2,1)} %broadcast_in_dim.69), calls=%async_computation | async-start | bytes 524288 | tf_op jit(solution)/shard_map/all_to_all | solution.py:611
  55.8 10.1 %all-to-all-done.all_ref = bf16[32,16,256]{2,1,0:T(8,128)(2,1)S(1)} async-done(((bf16[32,16,256]{2,1,0:T(8,128)(2,1)}), bf16[32,16,256]{2,1,0:T(8,128)(2,1)S(1)}, u32[]{:S(2)}, u32[]{:S(2)}) %all-to-all-start) | async-done | bytes 262176 | tf_op jit(solution)/shard_map/all_to_all | solution.py:611
  66.7 1.5 copy-done.21
  68.2 1.3 copy-done.34
  79.0 5.6 %question_back.1 = (bf16[320,256]{1,0:T(8,128)(2,1)}, bf16[3328,256]{1,0:T(8,128)(2,1)S(1)}) custom-call(s32[5]{0:T(128)S(1)} %copy-done.59, f32[8,256]{1,0:T(8,128)S(1)} %get-tuple-element.76.cls_ref, bf16[320,256]{1,0:T(8,128)(2,1)S(1)} %bitcast.130, bf16[320,256]{1,0:T(8,128)(2,1)S(1)} %bitcast.129, bf16[320,768]{1,0:T(8,128)(2,1)S(1)} %copy-done.40, ...), custom_call_target="tpu_custom_call" | custom-call | flops 1024000000 | bytes 3840000 | tf_op jit(solution)/shard_map/question_back/pallas_call | solution.py:454
  86.9 3.5 %ffn_back.1 = (f32[1280,256]{1,0:T(8,128)S(1)}, bf16[1280,256]{1,0:T(8,128)(2,1)S(1)}, bf16[1280,1024]{1,0:T(8,128)(2,1)S(1)}, f32[16,256]{1,0:T(8,128)S(1)}) custom-call(s32[5]{0:T(128)S(1)} %copy-done.69, f32[8,256]{1,0:T(8,128)S(1)} %get-tuple-element.88.cls_ref, bf16[1280,256]{1,0:T(8,128)(2,1)S(1)} %bitcast.125, f32[1280,256]{1,0:T(8,128)S(1)} %copy-done.19, ...), custom_call_target="tpu_custom_call" | custom-call | flops 1536000000 | bytes 10240000 | tf_op jit(solution)/shard_map/ffn_back/pallas_call | solution.py:486
  90.4 3.7 %attn_norm_back.1 = (f32[1280,256]{1,0:T(8,128)S(1)}, bf16[1280,256]{1,0:T(8,128)(2,1)S(1)}, f32[16,256]{1,0:T(8,128)S(1)}, bf16[256,256]{1,0:T(8,128)(2,1)S(1)}) custom-call(bf16[1280,1024]{1,0:T(8,128)(2,1)S(1)} %get-tuple-element.92.gpre_ref, bf16[2,256,1024]{2,1,0:T(8,128)(2,1)S(1)} %copy-done.1, f32[1280,256]{1,0:T(8,128)S(1)} %get-tuple-element.93.two_ref, ...), custom_call_target="tpu_custom_call" | custom-call | flops 1536000000 | bytes 10240000 | tf_op jit(solution)/shard_map/attn_norm_back/pallas_call | solution.py:500
  94.2 7.0 %attn_core_back.1 = (bf16[1280,256]{1,0:T(8,128)(2,1)}, f32[16,256]{1,0:T(8,128)S(1)}, bf16[768,256]{1,0:T(8,128)(2,1)S(1)}) custom-call(bf16[1280,256]{1,0:T(8,128)(2,1)S(1)} %get-tuple-element.97.dctx_ref, bf16[1280,768]{1,0:T(8,128)(2,1)S(1)} %copy-done.13, f32[5120,256]{1,0:T(8,128)S(1)} %bitcast.120, bf16[1280,256]{1,0:T(8,128)(2,1)S(1)} %bitcast.127, ...), custom_call_target="tpu_custom_call" | custom-call | flops 2560000000 | bytes 12800000 | tf_op jit(solution)/shard_map/attn_core_back/pallas_call | solution.py:514
  101.2 3.0 %ffn_weights.1 = bf16[3328,256]{1,0:T(8,128)(2,1)S(1)} custom-call(bf16[1280,1024]{1,0:T(8,128)(2,1)S(1)} %copy-done.9, bf16[1280,256]{1,0:T(8,128)(2,1)S(1)} %get-tuple-element.104.gffn_ref, bf16[1280,256]{1,0:T(8,128)(2,1)S(1)} %copy-done.24, bf16[1280,1024]{1,0:T(8,128)(2,1)S(1)} %get-tuple-element.92.gpre_ref, ...), custom_call_target="tpu_custom_call" | custom-call | flops 1536000000 | bytes 7680000 | tf_op jit(solution)/shard_map/ffn_weights/pallas_call | solution.py:531
  106.0 1.4 fusion.1
  108.5 1.5 collective-permute-start.2
  110.0 1.7 %collective-permute-start.3 = (bf16[416,256]{1,0:T(8,128)(2,1)S(1)}, bf16[416,256]{1,0:T(8,128)(2,1)S(1)}, u32[]{:S(2)}, u32[]{:S(2)}) collective-permute-start(bf16[416,256]{1,0:T(8,128)(2,1)S(1)} %get-tuple-element.132), channel_id=1, source_target_pairs={{0,6},{1,7},{2,4},{3,5},{4,2},{5,3},{6,0},{7,1},{8,14},{9,15},{10,... | collective-permute-start | bytes 638984 | tf_op jit(solution)/shard_map/ppermute | solution.py:563
  111.7 1.4 fusion
  113.5 1.5 collective-permute-start.16
  115.0 1.4 collective-permute-done.1
  116.4 1.2 collective-permute-start.17
  118.2 3.1 %collective-permute-done.2 = bf16[416,256]{1,0:T(8,128)(2,1)S(1)} collective-permute-done((bf16[416,256]{1,0:T(8,128)(2,1)}, bf16[416,256]{1,0:T(8,128)(2,1)S(1)}, u32[]{:S(2)}, u32[]{:S(2)}) %collective-permute-start.2) | collective-permute-done | bytes 213024 | tf_op jit(solution)/shard_map/ppermute | solution.py:563
  121.3 4.2 %collective-permute-done.15 = bf16[416,256]{1,0:T(8,128)(2,1)S(1)} collective-permute-done((bf16[416,256]{1,0:T(8,128)(2,1)S(1)}, bf16[416,256]{1,0:T(8,128)(2,1)S(1)}, u32[]{:S(2)}, u32[]{:S(2)}) %collective-permute-start.15) | collective-permute-done | bytes 213024 | tf_op jit(solution)/shard_map/ppermute | solution.py:563
  125.5 4.3 %collective-permute-done.16 = bf16[416,256]{1,0:T(8,128)(2,1)S(1)} collective-permute-done((bf16[416,256]{1,0:T(8,128)(2,1)S(1)}, bf16[416,256]{1,0:T(8,128)(2,1)S(1)}, u32[]{:S(2)}, u32[]{:S(2)}) %collective-permute-start.16) | collective-permute-done | bytes 213024 | tf_op jit(solution)/shard_map/ppermute | solution.py:563
  129.8 1.2 fusion.4
  131.8 1.2 collective-permute-start.19
  132.9 2.6 %collective-permute-start.20 = (bf16[104,256]{1,0:T(8,128)(2,1)S(1)}, bf16[104,256]{1,0:T(8,128)(2,1)S(1)}, u32[]{:S(2)}, u32[]{:S(2)}) collective-permute-start(bf16[104,256]{1,0:T(8,128)(2,1)S(1)} %get-tuple-element.135), channel_id=1, source_target_pairs={{0,24},{1,25},{2,26},{3,27},{4,28},{5,29},{6,30},{7,31},{8,16},{9,... | collective-permute-start | bytes 159752 | tf_op jit(solution)/shard_map/ppermute | solution.py:563
  135.6 1.8 %collective-permute-start.5 = (bf16[104,256]{1,0:T(8,128)(2,1)S(1)}, bf16[104,256]{1,0:T(8,128)(2,1)S(1)}, u32[]{:S(2)}, u32[]{:S(2)}) collective-permute-start(bf16[104,256]{1,0:T(8,128)(2,1)S(1)} %get-tuple-element.139), channel_id=1, source_target_pairs={{0,16},{1,17},{2,18},{3,19},{4,20},{5,21},{6,22},{7,23},{8,24},{9,... | collective-permute-start | bytes 159752 | tf_op jit(solution)/shard_map/ppermute | solution.py:563
  137.4 2.6 %collective-permute-start.6 = (bf16[104,256]{1,0:T(8,128)(2,1)S(1)}, bf16[104,256]{1,0:T(8,128)(2,1)S(1)}, u32[]{:S(2)}, u32[]{:S(2)}) collective-permute-start(bf16[104,256]{1,0:T(8,128)(2,1)S(1)} %get-tuple-element.138), channel_id=1, source_target_pairs={{0,24},{1,25},{2,26},{3,27},{4,28},{5,29},{6,30},{7,31},{8,16},{9,... | collective-permute-start | bytes 159752 | tf_op jit(solution)/shard_map/ppermute | solution.py:563
  140.0 1.1 collective-permute-start.21
  141.2 1.3 collective-permute-start.22
  142.5 2.0 %collective-permute-start.23 = (bf16[104,256]{1,0:T(8,128)(2,1)S(1)}, bf16[104,256]{1,0:T(8,128)(2,1)S(1)}, u32[]{:S(2)}, u32[]{:S(2)}) collective-permute-start(bf16[104,256]{1,0:T(8,128)(2,1)S(1)} %get-tuple-element.125), channel_id=1, source_target_pairs={{0,24},{1,25},{2,26},{3,27},{4,28},{5,29},{6,30},{7,31},{8,16},{9,... | collective-permute-start | bytes 159752 | tf_op jit(solution)/shard_map/ppermute | solution.py:563
  144.6 1.2 collective-permute-start.7
  145.7 1.3 collective-permute-start.8
  147.0 2.0 %collective-permute-start.9 = (bf16[104,256]{1,0:T(8,128)(2,1)S(1)}, bf16[104,256]{1,0:T(8,128)(2,1)S(1)}, u32[]{:S(2)}, u32[]{:S(2)}) collective-permute-start(bf16[104,256]{1,0:T(8,128)(2,1)S(1)} %get-tuple-element.127), channel_id=1, source_target_pairs={{0,24},{1,25},{2,26},{3,27},{4,28},{5,29},{6,30},{7,31},{8,16},{9,... | collective-permute-start | bytes 159752 | tf_op jit(solution)/shard_map/ppermute | solution.py:563
  149.1 1.4 collective-permute-start.24
  151.3 1.3 collective-permute-start.26
  153.0 1.4 collective-permute-start.10
  155.1 2.2 %collective-permute-done.24 = bf16[416,256]{1,0:T(8,128)(2,1)S(1)} collective-permute-done((bf16[416,256]{1,0:T(8,128)(2,1)S(1)}, bf16[416,256]{1,0:T(8,128)(2,1)S(1)}, u32[]{:S(2)}, u32[]{:S(2)}) %collective-permute-start.24) | collective-permute-done | bytes 213024 | tf_op jit(solution)/shard_map/ppermute | solution.py:563
  157.3 1.6 collective-permute-start.12
  159.0 1.8 %collective-permute-done.25 = bf16[416,256]{1,0:T(8,128)(2,1)S(1)} collective-permute-done((bf16[416,256]{1,0:T(8,128)(2,1)S(1)}, bf16[416,256]{1,0:T(8,128)(2,1)S(1)}, u32[]{:S(2)}, u32[]{:S(2)}) %collective-permute-start.25) | collective-permute-done | bytes 213024 | tf_op jit(solution)/shard_map/ppermute | solution.py:563
  163.1 2.2 %collective-permute-done.11 = bf16[416,256]{1,0:T(8,128)(2,1)S(1)} collective-permute-done((bf16[416,256]{1,0:T(8,128)(2,1)S(1)}, bf16[416,256]{1,0:T(8,128)(2,1)S(1)}, u32[]{:S(2)}, u32[]{:S(2)}) %collective-permute-start.11) | collective-permute-done | bytes 213024 | tf_op jit(solution)/shard_map/ppermute | solution.py:563
  167.0 1.9 %collective-permute-done.13 = bf16[1664,256]{1,0:T(8,128)(2,1)S(1)} collective-permute-done((bf16[1664,256]{1,0:T(8,128)(2,1)S(1)}, bf16[1664,256]{1,0:T(8,128)(2,1)S(1)}, u32[]{:S(2)}, u32[]{:S(2)}) %collective-permute-start.13) | collective-permute-done | bytes 852000 | tf_op jit(solution)/shard_map/ppermute | solution.py:563
  168.9 3.0 %unpack.1 = (f32[2,256,768]{2,1,0:T(8,128)}, f32[2,256,256]{2,1,0:T(8,128)}, f32[2,256,1024]{2,1,0:T(8,128)}, f32[2,1024,256]{2,1,0:T(8,128)}, f32[2,1024]{1,0:T...) custom-call(bf16[3328,256]{1,0:T(8,128)(2,1)S(1)} %bitcast.115, ...), custom_call_target="tpu_custom_call" | custom-call | tf_op jit(solution)/shard_map/unpack/pallas_call | solution.py:638
  (219 shorter events, 43.5 us)
Async XLA Ops:
  13.1 22.5 %copy-start.1 = (bf16[2,256,1024]{2,1,0:T(8,128)(2,1)S(1)}, bf16[2,256,1024]{2,1,0:T(8,128)(2,1)}, u32[]{:S(2)}) copy-start(bf16[2,256,1024]{2,1,0:T(8,128)(2,1)} %w1_ref.7) | copy-start | bytes 3145732
  13.1 22.5 %copy-start.3 = (bf16[2,1024,256]{2,1,0:T(8,128)(2,1)S(1)}, bf16[2,1024,256]{2,1,0:T(8,128)(2,1)}, u32[]{:S(2)}) copy-start(bf16[2,1024,256]{2,1,0:T(8,128)(2,1)} %w2_ref.7) | copy-start | bytes 3145732
  13.1 22.5 %copy-start.5 = (bf16[2,256,768]{2,1,0:T(8,128)(2,1)S(1)}, bf16[2,256,768]{2,1,0:T(8,128)(2,1)}, u32[]{:S(2)}) copy-start(bf16[2,256,768]{2,1,0:T(8,128)(2,1)} %wqkv_ref.7) | copy-start | bytes 2359300
  13.1 22.5 %copy-start.37 = (bf16[5,64,256]{2,1,0:T(8,128)(2,1)S(1)}, bf16[5,64,256]{2,1,0:T(8,128)(2,1)}, u32[]{:S(2)}) copy-start(bf16[5,64,256]{2,1,0:T(8,128)(2,1)} %param.20) | copy-start | bytes 491524
  13.1 22.5 %copy-start.55 = (bf16[2,256]{1,0:T(2,128)(2,1)S(1)}, bf16[2,256]{1,0:T(2,128)(2,1)}, u32[]{:S(2)}) copy-start(bf16[2,256]{1,0:T(2,128)(2,1)} %g2_ref.7) | copy-start | bytes 3076
  13.1 22.5 %copy-start.59 = (s32[5]{0:T(128)S(1)}, s32[5]{0:T(128)}, u32[]{:S(2)}) copy-start(s32[5]{0:T(128)} %len_ref.6) | copy-start | bytes 64
  13.1 22.5 %copy-start.65 = (bf16[2,256]{1,0:T(2,128)(2,1)S(1)}, bf16[2,256]{1,0:T(2,128)(2,1)}, u32[]{:S(2)}) copy-start(bf16[2,256]{1,0:T(2,128)(2,1)} %fb_ref.3) | copy-start | bytes 3076
  13.1 22.5 %copy-start.67 = (bf16[2,256]{1,0:T(2,128)(2,1)S(1)}, bf16[2,256]{1,0:T(2,128)(2,1)}, u32[]{:S(2)}) copy-start(bf16[2,256]{1,0:T(2,128)(2,1)} %b2_ref.3) | copy-start | bytes 3076
  35.5 11.7 %copy-start.18 = (f32[1280,256]{1,0:T(8,128)}, f32[1280,256]{1,0:T(8,128)S(1)}, u32[]{:S(2)}) copy-start(f32[1280,256]{1,0:T(8,128)S(1)} %get-tuple-element.89.n2_ref) | copy-start | bytes 3932164
  35.5 11.7 %copy-start.23 = (bf16[1280,256]{1,0:T(8,128)(2,1)}, bf16[1280,256]{1,0:T(8,128)(2,1)S(1)}, u32[]{:S(2)}) copy-start(bf16[1280,256]{1,0:T(8,128)(2,1)S(1)} %get-tuple-element.105.nb_ref) | copy-start | bytes 1966084
  35.6 19.9 %copy-start.71 = (s32[160]{0:T(256)S(1)}, s32[160]{0:T(256)}, u32[]{:S(2)}) copy-start(s32[160]{0:T(256)} %param.26) | copy-start | bytes 1924
  35.6 31.1 %copy-start.11 = (bf16[2,256,256]{2,1,0:T(8,128)(2,1)S(1)}, bf16[2,256,256]{2,1,0:T(8,128)(2,1)}, u32[]{:S(2)}) copy-start(bf16[2,256,256]{2,1,0:T(8,128)(2,1)} %wo_ref.7) | copy-start | bytes 786436
  35.6 31.1 %copy-start.57 = (bf16[2,256]{1,0:T(2,128)(2,1)S(1)}, bf16[2,256]{1,0:T(2,128)(2,1)}, u32[]{:S(2)}) copy-start(bf16[2,256]{1,0:T(2,128)(2,1)} %g1_ref.7) | copy-start | bytes 3076
  48.0 17.9 %all-to-all-start = ((bf16[32,16,256]{2,1,0:T(8,128)(2,1)}), bf16[32,16,256]{2,1,0:T(8,128)(2,1)S(1)}, u32[]{:S(2)}, u32[]{:S(2)}) async-start(bf16[32,16,256]{2,1,0:T(8,128)(2,1)} %broadcast_in_dim.69), calls=%async_computation | async-start | bytes 524288 | tf_op jit(solution)/shard_map/all_to_all | solution.py:611
  66.7 19.3 %slice-start.2 = ((s8[5242880]{0:T(1024)(128)(4,1)}), s8[4194304]{0:T(1024)(128)(4,1)S(1)}, s32[]{:S(2)}) async-start(s8[5242880]{0:T(1024)(128)(4,1)} %bitcast.121), calls=%async_computation.3 | async-start | bytes 8388608
  79.0 7.0 %slice-start.3 = ((s8[5242880]{0:T(1024)(128)(4,1)}), s8[1048576]{0:T(1024)(128)(4,1)S(1)}, s32[]{:S(2)}) async-start(s8[5242880]{0:T(1024)(128)(4,1)} %bitcast.121), calls=%async_computation.4 | async-start | bytes 2097152
  79.0 7.0 %copy-start.22 = (bf16[5,256,256]{2,1,0:T(8,128)(2,1)S(1)}, bf16[5,256,256]{2,1,0:T(8,128)(2,1)}, u32[]{:S(2)}) copy-start(bf16[5,256,256]{2,1,0:T(8,128)(2,1)} %param.23) | copy-start | bytes 1966084
  79.0 7.0 %copy-start.30 = (f32[1280,1]{1,0:T(8,128)S(1)}, f32[1280,1]{1,0:T(8,128)}, u32[]{:S(2)}) copy-start(f32[1280,1]{1,0:T(8,128)} %copy-done.29) | copy-start | bytes 15364
  84.6 9.5 %slice-start = ((s8[5242880]{0:T(1024)(128)(4,1)}), s8[4194304]{0:T(1024)(128)(4,1)S(1)}, s32[]{:S(2)}) async-start(s8[5242880]{0:T(1024)(128)(4,1)} %bitcast.119), calls=%async_computation.1 | async-start | bytes 8388608
  85.6 19.6 %collective-permute-start = (bf16[1664,256]{1,0:T(8,128)(2,1)}, bf16[1664,256]{1,0:T(8,128)(2,1)}, u32[]{:S(2)}, u32[]{:S(2)}) collective-permute-start(bf16[1664,256]{1,0:T(8,128)(2,1)} %dynamic-slice_bitcast_fusion.1), channel_id=1, source_target_pairs={{0,1},{1,0},{2,3},{3,2},{4,5},{5,4},{6,7},{7,6},{8,9},{9,8},{10,11... | collective-permute-start | bytes 2555912 | tf_op jit(solution)/shard_map/ppermute | solution.py:563
  86.8 7.3 %slice-start.1 = ((s8[5242880]{0:T(1024)(128)(4,1)}), s8[1048576]{0:T(1024)(128)(4,1)S(1)}, s32[]{:S(2)}) async-start(s8[5242880]{0:T(1024)(128)(4,1)} %bitcast.119), calls=%async_computation.2 | async-start | bytes 2097152
  105.2 6.5 %collective-permute-start.14 = (bf16[1664,256]{1,0:T(8,128)(2,1)}, bf16[1664,256]{1,0:T(8,128)(2,1)}, u32[]{:S(2)}, u32[]{:S(2)}) collective-permute-start(bf16[1664,256]{1,0:T(8,128)(2,1)} %dynamic-slice_bitcast_fusion), channel_id=1, source_target_pairs={{0,1},{1,0},{2,3},{3,2},{4,5},{5,4},{6,7},{7,6},{8,9},{9,8},{10,11... | collective-permute-start | bytes 2555912 | tf_op jit(solution)/shard_map/ppermute | solution.py:563
  108.2 8.1 %collective-permute-start.1 = (bf16[416,256]{1,0:T(8,128)(2,1)S(1)}, bf16[416,256]{1,0:T(8,128)(2,1)S(1)}, u32[]{:S(2)}, u32[]{:S(2)}) collective-permute-start(bf16[416,256]{1,0:T(8,128)(2,1)S(1)} %get-tuple-element.131), channel_id=1, source_target_pairs={{0,2},{1,3},{2,0},{3,1},{4,6},{5,7},{6,4},{7,5},{8,10},{9,11},{10,... | collective-permute-start | bytes 638984 | tf_op jit(solution)/shard_map/ppermute | solution.py:563
  108.5 12.8 %collective-permute-start.2 = (bf16[416,256]{1,0:T(8,128)(2,1)}, bf16[416,256]{1,0:T(8,128)(2,1)S(1)}, u32[]{:S(2)}, u32[]{:S(2)}) collective-permute-start(bf16[416,256]{1,0:T(8,128)(2,1)} %get-tuple-element.133), channel_id=1, source_target_pairs={{0,4},{1,5},{2,6},{3,7},{4,0},{5,1},{6,2},{7,3},{8,12},{9,13},{10,... | collective-permute-start | bytes 638984 | tf_op jit(solution)/shard_map/ppermute | solution.py:563
  110.0 11.4 %collective-permute-start.3 = (bf16[416,256]{1,0:T(8,128)(2,1)S(1)}, bf16[416,256]{1,0:T(8,128)(2,1)S(1)}, u32[]{:S(2)}, u32[]{:S(2)}) collective-permute-start(bf16[416,256]{1,0:T(8,128)(2,1)S(1)} %get-tuple-element.132), channel_id=1, source_target_pairs={{0,6},{1,7},{2,4},{3,5},{4,2},{5,3},{6,0},{7,1},{8,14},{9,15},{10,... | collective-permute-start | bytes 638984 | tf_op jit(solution)/shard_map/ppermute | solution.py:563
  113.2 12.3 %collective-permute-start.15 = (bf16[416,256]{1,0:T(8,128)(2,1)S(1)}, bf16[416,256]{1,0:T(8,128)(2,1)S(1)}, u32[]{:S(2)}, u32[]{:S(2)}) collective-permute-start(bf16[416,256]{1,0:T(8,128)(2,1)S(1)} %get-tuple-element.128), channel_id=1, source_target_pairs={{0,2},{1,3},{2,0},{3,1},{4,6},{5,7},{6,4},{7,5},{8,10},{9,11},{10,... | collective-permute-start | bytes 638984 | tf_op jit(solution)/shard_map/ppermute | solution.py:563
  113.5 16.3 %collective-permute-start.16 = (bf16[416,256]{1,0:T(8,128)(2,1)S(1)}, bf16[416,256]{1,0:T(8,128)(2,1)S(1)}, u32[]{:S(2)}, u32[]{:S(2)}) collective-permute-start(bf16[416,256]{1,0:T(8,128)(2,1)S(1)} %get-tuple-element.130), channel_id=1, source_target_pairs={{0,4},{1,5},{2,6},{3,7},{4,0},{5,1},{6,2},{7,3},{8,12},{9,13},{10,... | collective-permute-start | bytes 638984 | tf_op jit(solution)/shard_map/ppermute | solution.py:563
  116.4 13.5 %collective-permute-start.17 = (bf16[416,256]{1,0:T(8,128)(2,1)S(1)}, bf16[416,256]{1,0:T(8,128)(2,1)S(1)}, u32[]{:S(2)}, u32[]{:S(2)}) collective-permute-start(bf16[416,256]{1,0:T(8,128)(2,1)S(1)} %get-tuple-element.129), channel_id=1, source_target_pairs={{0,6},{1,7},{2,4},{3,5},{4,2},{5,3},{6,0},{7,1},{8,14},{9,15},{10,... | collective-permute-start | bytes 638984 | tf_op jit(solution)/shard_map/ppermute | solution.py:563
  131.0 6.3 %collective-permute-start.18 = (bf16[104,256]{1,0:T(8,128)(2,1)S(1)}, bf16[104,256]{1,0:T(8,128)(2,1)S(1)}, u32[]{:S(2)}, u32[]{:S(2)}) collective-permute-start(bf16[104,256]{1,0:T(8,128)(2,1)S(1)} %get-tuple-element.134), channel_id=1, source_target_pairs={{0,8},{1,9},{2,10},{3,11},{4,12},{5,13},{6,14},{7,15},{8,0},{9,1},... | collective-permute-start | bytes 159752 | tf_op jit(solution)/shard_map/ppermute | solution.py:563
  131.8 8.2 %collective-permute-start.19 = (bf16[104,256]{1,0:T(8,128)(2,1)S(1)}, bf16[104,256]{1,0:T(8,128)(2,1)S(1)}, u32[]{:S(2)}, u32[]{:S(2)}) collective-permute-start(bf16[104,256]{1,0:T(8,128)(2,1)S(1)} %get-tuple-element.136), channel_id=1, source_target_pairs={{0,16},{1,17},{2,18},{3,19},{4,20},{5,21},{6,22},{7,23},{8,24},{9,... | collective-permute-start | bytes 159752 | tf_op jit(solution)/shard_map/ppermute | solution.py:563
  132.9 7.1 %collective-permute-start.20 = (bf16[104,256]{1,0:T(8,128)(2,1)S(1)}, bf16[104,256]{1,0:T(8,128)(2,1)S(1)}, u32[]{:S(2)}, u32[]{:S(2)}) collective-permute-start(bf16[104,256]{1,0:T(8,128)(2,1)S(1)} %get-tuple-element.135), channel_id=1, source_target_pairs={{0,24},{1,25},{2,26},{3,27},{4,28},{5,29},{6,30},{7,31},{8,16},{9,... | collective-permute-start | bytes 159752 | tf_op jit(solution)/shard_map/ppermute | solution.py:563
  135.5 7.0 %collective-permute-start.4 = (bf16[104,256]{1,0:T(8,128)(2,1)S(1)}, bf16[104,256]{1,0:T(8,128)(2,1)S(1)}, u32[]{:S(2)}, u32[]{:S(2)}) collective-permute-start(bf16[104,256]{1,0:T(8,128)(2,1)S(1)} %get-tuple-element.137), channel_id=1, source_target_pairs={{0,8},{1,9},{2,10},{3,11},{4,12},{5,13},{6,14},{7,15},{8,0},{9,1},... | collective-permute-start | bytes 159752 | tf_op jit(solution)/shard_map/ppermute | solution.py:563
  135.6 8.9 %collective-permute-start.5 = (bf16[104,256]{1,0:T(8,128)(2,1)S(1)}, bf16[104,256]{1,0:T(8,128)(2,1)S(1)}, u32[]{:S(2)}, u32[]{:S(2)}) collective-permute-start(bf16[104,256]{1,0:T(8,128)(2,1)S(1)} %get-tuple-element.139), channel_id=1, source_target_pairs={{0,16},{1,17},{2,18},{3,19},{4,20},{5,21},{6,22},{7,23},{8,24},{9,... | collective-permute-start | bytes 159752 | tf_op jit(solution)/shard_map/ppermute | solution.py:563
  137.4 7.1 %collective-permute-start.6 = (bf16[104,256]{1,0:T(8,128)(2,1)S(1)}, bf16[104,256]{1,0:T(8,128)(2,1)S(1)}, u32[]{:S(2)}, u32[]{:S(2)}) collective-permute-start(bf16[104,256]{1,0:T(8,128)(2,1)S(1)} %get-tuple-element.138), channel_id=1, source_target_pairs={{0,24},{1,25},{2,26},{3,27},{4,28},{5,29},{6,30},{7,31},{8,16},{9,... | collective-permute-start | bytes 159752 | tf_op jit(solution)/shard_map/ppermute | solution.py:563
  140.0 7.0 %collective-permute-start.21 = (bf16[104,256]{1,0:T(8,128)(2,1)S(1)}, bf16[104,256]{1,0:T(8,128)(2,1)S(1)}, u32[]{:S(2)}, u32[]{:S(2)}) collective-permute-start(bf16[104,256]{1,0:T(8,128)(2,1)S(1)} %get-tuple-element.125), channel_id=1, source_target_pairs={{0,8},{1,9},{2,10},{3,11},{4,12},{5,13},{6,14},{7,15},{8,0},{9,1},... | collective-permute-start | bytes 159752 | tf_op jit(solution)/shard_map/ppermute | solution.py:563
  141.2 7.9 %collective-permute-start.22 = (bf16[104,256]{1,0:T(8,128)(2,1)S(1)}, bf16[104,256]{1,0:T(8,128)(2,1)S(1)}, u32[]{:S(2)}, u32[]{:S(2)}) collective-permute-start(bf16[104,256]{1,0:T(8,128)(2,1)S(1)} %get-tuple-element.125), channel_id=1, source_target_pairs={{0,16},{1,17},{2,18},{3,19},{4,20},{5,21},{6,22},{7,23},{8,24},{9,... | collective-permute-start | bytes 159752 | tf_op jit(solution)/shard_map/ppermute | solution.py:563
  142.5 6.5 %collective-permute-start.23 = (bf16[104,256]{1,0:T(8,128)(2,1)S(1)}, bf16[104,256]{1,0:T(8,128)(2,1)S(1)}, u32[]{:S(2)}, u32[]{:S(2)}) collective-permute-start(bf16[104,256]{1,0:T(8,128)(2,1)S(1)} %get-tuple-element.125), channel_id=1, source_target_pairs={{0,24},{1,25},{2,26},{3,27},{4,28},{5,29},{6,30},{7,31},{8,16},{9,... | collective-permute-start | bytes 159752 | tf_op jit(solution)/shard_map/ppermute | solution.py:563
  144.6 6.8 %collective-permute-start.7 = (bf16[104,256]{1,0:T(8,128)(2,1)S(1)}, bf16[104,256]{1,0:T(8,128)(2,1)S(1)}, u32[]{:S(2)}, u32[]{:S(2)}) collective-permute-start(bf16[104,256]{1,0:T(8,128)(2,1)S(1)} %get-tuple-element.127), channel_id=1, source_target_pairs={{0,8},{1,9},{2,10},{3,11},{4,12},{5,13},{6,14},{7,15},{8,0},{9,1},... | collective-permute-start | bytes 159752 | tf_op jit(solution)/shard_map/ppermute | solution.py:563
  145.7 6.9 %collective-permute-start.8 = (bf16[104,256]{1,0:T(8,128)(2,1)S(1)}, bf16[104,256]{1,0:T(8,128)(2,1)S(1)}, u32[]{:S(2)}, u32[]{:S(2)}) collective-permute-start(bf16[104,256]{1,0:T(8,128)(2,1)S(1)} %get-tuple-element.127), channel_id=1, source_target_pairs={{0,16},{1,17},{2,18},{3,19},{4,20},{5,21},{6,22},{7,23},{8,24},{9,... | collective-permute-start | bytes 159752 | tf_op jit(solution)/shard_map/ppermute | solution.py:563
  147.0 5.9 %collective-permute-start.9 = (bf16[104,256]{1,0:T(8,128)(2,1)S(1)}, bf16[104,256]{1,0:T(8,128)(2,1)S(1)}, u32[]{:S(2)}, u32[]{:S(2)}) collective-permute-start(bf16[104,256]{1,0:T(8,128)(2,1)S(1)} %get-tuple-element.127), channel_id=1, source_target_pairs={{0,24},{1,25},{2,26},{3,27},{4,28},{5,29},{6,30},{7,31},{8,16},{9,... | collective-permute-start | bytes 159752 | tf_op jit(solution)/shard_map/ppermute | solution.py:563
  149.1 8.3 %collective-permute-start.24 = (bf16[416,256]{1,0:T(8,128)(2,1)S(1)}, bf16[416,256]{1,0:T(8,128)(2,1)S(1)}, u32[]{:S(2)}, u32[]{:S(2)}) collective-permute-start(bf16[416,256]{1,0:T(8,128)(2,1)S(1)} %bitcast.147), channel_id=1, source_target_pairs={{0,2},{1,3},{2,0},{3,1},{4,6},{5,7},{6,4},{7,5},{8,10},{9,11},{10,... | collective-permute-start | bytes 638984 | tf_op jit(solution)/shard_map/ppermute | solution.py:563
  150.5 10.2 %collective-permute-start.25 = (bf16[416,256]{1,0:T(8,128)(2,1)S(1)}, bf16[416,256]{1,0:T(8,128)(2,1)S(1)}, u32[]{:S(2)}, u32[]{:S(2)}) collective-permute-start(bf16[416,256]{1,0:T(8,128)(2,1)S(1)} %bitcast.148), channel_id=1, source_target_pairs={{0,4},{1,5},{2,6},{3,7},{4,0},{5,1},{6,2},{7,3},{8,12},{9,13},{10,... | collective-permute-start | bytes 638984 | tf_op jit(solution)/shard_map/ppermute | solution.py:563
  151.3 10.6 %collective-permute-start.26 = (bf16[416,256]{1,0:T(8,128)(2,1)S(1)}, bf16[416,256]{1,0:T(8,128)(2,1)S(1)}, u32[]{:S(2)}, u32[]{:S(2)}) collective-permute-start(bf16[416,256]{1,0:T(8,128)(2,1)S(1)} %bitcast.149), channel_id=1, source_target_pairs={{0,6},{1,7},{2,4},{3,5},{4,2},{5,3},{6,0},{7,1},{8,14},{9,15},{10,... | collective-permute-start | bytes 638984 | tf_op jit(solution)/shard_map/ppermute | solution.py:563
  153.0 10.1 %collective-permute-start.10 = (bf16[416,256]{1,0:T(8,128)(2,1)S(1)}, bf16[416,256]{1,0:T(8,128)(2,1)S(1)}, u32[]{:S(2)}, u32[]{:S(2)}) collective-permute-start(bf16[416,256]{1,0:T(8,128)(2,1)S(1)} %bitcast.143), channel_id=1, source_target_pairs={{0,2},{1,3},{2,0},{3,1},{4,6},{5,7},{6,4},{7,5},{8,10},{9,11},{10,... | collective-permute-start | bytes 638984 | tf_op jit(solution)/shard_map/ppermute | solution.py:563
  154.4 10.9 %collective-permute-start.11 = (bf16[416,256]{1,0:T(8,128)(2,1)S(1)}, bf16[416,256]{1,0:T(8,128)(2,1)S(1)}, u32[]{:S(2)}, u32[]{:S(2)}) collective-permute-start(bf16[416,256]{1,0:T(8,128)(2,1)S(1)} %bitcast.144), channel_id=1, source_target_pairs={{0,4},{1,5},{2,6},{3,7},{4,0},{5,1},{6,2},{7,3},{8,12},{9,13},{10,... | collective-permute-start | bytes 638984 | tf_op jit(solution)/shard_map/ppermute | solution.py:563
  157.3 9.1 %collective-permute-start.12 = (bf16[416,256]{1,0:T(8,128)(2,1)S(1)}, bf16[416,256]{1,0:T(8,128)(2,1)S(1)}, u32[]{:S(2)}, u32[]{:S(2)}) collective-permute-start(bf16[416,256]{1,0:T(8,128)(2,1)S(1)} %bitcast.146), channel_id=1, source_target_pairs={{0,6},{1,7},{2,4},{3,5},{4,2},{5,3},{6,0},{7,1},{8,14},{9,15},{10,... | collective-permute-start | bytes 638984 | tf_op jit(solution)/shard_map/ppermute | solution.py:563
  161.9 5.0 %collective-permute-start.27 = (bf16[1664,256]{1,0:T(8,128)(2,1)S(1)}, bf16[1664,256]{1,0:T(8,128)(2,1)S(1)}, u32[]{:S(2)}, u32[]{:S(2)}) collective-permute-start(bf16[1664,256]{1,0:T(8,128)(2,1)S(1)} %bitcast.133), channel_id=1, source_target_pairs={{0,1},{1,0},{2,3},{3,2},{4,5},{5,4},{6,7},{7,6},{8,9},{9,8},{10,11... | collective-permute-start | bytes 2555912 | tf_op jit(solution)/shard_map/ppermute | solution.py:563
  166.4 2.4 %collective-permute-start.13 = (bf16[1664,256]{1,0:T(8,128)(2,1)S(1)}, bf16[1664,256]{1,0:T(8,128)(2,1)S(1)}, u32[]{:S(2)}, u32[]{:S(2)}) collective-permute-start(bf16[1664,256]{1,0:T(8,128)(2,1)S(1)} %bitcast.131), channel_id=1, source_target_pairs={{0,1},{1,0},{2,3},{3,2},{4,5},{5,4},{6,7},{7,6},{8,9},{9,8},{10,11... | collective-permute-start | bytes 2555912 | tf_op jit(solution)/shard_map/ppermute | solution.py:563
  (57 other events, 92.1 us)

commit v3 on v2

--- a/solution.py
+++ b/solution.py
@@ -409,8 +409,17 @@
     return whole((2, columns))
 
 
+def in_hbm(values):
+    return pltpu.with_memory_space_constraint(values, pltpu.HBM)
+
+
+def in_vmem(values):
+    return pltpu.with_memory_space_constraint(values, pltpu.VMEM)
+
+
 def forward(which, steps, seqs, length, lengths, x, weights):
-    wqkv, qb, vb, wo, ob, g1, b1, w1, hb, w2, fb, g2, b2 = weights
+    x = in_hbm(x)
+    wqkv, qb, vb, wo, ob, g1, b1, w1, hb, w2, fb, g2, b2 = [in_hbm(member) for member in weights]
     rows = seqs * length
     total = steps * rows
     stack = HEADS * length
@@ -424,6 +433,7 @@
     out_specs[1:1] = [whole((PAD, WIDTH))]
     out_shape[3:3] = [shape((steps * seqs * stack, length), f32)]
     out_specs[3:3] = [rows_of(seqs * stack, length)]
+    out_shape[1:] = [pltpu.VMEM(o.shape, o.dtype) for o in out_shape[1:]]
     return pl.pallas_call(
         functools.partial(forward_kernel, which, seqs, length),
         out_shape=out_shape,
@@ -448,7 +458,7 @@
 
 def question_backward(which, seqs, length, lengths, cls_grad, cot, x, saved, weights):
     wqkv, qb, vb, wo, ob, g1, b1, w1, hb, w2, fb, g2, b2 = weights
-    _, _, qkv, p, ctx, n1, r1, nb, gp, act, n2, r2 = saved
+    qkv, p, ctx, n1, r1, nb, gp, act, n2, r2 = [in_vmem(member) for member in saved[2:]]
     rows = seqs * length
     stack = HEADS * length
     return pl.pallas_call(
@@ -477,7 +487,7 @@
 
 def passage_backward(which, steps, length, lengths, cls_grad, cot, x, saved, weights):
     wqkv, qb, vb, wo, ob, g1, b1, w1, hb, w2, fb, g2, b2 = weights
-    _, _, qkv, p, ctx, n1, r1, nb, gp, act, n2, r2 = saved
+    qkv, p, ctx, n1, r1, nb, gp, act, n2, r2 = [in_vmem(member) for member in saved[2:]]
     rows = length
     total = steps * rows
     stack = HEADS * length

time: 173 us -> 164 us (0.948)
  local copies, waits for them, and re-layouts: 49.8 us -> 37.6 us
  Pallas kernels: 42.9 us -> 45.9 us
    unnamed x152 -> x118, local copies, waits for them, and re-layouts: 44.4 us -> 32.3 us
    pallas_call x2, Pallas kernels: 16.3 us -> 19.4 us  [forward(): pl.pallas_call(functools.partial(forward_kernel, which, seqs, length), ou...]
  transfers between devices with their start and end apart: 29 -> 29, of which waited for: 13 -> 13; matrix products, arithmetic and copies ran while one was open for 4% -> 4% of each run, Pallas kernels for 10% -> 11%
where the time goes in v3:
time: 164 us; the launch traced here: 163 us
  Pallas kernels  45.9 us (28%)
  starting transfers between devices  38.9 us (24%)
  local copies, waits for them, and re-layouts  37.6 us (23%)
  waiting for transfers between devices  34.9 us (21%)
  other arithmetic  4.07 us (2%)
    unnamed x118, local copies, waits for them, and re-layouts  32.3 us
    ppermute x28, starting transfers between devices, partner_send(): return lax.ppermute(values, 'dp', [(i, i ^ mask) for i in range(count)])  31.4 us
    ppermute x28, waiting for transfers between devices, partner_send(): return lax.ppermute(values, 'dp', [(i, i ^ mask) for i in range(count)])  24.9 us
    pallas_call x2, Pallas kernels, forward(): pl.pallas_call(functools.partial(forward_kernel, which, seqs, length), ou...  19.4 us
    all_to_all x1, waiting for transfers between devices, body(): lax.all_to_all(jnp.broadcast_to(own_cls[None], (count,) + own_cls.shape),...  10.1 us
    all_to_all x1, starting transfers between devices, body(): lax.all_to_all(jnp.broadcast_to(own_cls[None], (count,) + own_cls.shape),...  7.48 us
    pallas_call x1, Pallas kernels, passage_backward(): pl.pallas_call(functools.partial(attn_core_kernel, length), out_shape=[sh...  7 us
    pallas_call x1, Pallas kernels, question_backward(): pl.pallas_call(functools.partial(question_back_kernel, which, seqs, lengt...  5.54 us
  transfers between devices with their start and end apart: 29, of which 13 were waited for; matrix products, arithmetic and copies ran while one was open for 4% of the time, Pallas kernels for 11%

profile of v3, /device:TPU:0, one launch (start us, length us, event | category | flops | bytes accessed | tf_op | source)
XLA Modules:
  0.0 162.9 jit_solution(10877550499186225375)
XLA Ops:
  1.3 13.5 %forward.3 = (bf16[1280,256]{1,0:T(8,128)(2,1)}, f32[8,256]{1,0:T(8,128)S(1)}, bf16[1280,768]{1,0:T(8,128)(2,1)S(1)}, f32[5120,256]{1,0:T(8,128)S(1)}, bf16[1280...) custom-call(s32[5]{0:T(128)S(1)} %copy-done.51, ...), custom_call_target="tpu_custom_call" | custom-call | flops 2048000000 | bytes 15360000 | tf_op jit(solution)/shard_map/forward/pallas_call | solution.py:437
  14.8 2.3 %copy-done.3 = f32[5120,256]{1,0:T(8,128)} copy-done((f32[5120,256]{1,0:T(8,128)}, f32[5120,256]{1,0:T(8,128)S(1)}, u32[]{:S(2)}) %copy-start.3) | copy-done | bytes 5242904
  17.1 2.3 %copy-done.4 = f32[1280,1024]{1,0:T(8,128)} copy-done((f32[1280,1024]{1,0:T(8,128)}, f32[1280,1024]{1,0:T(8,128)S(1)}, u32[]{:S(2)}) %copy-start.4) | copy-done | bytes 5242904
  19.5 1.5 copy-done.5
  21.0 1.3 copy-done.8
  22.3 1.1 copy-done.12
  24.5 5.9 %forward.2 = (bf16[320,256]{1,0:T(8,128)(2,1)}, f32[8,256]{1,0:T(8,128)S(1)}, bf16[320,768]{1,0:T(8,128)(2,1)S(1)}, f32[1280,64]{1,0:T(8,128)S(1)}, bf16[320,256...) custom-call(s32[5]{0:T(128)S(1)} %copy-done.50, ...), custom_call_target="tpu_custom_call" | custom-call | flops 512000000 | bytes 3840000 | tf_op jit(solution)/shard_map/forward/pallas_call | solution.py:437
  38.8 7.5 %all-to-all-start = ((bf16[32,16,256]{2,1,0:T(8,128)(2,1)}), bf16[32,16,256]{2,1,0:T(8,128)(2,1)S(1)}, u32[]{:S(2)}, u32[]{:S(2)}) async-start(bf16[32,16,256]{2,1,0:T(8,128)(2,1)} %broadcast_in_dim.69), calls=%async_computation | async-start | bytes 524288 | tf_op jit(solution)/shard_map/all_to_all | solution.py:621
  46.6 10.1 %all-to-all-done.all_ref = bf16[32,16,256]{2,1,0:T(8,128)(2,1)S(1)} async-done(((bf16[32,16,256]{2,1,0:T(8,128)(2,1)}), bf16[32,16,256]{2,1,0:T(8,128)(2,1)S(1)}, u32[]{:S(2)}, u32[]{:S(2)}) %all-to-all-start) | async-done | bytes 262176 | tf_op jit(solution)/shard_map/all_to_all | solution.py:621
  57.6 1.5 copy-done.17
  59.0 1.2 copy-done.29
  60.3 1.1 copy-done.31
  69.8 5.5 %question_back.1 = (bf16[320,256]{1,0:T(8,128)(2,1)}, bf16[3328,256]{1,0:T(8,128)(2,1)S(1)}) custom-call(s32[5]{0:T(128)S(1)} %copy-done.50, f32[8,256]{1,0:T(8,128)S(1)} %get-tuple-element.76.cls_ref, bf16[320,256]{1,0:T(8,128)(2,1)S(1)} %bitcast.130, bf16[320,256]{1,0:T(8,128)(2,1)S(1)} %bitcast.129, bf16[320,768]{1,0:T(8,128)(2,1)S(1)} %copy-done.34, ...), custom_call_target="tpu_custom_call" | custom-call | flops 1024000000 | bytes 3840000 | tf_op jit(solution)/shard_map/question_back/pallas_call | solution.py:464
  77.6 3.5 %ffn_back.1 = (f32[1280,256]{1,0:T(8,128)S(1)}, bf16[1280,256]{1,0:T(8,128)(2,1)S(1)}, bf16[1280,1024]{1,0:T(8,128)(2,1)S(1)}, f32[16,256]{1,0:T(8,128)S(1)}) custom-call(s32[5]{0:T(128)S(1)} %copy-done.52, f32[8,256]{1,0:T(8,128)S(1)} %get-tuple-element.88.cls_ref, bf16[1280,256]{1,0:T(8,128)(2,1)S(1)} %bitcast.125, f32[1280,256]{1,0:T(8,128)S(1)} %copy-done.15, ...), custom_call_target="tpu_custom_call" | custom-call | flops 1536000000 | bytes 10240000 | tf_op jit(solution)/shard_map/ffn_back/pallas_call | solution.py:496
  81.2 3.7 %attn_norm_back.1 = (f32[1280,256]{1,0:T(8,128)S(1)}, bf16[1280,256]{1,0:T(8,128)(2,1)S(1)}, f32[16,256]{1,0:T(8,128)S(1)}, bf16[256,256]{1,0:T(8,128)(2,1)S(1)}) custom-call(bf16[1280,1024]{1,0:T(8,128)(2,1)S(1)} %get-tuple-element.92.gpre_ref, bf16[2,256,1024]{2,1,0:T(8,128)(2,1)S(1)} %copy-done, f32[1280,256]{1,0:T(8,128)S(1)} %get-tuple-element.93.two_ref, ...), custom_call_target="tpu_custom_call" | custom-call | flops 1536000000 | bytes 10240000 | tf_op jit(solution)/shard_map/attn_norm_back/pallas_call | solution.py:510
  85.0 7.0 %attn_core_back.1 = (bf16[1280,256]{1,0:T(8,128)(2,1)}, f32[16,256]{1,0:T(8,128)S(1)}, bf16[768,256]{1,0:T(8,128)(2,1)S(1)}) custom-call(bf16[1280,256]{1,0:T(8,128)(2,1)S(1)} %get-tuple-element.97.dctx_ref, bf16[1280,768]{1,0:T(8,128)(2,1)S(1)} %copy-done.9, f32[5120,256]{1,0:T(8,128)S(1)} %bitcast.120, bf16[1280,256]{1,0:T(8,128)(2,1)S(1)} %bitcast.127, ...), custom_call_target="tpu_custom_call" | custom-call | flops 2560000000 | bytes 12800000 | tf_op jit(solution)/shard_map/attn_core_back/pallas_call | solution.py:524
  92.0 3.0 %ffn_weights.1 = bf16[3328,256]{1,0:T(8,128)(2,1)S(1)} custom-call(bf16[1280,1024]{1,0:T(8,128)(2,1)S(1)} %copy-done.6, bf16[1280,256]{1,0:T(8,128)(2,1)S(1)} %get-tuple-element.104.gffn_ref, bf16[1280,256]{1,0:T(8,128)(2,1)S(1)} %copy-done.20, bf16[1280,1024]{1,0:T(8,128)(2,1)S(1)} %get-tuple-element.92.gpre_ref, ...), custom_call_target="tpu_custom_call" | custom-call | flops 1536000000 | bytes 7680000 | tf_op jit(solution)/shard_map/ffn_weights/pallas_call | solution.py:541
  96.8 1.4 fusion.1
  99.3 1.5 collective-permute-start.2
  100.8 1.7 %collective-permute-start.3 = (bf16[416,256]{1,0:T(8,128)(2,1)S(1)}, bf16[416,256]{1,0:T(8,128)(2,1)S(1)}, u32[]{:S(2)}, u32[]{:S(2)}) collective-permute-start(bf16[416,256]{1,0:T(8,128)(2,1)S(1)} %get-tuple-element.132), channel_id=1, source_target_pairs={{0,6},{1,7},{2,4},{3,5},{4,2},{5,3},{6,0},{7,1},{8,14},{9,15},{10,... | collective-permute-start | bytes 638984 | tf_op jit(solution)/shard_map/ppermute | solution.py:573
  102.5 1.4 fusion
  104.3 1.5 collective-permute-start.16
  105.8 1.3 collective-permute-done.1
  107.2 1.2 collective-permute-start.17
  109.0 3.1 %collective-permute-done.2 = bf16[416,256]{1,0:T(8,128)(2,1)S(1)} collective-permute-done((bf16[416,256]{1,0:T(8,128)(2,1)}, bf16[416,256]{1,0:T(8,128)(2,1)S(1)}, u32[]{:S(2)}, u32[]{:S(2)}) %collective-permute-start.2) | collective-permute-done | bytes 213024 | tf_op jit(solution)/shard_map/ppermute | solution.py:573
  112.1 4.2 %collective-permute-done.15 = bf16[416,256]{1,0:T(8,128)(2,1)S(1)} collective-permute-done((bf16[416,256]{1,0:T(8,128)(2,1)S(1)}, bf16[416,256]{1,0:T(8,128)(2,1)S(1)}, u32[]{:S(2)}, u32[]{:S(2)}) %collective-permute-start.15) | collective-permute-done | bytes 213024 | tf_op jit(solution)/shard_map/ppermute | solution.py:573
  116.3 4.3 %collective-permute-done.16 = bf16[416,256]{1,0:T(8,128)(2,1)S(1)} collective-permute-done((bf16[416,256]{1,0:T(8,128)(2,1)S(1)}, bf16[416,256]{1,0:T(8,128)(2,1)S(1)}, u32[]{:S(2)}, u32[]{:S(2)}) %collective-permute-start.16) | collective-permute-done | bytes 213024 | tf_op jit(solution)/shard_map/ppermute | solution.py:573
  120.6 1.2 fusion.4
  122.6 1.2 collective-permute-start.19
  123.7 2.6 %collective-permute-start.20 = (bf16[104,256]{1,0:T(8,128)(2,1)S(1)}, bf16[104,256]{1,0:T(8,128)(2,1)S(1)}, u32[]{:S(2)}, u32[]{:S(2)}) collective-permute-start(bf16[104,256]{1,0:T(8,128)(2,1)S(1)} %get-tuple-element.135), channel_id=1, source_target_pairs={{0,24},{1,25},{2,26},{3,27},{4,28},{5,29},{6,30},{7,31},{8,16},{9,... | collective-permute-start | bytes 159752 | tf_op jit(solution)/shard_map/ppermute | solution.py:573
  126.4 1.8 %collective-permute-start.5 = (bf16[104,256]{1,0:T(8,128)(2,1)S(1)}, bf16[104,256]{1,0:T(8,128)(2,1)S(1)}, u32[]{:S(2)}, u32[]{:S(2)}) collective-permute-start(bf16[104,256]{1,0:T(8,128)(2,1)S(1)} %get-tuple-element.139), channel_id=1, source_target_pairs={{0,16},{1,17},{2,18},{3,19},{4,20},{5,21},{6,22},{7,23},{8,24},{9,... | collective-permute-start | bytes 159752 | tf_op jit(solution)/shard_map/ppermute | solution.py:573
  128.2 2.6 %collective-permute-start.6 = (bf16[104,256]{1,0:T(8,128)(2,1)S(1)}, bf16[104,256]{1,0:T(8,128)(2,1)S(1)}, u32[]{:S(2)}, u32[]{:S(2)}) collective-permute-start(bf16[104,256]{1,0:T(8,128)(2,1)S(1)} %get-tuple-element.138), channel_id=1, source_target_pairs={{0,24},{1,25},{2,26},{3,27},{4,28},{5,29},{6,30},{7,31},{8,16},{9,... | collective-permute-start | bytes 159752 | tf_op jit(solution)/shard_map/ppermute | solution.py:573
  130.8 1.1 collective-permute-start.21
  132.0 1.3 collective-permute-start.22
  133.3 2.0 %collective-permute-start.23 = (bf16[104,256]{1,0:T(8,128)(2,1)S(1)}, bf16[104,256]{1,0:T(8,128)(2,1)S(1)}, u32[]{:S(2)}, u32[]{:S(2)}) collective-permute-start(bf16[104,256]{1,0:T(8,128)(2,1)S(1)} %get-tuple-element.125), channel_id=1, source_target_pairs={{0,24},{1,25},{2,26},{3,27},{4,28},{5,29},{6,30},{7,31},{8,16},{9,... | collective-permute-start | bytes 159752 | tf_op jit(solution)/shard_map/ppermute | solution.py:573
  135.4 1.2 collective-permute-start.7
  136.5 1.3 collective-permute-start.8
  137.8 2.0 %collective-permute-start.9 = (bf16[104,256]{1,0:T(8,128)(2,1)S(1)}, bf16[104,256]{1,0:T(8,128)(2,1)S(1)}, u32[]{:S(2)}, u32[]{:S(2)}) collective-permute-start(bf16[104,256]{1,0:T(8,128)(2,1)S(1)} %get-tuple-element.127), channel_id=1, source_target_pairs={{0,24},{1,25},{2,26},{3,27},{4,28},{5,29},{6,30},{7,31},{8,16},{9,... | collective-permute-start | bytes 159752 | tf_op jit(solution)/shard_map/ppermute | solution.py:573
  139.9 1.4 collective-permute-start.24
  142.1 1.4 collective-permute-start.26
  143.8 1.4 collective-permute-start.10
  145.9 2.3 %collective-permute-done.24 = bf16[416,256]{1,0:T(8,128)(2,1)S(1)} collective-permute-done((bf16[416,256]{1,0:T(8,128)(2,1)S(1)}, bf16[416,256]{1,0:T(8,128)(2,1)S(1)}, u32[]{:S(2)}, u32[]{:S(2)}) %collective-permute-start.24) | collective-permute-done | bytes 213024 | tf_op jit(solution)/shard_map/ppermute | solution.py:573
  148.1 1.5 collective-permute-start.12
  149.7 1.8 %collective-permute-done.25 = bf16[416,256]{1,0:T(8,128)(2,1)S(1)} collective-permute-done((bf16[416,256]{1,0:T(8,128)(2,1)S(1)}, bf16[416,256]{1,0:T(8,128)(2,1)S(1)}, u32[]{:S(2)}, u32[]{:S(2)}) %collective-permute-start.25) | collective-permute-done | bytes 213024 | tf_op jit(solution)/shard_map/ppermute | solution.py:573
  151.6 1.1 collective-permute-done.26
  153.9 2.2 %collective-permute-done.11 = bf16[416,256]{1,0:T(8,128)(2,1)S(1)} collective-permute-done((bf16[416,256]{1,0:T(8,128)(2,1)S(1)}, bf16[416,256]{1,0:T(8,128)(2,1)S(1)}, u32[]{:S(2)}, u32[]{:S(2)}) %collective-permute-start.11) | collective-permute-done | bytes 213024 | tf_op jit(solution)/shard_map/ppermute | solution.py:573
  157.8 1.9 %collective-permute-done.13 = bf16[1664,256]{1,0:T(8,128)(2,1)S(1)} collective-permute-done((bf16[1664,256]{1,0:T(8,128)(2,1)S(1)}, bf16[1664,256]{1,0:T(8,128)(2,1)S(1)}, u32[]{:S(2)}, u32[]{:S(2)}) %collective-permute-start.13) | collective-permute-done | bytes 852000 | tf_op jit(solution)/shard_map/ppermute | solution.py:573
  159.7 3.0 %unpack.1 = (f32[2,256,768]{2,1,0:T(8,128)}, f32[2,256,256]{2,1,0:T(8,128)}, f32[2,256,1024]{2,1,0:T(8,128)}, f32[2,1024,256]{2,1,0:T(8,128)}, f32[2,1024]{1,0:T...) custom-call(bf16[3328,256]{1,0:T(8,128)(2,1)S(1)} %bitcast.115, ...), custom_call_target="tpu_custom_call" | custom-call | tf_op jit(solution)/shard_map/unpack/pallas_call | solution.py:648
  (185 shorter events, 31.5 us)
Async XLA Ops:
  1.3 23.1 %copy-start.50 = (s32[5]{0:T(128)S(1)}, s32[5]{0:T(128)}, u32[]{:S(2)}) copy-start(s32[5]{0:T(128)} %len_ref.6) | copy-start | bytes 64
  24.4 13.6 %copy-start.21 = (bf16[1280,256]{1,0:T(8,128)(2,1)}, bf16[1280,256]{1,0:T(8,128)(2,1)S(1)}, u32[]{:S(2)}) copy-start(bf16[1280,256]{1,0:T(8,128)(2,1)S(1)} %get-tuple-element.96.ctx_ref) | copy-start | bytes 1966084
  24.4 13.6 %copy-start.23 = (f32[1280,1]{1,0:T(8,128)}, f32[1280,1]{1,0:T(8,128)S(1)}, u32[]{:S(2)}) copy-start(f32[1280,1]{1,0:T(8,128)S(1)} %get-tuple-element.95.r1_ref) | copy-start | bytes 15364
  24.4 13.6 %copy-start.25 = (f32[1280,1]{1,0:T(8,128)}, f32[1280,1]{1,0:T(8,128)S(1)}, u32[]{:S(2)}) copy-start(f32[1280,1]{1,0:T(8,128)S(1)} %get-tuple-element.90.r2_ref) | copy-start | bytes 15364
  24.4 21.9 %copy-start.54 = (s32[160]{0:T(256)S(1)}, s32[160]{0:T(256)}, u32[]{:S(2)}) copy-start(s32[160]{0:T(256)} %param.26) | copy-start | bytes 1924
  24.4 33.1 %copy-start = (bf16[2,256,1024]{2,1,0:T(8,128)(2,1)S(1)}, bf16[2,256,1024]{2,1,0:T(8,128)(2,1)}, u32[]{:S(2)}) copy-start(bf16[2,256,1024]{2,1,0:T(8,128)(2,1)} %w1_ref.7) | copy-start | bytes 3145732
  24.5 33.1 %copy-start.1 = (bf16[2,1024,256]{2,1,0:T(8,128)(2,1)S(1)}, bf16[2,1024,256]{2,1,0:T(8,128)(2,1)}, u32[]{:S(2)}) copy-start(bf16[2,1024,256]{2,1,0:T(8,128)(2,1)} %w2_ref.7) | copy-start | bytes 3145732
  24.5 33.1 %copy-start.2 = (bf16[2,256,768]{2,1,0:T(8,128)(2,1)S(1)}, bf16[2,256,768]{2,1,0:T(8,128)(2,1)}, u32[]{:S(2)}) copy-start(bf16[2,256,768]{2,1,0:T(8,128)(2,1)} %wqkv_ref.7) | copy-start | bytes 2359300
  24.5 33.1 %copy-start.7 = (bf16[2,256,256]{2,1,0:T(8,128)(2,1)S(1)}, bf16[2,256,256]{2,1,0:T(8,128)(2,1)}, u32[]{:S(2)}) copy-start(bf16[2,256,256]{2,1,0:T(8,128)(2,1)} %wo_ref.7) | copy-start | bytes 786436
  24.5 33.1 %copy-start.48 = (bf16[2,256]{1,0:T(2,128)(2,1)S(1)}, bf16[2,256]{1,0:T(2,128)(2,1)}, u32[]{:S(2)}) copy-start(bf16[2,256]{1,0:T(2,128)(2,1)} %g2_ref.7) | copy-start | bytes 3076
  24.5 33.1 %copy-start.49 = (bf16[2,256]{1,0:T(2,128)(2,1)S(1)}, bf16[2,256]{1,0:T(2,128)(2,1)}, u32[]{:S(2)}) copy-start(bf16[2,256]{1,0:T(2,128)(2,1)} %g1_ref.7) | copy-start | bytes 3076
  38.8 17.9 %all-to-all-start = ((bf16[32,16,256]{2,1,0:T(8,128)(2,1)}), bf16[32,16,256]{2,1,0:T(8,128)(2,1)S(1)}, u32[]{:S(2)}, u32[]{:S(2)}) async-start(bf16[32,16,256]{2,1,0:T(8,128)(2,1)} %broadcast_in_dim.69), calls=%async_computation | async-start | bytes 524288 | tf_op jit(solution)/shard_map/all_to_all | solution.py:621
  57.5 19.3 %slice-start.2 = ((s8[5242880]{0:T(1024)(128)(4,1)}), s8[4194304]{0:T(1024)(128)(4,1)S(1)}, s32[]{:S(2)}) async-start(s8[5242880]{0:T(1024)(128)(4,1)} %bitcast.121), calls=%async_computation.3 | async-start | bytes 8388608
  69.8 7.0 %slice-start.3 = ((s8[5242880]{0:T(1024)(128)(4,1)}), s8[1048576]{0:T(1024)(128)(4,1)S(1)}, s32[]{:S(2)}) async-start(s8[5242880]{0:T(1024)(128)(4,1)} %bitcast.121), calls=%async_computation.4 | async-start | bytes 2097152
  69.8 7.0 %copy-start.18 = (bf16[5,256,256]{2,1,0:T(8,128)(2,1)S(1)}, bf16[5,256,256]{2,1,0:T(8,128)(2,1)}, u32[]{:S(2)}) copy-start(bf16[5,256,256]{2,1,0:T(8,128)(2,1)} %param.23) | copy-start | bytes 1966084
  69.8 7.0 %copy-start.26 = (f32[1280,1]{1,0:T(8,128)S(1)}, f32[1280,1]{1,0:T(8,128)}, u32[]{:S(2)}) copy-start(f32[1280,1]{1,0:T(8,128)} %copy-done.25) | copy-start | bytes 15364
  75.4 9.5 %slice-start = ((s8[5242880]{0:T(1024)(128)(4,1)}), s8[4194304]{0:T(1024)(128)(4,1)S(1)}, s32[]{:S(2)}) async-start(s8[5242880]{0:T(1024)(128)(4,1)} %bitcast.119), calls=%async_computation.1 | async-start | bytes 8388608
  76.4 19.6 %collective-permute-start = (bf16[1664,256]{1,0:T(8,128)(2,1)}, bf16[1664,256]{1,0:T(8,128)(2,1)}, u32[]{:S(2)}, u32[]{:S(2)}) collective-permute-start(bf16[1664,256]{1,0:T(8,128)(2,1)} %dynamic-slice_bitcast_fusion.1), channel_id=1, source_target_pairs={{0,1},{1,0},{2,3},{3,2},{4,5},{5,4},{6,7},{7,6},{8,9},{9,8},{10,11... | collective-permute-start | bytes 2555912 | tf_op jit(solution)/shard_map/ppermute | solution.py:573
  77.6 7.3 %slice-start.1 = ((s8[5242880]{0:T(1024)(128)(4,1)}), s8[1048576]{0:T(1024)(128)(4,1)S(1)}, s32[]{:S(2)}) async-start(s8[5242880]{0:T(1024)(128)(4,1)} %bitcast.119), calls=%async_computation.2 | async-start | bytes 2097152
  85.0 7.0 %copy-start.6 = (bf16[1280,1024]{1,0:T(8,128)(2,1)S(1)}, bf16[1280,1024]{1,0:T(8,128)(2,1)}, u32[]{:S(2)}) copy-start(bf16[1280,1024]{1,0:T(8,128)(2,1)} %copy-done.5) | copy-start | bytes 7864324
  85.0 7.0 %copy-start.20 = (bf16[1280,256]{1,0:T(8,128)(2,1)S(1)}, bf16[1280,256]{1,0:T(8,128)(2,1)}, u32[]{:S(2)}) copy-start(bf16[1280,256]{1,0:T(8,128)(2,1)} %copy-done.19) | copy-start | bytes 1966084
  96.0 6.5 %collective-permute-start.14 = (bf16[1664,256]{1,0:T(8,128)(2,1)}, bf16[1664,256]{1,0:T(8,128)(2,1)}, u32[]{:S(2)}, u32[]{:S(2)}) collective-permute-start(bf16[1664,256]{1,0:T(8,128)(2,1)} %dynamic-slice_bitcast_fusion), channel_id=1, source_target_pairs={{0,1},{1,0},{2,3},{3,2},{4,5},{5,4},{6,7},{7,6},{8,9},{9,8},{10,11... | collective-permute-start | bytes 2555912 | tf_op jit(solution)/shard_map/ppermute | solution.py:573
  99.0 8.1 %collective-permute-start.1 = (bf16[416,256]{1,0:T(8,128)(2,1)S(1)}, bf16[416,256]{1,0:T(8,128)(2,1)S(1)}, u32[]{:S(2)}, u32[]{:S(2)}) collective-permute-start(bf16[416,256]{1,0:T(8,128)(2,1)S(1)} %get-tuple-element.131), channel_id=1, source_target_pairs={{0,2},{1,3},{2,0},{3,1},{4,6},{5,7},{6,4},{7,5},{8,10},{9,11},{10,... | collective-permute-start | bytes 638984 | tf_op jit(solution)/shard_map/ppermute | solution.py:573
  99.3 12.8 %collective-permute-start.2 = (bf16[416,256]{1,0:T(8,128)(2,1)}, bf16[416,256]{1,0:T(8,128)(2,1)S(1)}, u32[]{:S(2)}, u32[]{:S(2)}) collective-permute-start(bf16[416,256]{1,0:T(8,128)(2,1)} %get-tuple-element.133), channel_id=1, source_target_pairs={{0,4},{1,5},{2,6},{3,7},{4,0},{5,1},{6,2},{7,3},{8,12},{9,13},{10,... | collective-permute-start | bytes 638984 | tf_op jit(solution)/shard_map/ppermute | solution.py:573
  100.8 11.4 %collective-permute-start.3 = (bf16[416,256]{1,0:T(8,128)(2,1)S(1)}, bf16[416,256]{1,0:T(8,128)(2,1)S(1)}, u32[]{:S(2)}, u32[]{:S(2)}) collective-permute-start(bf16[416,256]{1,0:T(8,128)(2,1)S(1)} %get-tuple-element.132), channel_id=1, source_target_pairs={{0,6},{1,7},{2,4},{3,5},{4,2},{5,3},{6,0},{7,1},{8,14},{9,15},{10,... | collective-permute-start | bytes 638984 | tf_op jit(solution)/shard_map/ppermute | solution.py:573
  104.0 12.3 %collective-permute-start.15 = (bf16[416,256]{1,0:T(8,128)(2,1)S(1)}, bf16[416,256]{1,0:T(8,128)(2,1)S(1)}, u32[]{:S(2)}, u32[]{:S(2)}) collective-permute-start(bf16[416,256]{1,0:T(8,128)(2,1)S(1)} %get-tuple-element.128), channel_id=1, source_target_pairs={{0,2},{1,3},{2,0},{3,1},{4,6},{5,7},{6,4},{7,5},{8,10},{9,11},{10,... | collective-permute-start | bytes 638984 | tf_op jit(solution)/shard_map/ppermute | solution.py:573
  104.3 16.3 %collective-permute-start.16 = (bf16[416,256]{1,0:T(8,128)(2,1)S(1)}, bf16[416,256]{1,0:T(8,128)(2,1)S(1)}, u32[]{:S(2)}, u32[]{:S(2)}) collective-permute-start(bf16[416,256]{1,0:T(8,128)(2,1)S(1)} %get-tuple-element.130), channel_id=1, source_target_pairs={{0,4},{1,5},{2,6},{3,7},{4,0},{5,1},{6,2},{7,3},{8,12},{9,13},{10,... | collective-permute-start | bytes 638984 | tf_op jit(solution)/shard_map/ppermute | solution.py:573
  107.2 13.5 %collective-permute-start.17 = (bf16[416,256]{1,0:T(8,128)(2,1)S(1)}, bf16[416,256]{1,0:T(8,128)(2,1)S(1)}, u32[]{:S(2)}, u32[]{:S(2)}) collective-permute-start(bf16[416,256]{1,0:T(8,128)(2,1)S(1)} %get-tuple-element.129), channel_id=1, source_target_pairs={{0,6},{1,7},{2,4},{3,5},{4,2},{5,3},{6,0},{7,1},{8,14},{9,15},{10,... | collective-permute-start | bytes 638984 | tf_op jit(solution)/shard_map/ppermute | solution.py:573
  121.8 6.4 %collective-permute-start.18 = (bf16[104,256]{1,0:T(8,128)(2,1)S(1)}, bf16[104,256]{1,0:T(8,128)(2,1)S(1)}, u32[]{:S(2)}, u32[]{:S(2)}) collective-permute-start(bf16[104,256]{1,0:T(8,128)(2,1)S(1)} %get-tuple-element.134), channel_id=1, source_target_pairs={{0,8},{1,9},{2,10},{3,11},{4,12},{5,13},{6,14},{7,15},{8,0},{9,1},... | collective-permute-start | bytes 159752 | tf_op jit(solution)/shard_map/ppermute | solution.py:573
  122.6 8.2 %collective-permute-start.19 = (bf16[104,256]{1,0:T(8,128)(2,1)S(1)}, bf16[104,256]{1,0:T(8,128)(2,1)S(1)}, u32[]{:S(2)}, u32[]{:S(2)}) collective-permute-start(bf16[104,256]{1,0:T(8,128)(2,1)S(1)} %get-tuple-element.136), channel_id=1, source_target_pairs={{0,16},{1,17},{2,18},{3,19},{4,20},{5,21},{6,22},{7,23},{8,24},{9,... | collective-permute-start | bytes 159752 | tf_op jit(solution)/shard_map/ppermute | solution.py:573
  123.7 7.0 %collective-permute-start.20 = (bf16[104,256]{1,0:T(8,128)(2,1)S(1)}, bf16[104,256]{1,0:T(8,128)(2,1)S(1)}, u32[]{:S(2)}, u32[]{:S(2)}) collective-permute-start(bf16[104,256]{1,0:T(8,128)(2,1)S(1)} %get-tuple-element.135), channel_id=1, source_target_pairs={{0,24},{1,25},{2,26},{3,27},{4,28},{5,29},{6,30},{7,31},{8,16},{9,... | collective-permute-start | bytes 159752 | tf_op jit(solution)/shard_map/ppermute | solution.py:573
  126.3 7.0 %collective-permute-start.4 = (bf16[104,256]{1,0:T(8,128)(2,1)S(1)}, bf16[104,256]{1,0:T(8,128)(2,1)S(1)}, u32[]{:S(2)}, u32[]{:S(2)}) collective-permute-start(bf16[104,256]{1,0:T(8,128)(2,1)S(1)} %get-tuple-element.137), channel_id=1, source_target_pairs={{0,8},{1,9},{2,10},{3,11},{4,12},{5,13},{6,14},{7,15},{8,0},{9,1},... | collective-permute-start | bytes 159752 | tf_op jit(solution)/shard_map/ppermute | solution.py:573
  126.4 8.9 %collective-permute-start.5 = (bf16[104,256]{1,0:T(8,128)(2,1)S(1)}, bf16[104,256]{1,0:T(8,128)(2,1)S(1)}, u32[]{:S(2)}, u32[]{:S(2)}) collective-permute-start(bf16[104,256]{1,0:T(8,128)(2,1)S(1)} %get-tuple-element.139), channel_id=1, source_target_pairs={{0,16},{1,17},{2,18},{3,19},{4,20},{5,21},{6,22},{7,23},{8,24},{9,... | collective-permute-start | bytes 159752 | tf_op jit(solution)/shard_map/ppermute | solution.py:573
  128.2 7.1 %collective-permute-start.6 = (bf16[104,256]{1,0:T(8,128)(2,1)S(1)}, bf16[104,256]{1,0:T(8,128)(2,1)S(1)}, u32[]{:S(2)}, u32[]{:S(2)}) collective-permute-start(bf16[104,256]{1,0:T(8,128)(2,1)S(1)} %get-tuple-element.138), channel_id=1, source_target_pairs={{0,24},{1,25},{2,26},{3,27},{4,28},{5,29},{6,30},{7,31},{8,16},{9,... | collective-permute-start | bytes 159752 | tf_op jit(solution)/shard_map/ppermute | solution.py:573
  130.8 7.0 %collective-permute-start.21 = (bf16[104,256]{1,0:T(8,128)(2,1)S(1)}, bf16[104,256]{1,0:T(8,128)(2,1)S(1)}, u32[]{:S(2)}, u32[]{:S(2)}) collective-permute-start(bf16[104,256]{1,0:T(8,128)(2,1)S(1)} %get-tuple-element.125), channel_id=1, source_target_pairs={{0,8},{1,9},{2,10},{3,11},{4,12},{5,13},{6,14},{7,15},{8,0},{9,1},... | collective-permute-start | bytes 159752 | tf_op jit(solution)/shard_map/ppermute | solution.py:573
  132.0 7.9 %collective-permute-start.22 = (bf16[104,256]{1,0:T(8,128)(2,1)S(1)}, bf16[104,256]{1,0:T(8,128)(2,1)S(1)}, u32[]{:S(2)}, u32[]{:S(2)}) collective-permute-start(bf16[104,256]{1,0:T(8,128)(2,1)S(1)} %get-tuple-element.125), channel_id=1, source_target_pairs={{0,16},{1,17},{2,18},{3,19},{4,20},{5,21},{6,22},{7,23},{8,24},{9,... | collective-permute-start | bytes 159752 | tf_op jit(solution)/shard_map/ppermute | solution.py:573
  133.3 6.5 %collective-permute-start.23 = (bf16[104,256]{1,0:T(8,128)(2,1)S(1)}, bf16[104,256]{1,0:T(8,128)(2,1)S(1)}, u32[]{:S(2)}, u32[]{:S(2)}) collective-permute-start(bf16[104,256]{1,0:T(8,128)(2,1)S(1)} %get-tuple-element.125), channel_id=1, source_target_pairs={{0,24},{1,25},{2,26},{3,27},{4,28},{5,29},{6,30},{7,31},{8,16},{9,... | collective-permute-start | bytes 159752 | tf_op jit(solution)/shard_map/ppermute | solution.py:573
  135.4 6.7 %collective-permute-start.7 = (bf16[104,256]{1,0:T(8,128)(2,1)S(1)}, bf16[104,256]{1,0:T(8,128)(2,1)S(1)}, u32[]{:S(2)}, u32[]{:S(2)}) collective-permute-start(bf16[104,256]{1,0:T(8,128)(2,1)S(1)} %get-tuple-element.127), channel_id=1, source_target_pairs={{0,8},{1,9},{2,10},{3,11},{4,12},{5,13},{6,14},{7,15},{8,0},{9,1},... | collective-permute-start | bytes 159752 | tf_op jit(solution)/shard_map/ppermute | solution.py:573
  136.5 6.9 %collective-permute-start.8 = (bf16[104,256]{1,0:T(8,128)(2,1)S(1)}, bf16[104,256]{1,0:T(8,128)(2,1)S(1)}, u32[]{:S(2)}, u32[]{:S(2)}) collective-permute-start(bf16[104,256]{1,0:T(8,128)(2,1)S(1)} %get-tuple-element.127), channel_id=1, source_target_pairs={{0,16},{1,17},{2,18},{3,19},{4,20},{5,21},{6,22},{7,23},{8,24},{9,... | collective-permute-start | bytes 159752 | tf_op jit(solution)/shard_map/ppermute | solution.py:573
  137.8 5.9 %collective-permute-start.9 = (bf16[104,256]{1,0:T(8,128)(2,1)S(1)}, bf16[104,256]{1,0:T(8,128)(2,1)S(1)}, u32[]{:S(2)}, u32[]{:S(2)}) collective-permute-start(bf16[104,256]{1,0:T(8,128)(2,1)S(1)} %get-tuple-element.127), channel_id=1, source_target_pairs={{0,24},{1,25},{2,26},{3,27},{4,28},{5,29},{6,30},{7,31},{8,16},{9,... | collective-permute-start | bytes 159752 | tf_op jit(solution)/shard_map/ppermute | solution.py:573
  139.9 8.3 %collective-permute-start.24 = (bf16[416,256]{1,0:T(8,128)(2,1)S(1)}, bf16[416,256]{1,0:T(8,128)(2,1)S(1)}, u32[]{:S(2)}, u32[]{:S(2)}) collective-permute-start(bf16[416,256]{1,0:T(8,128)(2,1)S(1)} %bitcast.147), channel_id=1, source_target_pairs={{0,2},{1,3},{2,0},{3,1},{4,6},{5,7},{6,4},{7,5},{8,10},{9,11},{10,... | collective-permute-start | bytes 638984 | tf_op jit(solution)/shard_map/ppermute | solution.py:573
  141.3 10.3 %collective-permute-start.25 = (bf16[416,256]{1,0:T(8,128)(2,1)S(1)}, bf16[416,256]{1,0:T(8,128)(2,1)S(1)}, u32[]{:S(2)}, u32[]{:S(2)}) collective-permute-start(bf16[416,256]{1,0:T(8,128)(2,1)S(1)} %bitcast.148), channel_id=1, source_target_pairs={{0,4},{1,5},{2,6},{3,7},{4,0},{5,1},{6,2},{7,3},{8,12},{9,13},{10,... | collective-permute-start | bytes 638984 | tf_op jit(solution)/shard_map/ppermute | solution.py:573
  142.1 10.6 %collective-permute-start.26 = (bf16[416,256]{1,0:T(8,128)(2,1)S(1)}, bf16[416,256]{1,0:T(8,128)(2,1)S(1)}, u32[]{:S(2)}, u32[]{:S(2)}) collective-permute-start(bf16[416,256]{1,0:T(8,128)(2,1)S(1)} %bitcast.149), channel_id=1, source_target_pairs={{0,6},{1,7},{2,4},{3,5},{4,2},{5,3},{6,0},{7,1},{8,14},{9,15},{10,... | collective-permute-start | bytes 638984 | tf_op jit(solution)/shard_map/ppermute | solution.py:573
  143.8 10.1 %collective-permute-start.10 = (bf16[416,256]{1,0:T(8,128)(2,1)S(1)}, bf16[416,256]{1,0:T(8,128)(2,1)S(1)}, u32[]{:S(2)}, u32[]{:S(2)}) collective-permute-start(bf16[416,256]{1,0:T(8,128)(2,1)S(1)} %bitcast.143), channel_id=1, source_target_pairs={{0,2},{1,3},{2,0},{3,1},{4,6},{5,7},{6,4},{7,5},{8,10},{9,11},{10,... | collective-permute-start | bytes 638984 | tf_op jit(solution)/shard_map/ppermute | solution.py:573
  145.2 10.9 %collective-permute-start.11 = (bf16[416,256]{1,0:T(8,128)(2,1)S(1)}, bf16[416,256]{1,0:T(8,128)(2,1)S(1)}, u32[]{:S(2)}, u32[]{:S(2)}) collective-permute-start(bf16[416,256]{1,0:T(8,128)(2,1)S(1)} %bitcast.144), channel_id=1, source_target_pairs={{0,4},{1,5},{2,6},{3,7},{4,0},{5,1},{6,2},{7,3},{8,12},{9,13},{10,... | collective-permute-start | bytes 638984 | tf_op jit(solution)/shard_map/ppermute | solution.py:573
  148.1 9.1 %collective-permute-start.12 = (bf16[416,256]{1,0:T(8,128)(2,1)S(1)}, bf16[416,256]{1,0:T(8,128)(2,1)S(1)}, u32[]{:S(2)}, u32[]{:S(2)}) collective-permute-start(bf16[416,256]{1,0:T(8,128)(2,1)S(1)} %bitcast.146), channel_id=1, source_target_pairs={{0,6},{1,7},{2,4},{3,5},{4,2},{5,3},{6,0},{7,1},{8,14},{9,15},{10,... | collective-permute-start | bytes 638984 | tf_op jit(solution)/shard_map/ppermute | solution.py:573
  152.7 5.0 %collective-permute-start.27 = (bf16[1664,256]{1,0:T(8,128)(2,1)S(1)}, bf16[1664,256]{1,0:T(8,128)(2,1)S(1)}, u32[]{:S(2)}, u32[]{:S(2)}) collective-permute-start(bf16[1664,256]{1,0:T(8,128)(2,1)S(1)} %bitcast.133), channel_id=1, source_target_pairs={{0,1},{1,0},{2,3},{3,2},{4,5},{5,4},{6,7},{7,6},{8,9},{9,8},{10,11... | collective-permute-start | bytes 2555912 | tf_op jit(solution)/shard_map/ppermute | solution.py:573
  157.2 2.4 %collective-permute-start.13 = (bf16[1664,256]{1,0:T(8,128)(2,1)S(1)}, bf16[1664,256]{1,0:T(8,128)(2,1)S(1)}, u32[]{:S(2)}, u32[]{:S(2)}) collective-permute-start(bf16[1664,256]{1,0:T(8,128)(2,1)S(1)} %bitcast.131), channel_id=1, source_target_pairs={{0,1},{1,0},{2,3},{3,2},{4,5},{5,4},{6,7},{7,6},{8,9},{9,8},{10,11... | collective-permute-start | bytes 2555912 | tf_op jit(solution)/shard_map/ppermute | solution.py:573
  (40 other events, 67.7 us)

commit v4 on v2

v4 whole, which is shorter than its diff:
```python
import functools

import jax
import jax.numpy as jnp
from jax import lax
from jax.experimental import pallas as pl
from jax.experimental.pallas import tpu as pltpu
from jax.sharding import PartitionSpec as P

HEAD_DIM = 64
WIDTH = 256
HEADS = WIDTH // HEAD_DIM
HIDDEN = 1024
BLOCKS = HIDDEN // WIDTH
PAD = 8
VECTOR_ROWS = 16
HALF = 6 * WIDTH + 128
GROUP_ROWS = 2 * HALF
SOFT = 128
NORM = 64
GELU = 32
ln_eps = 1e-06
score_scale = 0.125
masked_score = -1e30
f32 = jnp.float32
bf16 = jnp.bfloat16

QUERY_BIAS, VALUE_BIAS, PROJ_BIAS, ATTN_GAIN, ATTN_SHIFT, DOWN_BIAS, FFN_GAIN, FFN_SHIFT = range(8)
UP_BIAS = 8


def dot(a, b):
    return lax.dot_general(a, b, (((1,), (0,)), ((), ())), preferred_element_type=f32)


def dot_nt(a, b):
    return lax.dot_general(a, b, (((1,), (1,)), ((), ())), preferred_element_type=f32)


def dot_tn(a, b):
    return lax.dot_general(a, b, (((0,), (0,)), ((), ())), preferred_element_type=f32)


def row_loop(rows, chunk, step):
    def body(index, carry):
        step(pl.multiple_of(index * chunk, chunk))
        return carry

    lax.fori_loop(0, rows // chunk, body, 0, unroll=rows // chunk)


def vector(ref, which):
    return ref[...].astype(f32)[which : which + 1]


def lane_head(rows):
    return lax.broadcasted_iota(jnp.int32, (rows, WIDTH), 1) // HEAD_DIM


def stack_heads(values):
    head = lane_head(values.shape[0])
    wide = values.astype(f32)
    return jnp.concatenate(
        [jnp.where(head == h, wide, 0.0).astype(bf16) for h in range(HEADS)], axis=0
    )


def pick_heads(stacked, rows):
    head = lane_head(rows)
    result = stacked[:rows]
    for h in range(1, HEADS):
        result = jnp.where(head == h, stacked[h * rows : (h + 1) * rows], result)
    return result


def block_rows(block):
    start = block * WIDTH if block < 6 else HALF + (block - 6) * WIDTH
    return slice(start, start + WIDTH)


VECTOR_START = 6 * WIDTH
QKV_BLOCK, PROJ_BLOCK, UP_BLOCK, DOWN_BLOCK = 0, 3, 4, 8


def normalize(value):
    centered = value - jnp.mean(value, axis=1, keepdims=True)
    inverse = lax.rsqrt(jnp.mean(centered * centered, axis=1, keepdims=True) + ln_eps)
    return centered * inverse, inverse


def masked_softmax(scores, size):
    part = scores * score_scale
    key = lax.broadcasted_iota(jnp.int32, part.shape, 1)
    part = jnp.where(key < size, part, masked_score)
    part = jnp.exp(part - jnp.max(part, axis=1, keepdims=True))
    return part * (1.0 / jnp.sum(part, axis=1, keepdims=True))


def gelu_parts(value):
    cumulative = 0.5 + 0.5 * lax.erf(value * 0.7071067811865476)
    density = jnp.exp(value * value * -0.5) * 0.3989422804014327
    return (value * cumulative).astype(bf16), cumulative + value * density


def first_rows(which, seqs, length, len_ref, x_ref, k_ref, v_ref, wqkv_ref, qb_ref, vb_ref, wo_ref, ob_ref, g1_ref, b1_ref, w1_ref, hb_ref, w2_ref, fb_ref, g2_ref, b2_ref):
    weights = wqkv_ref[which]
    x = x_ref[...]
    k_ref[...] = dot(x, weights[:, WIDTH : 2 * WIDTH]).astype(bf16)
    v_ref[...] = (dot(x, weights[:, 2 * WIDTH :]) + vector(vb_ref, which)).astype(bf16)
    contexts, inputs = [], []
    for s in range(seqs):
        first = x_ref[s * length : s * length + 16, :]
        query = (dot(first, weights[:, :WIDTH]) + vector(qb_ref, which)).astype(bf16)
        span = slice(s * length, (s + 1) * length)
        prob = masked_softmax(dot_nt(stack_heads(query), k_ref[span, :]), len_ref[s])
        contexts.append(pick_heads(dot(prob.astype(bf16), v_ref[span, :]), 16)[:1])
        inputs.append(first.astype(f32)[:1])
    filler = jnp.zeros((PAD - seqs, WIDTH), f32)
    context = jnp.concatenate(contexts + [filler], axis=0).astype(bf16)
    value = jnp.concatenate(inputs + [filler], axis=0)
    value = value + (dot(context, wo_ref[which]) + vector(ob_ref, which))
    unit, _ = normalize(value)
    normed = unit * vector(g1_ref, which) + vector(b1_ref, which)
    hidden = dot(normed.astype(bf16), w1_ref[which]) + vector(hb_ref, which)
    active, _ = gelu_parts(hidden)
    value = normed + (dot(active, w2_ref[which]) + vector(fb_ref, which))
    unit, _ = normalize(value)
    result = unit * vector(g2_ref, which) + vector(b2_ref, which)
    row = lax.broadcasted_iota(jnp.int32, result.shape, 0)
    return jnp.where(row < seqs, result, 0.0)


def first_kernel(seqs, lq_ref, lp_ref, xq_ref, xp_ref, *refs):
    weights, (cls_ref, kq_ref, vq_ref, kp_ref, vp_ref) = refs[:13], refs[13:]
    count = cls_ref.shape[0]
    question = first_rows(0, seqs, xq_ref.shape[0] // seqs, lq_ref, xq_ref, kq_ref, vq_ref, *weights)
    passage = first_rows(1, seqs, xp_ref.shape[0] // seqs, lp_ref, xp_ref, kp_ref, vp_ref, *weights)
    both = jnp.concatenate([question, passage], axis=0).astype(bf16)
    for i in range(count) if count <= 32 else ():
        cls_ref[i] = both
    if count > 32:

        def store(i, carry):
            cls_ref[i] = both
            return carry

        lax.fori_loop(0, count, store, 0)


def forward_phase(
    which, seqs, length, first,
    len_ref, x_ref, wqkv_ref, qb_ref, vb_ref, wo_ref, ob_ref, g1_ref, b1_ref,
    w1_ref, hb_ref, w2_ref, fb_ref, g2_ref, b2_ref,
    out_ref, qkv_ref, p_ref, ctx_ref, n1_ref, r1_ref, nb_ref, gp_ref, act_ref, n2_ref, r2_ref,
    wide_ref, score_ref, prob_ref,
):
    rows = seqs * length
    x = x_ref[...]
    qkv_ref[:, :WIDTH] = (dot(x, wqkv_ref[:, :WIDTH]) + vector(qb_ref, which)).astype(bf16)
    qkv_ref[:, WIDTH : 2 * WIDTH] = dot(x, wqkv_ref[:, WIDTH : 2 * WIDTH]).astype(bf16)
    qkv_ref[:, 2 * WIDTH :] = (dot(x, wqkv_ref[:, 2 * WIDTH :]) + vector(vb_ref, which)).astype(bf16)
    stack_rows = HEADS * length
    for s in range(seqs):
        span = slice(s * length, (s + 1) * length)
        stack = slice(s * stack_rows, (s + 1) * stack_rows)
        size = len_ref[first + s]
        score_ref[stack, :] = dot_nt(stack_heads(qkv_ref[span, :WIDTH]), qkv_ref[span, WIDTH : 2 * WIDTH])

        def softmax(row):
            here = pl.ds(s * stack_rows + row, SOFT)
            prob = masked_softmax(score_ref[here, :], size)
            p_ref[here, :] = prob
            prob_ref[here, :] = prob.astype(bf16)

        row_loop(stack_rows, SOFT, softmax)
        ctx_ref[span, :] = pick_heads(dot(prob_ref[stack, :], qkv_ref[span, 2 * WIDTH :]), length).astype(bf16)
    n2_ref[...] = dot(ctx_ref[...], wo_ref[...])
    ob, g1, b1 = vector(ob_ref, which), vector(g1_ref, which), vector(b1_ref, which)

    def first_norm(row):
        here = pl.ds(row, NORM)
        unit, inverse = normalize(x_ref[here, :].astype(f32) + (n2_ref[here, :] + ob))
        n1_ref[here, :] = unit
        r1_ref[here, :] = inverse
        nb_ref[here, :] = (unit * g1 + b1).astype(bf16)

    row_loop(rows, NORM, first_norm)
    wide_ref[...] = dot(nb_ref[...], w1_ref[...])
    hb = vector(hb_ref, which)

    def gelu(row):
        here = pl.ds(row, GELU)
        for j in range(BLOCKS):
            lanes = slice(j * WIDTH, (j + 1) * WIDTH)
            active, slope = gelu_parts(wide_ref[here, lanes] + hb[:, lanes])
            act_ref[here, lanes] = active
            gp_ref[here, lanes] = slope

    row_loop(rows, GELU, gelu)
    n2_ref[...] = dot(act_ref[...], w2_ref[...])
    fb, g2, b2 = vector(fb_ref, which), vector(g2_ref, which), vector(b2_ref, which)
    for s in range(seqs):
        size = len_ref[first + s]

        def second_norm(row):
            here = pl.ds(s * length + row, NORM)
            unit, inverse = normalize((n1_ref[here, :] * g1 + b1) + (n2_ref[here, :] + fb))
            n2_ref[here, :] = unit
            r2_ref[here, :] = inverse
            position = row + lax.broadcasted_iota(jnp.int32, (NORM, WIDTH), 0)
            out_ref[here, :] = jnp.where(position < size, unit * g2 + b2, 0.0).astype(bf16)

        row_loop(length, NORM, second_norm)


def add_row(vec_ref, row, values):
    vec_ref[row : row + 1, :] = vec_ref[row : row + 1, :] + jnp.sum(values, axis=0, keepdims=True)


def ffn_phase(which, seqs, length, first, len_ref, cls_ref, cot_ref, n2_ref, r2_ref, gp_ref, w2_ref, g2_ref, two_ref, gffn_ref, gpre_ref, vec_ref, wide_ref):
    g2 = vector(g2_ref, which)
    for s in range(seqs):
        size = len_ref[first + s]
        cls_row = cls_ref[pl.ds(first + s, 1), :]

        def norm_back(row):
            here = pl.ds(s * length + row, NORM)
            position = row + lax.broadcasted_iota(jnp.int32, (NORM, WIDTH), 0)
            grad = cot_ref[here, :].astype(f32) + jnp.where(position == 0, cls_row, 0.0)
            grad = jnp.where(position < size, grad, 0.0)
            unit = n2_ref[here, :]
            scaled = grad * g2
            first_mean = jnp.mean(scaled, axis=1, keepdims=True)
            second_mean = jnp.mean(scaled * unit, axis=1, keepdims=True)
            two = r2_ref[here, :] * (scaled - first_mean - unit * second_mean)
            low = two.astype(bf16)
            two_ref[here, :] = two
            gffn_ref[here, :] = low
            add_row(vec_ref, FFN_GAIN, grad * unit)
            add_row(vec_ref, FFN_SHIFT, grad)
            add_row(vec_ref, DOWN_BIAS, low.astype(f32))

        row_loop(length, NORM, norm_back)
    wide_ref[...] = dot_nt(gffn_ref[...], w2_ref[...])

    def gelu_back(row):
        here = pl.ds(row, GELU)
        for j in range(BLOCKS):
            lanes = slice(j * WIDTH, (j + 1) * WIDTH)
            low = (wide_ref[here, lanes] * gp_ref[here, lanes]).astype(bf16)
            gpre_ref[here, lanes] = low
            add_row(vec_ref, UP_BIAS + j, low.astype(f32))

    row_loop(seqs * length, GELU, gelu_back)


def attn_norm_phase(which, rows, gpre_ref, w1_ref, two_ref, n1_ref, r1_ref, g1_ref, wo_ref, one_ref, gatt_ref, dctx_ref, vec_ref):
    one_ref[...] = dot_nt(gpre_ref[...], w1_ref[...])
    g1 = vector(g1_ref, which)

    def norm_back(row):
        here = pl.ds(row, NORM)
        grad = two_ref[here, :] + one_ref[here, :]
        unit = n1_ref[here, :]
        scaled = grad * g1
        first_mean = jnp.mean(scaled, axis=1, keepdims=True)
        second_mean = jnp.mean(scaled * unit, axis=1, keepdims=True)
        one = r1_ref[here, :] * (scaled - first_mean - unit * second_mean)
        low = one.astype(bf16)
        one_ref[here, :] = one
        gatt_ref[here, :] = low
        add_row(vec_ref, ATTN_GAIN, grad * unit)
        add_row(vec_ref, ATTN_SHIFT, grad)
        add_row(vec_ref, PROJ_BIAS, low.astype(f32))

    row_loop(rows, NORM, norm_back)
    dctx_ref[...] = dot_nt(gatt_ref[...], wo_ref[...]).astype(bf16)


def attn_core_phase(seqs, length, dctx_ref, qkv_ref, p_ref, gqkv_ref, vec_ref, dp_ref, ds_ref, pb_ref):
    stack_rows = HEADS * length
    for s in range(seqs):
        span = slice(s * length, (s + 1) * length)
        context = stack_heads(dctx_ref[span, :])
        stack = slice(s * stack_rows, (s + 1) * stack_rows)
        dp_ref[stack, :] = dot_nt(context, qkv_ref[span, 2 * WIDTH :])

        def softmax_back(row):
            here = pl.ds(s * stack_rows + row, SOFT)
            prob = p_ref[here, :]
            grad = dp_ref[here, :]
            inner = jnp.sum(prob * grad, axis=1, keepdims=True)
            ds_ref[here, :] = (prob * (grad - inner)).astype(bf16)

        row_loop(stack_rows, SOFT, softmax_back)
        queries = stack_heads(qkv_ref[span, :WIDTH])
        grad_q = (pick_heads(dot(ds_ref[stack, :], qkv_ref[span, WIDTH : 2 * WIDTH]), length) * score_scale).astype(bf16)
        gqkv_ref[span, :WIDTH] = grad_q
        add_row(vec_ref, QUERY_BIAS, grad_q.astype(f32))
        gqkv_ref[span, WIDTH : 2 * WIDTH] = (dot_tn(ds_ref[stack, :], queries) * score_scale).astype(bf16)
        grad_v = dot_tn(pb_ref[stack, :], context).astype(bf16)
        gqkv_ref[span, 2 * WIDTH :] = grad_v
        add_row(vec_ref, VALUE_BIAS, grad_v.astype(f32))


def layer_kernel(
    which, steps, seqs, length,
    bit_ref, len_ref, cls_ref, x_ref, cot_ref,
    wqkv_ref, qb_ref, vb_ref, wo_ref, ob_ref, g1_ref, b1_ref, w1_ref, hb_ref, w2_ref, fb_ref, g2_ref, b2_ref,
    out_ref, gx_ref, keep_ref, send_ref,
    acc_ref, vec_ref, qkv_ref, p_ref, ctx_ref, n1_ref, r1_ref, nb_ref, gp_ref, act_ref, n2_ref, r2_ref,
    wide_ref, score_ref, prob_ref, two_ref, gffn_ref, gpre_ref, one_ref, gatt_ref, dctx_ref, gqkv_ref, ds_ref,
):
    rows = seqs * length
    step = pl.program_id(0)

    def start():
        vec_ref[...] = jnp.zeros_like(vec_ref)
        if steps > 1:
            acc_ref[...] = jnp.zeros_like(acc_ref)

    if steps > 1:
        pl.when(step == 0)(start)
    else:
        start()

    def add_block(block, value):
        if steps > 1:
            acc_ref[block_rows(block), :] += value
        else:
            acc_ref[block_rows(block), :] = value

    forward_phase(
        which, seqs, length, step * seqs,
        len_ref, x_ref, wqkv_ref, qb_ref, vb_ref, wo_ref, ob_ref, g1_ref, b1_ref,
        w1_ref, hb_ref, w2_ref, fb_ref, g2_ref, b2_ref,
        out_ref, qkv_ref, p_ref, ctx_ref, n1_ref, r1_ref, nb_ref, gp_ref, act_ref, n2_ref, r2_ref,
        wide_ref, score_ref, prob_ref,
    )
    ffn_phase(which, seqs, length, step * seqs, len_ref, cls_ref, cot_ref, n2_ref, r2_ref, gp_ref, w2_ref, g2_ref, two_ref, gffn_ref, gpre_ref, vec_ref, wide_ref)
    for j in range(BLOCKS):
        lanes = slice(j * WIDTH, (j + 1) * WIDTH)
        add_block(DOWN_BLOCK + j, dot_tn(act_ref[:, lanes], gffn_ref[...]))
        add_block(UP_BLOCK + j, dot_tn(nb_ref[...], gpre_ref[:, lanes]))
    attn_norm_phase(which, rows, gpre_ref, w1_ref, two_ref, n1_ref, r1_ref, g1_ref, wo_ref, one_ref, gatt_ref, dctx_ref, vec_ref)
    add_block(PROJ_BLOCK, dot_tn(ctx_ref[...], gatt_ref[...]))
    attn_core_phase(seqs, length, dctx_ref, qkv_ref, p_ref, gqkv_ref, vec_ref, score_ref, ds_ref, prob_ref)
    for j in range(3):
        add_block(QKV_BLOCK + j, dot_tn(x_ref[...], gqkv_ref[:, j * WIDTH : (j + 1) * WIDTH]))
    gx_ref[...] = (one_ref[...] + dot_nt(gqkv_ref[...], wqkv_ref[...])).astype(bf16)

    def finish():
        acc_ref[VECTOR_START : VECTOR_START + VECTOR_ROWS, :] = vec_ref[...]
        if steps == 1:
            acc_ref[VECTOR_START + VECTOR_ROWS : HALF, :] = jnp.zeros((HALF - VECTOR_START - VECTOR_ROWS, WIDTH), f32)
            acc_ref[HALF + 6 * WIDTH :, :] = jnp.zeros((HALF - 6 * WIDTH, WIDTH), f32)
        keep = pl.multiple_of(bit_ref[0] * HALF, HALF)
        send = pl.multiple_of((1 - bit_ref[0]) * HALF, HALF)
        keep_ref[...] = acc_ref[pl.ds(keep, HALF), :].astype(bf16)
        send_ref[...] = acc_ref[pl.ds(send, HALF), :].astype(bf16)

    if steps > 1:
        pl.when(step == steps - 1)(finish)
    else:
        finish()


def loss_kernel(local, me_ref, all_ref, hot_ref, own_hot_ref, loss_ref, gq_ref, gp_ref, q_ref, p_ref):
    count = all_ref.shape[0]
    me = me_ref[0]
    wide = all_ref[...].astype(f32)
    q_ref[...] = wide[:, :PAD].reshape(count * PAD, WIDTH).astype(bf16)
    p_ref[...] = wide[:, PAD:].reshape(count * PAD, WIDTH).astype(bf16)
    own_q = all_ref[me][:PAD]
    own_p = all_ref[me][PAD:]
    logits = dot_nt(own_q, p_ref[...]) * score_scale
    column = lax.broadcasted_iota(jnp.int32, logits.shape, 1)
    logits = jnp.where(column % PAD < local, logits, masked_score)
    top = jnp.max(logits, axis=1, keepdims=True)
    total = top + jnp.log(jnp.sum(jnp.exp(logits - top), axis=1, keepdims=True))
    hot = (column == own_hot_ref[...]).astype(f32)
    loss_ref[...] = jnp.broadcast_to(total - jnp.sum(logits * hot, axis=1, keepdims=True), loss_ref.shape)
    grad = (jnp.exp(logits - total) - hot).astype(bf16)
    gq_ref[...] = dot(grad, p_ref[...]) * score_scale
    gp_ref[...] = jnp.zeros_like(gp_ref)
    block = 256 if count * PAD % 256 == 0 else count * PAD

    def part(index, carry):
        start = pl.multiple_of(index * block, block)
        queries = q_ref[pl.ds(start, block), :]
        scores = dot_nt(p_ref[...], queries) * score_scale
        row = lax.broadcasted_iota(jnp.int32, scores.shape, 0)
        scores = jnp.where(row % PAD < local, scores, masked_score)
        peak = jnp.max(scores, axis=0, keepdims=True)
        sums = peak + jnp.log(jnp.sum(jnp.exp(scores - peak), axis=0, keepdims=True))
        own = dot_nt(own_p, queries) * score_scale
        own_row = lax.broadcasted_iota(jnp.int32, own.shape, 0)
        own_lane = lax.broadcasted_iota(jnp.int32, own.shape, 1)
        own_hits = (own_row + me * PAD == hot_ref[:, pl.ds(start, block)]).astype(f32)
        own_grad = jnp.where(own_lane % PAD < local, jnp.exp(own - sums) - own_hits, 0.0)
        gp_ref[...] += dot(own_grad.astype(bf16), queries) * score_scale
        return carry

    lax.fori_loop(0, count * PAD // block, part, 0)


def combine_kernel(radix, digit_ref, *refs):
    total_ref = refs[-1]
    sends = refs[-1 - (radix - 1) : -1]
    keep_ref = refs[-1 - radix]
    pieces = refs[: -1 - radix]
    total = pieces[0][...].astype(f32)
    for piece in pieces[1:]:
        total = total + piece[...].astype(f32)
    total_ref[...] = total
    part = total_ref.shape[0] // radix
    digit = digit_ref[0]

    def section(which):
        return total_ref[pl.ds(pl.multiple_of(which * part, part), part), :].astype(bf16)

    keep_ref[...] = section(digit)
    for step, ref in enumerate(sends, start=1):
        ref[...] = section(digit ^ step)


VECTOR_OUTS = (QUERY_BIAS, VALUE_BIAS, PROJ_BIAS, ATTN_GAIN, ATTN_SHIFT, DOWN_BIAS, FFN_GAIN, FFN_SHIFT)


def unpack_kernel(bit_ref, q_own_ref, q_ref, p_own_ref, p_ref, qkv_ref, proj_ref, up_ref, down_ref, up_bias_ref, *refs):
    vector_refs, whole_ref = refs[:-1], refs[-1]
    own = pl.multiple_of(bit_ref[0] * HALF, HALF)
    other = pl.multiple_of((1 - bit_ref[0]) * HALF, HALF)
    tails = []
    for which, (own_ref, other_ref) in enumerate(((q_own_ref, q_ref), (p_own_ref, p_ref))):
        ref = whole_ref.at[which]
        ref[pl.ds(own, HALF), :] = own_ref[...]
        ref[pl.ds(other, HALF), :] = other_ref[...]
        for j in range(3):
            qkv_ref[which, :, j * WIDTH : (j + 1) * WIDTH] = ref[block_rows(QKV_BLOCK + j), :].astype(f32)
        proj_ref[which] = ref[block_rows(PROJ_BLOCK), :].astype(f32)
        for j in range(BLOCKS):
            up_ref[which, :, j * WIDTH : (j + 1) * WIDTH] = ref[block_rows(UP_BLOCK + j), :].astype(f32)
            down_ref[which, j * WIDTH : (j + 1) * WIDTH, :] = ref[block_rows(DOWN_BLOCK + j), :].astype(f32)
        tails.append(ref[VECTOR_START : VECTOR_START + VECTOR_ROWS, :].astype(f32))
    for row, ref in zip(VECTOR_OUTS, vector_refs):
        for which in range(2):
            ref[which : which + 1, :] = tails[which][row : row + 1]
    for j in range(BLOCKS):
        for which in range(2):
            up_bias_ref[which : which + 1, j * WIDTH : (j + 1) * WIDTH] = tails[which][UP_BIAS + j : UP_BIAS + j + 1]


def smem():
    return pl.BlockSpec(memory_space=pltpu.SMEM)


def whole(shape):
    return pl.BlockSpec(shape, lambda i: (0,) * len(shape))


def rows_of(rows, columns):
    return pl.BlockSpec((rows, columns), lambda i: (i, 0))


def part_of(which, shape):
    return pl.BlockSpec((None,) + shape, lambda i: (which, 0, 0))


def params():
    return pltpu.CompilerParams(vmem_limit_bytes=24 * 1024 * 1024)


def shape(dims, kind):
    return jax.ShapeDtypeStruct(dims, kind)


def cost(flops, moved):
    return pl.CostEstimate(flops=flops, bytes_accessed=moved, transcendentals=0)


def pair(columns):
    return whole((2, columns))


def in_hbm(values):
    return pltpu.with_memory_space_constraint(values, pltpu.HBM)


def weight_specs(which):
    return [
        part_of(which, (WIDTH, 3 * WIDTH)), pair(WIDTH), pair(WIDTH), part_of(which, (WIDTH, WIDTH)),
        pair(WIDTH), pair(WIDTH), pair(WIDTH), part_of(which, (WIDTH, HIDDEN)), pair(HIDDEN),
        part_of(which, (HIDDEN, WIDTH)), pair(WIDTH), pair(WIDTH), pair(WIDTH),
    ]


def layer(which, steps, seqs, length, bit, lengths, cls_grad, x, cot, weights):
    rows = seqs * length
    total = steps * rows
    stack = seqs * HEADS * length
    return pl.pallas_call(
        functools.partial(layer_kernel, which, steps, seqs, length),
        out_shape=[shape((total, WIDTH), bf16), shape((total, WIDTH), bf16), shape((HALF, WIDTH), bf16), shape((HALF, WIDTH), bf16)],
        grid=(steps,),
        in_specs=[smem(), smem(), whole((PAD, WIDTH)), rows_of(rows, WIDTH), rows_of(rows, WIDTH)] + weight_specs(which),
        out_specs=[rows_of(rows, WIDTH), rows_of(rows, WIDTH), whole((HALF, WIDTH)), whole((HALF, WIDTH))],
        scratch_shapes=[
            pltpu.VMEM((GROUP_ROWS, WIDTH), f32), pltpu.VMEM((VECTOR_ROWS, WIDTH), f32),
            pltpu.VMEM((rows, 3 * WIDTH), bf16), pltpu.VMEM((stack, length), f32), pltpu.VMEM((rows, WIDTH), bf16),
            pltpu.VMEM((rows, WIDTH), f32), pltpu.VMEM((rows, 1), f32), pltpu.VMEM((rows, WIDTH), bf16),
            pltpu.VMEM((rows, HIDDEN), f32), pltpu.VMEM((rows, HIDDEN), bf16), pltpu.VMEM((rows, WIDTH), f32),
            pltpu.VMEM((rows, 1), f32), pltpu.VMEM((rows, HIDDEN), f32), pltpu.VMEM((stack, length), f32),
            pltpu.VMEM((stack, length), bf16), pltpu.VMEM((rows, WIDTH), f32), pltpu.VMEM((rows, WIDTH), bf16),
            pltpu.VMEM((rows, HIDDEN), bf16), pltpu.VMEM((rows, WIDTH), f32), pltpu.VMEM((rows, WIDTH), bf16),
            pltpu.VMEM((rows, WIDTH), bf16), pltpu.VMEM((rows, 3 * WIDTH), bf16), pltpu.VMEM((stack, length), bf16),
        ],
        compiler_params=params(),
        cost_estimate=cost(total * 6 * 800000, total * 4000),
        name="layer",
    )(bit, lengths, cls_grad, in_hbm(x), in_hbm(cot), *[in_hbm(member) for member in weights])


def stages(count):
    masks = []
    bit = 1
    while bit < count:
        masks.append(bit)
        bit = bit * 2
    groups = [masks[:1]]
    rest = masks[1:]
    while rest:
        groups.append(rest[:2])
        rest = rest[2:]
    return [group for group in groups if group]


def partner_send(values, mask, count):
    return lax.ppermute(values, "dp", [(i, i ^ mask) for i in range(count)])


def combos(group):
    return [index * group[0] for index in range(1, 2 ** len(group))]


def combine(pieces, group, me):
    radix = 2 ** len(group)
    digit = (me // group[0]) % radix
    rows = pieces[0].shape[0]
    part = rows // radix
    if part % 8 == 0:
        return pl.pallas_call(
            functools.partial(combine_kernel, radix),
            out_shape=[shape((part, WIDTH), bf16)] * radix,
            grid=(1,),
            in_specs=[smem()] + [whole((rows, WIDTH))] * len(pieces),
            out_specs=[whole((part, WIDTH))] * radix,
            scratch_shapes=[pltpu.VMEM((rows, WIDTH), f32)],
            compiler_params=params(),
            name="combine",
        )(digit.reshape(1), *pieces)
    total = pieces[0].astype(f32)
    for piece in pieces[1:]:
        total = total + piece.astype(f32)
    split = total.astype(bf16).reshape(radix, part, WIDTH)
    return [lax.dynamic_index_in_dim(split, digit ^ step, 0, keepdims=False) for step in range(radix)]


def reduce_scatter(keep, send, count, me):
    groups = stages(count)
    pieces = [keep, partner_send(send, groups[0][0], count)]
    for group in groups[1:]:
        own, *sends = combine(pieces, group, me)
        pieces = [own] + [partner_send(part, mask, count) for part, mask in zip(sends, combos(group))]
    total = pieces[0].astype(f32)
    for piece in pieces[1:]:
        total = total + piece.astype(f32)
    return total.astype(bf16)


def gather_back(buffer, count, me):
    groups = stages(count)
    for group in reversed(groups[1:]):
        radix = 2 ** len(group)
        digit = (me // group[0]) % radix
        joined = jnp.zeros((radix,) + buffer.shape, buffer.dtype)
        pieces = [buffer] + [partner_send(buffer, mask, count) for mask in combos(group)]
        for step, piece in enumerate(pieces):
            joined = lax.dynamic_update_index_in_dim(joined, piece, digit ^ step, 0)
        buffer = joined.reshape((radix * buffer.shape[0],) + buffer.shape[1:])
    return buffer, partner_send(buffer, groups[0][0], count)


def body(questions, passages, cot_questions, cot_passages, len_questions, len_passages, positive, *weights):
    local = questions.shape[0]
    question_length = questions.shape[1]
    passage_length = passages.shape[1]
    count = positive.shape[0] // local
    me = lax.axis_index("dp")
    bit = (me % 2).reshape(1)
    x_q = questions.reshape(-1, WIDTH)
    x_p = passages.reshape(-1, WIDTH)
    own_cls = pl.pallas_call(
        functools.partial(first_kernel, local),
        out_shape=shape((count, 2 * PAD, WIDTH), bf16),
        grid=(1,),
        in_specs=[smem(), smem(), whole(x_q.shape), whole(x_p.shape)] + [whole(member.shape) for member in weights],
        out_specs=whole((count, 2 * PAD, WIDTH)),
        scratch_shapes=[pltpu.VMEM(x_q.shape, bf16)] * 2 + [pltpu.VMEM(x_p.shape, bf16)] * 2,
        compiler_params=params(),
        name="first",
    )(len_questions, len_passages, in_hbm(x_q), in_hbm(x_p), *[in_hbm(member) for member in weights])
    all_cls = lax.all_to_all(own_cls, "dp", 0, 0, tiled=True)
    slots = positive // local * PAD + positive % local
    slots = jnp.pad(slots.reshape(count, local), ((0, 0), (0, PAD - local)), constant_values=-1)
    own_slots = lax.dynamic_slice_in_dim(slots, me, 1, axis=0).reshape(PAD, 1)
    loss, grad_cls_q, grad_cls_p = pl.pallas_call(
        functools.partial(loss_kernel, local),
        out_shape=[shape((PAD, 128), f32), shape((PAD, WIDTH), f32), shape((PAD, WIDTH), f32)],
        grid=(1,),
        in_specs=[smem(), whole((count, 2 * PAD, WIDTH)), whole((1, count * PAD)), whole((PAD, 1))],
        out_specs=[whole((PAD, 128)), whole((PAD, WIDTH)), whole((PAD, WIDTH))],
        scratch_shapes=[pltpu.VMEM((count * PAD, WIDTH), bf16), pltpu.VMEM((count * PAD, WIDTH), bf16)],
        compiler_params=params(),
        name="loss",
    )(me.reshape(1), all_cls, slots.reshape(1, -1), own_slots)
    loss_rows = loss[:local, 0]
    out_q, grad_q, keep_q, send_q = layer(
        0, 1, local, question_length, bit, len_questions, grad_cls_q, x_q, cot_questions.reshape(-1, WIDTH), weights
    )
    own_q, other_q = gather_back(reduce_scatter(keep_q, send_q, count, me), count, me)
    out_p, grad_p, keep_p, send_p = layer(
        1, local, 1, passage_length, bit, len_passages, grad_cls_p, x_p, cot_passages.reshape(-1, WIDTH), weights
    )
    own_p, other_p = gather_back(reduce_scatter(keep_p, send_p, count, me), count, me)
    dims = [(2, WIDTH, 3 * WIDTH), (2, WIDTH, WIDTH), (2, WIDTH, HIDDEN), (2, HIDDEN, WIDTH), (2, HIDDEN)]
    dims += [(2, WIDTH)] * len(VECTOR_OUTS)
    d_qkv, d_proj, d_up, d_down, up_bias, query_bias, value_bias, proj_bias, gain_a, shift_a, down_bias, gain_f, shift_f = pl.pallas_call(
        unpack_kernel,
        out_shape=[shape(d, f32) for d in dims],
        grid=(1,),
        in_specs=[smem()] + [whole((HALF, WIDTH))] * 4,
        out_specs=[whole(d) for d in dims],
        scratch_shapes=[pltpu.VMEM((2, GROUP_ROWS, WIDTH), bf16)],
        compiler_params=params(),
        name="unpack",
    )(bit, own_q, other_q, own_p, other_p)
    return (
        loss_rows, out_q.reshape(questions.shape), out_p.reshape(passages.shape),
        grad_q.reshape(questions.shape), grad_p.reshape(passages.shape),
        d_qkv, query_bias, value_bias, d_proj, proj_bias, gain_a, shift_a, d_up, up_bias, d_down,
        down_bias, gain_f, shift_f,
    )


def solution(mesh):
    split = P("dp", None, None)
    return jax.shard_map(
        body,
        mesh=mesh,
        in_specs=(split, split, split, split, P("dp"), P("dp")) + (P(),) * 14,
        out_specs=(P("dp"), split, split, split, split) + (P(),) * 13,
        check_vma=False,
    )
```

time: 173 us -> 128 us (0.74)
  local copies, waits for them, and re-layouts: 49.8 us -> 3.54 us
  Pallas kernels: 42.9 us -> 50.9 us
  other arithmetic: 4.07 us -> 0.1 us
  waiting for transfers between devices: 34.8 us -> 32 us
    unnamed x152 -> x14, local copies, waits for them, and re-layouts: 44.4 us -> 2.25 us
    pallas_call x7, Pallas kernels: 39.1 us -> 46.9 us  [the longest x2 36.6 us: layer(): pl.pallas_call(functools.partial(layer_kernel, which, steps, seqs, length...]
    convert_element_type x3 -> x0, other arithmetic: 3.96 us -> none  [reduce_scatter(): buffer = total.astype(bf16)]
    squeeze x6 -> x0, local copies, waits for them, and re-layouts: 2.91 us -> none  [reduce_scatter(): outgoing = lax.dynamic_index_in_dim(split, digit ^ step, 0, keepdims=False)]
    ppermute x28, waiting for transfers between devices: 24.7 us -> 21.9 us  [partner_send(): return lax.ppermute(values, 'dp', [(i, i ^ mask) for i in range(count)])]
  transfers between devices with their start and end apart: 29 -> 29, of which waited for: 13 -> 8; matrix products, arithmetic and copies ran while one was open for 4% -> 1% of each run, Pallas kernels for 10% -> 23%
where the time goes in v4:
time: 128 us
  Pallas kernels  50.9 us (40%)
  starting transfers between devices  40.4 us (32%)
  waiting for transfers between devices  32 us (25%)
  local copies, waits for them, and re-layouts  3.54 us (3%)
    pallas_call x2, Pallas kernels, layer(): pl.pallas_call(functools.partial(layer_kernel, which, steps, seqs, length...  36.6 us
    ppermute x28, starting transfers between devices, partner_send(): return lax.ppermute(values, 'dp', [(i, i ^ mask) for i in range(count)])  32.9 us
    ppermute x28, waiting for transfers between devices, partner_send(): return lax.ppermute(values, 'dp', [(i, i ^ mask) for i in range(count)])  21.9 us
    all_to_all x1, waiting for transfers between devices, body(): all_cls = lax.all_to_all(own_cls, 'dp', 0, 0, tiled=True)  10.1 us
    pallas_call x1, Pallas kernels, body(): pl.pallas_call(functools.partial(first_kernel, local), out_shape=shape((c...  8.55 us
    all_to_all x1, starting transfers between devices, body(): all_cls = lax.all_to_all(own_cls, 'dp', 0, 0, tiled=True)  7.48 us
    pallas_call x1, Pallas kernels, body(): pl.pallas_call(unpack_kernel, out_shape=[shape(d, f32) for d in dims], gr...  3.18 us
  transfers between devices with their start and end apart: 29, of which 8 were waited for; matrix products, arithmetic and copies ran while one was open for 1% of the time, Pallas kernels for 23%

profile of v4, /device:TPU:0, one launch (start us, length us, event | category | flops | bytes accessed | tf_op | source)
XLA Modules:
  0.0 128.0 jit_solution(697340627808891183)
XLA Ops:
  0.7 0.6 copy-done.2
  1.3 0.7 copy-done.4
  2.0 8.6 %first.1 = bf16[32,16,256]{2,1,0:T(8,128)(2,1)} custom-call(s32[5]{0:T(128)S(1)} %copy-done.2, s32[5]{0:T(128)S(1)} %copy-done.4, bf16[320,256]{1,0:T(8,128)(2,1)} %bitcast.66, bf16[1280,256]{1,0:T(8,128)(2,1)} %bitcast.64, bf16[2,256,768]{2,1,0:T(8,128)(2,1)} %wqkv_ref.3, bf16[2,256]{1,0:T(2,128)(2,1)} %qb_ref.3, bf16[2,256]{1,0:T(2,128)(2,1)} %vb_ref.3, ...), custom_call_target="tpu_custom_call" | custom-call | tf_op jit(solution)/shard_map/first/pallas_call | solution.py:603
  10.5 7.5 %all-to-all-start = ((bf16[32,16,256]{2,1,0:T(8,128)(2,1)}), bf16[32,16,256]{2,1,0:T(8,128)(2,1)S(1)}, u32[]{:S(2)}, u32[]{:S(2)}) async-start(bf16[32,16,256]{2,1,0:T(8,128)(2,1)} %first.1), calls=%async_computation | async-start | bytes 524288 | tf_op jit(solution)/shard_map/all_to_all | solution.py:613
  18.0 0.1 reshape.100
  18.2 0.1 reshape.101.hot_ref
  18.4 10.1 %all-to-all-done.all_ref = bf16[32,16,256]{2,1,0:T(8,128)(2,1)S(1)} async-done(((bf16[32,16,256]{2,1,0:T(8,128)(2,1)}), bf16[32,16,256]{2,1,0:T(8,128)(2,1)S(1)}, u32[]{:S(2)}, u32[]{:S(2)}) %all-to-all-start) | async-done | bytes 262176 | tf_op jit(solution)/shard_map/all_to_all | solution.py:613
  28.4 0.8 loss.1
  29.2 9.3 %layer.2 = (bf16[320,256]{1,0:T(8,128)(2,1)}, bf16[320,256]{1,0:T(8,128)(2,1)}, bf16[1664,256]{1,0:T(8,128)(2,1)S(1)}, bf16[1664,256]{1,0:T(8,128)(2,1)}) custom-call(s32[1]{0:T(128)} %bitcast.4.bit_ref, s32[5]{0:T(128)S(1)} %copy-done.3, f32[8,256]{1,0:T(8,128)S(1)} %get-tuple-element.59.cls_ref, bf16[320,256]{1,0:T(8,128)(2,1)} %bitcast.67, ...), custom_call_target="tpu_custom_call" | custom-call | flops 1536000000 | bytes 1280000 | tf_op jit(solution)/shard_map/layer/pallas_call | solution.py:502
  38.6 27.2 %layer.3 = (bf16[1280,256]{1,0:T(8,128)(2,1)}, bf16[1280,256]{1,0:T(8,128)(2,1)}, bf16[1664,256]{1,0:T(8,128)(2,1)S(1)}, bf16[1664,256]{1,0:T(8,128)(2,1)}) custom-call(s32[1]{0:T(128)} %bitcast.4.bit_ref, s32[5]{0:T(128)S(1)} %copy-done.5, f32[8,256]{1,0:T(8,128)S(1)} %get-tuple-element.61.cls_ref, bf16[1280,256]{1,0:T(8,128)(2,1)} %bitcast.65, ...), custom_call_target="tpu_custom_call" | custom-call | flops 6144000000 | bytes 5120000 | tf_op jit(solution)/shard_map/layer/pallas_call | solution.py:502
  65.8 0.5 collective-permute-start.14
  66.4 1.1 combine.4
  67.5 0.4 collective-permute-start.1
  67.8 1.4 %collective-permute-start.2 = (bf16[416,256]{1,0:T(8,128)(2,1)}, bf16[416,256]{1,0:T(8,128)(2,1)S(1)}, u32[]{:S(2)}, u32[]{:S(2)}) collective-permute-start(bf16[416,256]{1,0:T(8,128)(2,1)} %get-tuple-element.69), channel_id=1, source_target_pairs={{0,4},{1,5},{2,6},{3,7},{4,0},{5,1},{6,2},{7,3},{8,12},{9,13},{10,... | collective-permute-start | bytes 638984 | tf_op jit(solution)/shard_map/ppermute | solution.py:539
  69.2 1.7 %collective-permute-start.3 = (bf16[416,256]{1,0:T(8,128)(2,1)}, bf16[416,256]{1,0:T(8,128)(2,1)S(1)}, u32[]{:S(2)}, u32[]{:S(2)}) collective-permute-start(bf16[416,256]{1,0:T(8,128)(2,1)} %get-tuple-element.70), channel_id=1, source_target_pairs={{0,6},{1,7},{2,4},{3,5},{4,2},{5,3},{6,0},{7,1},{8,14},{9,15},{10,... | collective-permute-start | bytes 638984 | tf_op jit(solution)/shard_map/ppermute | solution.py:539
  71.0 0.4 combine.6
  71.3 0.4 collective-permute-start.15
  71.7 1.4 %collective-permute-start.16 = (bf16[416,256]{1,0:T(8,128)(2,1)S(1)}, bf16[416,256]{1,0:T(8,128)(2,1)S(1)}, u32[]{:S(2)}, u32[]{:S(2)}) collective-permute-start(bf16[416,256]{1,0:T(8,128)(2,1)S(1)} %get-tuple-element.79), channel_id=1, source_target_pairs={{0,4},{1,5},{2,6},{3,7},{4,0},{5,1},{6,2},{7,3},{8,12},{9,13},{10,... | collective-permute-start | bytes 638984 | tf_op jit(solution)/shard_map/ppermute | solution.py:539
  73.1 2.4 %collective-permute-done.1.refs_1_ = bf16[416,256]{1,0:T(8,128)(2,1)S(1)} collective-permute-done((bf16[416,256]{1,0:T(8,128)(2,1)S(1)}, bf16[416,256]{1,0:T(8,128)(2,1)S(1)}, u32[]{:S(2)}, u32[]{:S(2)}) %collective-permute-start.1) | collective-permute-done | bytes 213024 | tf_op jit(solution)/shard_map/ppermute | solution.py:539
  75.6 1.2 collective-permute-start.17
  76.8 3.9 %collective-permute-done.2.refs_2_ = bf16[416,256]{1,0:T(8,128)(2,1)S(1)} collective-permute-done((bf16[416,256]{1,0:T(8,128)(2,1)}, bf16[416,256]{1,0:T(8,128)(2,1)S(1)}, u32[]{:S(2)}, u32[]{:S(2)}) %collective-permute-start.2) | collective-permute-done | bytes 213024 | tf_op jit(solution)/shard_map/ppermute | solution.py:539
  80.7 0.9 copy-done.1
  81.6 0.2 combine.5
  81.8 0.7 collective-permute-start.4
  82.5 1.5 %collective-permute-start.5 = (bf16[104,256]{1,0:T(8,128)(2,1)S(1)}, bf16[104,256]{1,0:T(8,128)(2,1)S(1)}, u32[]{:S(2)}, u32[]{:S(2)}) collective-permute-start(bf16[104,256]{1,0:T(8,128)(2,1)S(1)} %get-tuple-element.73), channel_id=1, source_target_pairs={{0,16},{1,17},{2,18},{3,19},{4,20},{5,21},{6,22},{7,23},{8,24},{9,... | collective-permute-start | bytes 159752 | tf_op jit(solution)/shard_map/ppermute | solution.py:539
  84.0 0.7 collective-permute-done.15.refs_1_
  84.7 1.5 %collective-permute-start.6 = (bf16[104,256]{1,0:T(8,128)(2,1)S(1)}, bf16[104,256]{1,0:T(8,128)(2,1)S(1)}, u32[]{:S(2)}, u32[]{:S(2)}) collective-permute-start(bf16[104,256]{1,0:T(8,128)(2,1)S(1)} %get-tuple-element.74), channel_id=1, source_target_pairs={{0,24},{1,25},{2,26},{3,27},{4,28},{5,29},{6,30},{7,31},{8,16},{9,... | collective-permute-start | bytes 159752 | tf_op jit(solution)/shard_map/ppermute | solution.py:539
  86.3 2.8 %collective-permute-done.16.refs_2_ = bf16[416,256]{1,0:T(8,128)(2,1)S(1)} collective-permute-done((bf16[416,256]{1,0:T(8,128)(2,1)S(1)}, bf16[416,256]{1,0:T(8,128)(2,1)S(1)}, u32[]{:S(2)}, u32[]{:S(2)}) %collective-permute-start.16) | collective-permute-done | bytes 213024 | tf_op jit(solution)/shard_map/ppermute | solution.py:539
  89.1 0.2 combine.7
  89.2 0.7 collective-permute-start.18
  90.0 1.2 collective-permute-start.19
  91.1 2.6 %collective-permute-start.20 = (bf16[104,256]{1,0:T(8,128)(2,1)S(1)}, bf16[104,256]{1,0:T(8,128)(2,1)S(1)}, u32[]{:S(2)}, u32[]{:S(2)}) collective-permute-start(bf16[104,256]{1,0:T(8,128)(2,1)S(1)} %get-tuple-element.84), channel_id=1, source_target_pairs={{0,24},{1,25},{2,26},{3,27},{4,28},{5,29},{6,30},{7,31},{8,16},{9,... | collective-permute-start | bytes 159752 | tf_op jit(solution)/shard_map/ppermute | solution.py:539
  93.8 1.8 %collective-permute-start.7 = (bf16[104,256]{1,0:T(8,128)(2,1)S(1)}, bf16[104,256]{1,0:T(8,128)(2,1)S(1)}, u32[]{:S(2)}, u32[]{:S(2)}) collective-permute-start(bf16[104,256]{1,0:T(8,128)(2,1)S(1)} %get-tuple-element.101), channel_id=1, source_target_pairs={{0,8},{1,9},{2,10},{3,11},{4,12},{5,13},{6,14},{7,15},{8,0},{9,1},... | collective-permute-start | bytes 159752 | tf_op jit(solution)/shard_map/ppermute | solution.py:539
  95.6 2.6 %collective-permute-start.9 = (bf16[104,256]{1,0:T(8,128)(2,1)S(1)}, bf16[104,256]{1,0:T(8,128)(2,1)S(1)}, u32[]{:S(2)}, u32[]{:S(2)}) collective-permute-start(bf16[104,256]{1,0:T(8,128)(2,1)S(1)} %get-tuple-element.101), channel_id=1, source_target_pairs={{0,24},{1,25},{2,26},{3,27},{4,28},{5,29},{6,30},{7,31},{8,16},{9,... | collective-permute-start | bytes 159752 | tf_op jit(solution)/shard_map/ppermute | solution.py:539
  98.3 2.5 %collective-permute-start.22 = (bf16[104,256]{1,0:T(8,128)(2,1)S(1)}, bf16[104,256]{1,0:T(8,128)(2,1)S(1)}, u32[]{:S(2)}, u32[]{:S(2)}) collective-permute-start(bf16[104,256]{1,0:T(8,128)(2,1)S(1)} %get-tuple-element.99), channel_id=1, source_target_pairs={{0,16},{1,17},{2,18},{3,19},{4,20},{5,21},{6,22},{7,23},{8,24},{9,... | collective-permute-start | bytes 159752 | tf_op jit(solution)/shard_map/ppermute | solution.py:539
  100.8 0.2 collective-permute-start.21
  101.0 2.3 %collective-permute-start.23 = (bf16[104,256]{1,0:T(8,128)(2,1)S(1)}, bf16[104,256]{1,0:T(8,128)(2,1)S(1)}, u32[]{:S(2)}, u32[]{:S(2)}) collective-permute-start(bf16[104,256]{1,0:T(8,128)(2,1)S(1)} %get-tuple-element.99), channel_id=1, source_target_pairs={{0,24},{1,25},{2,26},{3,27},{4,28},{5,29},{6,30},{7,31},{8,16},{9,... | collective-permute-start | bytes 159752 | tf_op jit(solution)/shard_map/ppermute | solution.py:539
  103.3 1.5 %collective-permute-start.12 = (bf16[416,256]{1,0:T(8,128)(2,1)S(1)}, bf16[416,256]{1,0:T(8,128)(2,1)S(1)}, u32[]{:S(2)}, u32[]{:S(2)}) collective-permute-start(bf16[416,256]{1,0:T(8,128)(2,1)S(1)} %bitcast.60), channel_id=1, source_target_pairs={{0,6},{1,7},{2,4},{3,5},{4,2},{5,3},{6,0},{7,1},{8,14},{9,15},{10,... | collective-permute-start | bytes 638984 | tf_op jit(solution)/shard_map/ppermute | solution.py:539
  104.8 1.0 collective-permute-start.11
  105.9 1.0 collective-permute-start.10
  107.0 1.5 %collective-permute-start.26 = (bf16[416,256]{1,0:T(8,128)(2,1)S(1)}, bf16[416,256]{1,0:T(8,128)(2,1)S(1)}, u32[]{:S(2)}, u32[]{:S(2)}) collective-permute-start(bf16[416,256]{1,0:T(8,128)(2,1)S(1)} %bitcast.56), channel_id=1, source_target_pairs={{0,6},{1,7},{2,4},{3,5},{4,2},{5,3},{6,0},{7,1},{8,14},{9,15},{10,... | collective-permute-start | bytes 638984 | tf_op jit(solution)/shard_map/ppermute | solution.py:539
  108.5 1.8 %collective-permute-start.25 = (bf16[416,256]{1,0:T(8,128)(2,1)S(1)}, bf16[416,256]{1,0:T(8,128)(2,1)S(1)}, u32[]{:S(2)}, u32[]{:S(2)}) collective-permute-start(bf16[416,256]{1,0:T(8,128)(2,1)S(1)} %bitcast.57), channel_id=1, source_target_pairs={{0,4},{1,5},{2,6},{3,7},{4,0},{5,1},{6,2},{7,3},{8,12},{9,13},{10,... | collective-permute-start | bytes 638984 | tf_op jit(solution)/shard_map/ppermute | solution.py:539
  110.5 5.8 %collective-permute-done.10 = bf16[416,256]{1,0:T(8,128)(2,1)S(1)} collective-permute-done((bf16[416,256]{1,0:T(8,128)(2,1)S(1)}, bf16[416,256]{1,0:T(8,128)(2,1)S(1)}, u32[]{:S(2)}, u32[]{:S(2)}) %collective-permute-start.10) | collective-permute-done | bytes 213024 | tf_op jit(solution)/shard_map/ppermute | solution.py:539
  116.2 1.2 collective-permute-start.24
  117.6 4.5 %collective-permute-done.24 = bf16[416,256]{1,0:T(8,128)(2,1)S(1)} collective-permute-done((bf16[416,256]{1,0:T(8,128)(2,1)S(1)}, bf16[416,256]{1,0:T(8,128)(2,1)S(1)}, u32[]{:S(2)}, u32[]{:S(2)}) %collective-permute-start.24) | collective-permute-done | bytes 213024 | tf_op jit(solution)/shard_map/ppermute | solution.py:539
  122.3 0.6 slice_reduce_fusion
  122.9 1.7 %collective-permute-done.27.p_ref = bf16[1664,256]{1,0:T(8,128)(2,1)S(1)} collective-permute-done((bf16[1664,256]{1,0:T(8,128)(2,1)S(1)}, bf16[1664,256]{1,0:T(8,128)(2,1)S(1)}, u32[]{:S(2)}, u32[]{:S(2)}) %collective-permute-start.27) | collective-permute-done | bytes 852000 | tf_op jit(solution)/shard_map/ppermute | solution.py:539
  124.6 3.2 %unpack.1 = (f32[2,256,768]{2,1,0:T(8,128)}, f32[2,256,256]{2,1,0:T(8,128)}, f32[2,256,1024]{2,1,0:T(8,128)}, f32[2,1024,256]{2,1,0:T(8,128)}, f32[2,1024]{1,0:T...) custom-call(s32[1]{0:T(128)} %bitcast.4.bit_ref, ...), custom_call_target="tpu_custom_call" | custom-call | tf_op jit(solution)/shard_map/unpack/pallas_call | solution.py:638
  (60 shorter events, 0.9 us)
Async XLA Ops:
  0.7 0.7 copy-start.2
  1.3 0.7 copy-start.4
  2.0 16.1 %copy-start.6 = (s32[160]{0:T(256)S(1)}, s32[160]{0:T(256)}, u32[]{:S(2)}) copy-start(s32[160]{0:T(256)} %param.26) | copy-start | bytes 1924
  2.0 27.3 %copy-start.3 = (s32[5]{0:T(128)S(1)}, s32[5]{0:T(128)}, u32[]{:S(2)}) copy-start(s32[5]{0:T(128)} %len_ref.2) | copy-start | bytes 64
  10.5 17.9 %all-to-all-start = ((bf16[32,16,256]{2,1,0:T(8,128)(2,1)}), bf16[32,16,256]{2,1,0:T(8,128)(2,1)S(1)}, u32[]{:S(2)}, u32[]{:S(2)}) async-start(bf16[32,16,256]{2,1,0:T(8,128)(2,1)} %first.1), calls=%async_computation | async-start | bytes 524288 | tf_op jit(solution)/shard_map/all_to_all | solution.py:613
  29.2 9.4 %copy-start.5 = (s32[5]{0:T(128)S(1)}, s32[5]{0:T(128)}, u32[]{:S(2)}) copy-start(s32[5]{0:T(128)} %len_ref.3) | copy-start | bytes 64
  38.6 27.8 %collective-permute-start = (bf16[1664,256]{1,0:T(8,128)(2,1)}, bf16[1664,256]{1,0:T(8,128)(2,1)S(1)}, u32[]{:S(2)}, u32[]{:S(2)}) collective-permute-start(bf16[1664,256]{1,0:T(8,128)(2,1)} %get-tuple-element.66), channel_id=1, source_target_pairs={{0,1},{1,0},{2,3},{3,2},{4,5},{5,4},{6,7},{7,6},{8,9},{9,8},{10,11... | collective-permute-start | bytes 2555912 | tf_op jit(solution)/shard_map/ppermute | solution.py:539
  65.8 5.1 %collective-permute-start.14 = (bf16[1664,256]{1,0:T(8,128)(2,1)}, bf16[1664,256]{1,0:T(8,128)(2,1)S(1)}, u32[]{:S(2)}, u32[]{:S(2)}) collective-permute-start(bf16[1664,256]{1,0:T(8,128)(2,1)} %get-tuple-element.76), channel_id=1, source_target_pairs={{0,1},{1,0},{2,3},{3,2},{4,5},{5,4},{6,7},{7,6},{8,9},{9,8},{10,11... | collective-permute-start | bytes 2555912 | tf_op jit(solution)/shard_map/ppermute | solution.py:539
  67.5 8.1 %copy-start = (bf16[416,256]{1,0:T(8,128)(2,1)}, bf16[416,256]{1,0:T(8,128)(2,1)S(1)}, u32[]{:S(2)}) copy-start(bf16[416,256]{1,0:T(8,128)(2,1)S(1)} %get-tuple-element.67.refs_0_) | copy-start | bytes 638980
  67.5 8.1 %collective-permute-start.1 = (bf16[416,256]{1,0:T(8,128)(2,1)S(1)}, bf16[416,256]{1,0:T(8,128)(2,1)S(1)}, u32[]{:S(2)}, u32[]{:S(2)}) collective-permute-start(bf16[416,256]{1,0:T(8,128)(2,1)S(1)} %get-tuple-element.68), channel_id=1, source_target_pairs={{0,2},{1,3},{2,0},{3,1},{4,6},{5,7},{6,4},{7,5},{8,10},{9,11},{10,... | collective-permute-start | bytes 638984 | tf_op jit(solution)/shard_map/ppermute | solution.py:539
  67.8 12.9 %collective-permute-start.2 = (bf16[416,256]{1,0:T(8,128)(2,1)}, bf16[416,256]{1,0:T(8,128)(2,1)S(1)}, u32[]{:S(2)}, u32[]{:S(2)}) collective-permute-start(bf16[416,256]{1,0:T(8,128)(2,1)} %get-tuple-element.69), channel_id=1, source_target_pairs={{0,4},{1,5},{2,6},{3,7},{4,0},{5,1},{6,2},{7,3},{8,12},{9,13},{10,... | collective-permute-start | bytes 638984 | tf_op jit(solution)/shard_map/ppermute | solution.py:539
  69.2 11.5 %collective-permute-start.3 = (bf16[416,256]{1,0:T(8,128)(2,1)}, bf16[416,256]{1,0:T(8,128)(2,1)S(1)}, u32[]{:S(2)}, u32[]{:S(2)}) collective-permute-start(bf16[416,256]{1,0:T(8,128)(2,1)} %get-tuple-element.70), channel_id=1, source_target_pairs={{0,6},{1,7},{2,4},{3,5},{4,2},{5,3},{6,0},{7,1},{8,14},{9,15},{10,... | collective-permute-start | bytes 638984 | tf_op jit(solution)/shard_map/ppermute | solution.py:539
  71.3 13.4 %collective-permute-start.15 = (bf16[416,256]{1,0:T(8,128)(2,1)S(1)}, bf16[416,256]{1,0:T(8,128)(2,1)S(1)}, u32[]{:S(2)}, u32[]{:S(2)}) collective-permute-start(bf16[416,256]{1,0:T(8,128)(2,1)S(1)} %get-tuple-element.78), channel_id=1, source_target_pairs={{0,2},{1,3},{2,0},{3,1},{4,6},{5,7},{6,4},{7,5},{8,10},{9,11},{10,... | collective-permute-start | bytes 638984 | tf_op jit(solution)/shard_map/ppermute | solution.py:539
  71.7 17.3 %collective-permute-start.16 = (bf16[416,256]{1,0:T(8,128)(2,1)S(1)}, bf16[416,256]{1,0:T(8,128)(2,1)S(1)}, u32[]{:S(2)}, u32[]{:S(2)}) collective-permute-start(bf16[416,256]{1,0:T(8,128)(2,1)S(1)} %get-tuple-element.79), channel_id=1, source_target_pairs={{0,4},{1,5},{2,6},{3,7},{4,0},{5,1},{6,2},{7,3},{8,12},{9,13},{10,... | collective-permute-start | bytes 638984 | tf_op jit(solution)/shard_map/ppermute | solution.py:539
  75.6 13.5 %collective-permute-start.17 = (bf16[416,256]{1,0:T(8,128)(2,1)S(1)}, bf16[416,256]{1,0:T(8,128)(2,1)S(1)}, u32[]{:S(2)}, u32[]{:S(2)}) collective-permute-start(bf16[416,256]{1,0:T(8,128)(2,1)S(1)} %get-tuple-element.80), channel_id=1, source_target_pairs={{0,6},{1,7},{2,4},{3,5},{4,2},{5,3},{6,0},{7,1},{8,14},{9,15},{10,... | collective-permute-start | bytes 638984 | tf_op jit(solution)/shard_map/ppermute | solution.py:539
  80.7 0.9 copy-start.1
  81.8 9.3 %collective-permute-start.4 = (bf16[104,256]{1,0:T(8,128)(2,1)S(1)}, bf16[104,256]{1,0:T(8,128)(2,1)S(1)}, u32[]{:S(2)}, u32[]{:S(2)}) collective-permute-start(bf16[104,256]{1,0:T(8,128)(2,1)S(1)} %get-tuple-element.72), channel_id=1, source_target_pairs={{0,8},{1,9},{2,10},{3,11},{4,12},{5,13},{6,14},{7,15},{8,0},{9,1},... | collective-permute-start | bytes 159752 | tf_op jit(solution)/shard_map/ppermute | solution.py:539
  82.5 11.2 %collective-permute-start.5 = (bf16[104,256]{1,0:T(8,128)(2,1)S(1)}, bf16[104,256]{1,0:T(8,128)(2,1)S(1)}, u32[]{:S(2)}, u32[]{:S(2)}) collective-permute-start(bf16[104,256]{1,0:T(8,128)(2,1)S(1)} %get-tuple-element.73), channel_id=1, source_target_pairs={{0,16},{1,17},{2,18},{3,19},{4,20},{5,21},{6,22},{7,23},{8,24},{9,... | collective-permute-start | bytes 159752 | tf_op jit(solution)/shard_map/ppermute | solution.py:539
  84.7 9.0 %collective-permute-start.6 = (bf16[104,256]{1,0:T(8,128)(2,1)S(1)}, bf16[104,256]{1,0:T(8,128)(2,1)S(1)}, u32[]{:S(2)}, u32[]{:S(2)}) collective-permute-start(bf16[104,256]{1,0:T(8,128)(2,1)S(1)} %get-tuple-element.74), channel_id=1, source_target_pairs={{0,24},{1,25},{2,26},{3,27},{4,28},{5,29},{6,30},{7,31},{8,16},{9,... | collective-permute-start | bytes 159752 | tf_op jit(solution)/shard_map/ppermute | solution.py:539
  89.2 6.4 %collective-permute-start.18 = (bf16[104,256]{1,0:T(8,128)(2,1)S(1)}, bf16[104,256]{1,0:T(8,128)(2,1)S(1)}, u32[]{:S(2)}, u32[]{:S(2)}) collective-permute-start(bf16[104,256]{1,0:T(8,128)(2,1)S(1)} %get-tuple-element.82), channel_id=1, source_target_pairs={{0,8},{1,9},{2,10},{3,11},{4,12},{5,13},{6,14},{7,15},{8,0},{9,1},... | collective-permute-start | bytes 159752 | tf_op jit(solution)/shard_map/ppermute | solution.py:539
  90.0 8.3 %collective-permute-start.19 = (bf16[104,256]{1,0:T(8,128)(2,1)S(1)}, bf16[104,256]{1,0:T(8,128)(2,1)S(1)}, u32[]{:S(2)}, u32[]{:S(2)}) collective-permute-start(bf16[104,256]{1,0:T(8,128)(2,1)S(1)} %get-tuple-element.83), channel_id=1, source_target_pairs={{0,16},{1,17},{2,18},{3,19},{4,20},{5,21},{6,22},{7,23},{8,24},{9,... | collective-permute-start | bytes 159752 | tf_op jit(solution)/shard_map/ppermute | solution.py:539
  91.1 7.1 %collective-permute-start.20 = (bf16[104,256]{1,0:T(8,128)(2,1)S(1)}, bf16[104,256]{1,0:T(8,128)(2,1)S(1)}, u32[]{:S(2)}, u32[]{:S(2)}) collective-permute-start(bf16[104,256]{1,0:T(8,128)(2,1)S(1)} %get-tuple-element.84), channel_id=1, source_target_pairs={{0,24},{1,25},{2,26},{3,27},{4,28},{5,29},{6,30},{7,31},{8,16},{9,... | collective-permute-start | bytes 159752 | tf_op jit(solution)/shard_map/ppermute | solution.py:539
  93.8 9.5 %collective-permute-start.8 = (bf16[104,256]{1,0:T(8,128)(2,1)S(1)}, bf16[104,256]{1,0:T(8,128)(2,1)S(1)}, u32[]{:S(2)}, u32[]{:S(2)}) collective-permute-start(bf16[104,256]{1,0:T(8,128)(2,1)S(1)} %get-tuple-element.101), channel_id=1, source_target_pairs={{0,16},{1,17},{2,18},{3,19},{4,20},{5,21},{6,22},{7,23},{8,24},{9,... | collective-permute-start | bytes 159752 | tf_op jit(solution)/shard_map/ppermute | solution.py:539
  93.8 7.1 %collective-permute-start.7 = (bf16[104,256]{1,0:T(8,128)(2,1)S(1)}, bf16[104,256]{1,0:T(8,128)(2,1)S(1)}, u32[]{:S(2)}, u32[]{:S(2)}) collective-permute-start(bf16[104,256]{1,0:T(8,128)(2,1)S(1)} %get-tuple-element.101), channel_id=1, source_target_pairs={{0,8},{1,9},{2,10},{3,11},{4,12},{5,13},{6,14},{7,15},{8,0},{9,1},... | collective-permute-start | bytes 159752 | tf_op jit(solution)/shard_map/ppermute | solution.py:539
  95.6 7.7 %collective-permute-start.9 = (bf16[104,256]{1,0:T(8,128)(2,1)S(1)}, bf16[104,256]{1,0:T(8,128)(2,1)S(1)}, u32[]{:S(2)}, u32[]{:S(2)}) collective-permute-start(bf16[104,256]{1,0:T(8,128)(2,1)S(1)} %get-tuple-element.101), channel_id=1, source_target_pairs={{0,24},{1,25},{2,26},{3,27},{4,28},{5,29},{6,30},{7,31},{8,16},{9,... | collective-permute-start | bytes 159752 | tf_op jit(solution)/shard_map/ppermute | solution.py:539
  98.3 8.6 %collective-permute-start.22 = (bf16[104,256]{1,0:T(8,128)(2,1)S(1)}, bf16[104,256]{1,0:T(8,128)(2,1)S(1)}, u32[]{:S(2)}, u32[]{:S(2)}) collective-permute-start(bf16[104,256]{1,0:T(8,128)(2,1)S(1)} %get-tuple-element.99), channel_id=1, source_target_pairs={{0,16},{1,17},{2,18},{3,19},{4,20},{5,21},{6,22},{7,23},{8,24},{9,... | collective-permute-start | bytes 159752 | tf_op jit(solution)/shard_map/ppermute | solution.py:539
  100.8 5.1 %collective-permute-start.21 = (bf16[104,256]{1,0:T(8,128)(2,1)S(1)}, bf16[104,256]{1,0:T(8,128)(2,1)S(1)}, u32[]{:S(2)}, u32[]{:S(2)}) collective-permute-start(bf16[104,256]{1,0:T(8,128)(2,1)S(1)} %get-tuple-element.99), channel_id=1, source_target_pairs={{0,8},{1,9},{2,10},{3,11},{4,12},{5,13},{6,14},{7,15},{8,0},{9,1},... | collective-permute-start | bytes 159752 | tf_op jit(solution)/shard_map/ppermute | solution.py:539
  101.0 5.9 %collective-permute-start.23 = (bf16[104,256]{1,0:T(8,128)(2,1)S(1)}, bf16[104,256]{1,0:T(8,128)(2,1)S(1)}, u32[]{:S(2)}, u32[]{:S(2)}) collective-permute-start(bf16[104,256]{1,0:T(8,128)(2,1)S(1)} %get-tuple-element.99), channel_id=1, source_target_pairs={{0,24},{1,25},{2,26},{3,27},{4,28},{5,29},{6,30},{7,31},{8,16},{9,... | collective-permute-start | bytes 159752 | tf_op jit(solution)/shard_map/ppermute | solution.py:539
  103.3 14.2 %collective-permute-start.12 = (bf16[416,256]{1,0:T(8,128)(2,1)S(1)}, bf16[416,256]{1,0:T(8,128)(2,1)S(1)}, u32[]{:S(2)}, u32[]{:S(2)}) collective-permute-start(bf16[416,256]{1,0:T(8,128)(2,1)S(1)} %bitcast.60), channel_id=1, source_target_pairs={{0,6},{1,7},{2,4},{3,5},{4,2},{5,3},{6,0},{7,1},{8,14},{9,15},{10,... | collective-permute-start | bytes 638984 | tf_op jit(solution)/shard_map/ppermute | solution.py:539
  104.8 12.6 %collective-permute-start.11 = (bf16[416,256]{1,0:T(8,128)(2,1)S(1)}, bf16[416,256]{1,0:T(8,128)(2,1)S(1)}, u32[]{:S(2)}, u32[]{:S(2)}) collective-permute-start(bf16[416,256]{1,0:T(8,128)(2,1)S(1)} %bitcast.61), channel_id=1, source_target_pairs={{0,4},{1,5},{2,6},{3,7},{4,0},{5,1},{6,2},{7,3},{8,12},{9,13},{10,... | collective-permute-start | bytes 638984 | tf_op jit(solution)/shard_map/ppermute | solution.py:539
  105.9 10.4 %collective-permute-start.10 = (bf16[416,256]{1,0:T(8,128)(2,1)S(1)}, bf16[416,256]{1,0:T(8,128)(2,1)S(1)}, u32[]{:S(2)}, u32[]{:S(2)}) collective-permute-start(bf16[416,256]{1,0:T(8,128)(2,1)S(1)} %bitcast.62), channel_id=1, source_target_pairs={{0,2},{1,3},{2,0},{3,1},{4,6},{5,7},{6,4},{7,5},{8,10},{9,11},{10,... | collective-permute-start | bytes 638984 | tf_op jit(solution)/shard_map/ppermute | solution.py:539
  107.0 15.2 %collective-permute-start.26 = (bf16[416,256]{1,0:T(8,128)(2,1)S(1)}, bf16[416,256]{1,0:T(8,128)(2,1)S(1)}, u32[]{:S(2)}, u32[]{:S(2)}) collective-permute-start(bf16[416,256]{1,0:T(8,128)(2,1)S(1)} %bitcast.56), channel_id=1, source_target_pairs={{0,6},{1,7},{2,4},{3,5},{4,2},{5,3},{6,0},{7,1},{8,14},{9,15},{10,... | collective-permute-start | bytes 638984 | tf_op jit(solution)/shard_map/ppermute | solution.py:539
  108.5 13.7 %collective-permute-start.25 = (bf16[416,256]{1,0:T(8,128)(2,1)S(1)}, bf16[416,256]{1,0:T(8,128)(2,1)S(1)}, u32[]{:S(2)}, u32[]{:S(2)}) collective-permute-start(bf16[416,256]{1,0:T(8,128)(2,1)S(1)} %bitcast.57), channel_id=1, source_target_pairs={{0,4},{1,5},{2,6},{3,7},{4,0},{5,1},{6,2},{7,3},{8,12},{9,13},{10,... | collective-permute-start | bytes 638984 | tf_op jit(solution)/shard_map/ppermute | solution.py:539
  116.2 5.8 %collective-permute-start.24 = (bf16[416,256]{1,0:T(8,128)(2,1)S(1)}, bf16[416,256]{1,0:T(8,128)(2,1)S(1)}, u32[]{:S(2)}, u32[]{:S(2)}) collective-permute-start(bf16[416,256]{1,0:T(8,128)(2,1)S(1)} %bitcast.59), channel_id=1, source_target_pairs={{0,2},{1,3},{2,0},{3,1},{4,6},{5,7},{6,4},{7,5},{8,10},{9,11},{10,... | collective-permute-start | bytes 638984 | tf_op jit(solution)/shard_map/ppermute | solution.py:539
  117.6 5.3 %collective-permute-start.13 = (bf16[1664,256]{1,0:T(8,128)(2,1)S(1)}, bf16[1664,256]{1,0:T(8,128)(2,1)S(1)}, u32[]{:S(2)}, u32[]{:S(2)}) collective-permute-start(bf16[1664,256]{1,0:T(8,128)(2,1)S(1)} %bitcast.54), channel_id=1, source_target_pairs={{0,1},{1,0},{2,3},{3,2},{4,5},{5,4},{6,7},{7,6},{8,9},{9,8},{10,11... | collective-permute-start | bytes 2555912 | tf_op jit(solution)/shard_map/ppermute | solution.py:539
  122.2 2.4 %collective-permute-start.27 = (bf16[1664,256]{1,0:T(8,128)(2,1)S(1)}, bf16[1664,256]{1,0:T(8,128)(2,1)S(1)}, u32[]{:S(2)}, u32[]{:S(2)}) collective-permute-start(bf16[1664,256]{1,0:T(8,128)(2,1)S(1)} %bitcast.52), channel_id=1, source_target_pairs={{0,1},{1,0},{2,3},{3,2},{4,5},{5,4},{6,7},{7,6},{8,9},{9,8},{10,11... | collective-permute-start | bytes 2555912 | tf_op jit(solution)/shard_map/ppermute | solution.py:539

commit v5 on v4

--- a/solution.py
+++ b/solution.py
@@ -16,6 +16,7 @@
 VECTOR_ROWS = 16
 HALF = 6 * WIDTH + 128
 GROUP_ROWS = 2 * HALF
+ORDERED = True
 SOFT = 128
 NORM = 64
 GELU = 32
@@ -63,6 +64,10 @@
     return jnp.concatenate(
         [jnp.where(head == h, wide, 0.0).astype(bf16) for h in range(HEADS)], axis=0
     )
+
+
+def one_head(values, h):
+    return jnp.where(lane_head(values.shape[0]) == h, values.astype(f32), 0.0).astype(bf16)
 
 
 def pick_heads(stacked, rows):
@@ -147,14 +152,8 @@
         lax.fori_loop(0, count, store, 0)
 
 
-def forward_phase(
-    which, seqs, length, first,
-    len_ref, x_ref, wqkv_ref, qb_ref, vb_ref, wo_ref, ob_ref, g1_ref, b1_ref,
-    w1_ref, hb_ref, w2_ref, fb_ref, g2_ref, b2_ref,
-    out_ref, qkv_ref, p_ref, ctx_ref, n1_ref, r1_ref, nb_ref, gp_ref, act_ref, n2_ref, r2_ref,
-    wide_ref, score_ref, prob_ref,
-):
-    rows = seqs * length
+def attend_kernel(which, seqs, length, len_ref, x_ref, wqkv_ref, qb_ref, vb_ref, qkv_ref, p_ref, ctx_ref, score_ref, prob_ref):
+    step = pl.program_id(0)
     x = x_ref[...]
     qkv_ref[:, :WIDTH] = (dot(x, wqkv_ref[:, :WIDTH]) + vector(qb_ref, which)).astype(bf16)
     qkv_ref[:, WIDTH : 2 * WIDTH] = dot(x, wqkv_ref[:, WIDTH : 2 * WIDTH]).astype(bf16)
@@ -163,17 +162,28 @@
     for s in range(seqs):
         span = slice(s * length, (s + 1) * length)
         stack = slice(s * stack_rows, (s + 1) * stack_rows)
-        size = len_ref[first + s]
-        score_ref[stack, :] = dot_nt(stack_heads(qkv_ref[span, :WIDTH]), qkv_ref[span, WIDTH : 2 * WIDTH])
-
-        def softmax(row):
-            here = pl.ds(s * stack_rows + row, SOFT)
-            prob = masked_softmax(score_ref[here, :], size)
-            p_ref[here, :] = prob
-            prob_ref[here, :] = prob.astype(bf16)
-
-        row_loop(stack_rows, SOFT, softmax)
+        size = len_ref[step * seqs + s]
+        queries = qkv_ref[span, :WIDTH]
+        for h in range(HEADS):
+            start = s * stack_rows + h * length
+            score_ref[start : start + length, :] = dot_nt(one_head(queries, h), qkv_ref[span, WIDTH : 2 * WIDTH])
+
+            def softmax(row):
+                here = pl.ds(start + row, min(SOFT, length))
+                prob = masked_softmax(score_ref[here, :], size)
+                p_ref[here, :] = prob
+                prob_ref[here, :] = prob.astype(bf16)
+
+            row_loop(length, min(SOFT, length), softmax)
         ctx_ref[span, :] = pick_heads(dot(prob_ref[stack, :], qkv_ref[span, 2 * WIDTH :]), length).astype(bf16)
+
+
+def forward_phase(
+    which, seqs, length, first,
+    len_ref, x_ref, wo_ref, ob_ref, g1_ref, b1_ref, w1_ref, hb_ref, w2_ref, fb_ref, g2_ref, b2_ref,
+    out_ref, ctx_ref, n1_ref, r1_ref, nb_ref, gp_ref, act_ref, n2_ref, r2_ref, wide_ref,
+):
+    rows = seqs * length
     n2_ref[...] = dot(ctx_ref[...], wo_ref[...])
     ob, g1, b1 = vector(ob_ref, which), vector(g1_ref, which), vector(b1_ref, which)
 
@@ -185,18 +195,18 @@
         nb_ref[here, :] = (unit * g1 + b1).astype(bf16)
 
     row_loop(rows, NORM, first_norm)
-    wide_ref[...] = dot(nb_ref[...], w1_ref[...])
     hb = vector(hb_ref, which)
-
-    def gelu(row):
-        here = pl.ds(row, GELU)
-        for j in range(BLOCKS):
-            lanes = slice(j * WIDTH, (j + 1) * WIDTH)
+    for j in range(BLOCKS):
+        lanes = slice(j * WIDTH, (j + 1) * WIDTH)
+        wide_ref[:, lanes] = dot(nb_ref[...], w1_ref[:, lanes])
+
+        def gelu(row):
+            here = pl.ds(row, GELU)
             active, slope = gelu_parts(wide_ref[here, lanes] + hb[:, lanes])
             act_ref[here, lanes] = active
             gp_ref[here, lanes] = slope
 
-    row_loop(rows, GELU, gelu)
+        row_loop(rows, GELU, gelu)
     n2_ref[...] = dot(act_ref[...], w2_ref[...])
     fb, g2, b2 = vector(fb_ref, which), vector(g2_ref, which), vector(b2_ref, which)
     for s in range(seqs):
@@ -241,17 +251,17 @@
             add_row(vec_ref, DOWN_BIAS, low.astype(f32))
 
         row_loop(length, NORM, norm_back)
-    wide_ref[...] = dot_nt(gffn_ref[...], w2_ref[...])
-
-    def gelu_back(row):
-        here = pl.ds(row, GELU)
-        for j in range(BLOCKS):
-            lanes = slice(j * WIDTH, (j + 1) * WIDTH)
+    for j in range(BLOCKS):
+        lanes = slice(j * WIDTH, (j + 1) * WIDTH)
+        wide_ref[:, lanes] = dot_nt(gffn_ref[...], w2_ref[lanes, :])
+
+        def gelu_back(row):
+            here = pl.ds(row, GELU)
             low = (wide_ref[here, lanes] * gp_ref[here, lanes]).astype(bf16)
             gpre_ref[here, lanes] = low
             add_row(vec_ref, UP_BIAS + j, low.astype(f32))
 
-    row_loop(seqs * length, GELU, gelu_back)
+        row_loop(seqs * length, GELU, gelu_back)
 
 
 def attn_norm_phase(which, rows, gpre_ref, w1_ref, two_ref, n1_ref, r1_ref, g1_ref, wo_ref, one_ref, gatt_ref, dctx_ref, vec_ref):
@@ -281,18 +291,22 @@
     stack_rows = HEADS * length
     for s in range(seqs):
         span = slice(s * length, (s + 1) * length)
-        context = stack_heads(dctx_ref[span, :])
         stack = slice(s * stack_rows, (s + 1) * stack_rows)
-        dp_ref[stack, :] = dot_nt(context, qkv_ref[span, 2 * WIDTH :])
-
-        def softmax_back(row):
-            here = pl.ds(s * stack_rows + row, SOFT)
-            prob = p_ref[here, :]
-            grad = dp_ref[here, :]
-            inner = jnp.sum(prob * grad, axis=1, keepdims=True)
-            ds_ref[here, :] = (prob * (grad - inner)).astype(bf16)
-
-        row_loop(stack_rows, SOFT, softmax_back)
+        contexts = [one_head(dctx_ref[span, :], h) for h in range(HEADS)]
+        for h in range(HEADS):
+            start = s * stack_rows + h * length
+            dp_ref[start : start + length, :] = dot_nt(contexts[h], qkv_ref[span, 2 * WIDTH :])
+
+            def softmax_back(row):
+                here = pl.ds(start + row, min(SOFT, length))
+                prob = p_ref[here, :]
+                grad = dp_ref[here, :]
+                inner = jnp.sum(prob * grad, axis=1, keepdims=True)
+                ds_ref[here, :] = (prob * (grad - inner)).astype(bf16)
+                pb_ref[here, :] = prob.astype(bf16)
+
+            row_loop(length, min(SOFT, length), softmax_back)
+        context = jnp.concatenate(contexts, axis=0)
         queries = stack_heads(qkv_ref[span, :WIDTH])
         grad_q = (pick_heads(dot(ds_ref[stack, :], qkv_ref[span, WIDTH : 2 * WIDTH]), length) * score_scale).astype(bf16)
         gqkv_ref[span, :WIDTH] = grad_q
@@ -305,10 +319,10 @@
 
 def layer_kernel(
     which, steps, seqs, length,
-    bit_ref, len_ref, cls_ref, x_ref, cot_ref,
-    wqkv_ref, qb_ref, vb_ref, wo_ref, ob_ref, g1_ref, b1_ref, w1_ref, hb_ref, w2_ref, fb_ref, g2_ref, b2_ref,
+    bit_ref, len_ref, cls_ref, x_ref, cot_ref, qkv_ref, p_ref, ctx_ref,
+    wqkv_ref, wo_ref, ob_ref, g1_ref, b1_ref, w1_ref, hb_ref, w2_ref, fb_ref, g2_ref, b2_ref,
     out_ref, gx_ref, keep_ref, send_ref,
-    acc_ref, vec_ref, qkv_ref, p_ref, ctx_ref, n1_ref, r1_ref, nb_ref, gp_ref, act_ref, n2_ref, r2_ref,
+    acc_ref, vec_ref, n1_ref, r1_ref, nb_ref, gp_ref, act_ref, n2_ref, r2_ref,
     wide_ref, score_ref, prob_ref, two_ref, gffn_ref, gpre_ref, one_ref, gatt_ref, dctx_ref, gqkv_ref, ds_ref,
 ):
     rows = seqs * length
@@ -332,10 +346,8 @@
 
     forward_phase(
         which, seqs, length, step * seqs,
-        len_ref, x_ref, wqkv_ref, qb_ref, vb_ref, wo_ref, ob_ref, g1_ref, b1_ref,
-        w1_ref, hb_ref, w2_ref, fb_ref, g2_ref, b2_ref,
-        out_ref, qkv_ref, p_ref, ctx_ref, n1_ref, r1_ref, nb_ref, gp_ref, act_ref, n2_ref, r2_ref,
-        wide_ref, score_ref, prob_ref,
+        len_ref, x_ref, wo_ref, ob_ref, g1_ref, b1_ref, w1_ref, hb_ref, w2_ref, fb_ref, g2_ref, b2_ref,
+        out_ref, ctx_ref, n1_ref, r1_ref, nb_ref, gp_ref, act_ref, n2_ref, r2_ref, wide_ref,
     )
     ffn_phase(which, seqs, length, step * seqs, len_ref, cls_ref, cot_ref, n2_ref, r2_ref, gp_ref, w2_ref, g2_ref, two_ref, gffn_ref, gpre_ref, vec_ref, wide_ref)
     for j in range(BLOCKS):
@@ -487,27 +499,45 @@
     return pltpu.with_memory_space_constraint(values, pltpu.HBM)
 
 
-def weight_specs(which):
-    return [
-        part_of(which, (WIDTH, 3 * WIDTH)), pair(WIDTH), pair(WIDTH), part_of(which, (WIDTH, WIDTH)),
-        pair(WIDTH), pair(WIDTH), pair(WIDTH), part_of(which, (WIDTH, HIDDEN)), pair(HIDDEN),
-        part_of(which, (HIDDEN, WIDTH)), pair(WIDTH), pair(WIDTH), pair(WIDTH),
-    ]
-
-
-def layer(which, steps, seqs, length, bit, lengths, cls_grad, x, cot, weights):
+def attend(which, steps, seqs, length, lengths, x, weights):
+    wqkv, qb, vb, *_ = weights
     rows = seqs * length
     total = steps * rows
     stack = seqs * HEADS * length
     return pl.pallas_call(
+        functools.partial(attend_kernel, which, seqs, length),
+        out_shape=[
+            pltpu.HBM((total, 3 * WIDTH), bf16), pltpu.HBM((steps * stack, length), f32), pltpu.HBM((total, WIDTH), bf16),
+        ],
+        grid=(steps,),
+        in_specs=[smem(), rows_of(rows, WIDTH), part_of(which, (WIDTH, 3 * WIDTH)), pair(WIDTH), pair(WIDTH)],
+        out_specs=[rows_of(rows, 3 * WIDTH), rows_of(stack, length), rows_of(rows, WIDTH)],
+        scratch_shapes=[pltpu.VMEM((stack, length), f32), pltpu.VMEM((stack, length), bf16)],
+        compiler_params=params(),
+        cost_estimate=cost(total * 2 * 400000, total * 6000),
+        name="attend",
+    )(lengths, in_hbm(x), in_hbm(wqkv), in_hbm(qb), in_hbm(vb))
+
+
+def layer(which, steps, seqs, length, bit, lengths, cls_grad, x, cot, attended, weights):
+    rows = seqs * length
+    total = steps * rows
+    stack = seqs * HEADS * length
+    wqkv, _, _, *rest = weights
+    return pl.pallas_call(
         functools.partial(layer_kernel, which, steps, seqs, length),
         out_shape=[shape((total, WIDTH), bf16), shape((total, WIDTH), bf16), shape((HALF, WIDTH), bf16), shape((HALF, WIDTH), bf16)],
         grid=(steps,),
-        in_specs=[smem(), smem(), whole((PAD, WIDTH)), rows_of(rows, WIDTH), rows_of(rows, WIDTH)] + weight_specs(which),
+        in_specs=[
+            smem(), smem(), whole((PAD, WIDTH)), rows_of(rows, WIDTH), rows_of(rows, WIDTH),
+            rows_of(rows, 3 * WIDTH), rows_of(stack, length), rows_of(rows, WIDTH),
+            part_of(which, (WIDTH, 3 * WIDTH)), part_of(which, (WIDTH, WIDTH)),
+            pair(WIDTH), pair(WIDTH), pair(WIDTH), part_of(which, (WIDTH, HIDDEN)), pair(HIDDEN),
+            part_of(which, (HIDDEN, WIDTH)), pair(WIDTH), pair(WIDTH), pair(WIDTH),
+        ],
         out_specs=[rows_of(rows, WIDTH), rows_of(rows, WIDTH), whole((HALF, WIDTH)), whole((HALF, WIDTH))],
         scratch_shapes=[
             pltpu.VMEM((GROUP_ROWS, WIDTH), f32), pltpu.VMEM((VECTOR_ROWS, WIDTH), f32),
-            pltpu.VMEM((rows, 3 * WIDTH), bf16), pltpu.VMEM((stack, length), f32), pltpu.VMEM((rows, WIDTH), bf16),
             pltpu.VMEM((rows, WIDTH), f32), pltpu.VMEM((rows, 1), f32), pltpu.VMEM((rows, WIDTH), bf16),
             pltpu.VMEM((rows, HIDDEN), f32), pltpu.VMEM((rows, HIDDEN), bf16), pltpu.VMEM((rows, WIDTH), f32),
             pltpu.VMEM((rows, 1), f32), pltpu.VMEM((rows, HIDDEN), f32), pltpu.VMEM((stack, length), f32),
@@ -518,7 +548,7 @@
         compiler_params=params(),
         cost_estimate=cost(total * 6 * 800000, total * 4000),
         name="layer",
-    )(bit, lengths, cls_grad, in_hbm(x), in_hbm(cot), *[in_hbm(member) for member in weights])
+    )(bit, lengths, cls_grad, in_hbm(x), in_hbm(cot), *[in_hbm(member) for member in attended], in_hbm(wqkv), *[in_hbm(member) for member in rest])
 
 
 def stages(count):
@@ -566,29 +596,48 @@
     return [lax.dynamic_index_in_dim(split, digit ^ step, 0, keepdims=False) for step in range(radix)]
 
 
-def reduce_scatter(keep, send, count, me):
-    groups = stages(count)
-    pieces = [keep, partner_send(send, groups[0][0], count)]
-    for group in groups[1:]:
-        own, *sends = combine(pieces, group, me)
-        pieces = [own] + [partner_send(part, mask, count) for part, mask in zip(sends, combos(group))]
+def send_parts(cut, group, count):
+    own, *sends = cut
+    return [own] + [partner_send(part, mask, count) for part, mask in zip(sends, combos(group))]
+
+
+def send_whole(buffer, group, count):
+    return [buffer] + [partner_send(buffer, mask, count) for mask in combos(group)]
+
+
+def add_up(pieces):
     total = pieces[0].astype(f32)
     for piece in pieces[1:]:
         total = total + piece.astype(f32)
     return total.astype(bf16)
 
 
-def gather_back(buffer, count, me):
-    groups = stages(count)
-    for group in reversed(groups[1:]):
-        radix = 2 ** len(group)
-        digit = (me // group[0]) % radix
-        joined = jnp.zeros((radix,) + buffer.shape, buffer.dtype)
-        pieces = [buffer] + [partner_send(buffer, mask, count) for mask in combos(group)]
-        for step, piece in enumerate(pieces):
-            joined = lax.dynamic_update_index_in_dim(joined, piece, digit ^ step, 0)
-        buffer = joined.reshape((radix * buffer.shape[0],) + buffer.shape[1:])
-    return buffer, partner_send(buffer, groups[0][0], count)
+def join(pieces, group, me):
+    radix = 2 ** len(group)
+    digit = (me // group[0]) % radix
+    joined = jnp.zeros((radix,) + pieces[0].shape, pieces[0].dtype)
+    for step, piece in enumerate(pieces):
+        joined = lax.dynamic_update_index_in_dim(joined, piece, digit ^ step, 0)
+    return joined.reshape((radix * pieces[0].shape[0],) + pieces[0].shape[1:])
+
+
+def prepare(pieces, done, following, me):
+    reduce_done, group_done = done
+    reduce_next, group_next = following
+    if not reduce_done:
+        return [join(pieces, group_done, me)]
+    if reduce_next:
+        return combine(pieces, group_next, me)
+    return [add_up(pieces)]
+
+
+def launch(operands, stage, count):
+    reduce, group = stage
+    return send_parts(operands, group, count) if reduce else send_whole(operands[0], group, count)
+
+
+def after(values, *others):
+    return list(lax.optimization_barrier((tuple(values), others))[0])
 
 
 def body(questions, passages, cot_questions, cot_passages, len_questions, len_passages, positive, *weights):
@@ -610,7 +659,11 @@
         compiler_params=params(),
         name="first",
     )(len_questions, len_passages, in_hbm(x_q), in_hbm(x_p), *[in_hbm(member) for member in weights])
+    own_cls, x_q, x_p = lax.optimization_barrier((own_cls, x_q, x_p))
     all_cls = lax.all_to_all(own_cls, "dp", 0, 0, tiled=True)
+    attended_p = attend(1, local, 1, passage_length, len_passages, x_p, weights)
+    attended_q = attend(0, 1, local, question_length, len_questions, x_q, weights)
+    (all_cls,) = after([all_cls], attended_p[2], attended_q[2])
     slots = positive // local * PAD + positive % local
     slots = jnp.pad(slots.reshape(count, local), ((0, 0), (0, PAD - local)), constant_values=-1)
     own_slots = lax.dynamic_slice_in_dim(slots, me, 1, axis=0).reshape(PAD, 1)
@@ -626,13 +679,30 @@
     )(me.reshape(1), all_cls, slots.reshape(1, -1), own_slots)
     loss_rows = loss[:local, 0]
     out_q, grad_q, keep_q, send_q = layer(
-        0, 1, local, question_length, bit, len_questions, grad_cls_q, x_q, cot_questions.reshape(-1, WIDTH), weights
+        0, 1, local, question_length, bit, len_questions, grad_cls_q, x_q, cot_questions.reshape(-1, WIDTH),
+        attended_q, weights,
     )
-    own_q, other_q = gather_back(reduce_scatter(keep_q, send_q, count, me), count, me)
+    groups = stages(count)
+    steps = [(True, group) for group in groups] + [(False, group) for group in groups[::-1]]
+    operands_q = prepare([keep_q, partner_send(send_q, groups[0][0], count)], steps[0], steps[1], me)
+    (grad_cls_p,) = after([grad_cls_p], *operands_q)
+    pieces_q = launch(operands_q, steps[1], count)
     out_p, grad_p, keep_p, send_p = layer(
-        1, local, 1, passage_length, bit, len_passages, grad_cls_p, x_p, cot_passages.reshape(-1, WIDTH), weights
+        1, local, 1, passage_length, bit, len_passages, grad_cls_p, x_p, cot_passages.reshape(-1, WIDTH),
+        attended_p, weights,
     )
-    own_p, other_p = gather_back(reduce_scatter(keep_p, send_p, count, me), count, me)
+    (send_p,) = after([send_p], *pieces_q)
+    pieces_p = [keep_p, partner_send(send_p, groups[0][0], count)]
+    for place in range(len(steps)):
+        if place > 0:
+            pieces_p = after(pieces_p, *operands_q)
+            operands_p = prepare(pieces_p, steps[place - 1], steps[place], me)
+            pieces_p = launch(operands_p, steps[place], count)
+            pieces_q = after(pieces_q, *operands_p)
+        if place + 2 < len(steps):
+            operands_q = prepare(pieces_q, steps[place + 1], steps[place + 2], me)
+            pieces_q = launch(operands_q, steps[place + 2], count)
+    (own_q, other_q), (own_p, other_p) = pieces_q, pieces_p
     dims = [(2, WIDTH, 3 * WIDTH), (2, WIDTH, WIDTH), (2, WIDTH, HIDDEN), (2, HIDDEN, WIDTH), (2, HIDDEN)]
     dims += [(2, WIDTH)] * len(VECTOR_OUTS)
     d_qkv, d_proj, d_up, d_down, up_bias, query_bias, value_bias, proj_bias, gain_a, shift_a, down_bias, gain_f, shift_f = pl.pallas_call(

time: 128 us -> 119 us (0.930)
  waiting for transfers between devices: 32 us -> 18.2 us
  Pallas kernels: 50.9 us -> 54.8 us
    pallas_call x0 -> x2, Pallas kernels: none -> 10.3 us  [attend(): pl.pallas_call(functools.partial(attend_kernel, which, seqs, length), out...]
    all_to_all x1, waiting for transfers between devices: 10.1 us -> 0.01 us  [body(): all_cls = lax.all_to_all(own_cls, 'dp', 0, 0, tiled=True)]
    pallas_call x2, Pallas kernels: 36.6 us -> 30.9 us  [layer(): pl.pallas_call(functools.partial(layer_kernel, which, steps, seqs, length...]
    ppermute x28, waiting for transfers between devices: 21.9 us -> 18.2 us  [partner_send(): return lax.ppermute(values, 'dp', [(i, i ^ mask) for i in range(count)])]
  transfers between devices with their start and end apart: 29 -> 29, of which waited for: 8 -> 10; matrix products, arithmetic and copies ran while one was open for 1% -> 1% of each run, Pallas kernels for 23% -> 28%
where the time goes in v5:
time: 119 us; the launch traced here: 118 us
  Pallas kernels  54.8 us (46%)
  starting transfers between devices  41.3 us (35%)
  waiting for transfers between devices  18.2 us (15%)
  local copies, waits for them, and re-layouts  2.64 us (2%)
  between operations  1.19 us (1%)
    ppermute x28, starting transfers between devices, partner_send(): return lax.ppermute(values, 'dp', [(i, i ^ mask) for i in range(count)])  33.8 us
    pallas_call x2, Pallas kernels, layer(): pl.pallas_call(functools.partial(layer_kernel, which, steps, seqs, length...  30.9 us
    ppermute x28, waiting for transfers between devices, partner_send(): return lax.ppermute(values, 'dp', [(i, i ^ mask) for i in range(count)])  18.2 us
    pallas_call x2, Pallas kernels, attend(): pl.pallas_call(functools.partial(attend_kernel, which, seqs, length), out...  10.3 us
    pallas_call x1, Pallas kernels, body(): pl.pallas_call(functools.partial(first_kernel, local), out_shape=shape((c...  8.56 us
    all_to_all x1, starting transfers between devices, body(): all_cls = lax.all_to_all(own_cls, 'dp', 0, 0, tiled=True)  7.48 us
    pallas_call x1, Pallas kernels, body(): pl.pallas_call(unpack_kernel, out_shape=[shape(d, f32) for d in dims], gr...  3.18 us
  transfers between devices with their start and end apart: 29, of which 10 were waited for; matrix products, arithmetic and copies ran while one was open for 1% of the time, Pallas kernels for 28%

profile of v5, /device:TPU:0, one launch (start us, length us, event | category | flops | bytes accessed | tf_op | source)
XLA Modules:
  0.0 118.2 jit_solution(4570130909013813014)
XLA Ops:
  0.7 0.6 copy-done
  1.3 0.7 copy-done.2
  2.0 8.6 %first.1 = bf16[32,16,256]{2,1,0:T(8,128)(2,1)} custom-call(s32[5]{0:T(128)S(1)} %copy-done, s32[5]{0:T(128)S(1)} %copy-done.2, bf16[320,256]{1,0:T(8,128)(2,1)} %bitcast.62, bf16[1280,256]{1,0:T(8,128)(2,1)} %bitcast.65, bf16[2,256,768]{2,1,0:T(8,128)(2,1)} %wqkv_ref.7, bf16[2,256]{1,0:T(2,128)(2,1)} %qb_ref.3, bf16[2,256]{1,0:T(2,128)(2,1)} %vb_ref.3, ...), custom_call_target="tpu_custom_call" | custom-call | tf_op jit(solution)/shard_map/first/pallas_call | solution.py:652
  10.5 7.5 %all-to-all-start = ((bf16[32,16,256]{2,1,0:T(8,128)(2,1)}), bf16[32,16,256]{2,1,0:T(8,128)(2,1)S(1)}, u32[]{:S(2)}, u32[]{:S(2)}) async-start(bf16[32,16,256]{2,1,0:T(8,128)(2,1)} %first.1), calls=%async_computation | async-start | bytes 524288 | tf_op jit(solution)/shard_map/all_to_all | solution.py:663
  18.1 0.1 reshape.98
  18.4 3.3 %attend.3 = (bf16[320,768]{1,0:T(8,128)(2,1)}, f32[1280,64]{1,0:T(8,128)}, bf16[320,256]{1,0:T(8,128)(2,1)}) custom-call(s32[5]{0:T(128)S(1)} %copy-done.1, bf16[320,256]{1,0:T(8,128)(2,1)} %bitcast.63, bf16[2,256,768]{2,1,0:T(8,128)(2,1)} %wqkv_ref.7, bf16[2,256]{1,0:T(2,128)(2,1)} %qb_ref.3, bf16[2,256]{1,0:T(2,128)(2,1)} %vb_ref.3), custom_call_target="tpu_custom_call" | custom-call | flops 256000000 | bytes 1920000 | tf_op jit(solution)/shard_map/attend/pallas_call | solution.py:507
  21.7 7.0 %attend.2 = (bf16[1280,768]{1,0:T(8,128)(2,1)}, f32[5120,256]{1,0:T(8,128)}, bf16[1280,256]{1,0:T(8,128)(2,1)}) custom-call(s32[5]{0:T(128)S(1)} %copy-done.3, bf16[1280,256]{1,0:T(8,128)(2,1)} %bitcast.66, bf16[2,256,768]{2,1,0:T(8,128)(2,1)} %wqkv_ref.7, bf16[2,256]{1,0:T(2,128)(2,1)} %qb_ref.3, bf16[2,256]{1,0:T(2,128)(2,1)} %vb_ref.3), custom_call_target="tpu_custom_call" | custom-call | flops 1024000000 | bytes 7680000 | tf_op jit(solution)/shard_map/attend/pallas_call | solution.py:507
  28.6 0.8 loss.1
  29.4 8.3 %layer.2 = (bf16[320,256]{1,0:T(8,128)(2,1)}, bf16[320,256]{1,0:T(8,128)(2,1)}, bf16[1664,256]{1,0:T(8,128)(2,1)S(1)}, bf16[1664,256]{1,0:T(8,128)(2,1)S(1)}) custom-call(s32[1]{0:T(128)} %bitcast.4.bit_ref, s32[5]{0:T(128)S(1)} %copy-done.1, f32[8,256]{1,0:T(8,128)S(1)} %get-tuple-element.111.cls_ref, bf16[320,256]{1,0:T(8,128)(2,1)} %bitcast.64, ...), custom_call_target="tpu_custom_call" | custom-call | flops 1536000000 | bytes 1280000 | tf_op jit(solution)/shard_map/layer/pallas_call | solution.py:527
  37.8 2.3 %collective-permute-done.refs_1_ = bf16[1664,256]{1,0:T(8,128)(2,1)S(1)} collective-permute-done((bf16[1664,256]{1,0:T(8,128)(2,1)S(1)}, bf16[1664,256]{1,0:T(8,128)(2,1)S(1)}, u32[]{:S(2)}, u32[]{:S(2)}) %collective-permute-start) | collective-permute-done | bytes 852000 | tf_op jit(solution)/shard_map/ppermute | solution.py:569
  40.1 0.4 combine.4
  40.5 1.7 %collective-permute-start.1 = (bf16[416,256]{1,0:T(8,128)(2,1)S(1)}, bf16[416,256]{1,0:T(8,128)(2,1)S(1)}, u32[]{:S(2)}, u32[]{:S(2)}) collective-permute-start(bf16[416,256]{1,0:T(8,128)(2,1)S(1)} %get-tuple-element.119), channel_id=1, source_target_pairs={{0,2},{1,3},{2,0},{3,1},{4,6},{5,7},{6,4},{7,5},{8,10},{9,11},{10,... | collective-permute-start | bytes 638984 | tf_op jit(solution)/shard_map/ppermute | solution.py:569
  42.1 1.4 %collective-permute-start.2 = (bf16[416,256]{1,0:T(8,128)(2,1)S(1)}, bf16[416,256]{1,0:T(8,128)(2,1)S(1)}, u32[]{:S(2)}, u32[]{:S(2)}) collective-permute-start(bf16[416,256]{1,0:T(8,128)(2,1)S(1)} %get-tuple-element.120), channel_id=1, source_target_pairs={{0,4},{1,5},{2,6},{3,7},{4,0},{5,1},{6,2},{7,3},{8,12},{9,13},{10,... | collective-permute-start | bytes 638984 | tf_op jit(solution)/shard_map/ppermute | solution.py:569
  43.6 0.4 collective-permute-start.3
  44.0 22.6 %layer.3 = (bf16[1280,256]{1,0:T(8,128)(2,1)}, bf16[1280,256]{1,0:T(8,128)(2,1)}, bf16[1664,256]{1,0:T(8,128)(2,1)S(1)}, bf16[1664,256]{1,0:T(8,128)(2,1)S(1)}) custom-call(s32[1]{0:T(128)} %bitcast.4.bit_ref, s32[5]{0:T(128)S(1)} %copy-done.3, f32[8,256]{1,0:T(8,128)S(1)} %get-tuple-element.122.cls_ref, bf16[1280,256]{1,0:T(8,128)(2,1)} %bitcast.67, ...), custom_call_target="tpu_custom_call" | custom-call | flops 6144000000 | bytes 5120000 | tf_op jit(solution)/shard_map/layer/pallas_call | solution.py:527
  66.8 0.2 combine.5
  67.0 1.6 %collective-permute-start.4 = (bf16[104,256]{1,0:T(8,128)(2,1)S(1)}, bf16[104,256]{1,0:T(8,128)(2,1)S(1)}, u32[]{:S(2)}, u32[]{:S(2)}) collective-permute-start(bf16[104,256]{1,0:T(8,128)(2,1)S(1)} %get-tuple-element.129), channel_id=1, source_target_pairs={{0,8},{1,9},{2,10},{3,11},{4,12},{5,13},{6,14},{7,15},{8,0},{9,1},... | collective-permute-start | bytes 159752 | tf_op jit(solution)/shard_map/ppermute | solution.py:569
  68.6 2.4 %collective-permute-start.5 = (bf16[104,256]{1,0:T(8,128)(2,1)S(1)}, bf16[104,256]{1,0:T(8,128)(2,1)S(1)}, u32[]{:S(2)}, u32[]{:S(2)}) collective-permute-start(bf16[104,256]{1,0:T(8,128)(2,1)S(1)} %get-tuple-element.130), channel_id=1, source_target_pairs={{0,16},{1,17},{2,18},{3,19},{4,20},{5,21},{6,22},{7,23},{8,24},{9,... | collective-permute-start | bytes 159752 | tf_op jit(solution)/shard_map/ppermute | solution.py:569
  71.1 0.4 collective-permute-start.6
  71.4 0.4 combine.6
  71.8 1.7 %collective-permute-start.11 = (bf16[416,256]{1,0:T(8,128)(2,1)S(1)}, bf16[416,256]{1,0:T(8,128)(2,1)S(1)}, u32[]{:S(2)}, u32[]{:S(2)}) collective-permute-start(bf16[416,256]{1,0:T(8,128)(2,1)S(1)} %get-tuple-element.138), channel_id=1, source_target_pairs={{0,2},{1,3},{2,0},{3,1},{4,6},{5,7},{6,4},{7,5},{8,10},{9,11},{10,... | collective-permute-start | bytes 638984 | tf_op jit(solution)/shard_map/ppermute | solution.py:569
  73.5 1.4 %collective-permute-start.12 = (bf16[416,256]{1,0:T(8,128)(2,1)S(1)}, bf16[416,256]{1,0:T(8,128)(2,1)S(1)}, u32[]{:S(2)}, u32[]{:S(2)}) collective-permute-start(bf16[416,256]{1,0:T(8,128)(2,1)S(1)} %get-tuple-element.139), channel_id=1, source_target_pairs={{0,4},{1,5},{2,6},{3,7},{4,0},{5,1},{6,2},{7,3},{8,12},{9,13},{10,... | collective-permute-start | bytes 638984 | tf_op jit(solution)/shard_map/ppermute | solution.py:569
  74.9 0.4 collective-permute-start.13
  75.4 1.6 %collective-permute-done.6 = bf16[104,256]{1,0:T(8,128)(2,1)S(1)} collective-permute-done((bf16[104,256]{1,0:T(8,128)(2,1)S(1)}, bf16[104,256]{1,0:T(8,128)(2,1)S(1)}, u32[]{:S(2)}, u32[]{:S(2)}) %collective-permute-start.6) | collective-permute-done | bytes 53280 | tf_op jit(solution)/shard_map/ppermute | solution.py:569
  77.1 2.4 %collective-permute-start.9 = (bf16[104,256]{1,0:T(8,128)(2,1)S(1)}, bf16[104,256]{1,0:T(8,128)(2,1)S(1)}, u32[]{:S(2)}, u32[]{:S(2)}) collective-permute-start(bf16[104,256]{1,0:T(8,128)(2,1)S(1)} %add_convert_fusion.1), channel_id=1, source_target_pairs={{0,16},{1,17},{2,18},{3,19},{4,20},{5,21},{6,22},{7,23},{8,24},{9,... | collective-permute-start | bytes 159752 | tf_op jit(solution)/shard_map/ppermute | solution.py:569
  79.5 0.6 collective-permute-done.11.refs_1_
  80.0 3.4 %collective-permute-start.10 = (bf16[104,256]{1,0:T(8,128)(2,1)S(1)}, bf16[104,256]{1,0:T(8,128)(2,1)S(1)}, u32[]{:S(2)}, u32[]{:S(2)}) collective-permute-start(bf16[104,256]{1,0:T(8,128)(2,1)S(1)} %add_convert_fusion.1), channel_id=1, source_target_pairs={{0,24},{1,25},{2,26},{3,27},{4,28},{5,29},{6,30},{7,31},{8,16},{9,... | collective-permute-start | bytes 159752 | tf_op jit(solution)/shard_map/ppermute | solution.py:569
  83.5 1.1 collective-permute-done.12.refs_2_
  84.5 0.2 combine.7
  84.7 0.6 collective-permute-start.17
  85.3 3.4 %collective-permute-start.18 = (bf16[104,256]{1,0:T(8,128)(2,1)S(1)}, bf16[104,256]{1,0:T(8,128)(2,1)S(1)}, u32[]{:S(2)}, u32[]{:S(2)}) collective-permute-start(bf16[104,256]{1,0:T(8,128)(2,1)S(1)} %get-tuple-element.151), channel_id=1, source_target_pairs={{0,16},{1,17},{2,18},{3,19},{4,20},{5,21},{6,22},{7,23},{8,24},{9,... | collective-permute-start | bytes 159752 | tf_op jit(solution)/shard_map/ppermute | solution.py:569
  88.7 0.5 collective-permute-start.19
  89.3 1.2 %collective-permute-start.14 = (bf16[416,256]{1,0:T(8,128)(2,1)S(1)}, bf16[416,256]{1,0:T(8,128)(2,1)S(1)}, u32[]{:S(2)}, u32[]{:S(2)}) collective-permute-start(bf16[416,256]{1,0:T(8,128)(2,1)S(1)} %bitcast.58), channel_id=1, source_target_pairs={{0,2},{1,3},{2,0},{3,1},{4,6},{5,7},{6,4},{7,5},{8,10},{9,11},{10,... | collective-permute-start | bytes 638984 | tf_op jit(solution)/shard_map/ppermute | solution.py:569
  90.5 0.8 collective-permute-start.15
  91.3 1.5 %collective-permute-start.16 = (bf16[416,256]{1,0:T(8,128)(2,1)S(1)}, bf16[416,256]{1,0:T(8,128)(2,1)S(1)}, u32[]{:S(2)}, u32[]{:S(2)}) collective-permute-start(bf16[416,256]{1,0:T(8,128)(2,1)S(1)} %bitcast.60), channel_id=1, source_target_pairs={{0,6},{1,7},{2,4},{3,5},{4,2},{5,3},{6,0},{7,1},{8,14},{9,15},{10,... | collective-permute-start | bytes 638984 | tf_op jit(solution)/shard_map/ppermute | solution.py:569
  92.8 2.3 %collective-permute-done.19 = bf16[104,256]{1,0:T(8,128)(2,1)S(1)} collective-permute-done((bf16[104,256]{1,0:T(8,128)(2,1)S(1)}, bf16[104,256]{1,0:T(8,128)(2,1)S(1)}, u32[]{:S(2)}, u32[]{:S(2)}) %collective-permute-start.19) | collective-permute-done | bytes 53280 | tf_op jit(solution)/shard_map/ppermute | solution.py:569
  95.3 1.5 %collective-permute-start.22 = (bf16[104,256]{1,0:T(8,128)(2,1)S(1)}, bf16[104,256]{1,0:T(8,128)(2,1)S(1)}, u32[]{:S(2)}, u32[]{:S(2)}) collective-permute-start(bf16[104,256]{1,0:T(8,128)(2,1)S(1)} %add_convert_fusion), channel_id=1, source_target_pairs={{0,16},{1,17},{2,18},{3,19},{4,20},{5,21},{6,22},{7,23},{8,24},{9,... | collective-permute-start | bytes 159752 | tf_op jit(solution)/shard_map/ppermute | solution.py:569
  96.8 3.0 %collective-permute-start.23 = (bf16[104,256]{1,0:T(8,128)(2,1)S(1)}, bf16[104,256]{1,0:T(8,128)(2,1)S(1)}, u32[]{:S(2)}, u32[]{:S(2)}) collective-permute-start(bf16[104,256]{1,0:T(8,128)(2,1)S(1)} %add_convert_fusion), channel_id=1, source_target_pairs={{0,24},{1,25},{2,26},{3,27},{4,28},{5,29},{6,30},{7,31},{8,16},{9,... | collective-permute-start | bytes 159752 | tf_op jit(solution)/shard_map/ppermute | solution.py:569
  100.0 0.4 collective-permute-done.22
  100.4 2.4 %collective-permute-done.23 = bf16[104,256]{1,0:T(8,128)(2,1)S(1)} collective-permute-done((bf16[104,256]{1,0:T(8,128)(2,1)S(1)}, bf16[104,256]{1,0:T(8,128)(2,1)S(1)}, u32[]{:S(2)}, u32[]{:S(2)}) %collective-permute-start.23) | collective-permute-done | bytes 53280 | tf_op jit(solution)/shard_map/ppermute | solution.py:569
  102.9 1.3 %collective-permute-start.24 = (bf16[416,256]{1,0:T(8,128)(2,1)S(1)}, bf16[416,256]{1,0:T(8,128)(2,1)S(1)}, u32[]{:S(2)}, u32[]{:S(2)}) collective-permute-start(bf16[416,256]{1,0:T(8,128)(2,1)S(1)} %bitcast.54), channel_id=1, source_target_pairs={{0,2},{1,3},{2,0},{3,1},{4,6},{5,7},{6,4},{7,5},{8,10},{9,11},{10,... | collective-permute-start | bytes 638984 | tf_op jit(solution)/shard_map/ppermute | solution.py:569
  104.1 0.8 collective-permute-start.25
  105.0 1.4 %collective-permute-start.26 = (bf16[416,256]{1,0:T(8,128)(2,1)S(1)}, bf16[416,256]{1,0:T(8,128)(2,1)S(1)}, u32[]{:S(2)}, u32[]{:S(2)}) collective-permute-start(bf16[416,256]{1,0:T(8,128)(2,1)S(1)} %bitcast.56), channel_id=1, source_target_pairs={{0,6},{1,7},{2,4},{3,5},{4,2},{5,3},{6,0},{7,1},{8,14},{9,15},{10,... | collective-permute-start | bytes 638984 | tf_op jit(solution)/shard_map/ppermute | solution.py:569
  106.4 2.4 %collective-permute-done.24 = bf16[416,256]{1,0:T(8,128)(2,1)S(1)} collective-permute-done((bf16[416,256]{1,0:T(8,128)(2,1)S(1)}, bf16[416,256]{1,0:T(8,128)(2,1)S(1)}, u32[]{:S(2)}, u32[]{:S(2)}) %collective-permute-start.24) | collective-permute-done | bytes 213024 | tf_op jit(solution)/shard_map/ppermute | solution.py:569
  108.8 3.5 %collective-permute-done.25 = bf16[416,256]{1,0:T(8,128)(2,1)S(1)} collective-permute-done((bf16[416,256]{1,0:T(8,128)(2,1)S(1)}, bf16[416,256]{1,0:T(8,128)(2,1)S(1)}, u32[]{:S(2)}, u32[]{:S(2)}) %collective-permute-start.25) | collective-permute-done | bytes 213024 | tf_op jit(solution)/shard_map/ppermute | solution.py:569
  112.5 0.6 slice_reduce_fusion
  113.1 1.7 %collective-permute-done.27.p_ref = bf16[1664,256]{1,0:T(8,128)(2,1)S(1)} collective-permute-done((bf16[1664,256]{1,0:T(8,128)(2,1)S(1)}, bf16[1664,256]{1,0:T(8,128)(2,1)S(1)}, u32[]{:S(2)}, u32[]{:S(2)}) %collective-permute-start.27) | collective-permute-done | bytes 852000 | tf_op jit(solution)/shard_map/ppermute | solution.py:569
  114.9 3.2 %unpack.1 = (f32[2,256,768]{2,1,0:T(8,128)}, f32[2,256,256]{2,1,0:T(8,128)}, f32[2,256,1024]{2,1,0:T(8,128)}, f32[2,1024,256]{2,1,0:T(8,128)}, f32[2,1024]{1,0:T...) custom-call(s32[1]{0:T(128)} %bitcast.4.bit_ref, ...), custom_call_target="tpu_custom_call" | custom-call | tf_op jit(solution)/shard_map/unpack/pallas_call | solution.py:708
  (60 shorter events, 1.1 us)
Async XLA Ops:
  0.7 0.7 copy-start
  1.3 0.7 copy-start.2
  2.0 16.1 %copy-start.4 = (s32[160]{0:T(256)S(1)}, s32[160]{0:T(256)}, u32[]{:S(2)}) copy-start(s32[160]{0:T(256)} %param.26) | copy-start | bytes 1924
  2.0 16.4 %copy-start.1 = (s32[5]{0:T(128)S(1)}, s32[5]{0:T(128)}, u32[]{:S(2)}) copy-start(s32[5]{0:T(128)} %len_ref.6) | copy-start | bytes 64
  2.0 19.7 %copy-start.3 = (s32[5]{0:T(128)S(1)}, s32[5]{0:T(128)}, u32[]{:S(2)}) copy-start(s32[5]{0:T(128)} %len_ref.7) | copy-start | bytes 64
  10.5 18.1 %all-to-all-start = ((bf16[32,16,256]{2,1,0:T(8,128)(2,1)}), bf16[32,16,256]{2,1,0:T(8,128)(2,1)S(1)}, u32[]{:S(2)}, u32[]{:S(2)}) async-start(bf16[32,16,256]{2,1,0:T(8,128)(2,1)} %first.1), calls=%async_computation | async-start | bytes 524288 | tf_op jit(solution)/shard_map/all_to_all | solution.py:663
  37.7 2.4 %collective-permute-start = (bf16[1664,256]{1,0:T(8,128)(2,1)S(1)}, bf16[1664,256]{1,0:T(8,128)(2,1)S(1)}, u32[]{:S(2)}, u32[]{:S(2)}) collective-permute-start(bf16[1664,256]{1,0:T(8,128)(2,1)S(1)} %get-tuple-element.117), channel_id=1, source_target_pairs={{0,1},{1,0},{2,3},{3,2},{4,5},{5,4},{6,7},{7,6},{8,9},{9,8},{10,11... | collective-permute-start | bytes 2555912 | tf_op jit(solution)/shard_map/ppermute | solution.py:569
  40.5 26.2 %collective-permute-start.1 = (bf16[416,256]{1,0:T(8,128)(2,1)S(1)}, bf16[416,256]{1,0:T(8,128)(2,1)S(1)}, u32[]{:S(2)}, u32[]{:S(2)}) collective-permute-start(bf16[416,256]{1,0:T(8,128)(2,1)S(1)} %get-tuple-element.119), channel_id=1, source_target_pairs={{0,2},{1,3},{2,0},{3,1},{4,6},{5,7},{6,4},{7,5},{8,10},{9,11},{10,... | collective-permute-start | bytes 638984 | tf_op jit(solution)/shard_map/ppermute | solution.py:569
  42.1 24.5 %collective-permute-start.2 = (bf16[416,256]{1,0:T(8,128)(2,1)S(1)}, bf16[416,256]{1,0:T(8,128)(2,1)S(1)}, u32[]{:S(2)}, u32[]{:S(2)}) collective-permute-start(bf16[416,256]{1,0:T(8,128)(2,1)S(1)} %get-tuple-element.120), channel_id=1, source_target_pairs={{0,4},{1,5},{2,6},{3,7},{4,0},{5,1},{6,2},{7,3},{8,12},{9,13},{10,... | collective-permute-start | bytes 638984 | tf_op jit(solution)/shard_map/ppermute | solution.py:569
  43.6 23.1 %collective-permute-start.3 = (bf16[416,256]{1,0:T(8,128)(2,1)S(1)}, bf16[416,256]{1,0:T(8,128)(2,1)S(1)}, u32[]{:S(2)}, u32[]{:S(2)}) collective-permute-start(bf16[416,256]{1,0:T(8,128)(2,1)S(1)} %get-tuple-element.121), channel_id=1, source_target_pairs={{0,6},{1,7},{2,4},{3,5},{4,2},{5,3},{6,0},{7,1},{8,14},{9,15},{10,... | collective-permute-start | bytes 638984 | tf_op jit(solution)/shard_map/ppermute | solution.py:569
  66.7 4.7 %collective-permute-start.7 = (bf16[1664,256]{1,0:T(8,128)(2,1)S(1)}, bf16[1664,256]{1,0:T(8,128)(2,1)S(1)}, u32[]{:S(2)}, u32[]{:S(2)}) collective-permute-start(bf16[1664,256]{1,0:T(8,128)(2,1)S(1)} %get-tuple-element.134), channel_id=1, source_target_pairs={{0,1},{1,0},{2,3},{3,2},{4,5},{5,4},{6,7},{7,6},{8,9},{9,8},{10,11... | collective-permute-start | bytes 2555912 | tf_op jit(solution)/shard_map/ppermute | solution.py:569
  67.0 7.9 %collective-permute-start.4 = (bf16[104,256]{1,0:T(8,128)(2,1)S(1)}, bf16[104,256]{1,0:T(8,128)(2,1)S(1)}, u32[]{:S(2)}, u32[]{:S(2)}) collective-permute-start(bf16[104,256]{1,0:T(8,128)(2,1)S(1)} %get-tuple-element.129), channel_id=1, source_target_pairs={{0,8},{1,9},{2,10},{3,11},{4,12},{5,13},{6,14},{7,15},{8,0},{9,1},... | collective-permute-start | bytes 159752 | tf_op jit(solution)/shard_map/ppermute | solution.py:569
  68.6 6.7 %collective-permute-start.5 = (bf16[104,256]{1,0:T(8,128)(2,1)S(1)}, bf16[104,256]{1,0:T(8,128)(2,1)S(1)}, u32[]{:S(2)}, u32[]{:S(2)}) collective-permute-start(bf16[104,256]{1,0:T(8,128)(2,1)S(1)} %get-tuple-element.130), channel_id=1, source_target_pairs={{0,16},{1,17},{2,18},{3,19},{4,20},{5,21},{6,22},{7,23},{8,24},{9,... | collective-permute-start | bytes 159752 | tf_op jit(solution)/shard_map/ppermute | solution.py:569
  71.1 5.9 %collective-permute-start.6 = (bf16[104,256]{1,0:T(8,128)(2,1)S(1)}, bf16[104,256]{1,0:T(8,128)(2,1)S(1)}, u32[]{:S(2)}, u32[]{:S(2)}) collective-permute-start(bf16[104,256]{1,0:T(8,128)(2,1)S(1)} %get-tuple-element.131), channel_id=1, source_target_pairs={{0,24},{1,25},{2,26},{3,27},{4,28},{5,29},{6,30},{7,31},{8,16},{9,... | collective-permute-start | bytes 159752 | tf_op jit(solution)/shard_map/ppermute | solution.py:569
  71.8 8.2 %collective-permute-start.11 = (bf16[416,256]{1,0:T(8,128)(2,1)S(1)}, bf16[416,256]{1,0:T(8,128)(2,1)S(1)}, u32[]{:S(2)}, u32[]{:S(2)}) collective-permute-start(bf16[416,256]{1,0:T(8,128)(2,1)S(1)} %get-tuple-element.138), channel_id=1, source_target_pairs={{0,2},{1,3},{2,0},{3,1},{4,6},{5,7},{6,4},{7,5},{8,10},{9,11},{10,... | collective-permute-start | bytes 638984 | tf_op jit(solution)/shard_map/ppermute | solution.py:569
  73.5 11.1 %collective-permute-start.12 = (bf16[416,256]{1,0:T(8,128)(2,1)S(1)}, bf16[416,256]{1,0:T(8,128)(2,1)S(1)}, u32[]{:S(2)}, u32[]{:S(2)}) collective-permute-start(bf16[416,256]{1,0:T(8,128)(2,1)S(1)} %get-tuple-element.139), channel_id=1, source_target_pairs={{0,4},{1,5},{2,6},{3,7},{4,0},{5,1},{6,2},{7,3},{8,12},{9,13},{10,... | collective-permute-start | bytes 638984 | tf_op jit(solution)/shard_map/ppermute | solution.py:569
  74.9 9.6 %collective-permute-start.13 = (bf16[416,256]{1,0:T(8,128)(2,1)S(1)}, bf16[416,256]{1,0:T(8,128)(2,1)S(1)}, u32[]{:S(2)}, u32[]{:S(2)}) collective-permute-start(bf16[416,256]{1,0:T(8,128)(2,1)S(1)} %get-tuple-element.140), channel_id=1, source_target_pairs={{0,6},{1,7},{2,4},{3,5},{4,2},{5,3},{6,0},{7,1},{8,14},{9,15},{10,... | collective-permute-start | bytes 638984 | tf_op jit(solution)/shard_map/ppermute | solution.py:569
  77.0 11.6 %collective-permute-start.8 = (bf16[104,256]{1,0:T(8,128)(2,1)S(1)}, bf16[104,256]{1,0:T(8,128)(2,1)S(1)}, u32[]{:S(2)}, u32[]{:S(2)}) collective-permute-start(bf16[104,256]{1,0:T(8,128)(2,1)S(1)} %add_convert_fusion.1), channel_id=1, source_target_pairs={{0,8},{1,9},{2,10},{3,11},{4,12},{5,13},{6,14},{7,15},{8,0},{9,1},... | collective-permute-start | bytes 159752 | tf_op jit(solution)/shard_map/ppermute | solution.py:569
  77.1 12.1 %collective-permute-start.9 = (bf16[104,256]{1,0:T(8,128)(2,1)S(1)}, bf16[104,256]{1,0:T(8,128)(2,1)S(1)}, u32[]{:S(2)}, u32[]{:S(2)}) collective-permute-start(bf16[104,256]{1,0:T(8,128)(2,1)S(1)} %add_convert_fusion.1), channel_id=1, source_target_pairs={{0,16},{1,17},{2,18},{3,19},{4,20},{5,21},{6,22},{7,23},{8,24},{9,... | collective-permute-start | bytes 159752 | tf_op jit(solution)/shard_map/ppermute | solution.py:569
  80.0 9.2 %collective-permute-start.10 = (bf16[104,256]{1,0:T(8,128)(2,1)S(1)}, bf16[104,256]{1,0:T(8,128)(2,1)S(1)}, u32[]{:S(2)}, u32[]{:S(2)}) collective-permute-start(bf16[104,256]{1,0:T(8,128)(2,1)S(1)} %add_convert_fusion.1), channel_id=1, source_target_pairs={{0,24},{1,25},{2,26},{3,27},{4,28},{5,29},{6,30},{7,31},{8,16},{9,... | collective-permute-start | bytes 159752 | tf_op jit(solution)/shard_map/ppermute | solution.py:569
  84.7 6.6 %collective-permute-start.17 = (bf16[104,256]{1,0:T(8,128)(2,1)S(1)}, bf16[104,256]{1,0:T(8,128)(2,1)S(1)}, u32[]{:S(2)}, u32[]{:S(2)}) collective-permute-start(bf16[104,256]{1,0:T(8,128)(2,1)S(1)} %get-tuple-element.150), channel_id=1, source_target_pairs={{0,8},{1,9},{2,10},{3,11},{4,12},{5,13},{6,14},{7,15},{8,0},{9,1},... | collective-permute-start | bytes 159752 | tf_op jit(solution)/shard_map/ppermute | solution.py:569
  85.3 7.5 %collective-permute-start.18 = (bf16[104,256]{1,0:T(8,128)(2,1)S(1)}, bf16[104,256]{1,0:T(8,128)(2,1)S(1)}, u32[]{:S(2)}, u32[]{:S(2)}) collective-permute-start(bf16[104,256]{1,0:T(8,128)(2,1)S(1)} %get-tuple-element.151), channel_id=1, source_target_pairs={{0,16},{1,17},{2,18},{3,19},{4,20},{5,21},{6,22},{7,23},{8,24},{9,... | collective-permute-start | bytes 159752 | tf_op jit(solution)/shard_map/ppermute | solution.py:569
  88.7 6.5 %collective-permute-start.19 = (bf16[104,256]{1,0:T(8,128)(2,1)S(1)}, bf16[104,256]{1,0:T(8,128)(2,1)S(1)}, u32[]{:S(2)}, u32[]{:S(2)}) collective-permute-start(bf16[104,256]{1,0:T(8,128)(2,1)S(1)} %get-tuple-element.152), channel_id=1, source_target_pairs={{0,24},{1,25},{2,26},{3,27},{4,28},{5,29},{6,30},{7,31},{8,16},{9,... | collective-permute-start | bytes 159752 | tf_op jit(solution)/shard_map/ppermute | solution.py:569
  89.3 7.6 %collective-permute-start.14 = (bf16[416,256]{1,0:T(8,128)(2,1)S(1)}, bf16[416,256]{1,0:T(8,128)(2,1)S(1)}, u32[]{:S(2)}, u32[]{:S(2)}) collective-permute-start(bf16[416,256]{1,0:T(8,128)(2,1)S(1)} %bitcast.58), channel_id=1, source_target_pairs={{0,2},{1,3},{2,0},{3,1},{4,6},{5,7},{6,4},{7,5},{8,10},{9,11},{10,... | collective-permute-start | bytes 638984 | tf_op jit(solution)/shard_map/ppermute | solution.py:569
  90.5 9.3 %collective-permute-start.15 = (bf16[416,256]{1,0:T(8,128)(2,1)S(1)}, bf16[416,256]{1,0:T(8,128)(2,1)S(1)}, u32[]{:S(2)}, u32[]{:S(2)}) collective-permute-start(bf16[416,256]{1,0:T(8,128)(2,1)S(1)} %bitcast.59), channel_id=1, source_target_pairs={{0,4},{1,5},{2,6},{3,7},{4,0},{5,1},{6,2},{7,3},{8,12},{9,13},{10,... | collective-permute-start | bytes 638984 | tf_op jit(solution)/shard_map/ppermute | solution.py:569
  91.3 8.5 %collective-permute-start.16 = (bf16[416,256]{1,0:T(8,128)(2,1)S(1)}, bf16[416,256]{1,0:T(8,128)(2,1)S(1)}, u32[]{:S(2)}, u32[]{:S(2)}) collective-permute-start(bf16[416,256]{1,0:T(8,128)(2,1)S(1)} %bitcast.60), channel_id=1, source_target_pairs={{0,6},{1,7},{2,4},{3,5},{4,2},{5,3},{6,0},{7,1},{8,14},{9,15},{10,... | collective-permute-start | bytes 638984 | tf_op jit(solution)/shard_map/ppermute | solution.py:569
  95.2 4.8 %collective-permute-start.21 = (bf16[104,256]{1,0:T(8,128)(2,1)S(1)}, bf16[104,256]{1,0:T(8,128)(2,1)S(1)}, u32[]{:S(2)}, u32[]{:S(2)}) collective-permute-start(bf16[104,256]{1,0:T(8,128)(2,1)S(1)} %add_convert_fusion), channel_id=1, source_target_pairs={{0,8},{1,9},{2,10},{3,11},{4,12},{5,13},{6,14},{7,15},{8,0},{9,1},... | collective-permute-start | bytes 159752 | tf_op jit(solution)/shard_map/ppermute | solution.py:569
  95.3 5.1 %collective-permute-start.22 = (bf16[104,256]{1,0:T(8,128)(2,1)S(1)}, bf16[104,256]{1,0:T(8,128)(2,1)S(1)}, u32[]{:S(2)}, u32[]{:S(2)}) collective-permute-start(bf16[104,256]{1,0:T(8,128)(2,1)S(1)} %add_convert_fusion), channel_id=1, source_target_pairs={{0,16},{1,17},{2,18},{3,19},{4,20},{5,21},{6,22},{7,23},{8,24},{9,... | collective-permute-start | bytes 159752 | tf_op jit(solution)/shard_map/ppermute | solution.py:569
  96.8 5.9 %collective-permute-start.23 = (bf16[104,256]{1,0:T(8,128)(2,1)S(1)}, bf16[104,256]{1,0:T(8,128)(2,1)S(1)}, u32[]{:S(2)}, u32[]{:S(2)}) collective-permute-start(bf16[104,256]{1,0:T(8,128)(2,1)S(1)} %add_convert_fusion), channel_id=1, source_target_pairs={{0,24},{1,25},{2,26},{3,27},{4,28},{5,29},{6,30},{7,31},{8,16},{9,... | collective-permute-start | bytes 159752 | tf_op jit(solution)/shard_map/ppermute | solution.py:569
  102.9 5.9 %collective-permute-start.24 = (bf16[416,256]{1,0:T(8,128)(2,1)S(1)}, bf16[416,256]{1,0:T(8,128)(2,1)S(1)}, u32[]{:S(2)}, u32[]{:S(2)}) collective-permute-start(bf16[416,256]{1,0:T(8,128)(2,1)S(1)} %bitcast.54), channel_id=1, source_target_pairs={{0,2},{1,3},{2,0},{3,1},{4,6},{5,7},{6,4},{7,5},{8,10},{9,11},{10,... | collective-permute-start | bytes 638984 | tf_op jit(solution)/shard_map/ppermute | solution.py:569
  104.1 8.1 %collective-permute-start.25 = (bf16[416,256]{1,0:T(8,128)(2,1)S(1)}, bf16[416,256]{1,0:T(8,128)(2,1)S(1)}, u32[]{:S(2)}, u32[]{:S(2)}) collective-permute-start(bf16[416,256]{1,0:T(8,128)(2,1)S(1)} %bitcast.55), channel_id=1, source_target_pairs={{0,4},{1,5},{2,6},{3,7},{4,0},{5,1},{6,2},{7,3},{8,12},{9,13},{10,... | collective-permute-start | bytes 638984 | tf_op jit(solution)/shard_map/ppermute | solution.py:569
  105.0 7.3 %collective-permute-start.26 = (bf16[416,256]{1,0:T(8,128)(2,1)S(1)}, bf16[416,256]{1,0:T(8,128)(2,1)S(1)}, u32[]{:S(2)}, u32[]{:S(2)}) collective-permute-start(bf16[416,256]{1,0:T(8,128)(2,1)S(1)} %bitcast.56), channel_id=1, source_target_pairs={{0,6},{1,7},{2,4},{3,5},{4,2},{5,3},{6,0},{7,1},{8,14},{9,15},{10,... | collective-permute-start | bytes 638984 | tf_op jit(solution)/shard_map/ppermute | solution.py:569
  106.4 6.7 %collective-permute-start.20 = (bf16[1664,256]{1,0:T(8,128)(2,1)S(1)}, bf16[1664,256]{1,0:T(8,128)(2,1)S(1)}, u32[]{:S(2)}, u32[]{:S(2)}) collective-permute-start(bf16[1664,256]{1,0:T(8,128)(2,1)S(1)} %bitcast.52), channel_id=1, source_target_pairs={{0,1},{1,0},{2,3},{3,2},{4,5},{5,4},{6,7},{7,6},{8,9},{9,8},{10,11... | collective-permute-start | bytes 2555912 | tf_op jit(solution)/shard_map/ppermute | solution.py:569
  112.4 2.4 %collective-permute-start.27 = (bf16[1664,256]{1,0:T(8,128)(2,1)S(1)}, bf16[1664,256]{1,0:T(8,128)(2,1)S(1)}, u32[]{:S(2)}, u32[]{:S(2)}) collective-permute-start(bf16[1664,256]{1,0:T(8,128)(2,1)S(1)} %bitcast.50), channel_id=1, source_target_pairs={{0,1},{1,0},{2,3},{3,2},{4,5},{5,4},{6,7},{7,6},{8,9},{9,8},{10,11... | collective-permute-start | bytes 2555912 | tf_op jit(solution)/shard_map/ppermute | solution.py:569

commit v6 on v5

--- a/solution.py
+++ b/solution.py
@@ -16,7 +16,6 @@
 VECTOR_ROWS = 16
 HALF = 6 * WIDTH + 128
 GROUP_ROWS = 2 * HALF
-ORDERED = True
 SOFT = 128
 NORM = 64
 GELU = 32
@@ -108,27 +107,29 @@
 
 
 def first_rows(which, seqs, length, len_ref, x_ref, k_ref, v_ref, wqkv_ref, qb_ref, vb_ref, wo_ref, ob_ref, g1_ref, b1_ref, w1_ref, hb_ref, w2_ref, fb_ref, g2_ref, b2_ref):
-    weights = wqkv_ref[which]
+    rows = seqs * length
+    firsts = [x_ref[s * length : s * length + 16, :].astype(f32)[:1] for s in range(seqs)]
+    filler = jnp.zeros((PAD - seqs, WIDTH), f32)
+    inputs = jnp.concatenate(firsts + [filler], axis=0)
+    queries = (dot(inputs.astype(bf16), wqkv_ref[:, :WIDTH]) + vector(qb_ref, which)).astype(bf16).astype(f32)
     x = x_ref[...]
-    k_ref[...] = dot(x, weights[:, WIDTH : 2 * WIDTH]).astype(bf16)
-    v_ref[...] = (dot(x, weights[:, 2 * WIDTH :]) + vector(vb_ref, which)).astype(bf16)
-    contexts, inputs = [], []
+    k_ref[:rows, :] = dot(x, wqkv_ref[:, WIDTH : 2 * WIDTH]).astype(bf16)
+    v_ref[:rows, :] = (dot(x, wqkv_ref[:, 2 * WIDTH :]) + vector(vb_ref, which)).astype(bf16)
+    own_lanes = lane_head(PAD) == lax.broadcasted_iota(jnp.int32, (PAD, WIDTH), 0)
+    contexts = []
     for s in range(seqs):
-        first = x_ref[s * length : s * length + 16, :]
-        query = (dot(first, weights[:, :WIDTH]) + vector(qb_ref, which)).astype(bf16)
         span = slice(s * length, (s + 1) * length)
-        prob = masked_softmax(dot_nt(stack_heads(query), k_ref[span, :]), len_ref[s])
-        contexts.append(pick_heads(dot(prob.astype(bf16), v_ref[span, :]), 16)[:1])
-        inputs.append(first.astype(f32)[:1])
-    filler = jnp.zeros((PAD - seqs, WIDTH), f32)
+        heads = jnp.where(own_lanes, queries[s : s + 1], 0.0).astype(bf16)
+        prob = masked_softmax(dot_nt(heads, k_ref[span, :]), len_ref[s])
+        context = dot(prob.astype(bf16), v_ref[span, :])
+        contexts.append(jnp.sum(jnp.where(own_lanes, context, 0.0), axis=0, keepdims=True))
     context = jnp.concatenate(contexts + [filler], axis=0).astype(bf16)
-    value = jnp.concatenate(inputs + [filler], axis=0)
-    value = value + (dot(context, wo_ref[which]) + vector(ob_ref, which))
+    value = inputs + (dot(context, wo_ref[...]) + vector(ob_ref, which))
     unit, _ = normalize(value)
     normed = unit * vector(g1_ref, which) + vector(b1_ref, which)
-    hidden = dot(normed.astype(bf16), w1_ref[which]) + vector(hb_ref, which)
+    hidden = dot(normed.astype(bf16), w1_ref[...]) + vector(hb_ref, which)
     active, _ = gelu_parts(hidden)
-    value = normed + (dot(active, w2_ref[which]) + vector(fb_ref, which))
+    value = normed + (dot(active, w2_ref[...]) + vector(fb_ref, which))
     unit, _ = normalize(value)
     result = unit * vector(g2_ref, which) + vector(b2_ref, which)
     row = lax.broadcasted_iota(jnp.int32, result.shape, 0)
@@ -136,20 +137,22 @@
 
 
 def first_kernel(seqs, lq_ref, lp_ref, xq_ref, xp_ref, *refs):
-    weights, (cls_ref, kq_ref, vq_ref, kp_ref, vp_ref) = refs[:13], refs[13:]
-    count = cls_ref.shape[0]
-    question = first_rows(0, seqs, xq_ref.shape[0] // seqs, lq_ref, xq_ref, kq_ref, vq_ref, *weights)
-    passage = first_rows(1, seqs, xp_ref.shape[0] // seqs, lp_ref, xp_ref, kp_ref, vp_ref, *weights)
-    both = jnp.concatenate([question, passage], axis=0).astype(bf16)
-    for i in range(count) if count <= 32 else ():
-        cls_ref[i] = both
-    if count > 32:
+    weights, (cls_ref, k_ref, v_ref, passage_ref) = refs[:13], refs[13:]
+
+    @pl.when(pl.program_id(0) == 0)
+    def _():
+        passage_ref[...] = first_rows(1, seqs, xp_ref.shape[0] // seqs, lp_ref, xp_ref, k_ref, v_ref, *weights)
+
+    @pl.when(pl.program_id(0) == 1)
+    def _():
+        question = first_rows(0, seqs, xq_ref.shape[0] // seqs, lq_ref, xq_ref, k_ref, v_ref, *weights)
+        both = jnp.concatenate([question, passage_ref[...]], axis=0).astype(bf16)
 
         def store(i, carry):
             cls_ref[i] = both
             return carry
 
-        lax.fori_loop(0, count, store, 0)
+        lax.fori_loop(0, cls_ref.shape[0], store, 0)
 
 
 def attend_kernel(which, seqs, length, len_ref, x_ref, wqkv_ref, qb_ref, vb_ref, qkv_ref, p_ref, ctx_ref, score_ref, prob_ref):
@@ -497,6 +500,26 @@
 
 def in_hbm(values):
     return pltpu.with_memory_space_constraint(values, pltpu.HBM)
+
+
+def first_call(count, local, len_questions, len_passages, x_q, x_p, weights):
+    def matrix(rows, columns):
+        return pl.BlockSpec((None, rows, columns), lambda i: (1 - i, 0, 0))
+
+    specs = [
+        matrix(WIDTH, 3 * WIDTH), pair(WIDTH), pair(WIDTH), matrix(WIDTH, WIDTH), pair(WIDTH), pair(WIDTH), pair(WIDTH),
+        matrix(WIDTH, HIDDEN), pair(HIDDEN), matrix(HIDDEN, WIDTH), pair(WIDTH), pair(WIDTH), pair(WIDTH),
+    ]
+    return pl.pallas_call(
+        functools.partial(first_kernel, local),
+        out_shape=shape((count, 2 * PAD, WIDTH), bf16),
+        grid=(2,),
+        in_specs=[smem(), smem(), whole(x_q.shape), whole(x_p.shape)] + specs,
+        out_specs=whole((count, 2 * PAD, WIDTH)),
+        scratch_shapes=[pltpu.VMEM(x_p.shape, bf16), pltpu.VMEM(x_p.shape, bf16), pltpu.VMEM((PAD, WIDTH), f32)],
+        compiler_params=params(),
+        name="first",
+    )(in_hbm(len_questions), in_hbm(len_passages), in_hbm(x_q), in_hbm(x_p), *[in_hbm(member) for member in weights])
 
 
 def attend(which, steps, seqs, length, lengths, x, weights):
@@ -649,16 +672,7 @@
     bit = (me % 2).reshape(1)
     x_q = questions.reshape(-1, WIDTH)
     x_p = passages.reshape(-1, WIDTH)
-    own_cls = pl.pallas_call(
-        functools.partial(first_kernel, local),
-        out_shape=shape((count, 2 * PAD, WIDTH), bf16),
-        grid=(1,),
-        in_specs=[smem(), smem(), whole(x_q.shape), whole(x_p.shape)] + [whole(member.shape) for member in weights],
-        out_specs=whole((count, 2 * PAD, WIDTH)),
-        scratch_shapes=[pltpu.VMEM(x_q.shape, bf16)] * 2 + [pltpu.VMEM(x_p.shape, bf16)] * 2,
-        compiler_params=params(),
-        name="first",
-    )(len_questions, len_passages, in_hbm(x_q), in_hbm(x_p), *[in_hbm(member) for member in weights])
+    own_cls = first_call(count, local, len_questions, len_passages, x_q, x_p, weights)
     own_cls, x_q, x_p = lax.optimization_barrier((own_cls, x_q, x_p))
     all_cls = lax.all_to_all(own_cls, "dp", 0, 0, tiled=True)
     attended_p = attend(1, local, 1, passage_length, len_passages, x_p, weights)

time: 119 us -> 116 us (0.975)
  local copies, waits for them, and re-layouts: 2.64 us -> 1.34 us
    unnamed x10 -> x6, local copies, waits for them, and re-layouts: 1.31 us -> 0.01 us
  transfers between devices with their start and end apart: 29 -> 29, of which waited for: 10 -> 10; matrix products, arithmetic and copies ran while one was open for 1% -> 1% of each run, Pallas kernels for 28% -> 29%
where the time goes in v6:
time: 116 us
  Pallas kernels  53.7 us (46%)
  starting transfers between devices  41.5 us (36%)
  waiting for transfers between devices  18 us (16%)
  local copies, waits for them, and re-layouts  1.34 us (1%)
  between operations  1.18 us (1%)
    ppermute x28, starting transfers between devices, partner_send(): return lax.ppermute(values, 'dp', [(i, i ^ mask) for i in range(count)])  34.2 us
    pallas_call x2, Pallas kernels, layer(): pl.pallas_call(functools.partial(layer_kernel, which, steps, seqs, length...  30.9 us
    ppermute x28, waiting for transfers between devices, partner_send(): return lax.ppermute(values, 'dp', [(i, i ^ mask) for i in range(count)])  18 us
    pallas_call x2, Pallas kernels, attend(): pl.pallas_call(functools.partial(attend_kernel, which, seqs, length), out...  10.2 us
    pallas_call x1, Pallas kernels, first_call(): pl.pallas_call(functools.partial(first_kernel, local), out_shape=shape((c...  7.51 us
    all_to_all x1, starting transfers between devices, body(): all_cls = lax.all_to_all(own_cls, 'dp', 0, 0, tiled=True)  7.3 us
    pallas_call x1, Pallas kernels, body(): pl.pallas_call(unpack_kernel, out_shape=[shape(d, f32) for d in dims], gr...  3.18 us
  transfers between devices with their start and end apart: 29, of which 10 were waited for; matrix products, arithmetic and copies ran while one was open for 1% of the time, Pallas kernels for 29%

profile of v6, /device:TPU:0, one launch (start us, length us, event | category | flops | bytes accessed | tf_op | source)
XLA Modules:
  0.0 115.9 jit_solution(6894915380467031176)
XLA Ops:
  0.7 7.5 %first.1 = bf16[32,16,256]{2,1,0:T(8,128)(2,1)} custom-call(s32[5]{0:T(128)} %len_ref.6, s32[5]{0:T(128)} %len_ref.7, bf16[320,256]{1,0:T(8,128)(2,1)} %bitcast.62, bf16[1280,256]{1,0:T(8,128)(2,1)} %bitcast.65, bf16[2,256,768]{2,1,0:T(8,128)(2,1)} %wqkv_ref.7, bf16[2,256]{1,0:T(2,128)(2,1)} %qb_ref.3, bf16[2,256]{1,0:T(2,128)(2,1)} %vb_ref.3, ...), custom_call_target="tpu_custom_call" | custom-call | tf_op jit(solution)/shard_map/first/pallas_call | solution.py:513
  8.2 7.3 %all-to-all-start = ((bf16[32,16,256]{2,1,0:T(8,128)(2,1)}), bf16[32,16,256]{2,1,0:T(8,128)(2,1)S(1)}, u32[]{:S(2)}, u32[]{:S(2)}) async-start(bf16[32,16,256]{2,1,0:T(8,128)(2,1)} %first.1), calls=%async_computation | async-start | bytes 524288 | tf_op jit(solution)/shard_map/all_to_all | solution.py:677
  15.5 0.1 reshape.98
  15.7 0.1 reshape.99.hot_ref
  15.8 3.3 %attend.3 = (bf16[320,768]{1,0:T(8,128)(2,1)}, f32[1280,64]{1,0:T(8,128)}, bf16[320,256]{1,0:T(8,128)(2,1)}) custom-call(s32[5]{0:T(128)S(1)} %copy-done, bf16[320,256]{1,0:T(8,128)(2,1)} %bitcast.63, bf16[2,256,768]{2,1,0:T(8,128)(2,1)} %wqkv_ref.7, bf16[2,256]{1,0:T(2,128)(2,1)} %qb_ref.3, bf16[2,256]{1,0:T(2,128)(2,1)} %vb_ref.3), custom_call_target="tpu_custom_call" | custom-call | flops 256000000 | bytes 1920000 | tf_op jit(solution)/shard_map/attend/pallas_call | solution.py:530
  19.1 7.0 %attend.2 = (bf16[1280,768]{1,0:T(8,128)(2,1)}, f32[5120,256]{1,0:T(8,128)}, bf16[1280,256]{1,0:T(8,128)(2,1)}) custom-call(s32[5]{0:T(128)S(1)} %copy-done.1, bf16[1280,256]{1,0:T(8,128)(2,1)} %bitcast.66, bf16[2,256,768]{2,1,0:T(8,128)(2,1)} %wqkv_ref.7, bf16[2,256]{1,0:T(2,128)(2,1)} %qb_ref.3, bf16[2,256]{1,0:T(2,128)(2,1)} %vb_ref.3), custom_call_target="tpu_custom_call" | custom-call | flops 1024000000 | bytes 7680000 | tf_op jit(solution)/shard_map/attend/pallas_call | solution.py:530
  26.1 0.8 loss.1
  26.9 8.3 %layer.2 = (bf16[320,256]{1,0:T(8,128)(2,1)}, bf16[320,256]{1,0:T(8,128)(2,1)}, bf16[1664,256]{1,0:T(8,128)(2,1)S(1)}, bf16[1664,256]{1,0:T(8,128)(2,1)S(1)}) custom-call(s32[1]{0:T(128)} %bitcast.4.bit_ref, s32[5]{0:T(128)S(1)} %copy-done, f32[8,256]{1,0:T(8,128)S(1)} %get-tuple-element.111.cls_ref, bf16[320,256]{1,0:T(8,128)(2,1)} %bitcast.64, ...), custom_call_target="tpu_custom_call" | custom-call | flops 1536000000 | bytes 1280000 | tf_op jit(solution)/shard_map/layer/pallas_call | solution.py:550
  35.2 0.3 collective-permute-start
  35.4 2.1 %collective-permute-done.refs_1_ = bf16[1664,256]{1,0:T(8,128)(2,1)S(1)} collective-permute-done((bf16[1664,256]{1,0:T(8,128)(2,1)S(1)}, bf16[1664,256]{1,0:T(8,128)(2,1)S(1)}, u32[]{:S(2)}, u32[]{:S(2)}) %collective-permute-start) | collective-permute-done | bytes 852000 | tf_op jit(solution)/shard_map/ppermute | solution.py:592
  37.6 0.4 combine.4
  37.9 1.9 %collective-permute-start.1 = (bf16[416,256]{1,0:T(8,128)(2,1)S(1)}, bf16[416,256]{1,0:T(8,128)(2,1)S(1)}, u32[]{:S(2)}, u32[]{:S(2)}) collective-permute-start(bf16[416,256]{1,0:T(8,128)(2,1)S(1)} %get-tuple-element.119), channel_id=1, source_target_pairs={{0,2},{1,3},{2,0},{3,1},{4,6},{5,7},{6,4},{7,5},{8,10},{9,11},{10,... | collective-permute-start | bytes 638984 | tf_op jit(solution)/shard_map/ppermute | solution.py:592
  39.8 1.4 %collective-permute-start.2 = (bf16[416,256]{1,0:T(8,128)(2,1)S(1)}, bf16[416,256]{1,0:T(8,128)(2,1)S(1)}, u32[]{:S(2)}, u32[]{:S(2)}) collective-permute-start(bf16[416,256]{1,0:T(8,128)(2,1)S(1)} %get-tuple-element.120), channel_id=1, source_target_pairs={{0,4},{1,5},{2,6},{3,7},{4,0},{5,1},{6,2},{7,3},{8,12},{9,13},{10,... | collective-permute-start | bytes 638984 | tf_op jit(solution)/shard_map/ppermute | solution.py:592
  41.2 0.3 collective-permute-start.3
  41.5 22.6 %layer.3 = (bf16[1280,256]{1,0:T(8,128)(2,1)}, bf16[1280,256]{1,0:T(8,128)(2,1)}, bf16[1664,256]{1,0:T(8,128)(2,1)S(1)}, bf16[1664,256]{1,0:T(8,128)(2,1)S(1)}) custom-call(s32[1]{0:T(128)} %bitcast.4.bit_ref, s32[5]{0:T(128)S(1)} %copy-done.1, f32[8,256]{1,0:T(8,128)S(1)} %get-tuple-element.122.cls_ref, bf16[1280,256]{1,0:T(8,128)(2,1)} %bitcast.67, ...), custom_call_target="tpu_custom_call" | custom-call | flops 6144000000 | bytes 5120000 | tf_op jit(solution)/shard_map/layer/pallas_call | solution.py:550
  64.2 0.2 combine.5
  64.4 1.8 %collective-permute-start.4 = (bf16[104,256]{1,0:T(8,128)(2,1)S(1)}, bf16[104,256]{1,0:T(8,128)(2,1)S(1)}, u32[]{:S(2)}, u32[]{:S(2)}) collective-permute-start(bf16[104,256]{1,0:T(8,128)(2,1)S(1)} %get-tuple-element.129), channel_id=1, source_target_pairs={{0,8},{1,9},{2,10},{3,11},{4,12},{5,13},{6,14},{7,15},{8,0},{9,1},... | collective-permute-start | bytes 159752 | tf_op jit(solution)/shard_map/ppermute | solution.py:592
  66.3 2.4 %collective-permute-start.5 = (bf16[104,256]{1,0:T(8,128)(2,1)S(1)}, bf16[104,256]{1,0:T(8,128)(2,1)S(1)}, u32[]{:S(2)}, u32[]{:S(2)}) collective-permute-start(bf16[104,256]{1,0:T(8,128)(2,1)S(1)} %get-tuple-element.130), channel_id=1, source_target_pairs={{0,16},{1,17},{2,18},{3,19},{4,20},{5,21},{6,22},{7,23},{8,24},{9,... | collective-permute-start | bytes 159752 | tf_op jit(solution)/shard_map/ppermute | solution.py:592
  68.7 0.2 collective-permute-start.6
  68.9 0.4 combine.6
  69.2 1.9 %collective-permute-start.11 = (bf16[416,256]{1,0:T(8,128)(2,1)S(1)}, bf16[416,256]{1,0:T(8,128)(2,1)S(1)}, u32[]{:S(2)}, u32[]{:S(2)}) collective-permute-start(bf16[416,256]{1,0:T(8,128)(2,1)S(1)} %get-tuple-element.138), channel_id=1, source_target_pairs={{0,2},{1,3},{2,0},{3,1},{4,6},{5,7},{6,4},{7,5},{8,10},{9,11},{10,... | collective-permute-start | bytes 638984 | tf_op jit(solution)/shard_map/ppermute | solution.py:592
  71.1 1.4 %collective-permute-start.12 = (bf16[416,256]{1,0:T(8,128)(2,1)S(1)}, bf16[416,256]{1,0:T(8,128)(2,1)S(1)}, u32[]{:S(2)}, u32[]{:S(2)}) collective-permute-start(bf16[416,256]{1,0:T(8,128)(2,1)S(1)} %get-tuple-element.139), channel_id=1, source_target_pairs={{0,4},{1,5},{2,6},{3,7},{4,0},{5,1},{6,2},{7,3},{8,12},{9,13},{10,... | collective-permute-start | bytes 638984 | tf_op jit(solution)/shard_map/ppermute | solution.py:592
  72.6 0.3 collective-permute-start.13
  72.8 1.8 %collective-permute-done.6 = bf16[104,256]{1,0:T(8,128)(2,1)S(1)} collective-permute-done((bf16[104,256]{1,0:T(8,128)(2,1)S(1)}, bf16[104,256]{1,0:T(8,128)(2,1)S(1)}, u32[]{:S(2)}, u32[]{:S(2)}) %collective-permute-start.6) | collective-permute-done | bytes 53280 | tf_op jit(solution)/shard_map/ppermute | solution.py:592
  74.7 2.4 %collective-permute-start.9 = (bf16[104,256]{1,0:T(8,128)(2,1)S(1)}, bf16[104,256]{1,0:T(8,128)(2,1)S(1)}, u32[]{:S(2)}, u32[]{:S(2)}) collective-permute-start(bf16[104,256]{1,0:T(8,128)(2,1)S(1)} %add_convert_fusion.1), channel_id=1, source_target_pairs={{0,16},{1,17},{2,18},{3,19},{4,20},{5,21},{6,22},{7,23},{8,24},{9,... | collective-permute-start | bytes 159752 | tf_op jit(solution)/shard_map/ppermute | solution.py:592
  77.1 0.4 collective-permute-done.11.refs_1_
  77.5 3.6 %collective-permute-start.10 = (bf16[104,256]{1,0:T(8,128)(2,1)S(1)}, bf16[104,256]{1,0:T(8,128)(2,1)S(1)}, u32[]{:S(2)}, u32[]{:S(2)}) collective-permute-start(bf16[104,256]{1,0:T(8,128)(2,1)S(1)} %add_convert_fusion.1), channel_id=1, source_target_pairs={{0,24},{1,25},{2,26},{3,27},{4,28},{5,29},{6,30},{7,31},{8,16},{9,... | collective-permute-start | bytes 159752 | tf_op jit(solution)/shard_map/ppermute | solution.py:592
  81.1 1.1 collective-permute-done.12.refs_2_
  82.2 0.2 combine.7
  82.4 0.6 collective-permute-start.17
  83.0 3.4 %collective-permute-start.18 = (bf16[104,256]{1,0:T(8,128)(2,1)S(1)}, bf16[104,256]{1,0:T(8,128)(2,1)S(1)}, u32[]{:S(2)}, u32[]{:S(2)}) collective-permute-start(bf16[104,256]{1,0:T(8,128)(2,1)S(1)} %get-tuple-element.151), channel_id=1, source_target_pairs={{0,16},{1,17},{2,18},{3,19},{4,20},{5,21},{6,22},{7,23},{8,24},{9,... | collective-permute-start | bytes 159752 | tf_op jit(solution)/shard_map/ppermute | solution.py:592
  86.3 0.5 collective-permute-start.19
  86.9 1.2 %collective-permute-start.14 = (bf16[416,256]{1,0:T(8,128)(2,1)S(1)}, bf16[416,256]{1,0:T(8,128)(2,1)S(1)}, u32[]{:S(2)}, u32[]{:S(2)}) collective-permute-start(bf16[416,256]{1,0:T(8,128)(2,1)S(1)} %bitcast.58), channel_id=1, source_target_pairs={{0,2},{1,3},{2,0},{3,1},{4,6},{5,7},{6,4},{7,5},{8,10},{9,11},{10,... | collective-permute-start | bytes 638984 | tf_op jit(solution)/shard_map/ppermute | solution.py:592
  88.1 0.8 collective-permute-start.15
  89.0 1.5 %collective-permute-start.16 = (bf16[416,256]{1,0:T(8,128)(2,1)S(1)}, bf16[416,256]{1,0:T(8,128)(2,1)S(1)}, u32[]{:S(2)}, u32[]{:S(2)}) collective-permute-start(bf16[416,256]{1,0:T(8,128)(2,1)S(1)} %bitcast.60), channel_id=1, source_target_pairs={{0,6},{1,7},{2,4},{3,5},{4,2},{5,3},{6,0},{7,1},{8,14},{9,15},{10,... | collective-permute-start | bytes 638984 | tf_op jit(solution)/shard_map/ppermute | solution.py:592
  90.5 2.3 %collective-permute-done.19 = bf16[104,256]{1,0:T(8,128)(2,1)S(1)} collective-permute-done((bf16[104,256]{1,0:T(8,128)(2,1)S(1)}, bf16[104,256]{1,0:T(8,128)(2,1)S(1)}, u32[]{:S(2)}, u32[]{:S(2)}) %collective-permute-start.19) | collective-permute-done | bytes 53280 | tf_op jit(solution)/shard_map/ppermute | solution.py:592
  92.9 1.5 %collective-permute-start.22 = (bf16[104,256]{1,0:T(8,128)(2,1)S(1)}, bf16[104,256]{1,0:T(8,128)(2,1)S(1)}, u32[]{:S(2)}, u32[]{:S(2)}) collective-permute-start(bf16[104,256]{1,0:T(8,128)(2,1)S(1)} %add_convert_fusion), channel_id=1, source_target_pairs={{0,16},{1,17},{2,18},{3,19},{4,20},{5,21},{6,22},{7,23},{8,24},{9,... | collective-permute-start | bytes 159752 | tf_op jit(solution)/shard_map/ppermute | solution.py:592
  94.5 3.0 %collective-permute-start.23 = (bf16[104,256]{1,0:T(8,128)(2,1)S(1)}, bf16[104,256]{1,0:T(8,128)(2,1)S(1)}, u32[]{:S(2)}, u32[]{:S(2)}) collective-permute-start(bf16[104,256]{1,0:T(8,128)(2,1)S(1)} %add_convert_fusion), channel_id=1, source_target_pairs={{0,24},{1,25},{2,26},{3,27},{4,28},{5,29},{6,30},{7,31},{8,16},{9,... | collective-permute-start | bytes 159752 | tf_op jit(solution)/shard_map/ppermute | solution.py:592
  97.7 0.4 collective-permute-done.22
  98.0 2.4 %collective-permute-done.23 = bf16[104,256]{1,0:T(8,128)(2,1)S(1)} collective-permute-done((bf16[104,256]{1,0:T(8,128)(2,1)S(1)}, bf16[104,256]{1,0:T(8,128)(2,1)S(1)}, u32[]{:S(2)}, u32[]{:S(2)}) %collective-permute-start.23) | collective-permute-done | bytes 53280 | tf_op jit(solution)/shard_map/ppermute | solution.py:592
  100.5 1.3 %collective-permute-start.24 = (bf16[416,256]{1,0:T(8,128)(2,1)S(1)}, bf16[416,256]{1,0:T(8,128)(2,1)S(1)}, u32[]{:S(2)}, u32[]{:S(2)}) collective-permute-start(bf16[416,256]{1,0:T(8,128)(2,1)S(1)} %bitcast.54), channel_id=1, source_target_pairs={{0,2},{1,3},{2,0},{3,1},{4,6},{5,7},{6,4},{7,5},{8,10},{9,11},{10,... | collective-permute-start | bytes 638984 | tf_op jit(solution)/shard_map/ppermute | solution.py:592
  101.8 0.8 collective-permute-start.25
  102.6 1.4 %collective-permute-start.26 = (bf16[416,256]{1,0:T(8,128)(2,1)S(1)}, bf16[416,256]{1,0:T(8,128)(2,1)S(1)}, u32[]{:S(2)}, u32[]{:S(2)}) collective-permute-start(bf16[416,256]{1,0:T(8,128)(2,1)S(1)} %bitcast.56), channel_id=1, source_target_pairs={{0,6},{1,7},{2,4},{3,5},{4,2},{5,3},{6,0},{7,1},{8,14},{9,15},{10,... | collective-permute-start | bytes 638984 | tf_op jit(solution)/shard_map/ppermute | solution.py:592
  104.1 2.4 %collective-permute-done.24 = bf16[416,256]{1,0:T(8,128)(2,1)S(1)} collective-permute-done((bf16[416,256]{1,0:T(8,128)(2,1)S(1)}, bf16[416,256]{1,0:T(8,128)(2,1)S(1)}, u32[]{:S(2)}, u32[]{:S(2)}) %collective-permute-start.24) | collective-permute-done | bytes 213024 | tf_op jit(solution)/shard_map/ppermute | solution.py:592
  106.4 3.5 %collective-permute-done.25 = bf16[416,256]{1,0:T(8,128)(2,1)S(1)} collective-permute-done((bf16[416,256]{1,0:T(8,128)(2,1)S(1)}, bf16[416,256]{1,0:T(8,128)(2,1)S(1)}, u32[]{:S(2)}, u32[]{:S(2)}) %collective-permute-start.25) | collective-permute-done | bytes 213024 | tf_op jit(solution)/shard_map/ppermute | solution.py:592
  110.2 0.6 slice_reduce_fusion
  110.8 1.7 %collective-permute-done.27.p_ref = bf16[1664,256]{1,0:T(8,128)(2,1)S(1)} collective-permute-done((bf16[1664,256]{1,0:T(8,128)(2,1)S(1)}, bf16[1664,256]{1,0:T(8,128)(2,1)S(1)}, u32[]{:S(2)}, u32[]{:S(2)}) %collective-permute-start.27) | collective-permute-done | bytes 852000 | tf_op jit(solution)/shard_map/ppermute | solution.py:592
  112.5 3.2 %unpack.1 = (f32[2,256,768]{2,1,0:T(8,128)}, f32[2,256,256]{2,1,0:T(8,128)}, f32[2,256,1024]{2,1,0:T(8,128)}, f32[2,1024,256]{2,1,0:T(8,128)}, f32[2,1024]{1,0:T...) custom-call(s32[1]{0:T(128)} %bitcast.4.bit_ref, ...), custom_call_target="tpu_custom_call" | custom-call | tf_op jit(solution)/shard_map/unpack/pallas_call | solution.py:722
  (56 shorter events, 1.0 us)
Async XLA Ops:
  0.7 14.9 %copy-start.2 = (s32[160]{0:T(256)S(1)}, s32[160]{0:T(256)}, u32[]{:S(2)}) copy-start(s32[160]{0:T(256)} %param.26) | copy-start | bytes 1924
  0.7 15.2 %copy-start = (s32[5]{0:T(128)S(1)}, s32[5]{0:T(128)}, u32[]{:S(2)}) copy-start(s32[5]{0:T(128)} %len_ref.6) | copy-start | bytes 64
  0.7 18.5 %copy-start.1 = (s32[5]{0:T(128)S(1)}, s32[5]{0:T(128)}, u32[]{:S(2)}) copy-start(s32[5]{0:T(128)} %len_ref.7) | copy-start | bytes 64
  8.2 17.9 %all-to-all-start = ((bf16[32,16,256]{2,1,0:T(8,128)(2,1)}), bf16[32,16,256]{2,1,0:T(8,128)(2,1)S(1)}, u32[]{:S(2)}, u32[]{:S(2)}) async-start(bf16[32,16,256]{2,1,0:T(8,128)(2,1)} %first.1), calls=%async_computation | async-start | bytes 524288 | tf_op jit(solution)/shard_map/all_to_all | solution.py:677
  35.2 2.4 %collective-permute-start = (bf16[1664,256]{1,0:T(8,128)(2,1)S(1)}, bf16[1664,256]{1,0:T(8,128)(2,1)S(1)}, u32[]{:S(2)}, u32[]{:S(2)}) collective-permute-start(bf16[1664,256]{1,0:T(8,128)(2,1)S(1)} %get-tuple-element.117), channel_id=1, source_target_pairs={{0,1},{1,0},{2,3},{3,2},{4,5},{5,4},{6,7},{7,6},{8,9},{9,8},{10,11... | collective-permute-start | bytes 2555912 | tf_op jit(solution)/shard_map/ppermute | solution.py:592
  37.9 26.2 %collective-permute-start.1 = (bf16[416,256]{1,0:T(8,128)(2,1)S(1)}, bf16[416,256]{1,0:T(8,128)(2,1)S(1)}, u32[]{:S(2)}, u32[]{:S(2)}) collective-permute-start(bf16[416,256]{1,0:T(8,128)(2,1)S(1)} %get-tuple-element.119), channel_id=1, source_target_pairs={{0,2},{1,3},{2,0},{3,1},{4,6},{5,7},{6,4},{7,5},{8,10},{9,11},{10,... | collective-permute-start | bytes 638984 | tf_op jit(solution)/shard_map/ppermute | solution.py:592
  39.8 24.4 %collective-permute-start.2 = (bf16[416,256]{1,0:T(8,128)(2,1)S(1)}, bf16[416,256]{1,0:T(8,128)(2,1)S(1)}, u32[]{:S(2)}, u32[]{:S(2)}) collective-permute-start(bf16[416,256]{1,0:T(8,128)(2,1)S(1)} %get-tuple-element.120), channel_id=1, source_target_pairs={{0,4},{1,5},{2,6},{3,7},{4,0},{5,1},{6,2},{7,3},{8,12},{9,13},{10,... | collective-permute-start | bytes 638984 | tf_op jit(solution)/shard_map/ppermute | solution.py:592
  41.2 22.9 %collective-permute-start.3 = (bf16[416,256]{1,0:T(8,128)(2,1)S(1)}, bf16[416,256]{1,0:T(8,128)(2,1)S(1)}, u32[]{:S(2)}, u32[]{:S(2)}) collective-permute-start(bf16[416,256]{1,0:T(8,128)(2,1)S(1)} %get-tuple-element.121), channel_id=1, source_target_pairs={{0,6},{1,7},{2,4},{3,5},{4,2},{5,3},{6,0},{7,1},{8,14},{9,15},{10,... | collective-permute-start | bytes 638984 | tf_op jit(solution)/shard_map/ppermute | solution.py:592
  64.1 4.7 %collective-permute-start.7 = (bf16[1664,256]{1,0:T(8,128)(2,1)S(1)}, bf16[1664,256]{1,0:T(8,128)(2,1)S(1)}, u32[]{:S(2)}, u32[]{:S(2)}) collective-permute-start(bf16[1664,256]{1,0:T(8,128)(2,1)S(1)} %get-tuple-element.134), channel_id=1, source_target_pairs={{0,1},{1,0},{2,3},{3,2},{4,5},{5,4},{6,7},{7,6},{8,9},{9,8},{10,11... | collective-permute-start | bytes 2555912 | tf_op jit(solution)/shard_map/ppermute | solution.py:592
  64.4 8.1 %collective-permute-start.4 = (bf16[104,256]{1,0:T(8,128)(2,1)S(1)}, bf16[104,256]{1,0:T(8,128)(2,1)S(1)}, u32[]{:S(2)}, u32[]{:S(2)}) collective-permute-start(bf16[104,256]{1,0:T(8,128)(2,1)S(1)} %get-tuple-element.129), channel_id=1, source_target_pairs={{0,8},{1,9},{2,10},{3,11},{4,12},{5,13},{6,14},{7,15},{8,0},{9,1},... | collective-permute-start | bytes 159752 | tf_op jit(solution)/shard_map/ppermute | solution.py:592
  66.3 6.5 %collective-permute-start.5 = (bf16[104,256]{1,0:T(8,128)(2,1)S(1)}, bf16[104,256]{1,0:T(8,128)(2,1)S(1)}, u32[]{:S(2)}, u32[]{:S(2)}) collective-permute-start(bf16[104,256]{1,0:T(8,128)(2,1)S(1)} %get-tuple-element.130), channel_id=1, source_target_pairs={{0,16},{1,17},{2,18},{3,19},{4,20},{5,21},{6,22},{7,23},{8,24},{9,... | collective-permute-start | bytes 159752 | tf_op jit(solution)/shard_map/ppermute | solution.py:592
  68.7 5.9 %collective-permute-start.6 = (bf16[104,256]{1,0:T(8,128)(2,1)S(1)}, bf16[104,256]{1,0:T(8,128)(2,1)S(1)}, u32[]{:S(2)}, u32[]{:S(2)}) collective-permute-start(bf16[104,256]{1,0:T(8,128)(2,1)S(1)} %get-tuple-element.131), channel_id=1, source_target_pairs={{0,24},{1,25},{2,26},{3,27},{4,28},{5,29},{6,30},{7,31},{8,16},{9,... | collective-permute-start | bytes 159752 | tf_op jit(solution)/shard_map/ppermute | solution.py:592
  69.2 8.2 %collective-permute-start.11 = (bf16[416,256]{1,0:T(8,128)(2,1)S(1)}, bf16[416,256]{1,0:T(8,128)(2,1)S(1)}, u32[]{:S(2)}, u32[]{:S(2)}) collective-permute-start(bf16[416,256]{1,0:T(8,128)(2,1)S(1)} %get-tuple-element.138), channel_id=1, source_target_pairs={{0,2},{1,3},{2,0},{3,1},{4,6},{5,7},{6,4},{7,5},{8,10},{9,11},{10,... | collective-permute-start | bytes 638984 | tf_op jit(solution)/shard_map/ppermute | solution.py:592
  71.1 11.1 %collective-permute-start.12 = (bf16[416,256]{1,0:T(8,128)(2,1)S(1)}, bf16[416,256]{1,0:T(8,128)(2,1)S(1)}, u32[]{:S(2)}, u32[]{:S(2)}) collective-permute-start(bf16[416,256]{1,0:T(8,128)(2,1)S(1)} %get-tuple-element.139), channel_id=1, source_target_pairs={{0,4},{1,5},{2,6},{3,7},{4,0},{5,1},{6,2},{7,3},{8,12},{9,13},{10,... | collective-permute-start | bytes 638984 | tf_op jit(solution)/shard_map/ppermute | solution.py:592
  72.6 9.6 %collective-permute-start.13 = (bf16[416,256]{1,0:T(8,128)(2,1)S(1)}, bf16[416,256]{1,0:T(8,128)(2,1)S(1)}, u32[]{:S(2)}, u32[]{:S(2)}) collective-permute-start(bf16[416,256]{1,0:T(8,128)(2,1)S(1)} %get-tuple-element.140), channel_id=1, source_target_pairs={{0,6},{1,7},{2,4},{3,5},{4,2},{5,3},{6,0},{7,1},{8,14},{9,15},{10,... | collective-permute-start | bytes 638984 | tf_op jit(solution)/shard_map/ppermute | solution.py:592
  74.7 11.7 %collective-permute-start.8 = (bf16[104,256]{1,0:T(8,128)(2,1)S(1)}, bf16[104,256]{1,0:T(8,128)(2,1)S(1)}, u32[]{:S(2)}, u32[]{:S(2)}) collective-permute-start(bf16[104,256]{1,0:T(8,128)(2,1)S(1)} %add_convert_fusion.1), channel_id=1, source_target_pairs={{0,8},{1,9},{2,10},{3,11},{4,12},{5,13},{6,14},{7,15},{8,0},{9,1},... | collective-permute-start | bytes 159752 | tf_op jit(solution)/shard_map/ppermute | solution.py:592
  74.7 12.1 %collective-permute-start.9 = (bf16[104,256]{1,0:T(8,128)(2,1)S(1)}, bf16[104,256]{1,0:T(8,128)(2,1)S(1)}, u32[]{:S(2)}, u32[]{:S(2)}) collective-permute-start(bf16[104,256]{1,0:T(8,128)(2,1)S(1)} %add_convert_fusion.1), channel_id=1, source_target_pairs={{0,16},{1,17},{2,18},{3,19},{4,20},{5,21},{6,22},{7,23},{8,24},{9,... | collective-permute-start | bytes 159752 | tf_op jit(solution)/shard_map/ppermute | solution.py:592
  77.5 9.3 %collective-permute-start.10 = (bf16[104,256]{1,0:T(8,128)(2,1)S(1)}, bf16[104,256]{1,0:T(8,128)(2,1)S(1)}, u32[]{:S(2)}, u32[]{:S(2)}) collective-permute-start(bf16[104,256]{1,0:T(8,128)(2,1)S(1)} %add_convert_fusion.1), channel_id=1, source_target_pairs={{0,24},{1,25},{2,26},{3,27},{4,28},{5,29},{6,30},{7,31},{8,16},{9,... | collective-permute-start | bytes 159752 | tf_op jit(solution)/shard_map/ppermute | solution.py:592
  82.4 6.6 %collective-permute-start.17 = (bf16[104,256]{1,0:T(8,128)(2,1)S(1)}, bf16[104,256]{1,0:T(8,128)(2,1)S(1)}, u32[]{:S(2)}, u32[]{:S(2)}) collective-permute-start(bf16[104,256]{1,0:T(8,128)(2,1)S(1)} %get-tuple-element.150), channel_id=1, source_target_pairs={{0,8},{1,9},{2,10},{3,11},{4,12},{5,13},{6,14},{7,15},{8,0},{9,1},... | collective-permute-start | bytes 159752 | tf_op jit(solution)/shard_map/ppermute | solution.py:592
  83.0 7.5 %collective-permute-start.18 = (bf16[104,256]{1,0:T(8,128)(2,1)S(1)}, bf16[104,256]{1,0:T(8,128)(2,1)S(1)}, u32[]{:S(2)}, u32[]{:S(2)}) collective-permute-start(bf16[104,256]{1,0:T(8,128)(2,1)S(1)} %get-tuple-element.151), channel_id=1, source_target_pairs={{0,16},{1,17},{2,18},{3,19},{4,20},{5,21},{6,22},{7,23},{8,24},{9,... | collective-permute-start | bytes 159752 | tf_op jit(solution)/shard_map/ppermute | solution.py:592
  86.3 6.5 %collective-permute-start.19 = (bf16[104,256]{1,0:T(8,128)(2,1)S(1)}, bf16[104,256]{1,0:T(8,128)(2,1)S(1)}, u32[]{:S(2)}, u32[]{:S(2)}) collective-permute-start(bf16[104,256]{1,0:T(8,128)(2,1)S(1)} %get-tuple-element.152), channel_id=1, source_target_pairs={{0,24},{1,25},{2,26},{3,27},{4,28},{5,29},{6,30},{7,31},{8,16},{9,... | collective-permute-start | bytes 159752 | tf_op jit(solution)/shard_map/ppermute | solution.py:592
  86.9 7.6 %collective-permute-start.14 = (bf16[416,256]{1,0:T(8,128)(2,1)S(1)}, bf16[416,256]{1,0:T(8,128)(2,1)S(1)}, u32[]{:S(2)}, u32[]{:S(2)}) collective-permute-start(bf16[416,256]{1,0:T(8,128)(2,1)S(1)} %bitcast.58), channel_id=1, source_target_pairs={{0,2},{1,3},{2,0},{3,1},{4,6},{5,7},{6,4},{7,5},{8,10},{9,11},{10,... | collective-permute-start | bytes 638984 | tf_op jit(solution)/shard_map/ppermute | solution.py:592
  88.1 9.3 %collective-permute-start.15 = (bf16[416,256]{1,0:T(8,128)(2,1)S(1)}, bf16[416,256]{1,0:T(8,128)(2,1)S(1)}, u32[]{:S(2)}, u32[]{:S(2)}) collective-permute-start(bf16[416,256]{1,0:T(8,128)(2,1)S(1)} %bitcast.59), channel_id=1, source_target_pairs={{0,4},{1,5},{2,6},{3,7},{4,0},{5,1},{6,2},{7,3},{8,12},{9,13},{10,... | collective-permute-start | bytes 638984 | tf_op jit(solution)/shard_map/ppermute | solution.py:592
  89.0 8.5 %collective-permute-start.16 = (bf16[416,256]{1,0:T(8,128)(2,1)S(1)}, bf16[416,256]{1,0:T(8,128)(2,1)S(1)}, u32[]{:S(2)}, u32[]{:S(2)}) collective-permute-start(bf16[416,256]{1,0:T(8,128)(2,1)S(1)} %bitcast.60), channel_id=1, source_target_pairs={{0,6},{1,7},{2,4},{3,5},{4,2},{5,3},{6,0},{7,1},{8,14},{9,15},{10,... | collective-permute-start | bytes 638984 | tf_op jit(solution)/shard_map/ppermute | solution.py:592
  92.9 4.8 %collective-permute-start.21 = (bf16[104,256]{1,0:T(8,128)(2,1)S(1)}, bf16[104,256]{1,0:T(8,128)(2,1)S(1)}, u32[]{:S(2)}, u32[]{:S(2)}) collective-permute-start(bf16[104,256]{1,0:T(8,128)(2,1)S(1)} %add_convert_fusion), channel_id=1, source_target_pairs={{0,8},{1,9},{2,10},{3,11},{4,12},{5,13},{6,14},{7,15},{8,0},{9,1},... | collective-permute-start | bytes 159752 | tf_op jit(solution)/shard_map/ppermute | solution.py:592
  92.9 5.1 %collective-permute-start.22 = (bf16[104,256]{1,0:T(8,128)(2,1)S(1)}, bf16[104,256]{1,0:T(8,128)(2,1)S(1)}, u32[]{:S(2)}, u32[]{:S(2)}) collective-permute-start(bf16[104,256]{1,0:T(8,128)(2,1)S(1)} %add_convert_fusion), channel_id=1, source_target_pairs={{0,16},{1,17},{2,18},{3,19},{4,20},{5,21},{6,22},{7,23},{8,24},{9,... | collective-permute-start | bytes 159752 | tf_op jit(solution)/shard_map/ppermute | solution.py:592
  94.5 5.9 %collective-permute-start.23 = (bf16[104,256]{1,0:T(8,128)(2,1)S(1)}, bf16[104,256]{1,0:T(8,128)(2,1)S(1)}, u32[]{:S(2)}, u32[]{:S(2)}) collective-permute-start(bf16[104,256]{1,0:T(8,128)(2,1)S(1)} %add_convert_fusion), channel_id=1, source_target_pairs={{0,24},{1,25},{2,26},{3,27},{4,28},{5,29},{6,30},{7,31},{8,16},{9,... | collective-permute-start | bytes 159752 | tf_op jit(solution)/shard_map/ppermute | solution.py:592
  100.5 5.9 %collective-permute-start.24 = (bf16[416,256]{1,0:T(8,128)(2,1)S(1)}, bf16[416,256]{1,0:T(8,128)(2,1)S(1)}, u32[]{:S(2)}, u32[]{:S(2)}) collective-permute-start(bf16[416,256]{1,0:T(8,128)(2,1)S(1)} %bitcast.54), channel_id=1, source_target_pairs={{0,2},{1,3},{2,0},{3,1},{4,6},{5,7},{6,4},{7,5},{8,10},{9,11},{10,... | collective-permute-start | bytes 638984 | tf_op jit(solution)/shard_map/ppermute | solution.py:592
  101.8 8.1 %collective-permute-start.25 = (bf16[416,256]{1,0:T(8,128)(2,1)S(1)}, bf16[416,256]{1,0:T(8,128)(2,1)S(1)}, u32[]{:S(2)}, u32[]{:S(2)}) collective-permute-start(bf16[416,256]{1,0:T(8,128)(2,1)S(1)} %bitcast.55), channel_id=1, source_target_pairs={{0,4},{1,5},{2,6},{3,7},{4,0},{5,1},{6,2},{7,3},{8,12},{9,13},{10,... | collective-permute-start | bytes 638984 | tf_op jit(solution)/shard_map/ppermute | solution.py:592
  102.6 7.3 %collective-permute-start.26 = (bf16[416,256]{1,0:T(8,128)(2,1)S(1)}, bf16[416,256]{1,0:T(8,128)(2,1)S(1)}, u32[]{:S(2)}, u32[]{:S(2)}) collective-permute-start(bf16[416,256]{1,0:T(8,128)(2,1)S(1)} %bitcast.56), channel_id=1, source_target_pairs={{0,6},{1,7},{2,4},{3,5},{4,2},{5,3},{6,0},{7,1},{8,14},{9,15},{10,... | collective-permute-start | bytes 638984 | tf_op jit(solution)/shard_map/ppermute | solution.py:592
  104.1 6.7 %collective-permute-start.20 = (bf16[1664,256]{1,0:T(8,128)(2,1)S(1)}, bf16[1664,256]{1,0:T(8,128)(2,1)S(1)}, u32[]{:S(2)}, u32[]{:S(2)}) collective-permute-start(bf16[1664,256]{1,0:T(8,128)(2,1)S(1)} %bitcast.52), channel_id=1, source_target_pairs={{0,1},{1,0},{2,3},{3,2},{4,5},{5,4},{6,7},{7,6},{8,9},{9,8},{10,11... | collective-permute-start | bytes 2555912 | tf_op jit(solution)/shard_map/ppermute | solution.py:592
  110.1 2.4 %collective-permute-start.27 = (bf16[1664,256]{1,0:T(8,128)(2,1)S(1)}, bf16[1664,256]{1,0:T(8,128)(2,1)S(1)}, u32[]{:S(2)}, u32[]{:S(2)}) collective-permute-start(bf16[1664,256]{1,0:T(8,128)(2,1)S(1)} %bitcast.50), channel_id=1, source_target_pairs={{0,1},{1,0},{2,3},{3,2},{4,5},{5,4},{6,7},{7,6},{8,9},{9,8},{10,11... | collective-permute-start | bytes 2555912 | tf_op jit(solution)/shard_map/ppermute | solution.py:592

commit v7 on v6

--- a/solution.py
+++ b/solution.py
@@ -106,53 +106,65 @@
     return (value * cumulative).astype(bf16), cumulative + value * density
 
 
-def first_rows(which, seqs, length, len_ref, x_ref, k_ref, v_ref, wqkv_ref, qb_ref, vb_ref, wo_ref, ob_ref, g1_ref, b1_ref, w1_ref, hb_ref, w2_ref, fb_ref, g2_ref, b2_ref):
-    rows = seqs * length
-    firsts = [x_ref[s * length : s * length + 16, :].astype(f32)[:1] for s in range(seqs)]
+def first_kernel(
+    seqs, lq_ref, lp_ref, xq_ref, xp_ref,
+    wqkv_ref, qb_ref, vb_ref, wo_ref, ob_ref, g1_ref, b1_ref, w1_ref, hb_ref, w2_ref, fb_ref, g2_ref, b2_ref,
+    cls_ref,
+    kq_ref, vq_ref, kp_ref, vp_ref,
+):
+    sides = ((0, xq_ref, kq_ref, vq_ref, lq_ref), (1, xp_ref, kp_ref, vp_ref, lp_ref))
     filler = jnp.zeros((PAD - seqs, WIDTH), f32)
-    inputs = jnp.concatenate(firsts + [filler], axis=0)
-    queries = (dot(inputs.astype(bf16), wqkv_ref[:, :WIDTH]) + vector(qb_ref, which)).astype(bf16).astype(f32)
-    x = x_ref[...]
-    k_ref[:rows, :] = dot(x, wqkv_ref[:, WIDTH : 2 * WIDTH]).astype(bf16)
-    v_ref[:rows, :] = (dot(x, wqkv_ref[:, 2 * WIDTH :]) + vector(vb_ref, which)).astype(bf16)
+    inputs = []
+    for which, x_ref, *_ in sides:
+        length = x_ref.shape[0] // seqs
+        firsts = [x_ref[s * length : s * length + 16, :].astype(f32)[:1] for s in range(seqs)]
+        inputs.append(jnp.concatenate(firsts + [filler], axis=0))
     own_lanes = lane_head(PAD) == lax.broadcasted_iota(jnp.int32, (PAD, WIDTH), 0)
-    contexts = []
-    for s in range(seqs):
-        span = slice(s * length, (s + 1) * length)
-        heads = jnp.where(own_lanes, queries[s : s + 1], 0.0).astype(bf16)
-        prob = masked_softmax(dot_nt(heads, k_ref[span, :]), len_ref[s])
-        context = dot(prob.astype(bf16), v_ref[span, :])
-        contexts.append(jnp.sum(jnp.where(own_lanes, context, 0.0), axis=0, keepdims=True))
-    context = jnp.concatenate(contexts + [filler], axis=0).astype(bf16)
-    value = inputs + (dot(context, wo_ref[...]) + vector(ob_ref, which))
-    unit, _ = normalize(value)
-    normed = unit * vector(g1_ref, which) + vector(b1_ref, which)
-    hidden = dot(normed.astype(bf16), w1_ref[...]) + vector(hb_ref, which)
-    active, _ = gelu_parts(hidden)
-    value = normed + (dot(active, w2_ref[...]) + vector(fb_ref, which))
-    unit, _ = normalize(value)
-    result = unit * vector(g2_ref, which) + vector(b2_ref, which)
-    row = lax.broadcasted_iota(jnp.int32, result.shape, 0)
-    return jnp.where(row < seqs, result, 0.0)
-
-
-def first_kernel(seqs, lq_ref, lp_ref, xq_ref, xp_ref, *refs):
-    weights, (cls_ref, k_ref, v_ref, passage_ref) = refs[:13], refs[13:]
-
-    @pl.when(pl.program_id(0) == 0)
-    def _():
-        passage_ref[...] = first_rows(1, seqs, xp_ref.shape[0] // seqs, lp_ref, xp_ref, k_ref, v_ref, *weights)
-
-    @pl.when(pl.program_id(0) == 1)
-    def _():
-        question = first_rows(0, seqs, xq_ref.shape[0] // seqs, lq_ref, xq_ref, k_ref, v_ref, *weights)
-        both = jnp.concatenate([question, passage_ref[...]], axis=0).astype(bf16)
-
-        def store(i, carry):
-            cls_ref[i] = both
-            return carry
-
-        lax.fori_loop(0, cls_ref.shape[0], store, 0)
+    queries = [
+        (dot(inputs[which].astype(bf16), wqkv_ref[which, :, :WIDTH]) + vector(qb_ref, which)).astype(bf16).astype(f32)
+        for which in range(2)
+    ]
+    for which, x_ref, k_ref, v_ref, _ in sides:
+        x = x_ref[...]
+        k_ref[...] = dot(x, wqkv_ref[which, :, WIDTH : 2 * WIDTH]).astype(bf16)
+        v_ref[...] = (dot(x, wqkv_ref[which, :, 2 * WIDTH :]) + vector(vb_ref, which)).astype(bf16)
+    context = []
+    for which, x_ref, k_ref, v_ref, len_ref in sides:
+        length = x_ref.shape[0] // seqs
+        spans = [slice(s * length, (s + 1) * length) for s in range(seqs)]
+        scores, sizes = [], []
+        for s, span in enumerate(spans):
+            heads = jnp.where(own_lanes, queries[which][s : s + 1], 0.0).astype(bf16)
+            scores.append(dot_nt(heads, k_ref[span, :]))
+            sizes.append(jnp.full((PAD, length), len_ref[s], jnp.int32))
+        prob = masked_softmax(jnp.concatenate(scores, axis=0), jnp.concatenate(sizes, axis=0)).astype(f32)
+        rows = []
+        for s, span in enumerate(spans):
+            mixed = dot(prob[s * PAD : (s + 1) * PAD].astype(bf16), v_ref[span, :])
+            rows.append(jnp.sum(jnp.where(own_lanes, mixed, 0.0), axis=0, keepdims=True))
+        context.append(jnp.concatenate(rows + [filler], axis=0).astype(bf16))
+    normed = []
+    for which in range(2):
+        value = inputs[which] + (dot(context[which], wo_ref[which]) + vector(ob_ref, which))
+        unit, _ = normalize(value)
+        normed.append(unit * vector(g1_ref, which) + vector(b1_ref, which))
+    active = []
+    for which in range(2):
+        active.append(gelu_parts(dot(normed[which].astype(bf16), w1_ref[which]) + vector(hb_ref, which))[0])
+    results = []
+    for which in range(2):
+        value = normed[which] + (dot(active[which], w2_ref[which]) + vector(fb_ref, which))
+        unit, _ = normalize(value)
+        result = unit * vector(g2_ref, which) + vector(b2_ref, which)
+        row = lax.broadcasted_iota(jnp.int32, result.shape, 0)
+        results.append(jnp.where(row < seqs, result, 0.0))
+    both = jnp.concatenate(results, axis=0).astype(bf16)
+
+    def store(i, carry):
+        cls_ref[i] = both
+        return carry
+
+    lax.fori_loop(0, cls_ref.shape[0], store, 0)
 
 
 def attend_kernel(which, seqs, length, len_ref, x_ref, wqkv_ref, qb_ref, vb_ref, qkv_ref, p_ref, ctx_ref, score_ref, prob_ref):
@@ -442,22 +454,31 @@
 VECTOR_OUTS = (QUERY_BIAS, VALUE_BIAS, PROJ_BIAS, ATTN_GAIN, ATTN_SHIFT, DOWN_BIAS, FFN_GAIN, FFN_SHIFT)
 
 
-def unpack_kernel(bit_ref, q_own_ref, q_ref, p_own_ref, p_ref, qkv_ref, proj_ref, up_ref, down_ref, up_bias_ref, *refs):
-    vector_refs, whole_ref = refs[:-1], refs[-1]
-    own = pl.multiple_of(bit_ref[0] * HALF, HALF)
-    other = pl.multiple_of((1 - bit_ref[0]) * HALF, HALF)
-    tails = []
-    for which, (own_ref, other_ref) in enumerate(((q_own_ref, q_ref), (p_own_ref, p_ref))):
-        ref = whole_ref.at[which]
-        ref[pl.ds(own, HALF), :] = own_ref[...]
-        ref[pl.ds(other, HALF), :] = other_ref[...]
-        for j in range(3):
-            qkv_ref[which, :, j * WIDTH : (j + 1) * WIDTH] = ref[block_rows(QKV_BLOCK + j), :].astype(f32)
-        proj_ref[which] = ref[block_rows(PROJ_BLOCK), :].astype(f32)
-        for j in range(BLOCKS):
-            up_ref[which, :, j * WIDTH : (j + 1) * WIDTH] = ref[block_rows(UP_BLOCK + j), :].astype(f32)
-            down_ref[which, j * WIDTH : (j + 1) * WIDTH, :] = ref[block_rows(DOWN_BLOCK + j), :].astype(f32)
-        tails.append(ref[VECTOR_START : VECTOR_START + VECTOR_ROWS, :].astype(f32))
+def spread(which, ref, qkv_ref, proj_ref, up_ref, down_ref):
+    for j in range(3):
+        qkv_ref[:, j * WIDTH : (j + 1) * WIDTH] = ref[block_rows(QKV_BLOCK + j), :].astype(f32)
+    proj_ref[...] = ref[block_rows(PROJ_BLOCK), :].astype(f32)
+    for j in range(BLOCKS):
+        up_ref[:, j * WIDTH : (j + 1) * WIDTH] = ref[block_rows(UP_BLOCK + j), :].astype(f32)
+        down_ref[j * WIDTH : (j + 1) * WIDTH, :] = ref[block_rows(DOWN_BLOCK + j), :].astype(f32)
+    return ref[VECTOR_START : VECTOR_START + VECTOR_ROWS, :].astype(f32)
+
+
+def question_unpack_kernel(bit_ref, own_ref, other_ref, qkv_ref, proj_ref, up_ref, down_ref, tail_ref, whole_ref):
+    whole_ref[pl.ds(pl.multiple_of(bit_ref[0] * HALF, HALF), HALF), :] = own_ref[...]
+    whole_ref[pl.ds(pl.multiple_of((1 - bit_ref[0]) * HALF, HALF), HALF), :] = other_ref[...]
+    tail_ref[...] = spread(0, whole_ref, qkv_ref, proj_ref, up_ref, down_ref)
+
+
+def passage_unpack_kernel(parts, bit_ref, digit_ref, *refs):
+    own_refs, other_refs, (tail_ref, *_) = refs[:parts], refs[parts : 2 * parts], refs[2 * parts : 2 * parts + 5]
+    qkv_ref, proj_ref, up_ref, down_ref, up_bias_ref, *vector_refs, whole_ref = refs[2 * parts + 5 :]
+    size = HALF // parts
+    for half, halves in ((bit_ref[0], own_refs), (1 - bit_ref[0], other_refs)):
+        for step, ref in enumerate(halves):
+            start = half * HALF + (digit_ref[0] ^ step) * size
+            whole_ref[pl.ds(pl.multiple_of(start, 8), size), :] = ref[...]
+    tails = (tail_ref[...], spread(1, whole_ref, qkv_ref, proj_ref, up_ref, down_ref))
     for row, ref in zip(VECTOR_OUTS, vector_refs):
         for which in range(2):
             ref[which : which + 1, :] = tails[which][row : row + 1]
@@ -503,20 +524,13 @@
 
 
 def first_call(count, local, len_questions, len_passages, x_q, x_p, weights):
-    def matrix(rows, columns):
-        return pl.BlockSpec((None, rows, columns), lambda i: (1 - i, 0, 0))
-
-    specs = [
-        matrix(WIDTH, 3 * WIDTH), pair(WIDTH), pair(WIDTH), matrix(WIDTH, WIDTH), pair(WIDTH), pair(WIDTH), pair(WIDTH),
-        matrix(WIDTH, HIDDEN), pair(HIDDEN), matrix(HIDDEN, WIDTH), pair(WIDTH), pair(WIDTH), pair(WIDTH),
-    ]
     return pl.pallas_call(
         functools.partial(first_kernel, local),
         out_shape=shape((count, 2 * PAD, WIDTH), bf16),
-        grid=(2,),
-        in_specs=[smem(), smem(), whole(x_q.shape), whole(x_p.shape)] + specs,
+        grid=(1,),
+        in_specs=[smem(), smem(), whole(x_q.shape), whole(x_p.shape)] + [whole(member.shape) for member in weights],
         out_specs=whole((count, 2 * PAD, WIDTH)),
-        scratch_shapes=[pltpu.VMEM(x_p.shape, bf16), pltpu.VMEM(x_p.shape, bf16), pltpu.VMEM((PAD, WIDTH), f32)],
+        scratch_shapes=[pltpu.VMEM(x_q.shape, bf16)] * 2 + [pltpu.VMEM(x_p.shape, bf16)] * 2,
         compiler_params=params(),
         name="first",
     )(in_hbm(len_questions), in_hbm(len_passages), in_hbm(x_q), in_hbm(x_p), *[in_hbm(member) for member in weights])
@@ -708,7 +722,7 @@
     (send_p,) = after([send_p], *pieces_q)
     pieces_p = [keep_p, partner_send(send_p, groups[0][0], count)]
     for place in range(len(steps)):
-        if place > 0:
+        if 0 < place < len(steps) - 1:
             pieces_p = after(pieces_p, *operands_q)
             operands_p = prepare(pieces_p, steps[place - 1], steps[place], me)
             pieces_p = launch(operands_p, steps[place], count)
@@ -716,19 +730,39 @@
         if place + 2 < len(steps):
             operands_q = prepare(pieces_q, steps[place + 1], steps[place + 2], me)
             pieces_q = launch(operands_q, steps[place + 2], count)
-    (own_q, other_q), (own_p, other_p) = pieces_q, pieces_p
-    dims = [(2, WIDTH, 3 * WIDTH), (2, WIDTH, WIDTH), (2, WIDTH, HIDDEN), (2, HIDDEN, WIDTH), (2, HIDDEN)]
-    dims += [(2, WIDTH)] * len(VECTOR_OUTS)
+    own_q, other_q = pieces_q
+    parts = len(pieces_p)
+    digit = (me // groups[1][0] % parts).reshape(1)
+    dims = [(WIDTH, 3 * WIDTH), (WIDTH, WIDTH), (WIDTH, HIDDEN), (HIDDEN, WIDTH)]
+    matrices = [shape((2,) + d, f32) for d in dims]
+    *halves, tail = pl.pallas_call(
+        question_unpack_kernel,
+        out_shape=matrices + [shape((VECTOR_ROWS, WIDTH), f32)],
+        grid=(1,),
+        in_specs=[smem()] + [whole((HALF, WIDTH))] * 2,
+        out_specs=[part_of(0, d) for d in dims] + [whole((VECTOR_ROWS, WIDTH))],
+        scratch_shapes=[pltpu.VMEM((GROUP_ROWS, WIDTH), bf16)],
+        compiler_params=params(),
+        name="unpack_q",
+    )(bit, own_q, other_q)
+    own_piece, *came = pieces_p
+    came = after(came, tail, loss_rows)
+    pieces_p = [own_piece] + came
+    other_p = [partner_send(piece, groups[0][0], count) for piece in pieces_p]
+    vectors = [(2, HIDDEN)] + [(2, WIDTH)] * len(VECTOR_OUTS)
+    first_alias = 2 + 2 * parts + 1
     d_qkv, d_proj, d_up, d_down, up_bias, query_bias, value_bias, proj_bias, gain_a, shift_a, down_bias, gain_f, shift_f = pl.pallas_call(
-        unpack_kernel,
-        out_shape=[shape(d, f32) for d in dims],
+        functools.partial(passage_unpack_kernel, parts),
+        out_shape=matrices + [shape(d, f32) for d in vectors],
         grid=(1,),
-        in_specs=[smem()] + [whole((HALF, WIDTH))] * 4,
-        out_specs=[whole(d) for d in dims],
-        scratch_shapes=[pltpu.VMEM((2, GROUP_ROWS, WIDTH), bf16)],
+        in_specs=[smem(), smem()] + [whole((HALF // parts, WIDTH))] * (2 * parts) + [whole((VECTOR_ROWS, WIDTH))]
+        + [pl.BlockSpec(memory_space=pl.ANY)] * 4,
+        out_specs=[part_of(1, d) for d in dims] + [whole(d) for d in vectors],
+        scratch_shapes=[pltpu.VMEM((GROUP_ROWS, WIDTH), bf16)],
+        input_output_aliases={first_alias + i: i for i in range(4)},
         compiler_params=params(),
-        name="unpack",
-    )(bit, own_q, other_q, own_p, other_p)
+        name="unpack_p",
+    )(bit, digit, *pieces_p, *other_p, tail, *halves)
     return (
         loss_rows, out_q.reshape(questions.shape), out_p.reshape(passages.shape),
         grad_q.reshape(questions.shape), grad_p.reshape(passages.shape),

time: 116 us -> 113 us (0.974)
  starting transfers between devices: 41.5 us -> 38.1 us
  waiting for transfers between devices: 18 us -> 20.2 us
  Pallas kernels: 53.7 us -> 51.8 us
    ppermute x28 -> x31, starting transfers between devices: 34.2 us -> 30.8 us  [partner_send(): return lax.ppermute(values, 'dp', [(i, i ^ mask) for i in range(count)])]
    pallas_call x1, Pallas kernels: 7.51 us -> 5.22 us  [first_call(): pl.pallas_call(functools.partial(first_kernel, local), out_shape=shape((c...]
    ppermute x28 -> x31, waiting for transfers between devices: 18 us -> 20.2 us  [partner_send(): return lax.ppermute(values, 'dp', [(i, i ^ mask) for i in range(count)])]
    pallas_call x1 -> x2, Pallas kernels: 3.18 us -> 3.61 us  [the longest x1 1.82 us: body(): pl.pallas_call(functools.partial(passage_unpack_kernel, parts), out_shape...]
  transfers between devices with their start and end apart: 29 -> 32, of which waited for: 10 -> 15; matrix products, arithmetic and copies ran while one was open for 1% -> 1% of each run, Pallas kernels for 29% -> 31%
where the time goes in v7:
time: 113 us
  Pallas kernels  51.8 us (46%)
  starting transfers between devices  38.1 us (34%)
  waiting for transfers between devices  20.2 us (18%)
  local copies, waits for them, and re-layouts  1.19 us (1%)
    pallas_call x2, Pallas kernels, layer(): pl.pallas_call(functools.partial(layer_kernel, which, steps, seqs, length...  30.9 us
    ppermute x31, starting transfers between devices, partner_send(): return lax.ppermute(values, 'dp', [(i, i ^ mask) for i in range(count)])  30.8 us
    ppermute x31, waiting for transfers between devices, partner_send(): return lax.ppermute(values, 'dp', [(i, i ^ mask) for i in range(count)])  20.2 us
    pallas_call x2, Pallas kernels, attend(): pl.pallas_call(functools.partial(attend_kernel, which, seqs, length), out...  10.2 us
    all_to_all x1, starting transfers between devices, body(): all_cls = lax.all_to_all(own_cls, 'dp', 0, 0, tiled=True)  7.3 us
    pallas_call x1, Pallas kernels, first_call(): pl.pallas_call(functools.partial(first_kernel, local), out_shape=shape((c...  5.22 us
  transfers between devices with their start and end apart: 32, of which 15 were waited for; matrix products, arithmetic and copies ran while one was open for 1% of the time, Pallas kernels for 31%

profile of v7, /device:TPU:0, one launch (start us, length us, event | category | flops | bytes accessed | tf_op | source)
XLA Modules:
  0.0 112.5 jit_solution(2010293574611415117)
XLA Ops:
  0.7 5.2 %first.1 = bf16[32,16,256]{2,1,0:T(8,128)(2,1)} custom-call(s32[5]{0:T(128)} %len_ref.6, s32[5]{0:T(128)} %len_ref.7, bf16[320,256]{1,0:T(8,128)(2,1)} %bitcast.52, bf16[1280,256]{1,0:T(8,128)(2,1)} %bitcast.55, bf16[2,256,768]{2,1,0:T(8,128)(2,1)} %wqkv_ref.9, bf16[2,256]{1,0:T(2,128)(2,1)} %qb_ref.5, bf16[2,256]{1,0:T(2,128)(2,1)} %vb_ref.5, ...), custom_call_target="tpu_custom_call" | custom-call | tf_op jit(solution)/shard_map/first/pallas_call | solution.py:527
  5.9 7.3 %all-to-all-start = ((bf16[32,16,256]{2,1,0:T(8,128)(2,1)}), bf16[32,16,256]{2,1,0:T(8,128)(2,1)S(1)}, u32[]{:S(2)}, u32[]{:S(2)}) async-start(bf16[32,16,256]{2,1,0:T(8,128)(2,1)} %first.1), calls=%async_computation | async-start | bytes 524288 | tf_op jit(solution)/shard_map/all_to_all | solution.py:691
  13.6 3.3 %attend.3 = (bf16[320,768]{1,0:T(8,128)(2,1)}, f32[1280,64]{1,0:T(8,128)}, bf16[320,256]{1,0:T(8,128)(2,1)}) custom-call(s32[5]{0:T(128)S(1)} %copy-done, bf16[320,256]{1,0:T(8,128)(2,1)} %bitcast.53, bf16[2,256,768]{2,1,0:T(8,128)(2,1)} %wqkv_ref.9, bf16[2,256]{1,0:T(2,128)(2,1)} %qb_ref.5, bf16[2,256]{1,0:T(2,128)(2,1)} %vb_ref.5), custom_call_target="tpu_custom_call" | custom-call | flops 256000000 | bytes 1920000 | tf_op jit(solution)/shard_map/attend/pallas_call | solution.py:544
  16.8 7.0 %attend.2 = (bf16[1280,768]{1,0:T(8,128)(2,1)}, f32[5120,256]{1,0:T(8,128)}, bf16[1280,256]{1,0:T(8,128)(2,1)}) custom-call(s32[5]{0:T(128)S(1)} %copy-done.1, bf16[1280,256]{1,0:T(8,128)(2,1)} %bitcast.56, bf16[2,256,768]{2,1,0:T(8,128)(2,1)} %wqkv_ref.9, bf16[2,256]{1,0:T(2,128)(2,1)} %qb_ref.5, bf16[2,256]{1,0:T(2,128)(2,1)} %vb_ref.5), custom_call_target="tpu_custom_call" | custom-call | flops 1024000000 | bytes 7680000 | tf_op jit(solution)/shard_map/attend/pallas_call | solution.py:544
  23.8 0.8 loss.1
  24.6 8.3 %layer.2 = (bf16[320,256]{1,0:T(8,128)(2,1)}, bf16[320,256]{1,0:T(8,128)(2,1)}, bf16[1664,256]{1,0:T(8,128)(2,1)S(1)}, bf16[1664,256]{1,0:T(8,128)(2,1)S(1)}) custom-call(s32[1]{0:T(128)} %bitcast.4.bit_ref, s32[5]{0:T(128)S(1)} %copy-done, f32[8,256]{1,0:T(8,128)S(1)} %get-tuple-element.113.cls_ref, bf16[320,256]{1,0:T(8,128)(2,1)} %bitcast.54, ...), custom_call_target="tpu_custom_call" | custom-call | flops 1536000000 | bytes 1280000 | tf_op jit(solution)/shard_map/layer/pallas_call | solution.py:564
  33.1 2.1 %collective-permute-done.refs_1_ = bf16[1664,256]{1,0:T(8,128)(2,1)S(1)} collective-permute-done((bf16[1664,256]{1,0:T(8,128)(2,1)S(1)}, bf16[1664,256]{1,0:T(8,128)(2,1)S(1)}, u32[]{:S(2)}, u32[]{:S(2)}) %collective-permute-start) | collective-permute-done | bytes 852000 | tf_op jit(solution)/shard_map/ppermute | solution.py:606
  35.3 0.4 combine.4
  35.6 1.8 %collective-permute-start.1 = (bf16[416,256]{1,0:T(8,128)(2,1)S(1)}, bf16[416,256]{1,0:T(8,128)(2,1)S(1)}, u32[]{:S(2)}, u32[]{:S(2)}) collective-permute-start(bf16[416,256]{1,0:T(8,128)(2,1)S(1)} %get-tuple-element.121), channel_id=1, source_target_pairs={{0,2},{1,3},{2,0},{3,1},{4,6},{5,7},{6,4},{7,5},{8,10},{9,11},{10,... | collective-permute-start | bytes 638984 | tf_op jit(solution)/shard_map/ppermute | solution.py:606
  37.5 1.4 %collective-permute-start.2 = (bf16[416,256]{1,0:T(8,128)(2,1)S(1)}, bf16[416,256]{1,0:T(8,128)(2,1)S(1)}, u32[]{:S(2)}, u32[]{:S(2)}) collective-permute-start(bf16[416,256]{1,0:T(8,128)(2,1)S(1)} %get-tuple-element.122), channel_id=1, source_target_pairs={{0,4},{1,5},{2,6},{3,7},{4,0},{5,1},{6,2},{7,3},{8,12},{9,13},{10,... | collective-permute-start | bytes 638984 | tf_op jit(solution)/shard_map/ppermute | solution.py:606
  38.9 0.3 collective-permute-start.3
  39.2 22.6 %layer.3 = (bf16[1280,256]{1,0:T(8,128)(2,1)}, bf16[1280,256]{1,0:T(8,128)(2,1)}, bf16[1664,256]{1,0:T(8,128)(2,1)S(1)}, bf16[1664,256]{1,0:T(8,128)(2,1)S(1)}) custom-call(s32[1]{0:T(128)} %bitcast.4.bit_ref, s32[5]{0:T(128)S(1)} %copy-done.1, f32[8,256]{1,0:T(8,128)S(1)} %get-tuple-element.124.cls_ref, bf16[1280,256]{1,0:T(8,128)(2,1)} %bitcast.57, ...), custom_call_target="tpu_custom_call" | custom-call | flops 6144000000 | bytes 5120000 | tf_op jit(solution)/shard_map/layer/pallas_call | solution.py:564
  62.2 1.8 %collective-permute-start.8 = (bf16[104,256]{1,0:T(8,128)(2,1)S(1)}, bf16[104,256]{1,0:T(8,128)(2,1)S(1)}, u32[]{:S(2)}, u32[]{:S(2)}) collective-permute-start(bf16[104,256]{1,0:T(8,128)(2,1)S(1)} %get-tuple-element.134), channel_id=1, source_target_pairs={{0,8},{1,9},{2,10},{3,11},{4,12},{5,13},{6,14},{7,15},{8,0},{9,1},... | collective-permute-start | bytes 159752 | tf_op jit(solution)/shard_map/ppermute | solution.py:606
  64.0 2.4 %collective-permute-start.9 = (bf16[104,256]{1,0:T(8,128)(2,1)S(1)}, bf16[104,256]{1,0:T(8,128)(2,1)S(1)}, u32[]{:S(2)}, u32[]{:S(2)}) collective-permute-start(bf16[104,256]{1,0:T(8,128)(2,1)S(1)} %get-tuple-element.135), channel_id=1, source_target_pairs={{0,16},{1,17},{2,18},{3,19},{4,20},{5,21},{6,22},{7,23},{8,24},{9,... | collective-permute-start | bytes 159752 | tf_op jit(solution)/shard_map/ppermute | solution.py:606
  66.6 0.4 combine.6
  67.0 1.8 %collective-permute-start.5 = (bf16[416,256]{1,0:T(8,128)(2,1)S(1)}, bf16[416,256]{1,0:T(8,128)(2,1)S(1)}, u32[]{:S(2)}, u32[]{:S(2)}) collective-permute-start(bf16[416,256]{1,0:T(8,128)(2,1)S(1)} %get-tuple-element.140), channel_id=1, source_target_pairs={{0,2},{1,3},{2,0},{3,1},{4,6},{5,7},{6,4},{7,5},{8,10},{9,11},{10,... | collective-permute-start | bytes 638984 | tf_op jit(solution)/shard_map/ppermute | solution.py:606
  68.8 1.4 %collective-permute-start.6 = (bf16[416,256]{1,0:T(8,128)(2,1)S(1)}, bf16[416,256]{1,0:T(8,128)(2,1)S(1)}, u32[]{:S(2)}, u32[]{:S(2)}) collective-permute-start(bf16[416,256]{1,0:T(8,128)(2,1)S(1)} %get-tuple-element.141), channel_id=1, source_target_pairs={{0,4},{1,5},{2,6},{3,7},{4,0},{5,1},{6,2},{7,3},{8,12},{9,13},{10,... | collective-permute-start | bytes 638984 | tf_op jit(solution)/shard_map/ppermute | solution.py:606
  70.2 0.3 collective-permute-start.7
  70.5 1.8 %collective-permute-done.10 = bf16[104,256]{1,0:T(8,128)(2,1)S(1)} collective-permute-done((bf16[104,256]{1,0:T(8,128)(2,1)S(1)}, bf16[104,256]{1,0:T(8,128)(2,1)S(1)}, u32[]{:S(2)}, u32[]{:S(2)}) %collective-permute-start.10) | collective-permute-done | bytes 53280 | tf_op jit(solution)/shard_map/ppermute | solution.py:606
  72.3 1.9 %collective-permute-start.16 = (bf16[104,256]{1,0:T(8,128)(2,1)S(1)}, bf16[104,256]{1,0:T(8,128)(2,1)S(1)}, u32[]{:S(2)}, u32[]{:S(2)}) collective-permute-start(bf16[104,256]{1,0:T(8,128)(2,1)S(1)} %add_convert_fusion.1), channel_id=1, source_target_pairs={{0,24},{1,25},{2,26},{3,27},{4,28},{5,29},{6,30},{7,31},{8,16},{9,... | collective-permute-start | bytes 159752 | tf_op jit(solution)/shard_map/ppermute | solution.py:606
  74.2 1.0 collective-permute-done.5.refs_1_
  75.2 1.6 %collective-permute-start.14 = (bf16[104,256]{1,0:T(8,128)(2,1)S(1)}, bf16[104,256]{1,0:T(8,128)(2,1)S(1)}, u32[]{:S(2)}, u32[]{:S(2)}) collective-permute-start(bf16[104,256]{1,0:T(8,128)(2,1)S(1)} %add_convert_fusion.1), channel_id=1, source_target_pairs={{0,8},{1,9},{2,10},{3,11},{4,12},{5,13},{6,14},{7,15},{8,0},{9,1},... | collective-permute-start | bytes 159752 | tf_op jit(solution)/shard_map/ppermute | solution.py:606
  76.8 3.1 %collective-permute-done.6.refs_2_ = bf16[416,256]{1,0:T(8,128)(2,1)S(1)} collective-permute-done((bf16[416,256]{1,0:T(8,128)(2,1)S(1)}, bf16[416,256]{1,0:T(8,128)(2,1)S(1)}, u32[]{:S(2)}, u32[]{:S(2)}) %collective-permute-start.6) | collective-permute-done | bytes 213024 | tf_op jit(solution)/shard_map/ppermute | solution.py:606
  80.0 0.6 collective-permute-start.11
  80.7 3.3 %collective-permute-start.12 = (bf16[104,256]{1,0:T(8,128)(2,1)S(1)}, bf16[104,256]{1,0:T(8,128)(2,1)S(1)}, u32[]{:S(2)}, u32[]{:S(2)}) collective-permute-start(bf16[104,256]{1,0:T(8,128)(2,1)S(1)} %get-tuple-element.153), channel_id=1, source_target_pairs={{0,16},{1,17},{2,18},{3,19},{4,20},{5,21},{6,22},{7,23},{8,24},{9,... | collective-permute-start | bytes 159752 | tf_op jit(solution)/shard_map/ppermute | solution.py:606
  84.0 0.5 collective-permute-start.13
  84.6 1.5 %collective-permute-start.22 = (bf16[416,256]{1,0:T(8,128)(2,1)S(1)}, bf16[416,256]{1,0:T(8,128)(2,1)S(1)}, u32[]{:S(2)}, u32[]{:S(2)}) collective-permute-start(bf16[416,256]{1,0:T(8,128)(2,1)S(1)} %bitcast.48), channel_id=1, source_target_pairs={{0,6},{1,7},{2,4},{3,5},{4,2},{5,3},{6,0},{7,1},{8,14},{9,15},{10,... | collective-permute-start | bytes 638984 | tf_op jit(solution)/shard_map/ppermute | solution.py:606
  86.1 1.2 %collective-permute-start.21 = (bf16[416,256]{1,0:T(8,128)(2,1)S(1)}, bf16[416,256]{1,0:T(8,128)(2,1)S(1)}, u32[]{:S(2)}, u32[]{:S(2)}) collective-permute-start(bf16[416,256]{1,0:T(8,128)(2,1)S(1)} %bitcast.49), channel_id=1, source_target_pairs={{0,4},{1,5},{2,6},{3,7},{4,0},{5,1},{6,2},{7,3},{8,12},{9,13},{10,... | collective-permute-start | bytes 638984 | tf_op jit(solution)/shard_map/ppermute | solution.py:606
  87.3 0.9 collective-permute-start.20
  88.2 1.8 %collective-permute-done.13 = bf16[104,256]{1,0:T(8,128)(2,1)S(1)} collective-permute-done((bf16[104,256]{1,0:T(8,128)(2,1)S(1)}, bf16[104,256]{1,0:T(8,128)(2,1)S(1)}, u32[]{:S(2)}, u32[]{:S(2)}) %collective-permute-start.13) | collective-permute-done | bytes 53280 | tf_op jit(solution)/shard_map/ppermute | solution.py:606
  90.0 1.6 %collective-permute-start.19 = (bf16[104,256]{1,0:T(8,128)(2,1)S(1)}, bf16[104,256]{1,0:T(8,128)(2,1)S(1)}, u32[]{:S(2)}, u32[]{:S(2)}) collective-permute-start(bf16[104,256]{1,0:T(8,128)(2,1)S(1)} %add_convert_fusion), channel_id=1, source_target_pairs={{0,24},{1,25},{2,26},{3,27},{4,28},{5,29},{6,30},{7,31},{8,16},{9,... | collective-permute-start | bytes 159752 | tf_op jit(solution)/shard_map/ppermute | solution.py:606
  91.6 1.2 %collective-permute-done.22 = bf16[416,256]{1,0:T(8,128)(2,1)S(1)} collective-permute-done((bf16[416,256]{1,0:T(8,128)(2,1)S(1)}, bf16[416,256]{1,0:T(8,128)(2,1)S(1)}, u32[]{:S(2)}, u32[]{:S(2)}) %collective-permute-start.22) | collective-permute-done | bytes 213024 | tf_op jit(solution)/shard_map/ppermute | solution.py:606
  92.8 1.6 %collective-permute-start.17 = (bf16[104,256]{1,0:T(8,128)(2,1)S(1)}, bf16[104,256]{1,0:T(8,128)(2,1)S(1)}, u32[]{:S(2)}, u32[]{:S(2)}) collective-permute-start(bf16[104,256]{1,0:T(8,128)(2,1)S(1)} %add_convert_fusion), channel_id=1, source_target_pairs={{0,8},{1,9},{2,10},{3,11},{4,12},{5,13},{6,14},{7,15},{8,0},{9,1},... | collective-permute-start | bytes 159752 | tf_op jit(solution)/shard_map/ppermute | solution.py:606
  94.4 0.5 collective-permute-done.21
  95.2 0.8 collective-permute-done.19
  96.0 1.2 %collective-permute-done.18 = bf16[104,256]{1,0:T(8,128)(2,1)S(1)} collective-permute-done((bf16[104,256]{1,0:T(8,128)(2,1)S(1)}, bf16[104,256]{1,0:T(8,128)(2,1)S(1)}, u32[]{:S(2)}, u32[]{:S(2)}) %collective-permute-start.18) | collective-permute-done | bytes 53280 | tf_op jit(solution)/shard_map/ppermute | solution.py:606
  97.6 1.6 %collective-permute-start.25 = (bf16[416,256]{1,0:T(8,128)(2,1)S(1)}, bf16[416,256]{1,0:T(8,128)(2,1)S(1)}, u32[]{:S(2)}, u32[]{:S(2)}) collective-permute-start(bf16[416,256]{1,0:T(8,128)(2,1)S(1)} %bitcast.43), channel_id=1, source_target_pairs={{0,6},{1,7},{2,4},{3,5},{4,2},{5,3},{6,0},{7,1},{8,14},{9,15},{10,... | collective-permute-start | bytes 638984 | tf_op jit(solution)/shard_map/ppermute | solution.py:606
  99.1 1.4 %collective-permute-start.24 = (bf16[416,256]{1,0:T(8,128)(2,1)S(1)}, bf16[416,256]{1,0:T(8,128)(2,1)S(1)}, u32[]{:S(2)}, u32[]{:S(2)}) collective-permute-start(bf16[416,256]{1,0:T(8,128)(2,1)S(1)} %bitcast.44), channel_id=1, source_target_pairs={{0,4},{1,5},{2,6},{3,7},{4,0},{5,1},{6,2},{7,3},{8,12},{9,13},{10,... | collective-permute-start | bytes 638984 | tf_op jit(solution)/shard_map/ppermute | solution.py:606
  100.5 0.6 collective-permute-start.23
  101.1 0.6 slice_reduce_fusion
  101.7 1.8 %unpack_q.1 = (f32[2,256,768]{2,1,0:T(8,128)}, f32[2,256,256]{2,1,0:T(8,128)}, f32[2,256,1024]{2,1,0:T(8,128)}, f32[2,1024,256]{2,1,0:T(8,128)}, f32[16,256]{1,0:T(8,128)S(1)}) custom-call(s32[1]{0:T(128)} %bitcast.4.bit_ref, bf16[1664,256]{1,0:T(8,128)(2,1)S(1)} %bitcast.42, bf16[1664,256]{1,0:T(8,128)(2,1)S(1)} %collective-permute-done.26.other_ref), custom_call_target="tpu_custom_call" | custom-call | tf_op jit(solution)/shard_map/unpack_q/pallas_call | solution.py:738
  103.5 2.7 %collective-permute-done.25.refs_3_ = bf16[416,256]{1,0:T(8,128)(2,1)S(1)} collective-permute-done((bf16[416,256]{1,0:T(8,128)(2,1)S(1)}, bf16[416,256]{1,0:T(8,128)(2,1)S(1)}, u32[]{:S(2)}, u32[]{:S(2)}) %collective-permute-start.25) | collective-permute-done | bytes 213024 | tf_op jit(solution)/shard_map/ppermute | solution.py:606
  106.3 2.2 %collective-permute-done.24.refs_2_ = bf16[416,256]{1,0:T(8,128)(2,1)S(1)} collective-permute-done((bf16[416,256]{1,0:T(8,128)(2,1)S(1)}, bf16[416,256]{1,0:T(8,128)(2,1)S(1)}, u32[]{:S(2)}, u32[]{:S(2)}) %collective-permute-start.24) | collective-permute-done | bytes 213024 | tf_op jit(solution)/shard_map/ppermute | solution.py:606
  108.5 0.5 collective-permute-start.29
  109.0 0.9 collective-permute-done.28.refs_5_
  109.9 0.3 collective-permute-done.29.refs_6_
  110.3 0.3 collective-permute-done.30.refs_7_
  110.6 1.8 %unpack_p.1 = (f32[2,256,768]{2,1,0:T(8,128)}, f32[2,256,256]{2,1,0:T(8,128)}, f32[2,256,1024]{2,1,0:T(8,128)}, f32[2,1024,256]{2,1,0:T(8,128)}, f32[2,1024]{1,0...) custom-call(s32[1]{0:T(128)} %bitcast.4.bit_ref, ...), custom_call_target="tpu_custom_call", output_to_operand_aliasing={{0}: (11, {}), {1}: (12, {}), {2}: (13, {}), {3}: (14, {})} | custom-call | tf_op jit(solution)/shard_map/unpack_p/pallas_call | solution.py:754
  (58 shorter events, 1.9 us)
Async XLA Ops:
  0.7 12.6 %copy-start.2 = (s32[160]{0:T(256)S(1)}, s32[160]{0:T(256)}, u32[]{:S(2)}) copy-start(s32[160]{0:T(256)} %param.26) | copy-start | bytes 1924
  0.7 12.9 %copy-start = (s32[5]{0:T(128)S(1)}, s32[5]{0:T(128)}, u32[]{:S(2)}) copy-start(s32[5]{0:T(128)} %len_ref.6) | copy-start | bytes 64
  0.7 16.2 %copy-start.1 = (s32[5]{0:T(128)S(1)}, s32[5]{0:T(128)}, u32[]{:S(2)}) copy-start(s32[5]{0:T(128)} %len_ref.7) | copy-start | bytes 64
  5.9 17.9 %all-to-all-start = ((bf16[32,16,256]{2,1,0:T(8,128)(2,1)}), bf16[32,16,256]{2,1,0:T(8,128)(2,1)S(1)}, u32[]{:S(2)}, u32[]{:S(2)}) async-start(bf16[32,16,256]{2,1,0:T(8,128)(2,1)} %first.1), calls=%async_computation | async-start | bytes 524288 | tf_op jit(solution)/shard_map/all_to_all | solution.py:691
  32.9 2.4 %collective-permute-start = (bf16[1664,256]{1,0:T(8,128)(2,1)S(1)}, bf16[1664,256]{1,0:T(8,128)(2,1)S(1)}, u32[]{:S(2)}, u32[]{:S(2)}) collective-permute-start(bf16[1664,256]{1,0:T(8,128)(2,1)S(1)} %get-tuple-element.119), channel_id=1, source_target_pairs={{0,1},{1,0},{2,3},{3,2},{4,5},{5,4},{6,7},{7,6},{8,9},{9,8},{10,11... | collective-permute-start | bytes 2555912 | tf_op jit(solution)/shard_map/ppermute | solution.py:606
  35.6 26.2 %collective-permute-start.1 = (bf16[416,256]{1,0:T(8,128)(2,1)S(1)}, bf16[416,256]{1,0:T(8,128)(2,1)S(1)}, u32[]{:S(2)}, u32[]{:S(2)}) collective-permute-start(bf16[416,256]{1,0:T(8,128)(2,1)S(1)} %get-tuple-element.121), channel_id=1, source_target_pairs={{0,2},{1,3},{2,0},{3,1},{4,6},{5,7},{6,4},{7,5},{8,10},{9,11},{10,... | collective-permute-start | bytes 638984 | tf_op jit(solution)/shard_map/ppermute | solution.py:606
  37.5 24.4 %collective-permute-start.2 = (bf16[416,256]{1,0:T(8,128)(2,1)S(1)}, bf16[416,256]{1,0:T(8,128)(2,1)S(1)}, u32[]{:S(2)}, u32[]{:S(2)}) collective-permute-start(bf16[416,256]{1,0:T(8,128)(2,1)S(1)} %get-tuple-element.122), channel_id=1, source_target_pairs={{0,4},{1,5},{2,6},{3,7},{4,0},{5,1},{6,2},{7,3},{8,12},{9,13},{10,... | collective-permute-start | bytes 638984 | tf_op jit(solution)/shard_map/ppermute | solution.py:606
  38.9 22.9 %collective-permute-start.3 = (bf16[416,256]{1,0:T(8,128)(2,1)S(1)}, bf16[416,256]{1,0:T(8,128)(2,1)S(1)}, u32[]{:S(2)}, u32[]{:S(2)}) collective-permute-start(bf16[416,256]{1,0:T(8,128)(2,1)S(1)} %get-tuple-element.123), channel_id=1, source_target_pairs={{0,6},{1,7},{2,4},{3,5},{4,2},{5,3},{6,0},{7,1},{8,14},{9,15},{10,... | collective-permute-start | bytes 638984 | tf_op jit(solution)/shard_map/ppermute | solution.py:606
  61.9 4.7 %collective-permute-start.4 = (bf16[1664,256]{1,0:T(8,128)(2,1)S(1)}, bf16[1664,256]{1,0:T(8,128)(2,1)S(1)}, u32[]{:S(2)}, u32[]{:S(2)}) collective-permute-start(bf16[1664,256]{1,0:T(8,128)(2,1)S(1)} %get-tuple-element.132), channel_id=1, source_target_pairs={{0,1},{1,0},{2,3},{3,2},{4,5},{5,4},{6,7},{7,6},{8,9},{9,8},{10,11... | collective-permute-start | bytes 2555912 | tf_op jit(solution)/shard_map/ppermute | solution.py:606
  62.2 8.1 %collective-permute-start.8 = (bf16[104,256]{1,0:T(8,128)(2,1)S(1)}, bf16[104,256]{1,0:T(8,128)(2,1)S(1)}, u32[]{:S(2)}, u32[]{:S(2)}) collective-permute-start(bf16[104,256]{1,0:T(8,128)(2,1)S(1)} %get-tuple-element.134), channel_id=1, source_target_pairs={{0,8},{1,9},{2,10},{3,11},{4,12},{5,13},{6,14},{7,15},{8,0},{9,1},... | collective-permute-start | bytes 159752 | tf_op jit(solution)/shard_map/ppermute | solution.py:606
  64.0 6.5 %collective-permute-start.9 = (bf16[104,256]{1,0:T(8,128)(2,1)S(1)}, bf16[104,256]{1,0:T(8,128)(2,1)S(1)}, u32[]{:S(2)}, u32[]{:S(2)}) collective-permute-start(bf16[104,256]{1,0:T(8,128)(2,1)S(1)} %get-tuple-element.135), channel_id=1, source_target_pairs={{0,16},{1,17},{2,18},{3,19},{4,20},{5,21},{6,22},{7,23},{8,24},{9,... | collective-permute-start | bytes 159752 | tf_op jit(solution)/shard_map/ppermute | solution.py:606
  66.4 5.9 %collective-permute-start.10 = (bf16[104,256]{1,0:T(8,128)(2,1)S(1)}, bf16[104,256]{1,0:T(8,128)(2,1)S(1)}, u32[]{:S(2)}, u32[]{:S(2)}) collective-permute-start(bf16[104,256]{1,0:T(8,128)(2,1)S(1)} %get-tuple-element.136), channel_id=1, source_target_pairs={{0,24},{1,25},{2,26},{3,27},{4,28},{5,29},{6,30},{7,31},{8,16},{9,... | collective-permute-start | bytes 159752 | tf_op jit(solution)/shard_map/ppermute | solution.py:606
  67.0 8.2 %collective-permute-start.5 = (bf16[416,256]{1,0:T(8,128)(2,1)S(1)}, bf16[416,256]{1,0:T(8,128)(2,1)S(1)}, u32[]{:S(2)}, u32[]{:S(2)}) collective-permute-start(bf16[416,256]{1,0:T(8,128)(2,1)S(1)} %get-tuple-element.140), channel_id=1, source_target_pairs={{0,2},{1,3},{2,0},{3,1},{4,6},{5,7},{6,4},{7,5},{8,10},{9,11},{10,... | collective-permute-start | bytes 638984 | tf_op jit(solution)/shard_map/ppermute | solution.py:606
  68.8 11.1 %collective-permute-start.6 = (bf16[416,256]{1,0:T(8,128)(2,1)S(1)}, bf16[416,256]{1,0:T(8,128)(2,1)S(1)}, u32[]{:S(2)}, u32[]{:S(2)}) collective-permute-start(bf16[416,256]{1,0:T(8,128)(2,1)S(1)} %get-tuple-element.141), channel_id=1, source_target_pairs={{0,4},{1,5},{2,6},{3,7},{4,0},{5,1},{6,2},{7,3},{8,12},{9,13},{10,... | collective-permute-start | bytes 638984 | tf_op jit(solution)/shard_map/ppermute | solution.py:606
  70.2 9.6 %collective-permute-start.7 = (bf16[416,256]{1,0:T(8,128)(2,1)S(1)}, bf16[416,256]{1,0:T(8,128)(2,1)S(1)}, u32[]{:S(2)}, u32[]{:S(2)}) collective-permute-start(bf16[416,256]{1,0:T(8,128)(2,1)S(1)} %get-tuple-element.142), channel_id=1, source_target_pairs={{0,6},{1,7},{2,4},{3,5},{4,2},{5,3},{6,0},{7,1},{8,14},{9,15},{10,... | collective-permute-start | bytes 638984 | tf_op jit(solution)/shard_map/ppermute | solution.py:606
  72.3 11.6 %collective-permute-start.16 = (bf16[104,256]{1,0:T(8,128)(2,1)S(1)}, bf16[104,256]{1,0:T(8,128)(2,1)S(1)}, u32[]{:S(2)}, u32[]{:S(2)}) collective-permute-start(bf16[104,256]{1,0:T(8,128)(2,1)S(1)} %add_convert_fusion.1), channel_id=1, source_target_pairs={{0,24},{1,25},{2,26},{3,27},{4,28},{5,29},{6,30},{7,31},{8,16},{9,... | collective-permute-start | bytes 159752 | tf_op jit(solution)/shard_map/ppermute | solution.py:606
  74.2 10.3 %collective-permute-start.15 = (bf16[104,256]{1,0:T(8,128)(2,1)S(1)}, bf16[104,256]{1,0:T(8,128)(2,1)S(1)}, u32[]{:S(2)}, u32[]{:S(2)}) collective-permute-start(bf16[104,256]{1,0:T(8,128)(2,1)S(1)} %add_convert_fusion.1), channel_id=1, source_target_pairs={{0,16},{1,17},{2,18},{3,19},{4,20},{5,21},{6,22},{7,23},{8,24},{9,... | collective-permute-start | bytes 159752 | tf_op jit(solution)/shard_map/ppermute | solution.py:606
  75.2 9.3 %collective-permute-start.14 = (bf16[104,256]{1,0:T(8,128)(2,1)S(1)}, bf16[104,256]{1,0:T(8,128)(2,1)S(1)}, u32[]{:S(2)}, u32[]{:S(2)}) collective-permute-start(bf16[104,256]{1,0:T(8,128)(2,1)S(1)} %add_convert_fusion.1), channel_id=1, source_target_pairs={{0,8},{1,9},{2,10},{3,11},{4,12},{5,13},{6,14},{7,15},{8,0},{9,1},... | collective-permute-start | bytes 159752 | tf_op jit(solution)/shard_map/ppermute | solution.py:606
  80.0 7.2 %collective-permute-start.11 = (bf16[104,256]{1,0:T(8,128)(2,1)S(1)}, bf16[104,256]{1,0:T(8,128)(2,1)S(1)}, u32[]{:S(2)}, u32[]{:S(2)}) collective-permute-start(bf16[104,256]{1,0:T(8,128)(2,1)S(1)} %get-tuple-element.152), channel_id=1, source_target_pairs={{0,8},{1,9},{2,10},{3,11},{4,12},{5,13},{6,14},{7,15},{8,0},{9,1},... | collective-permute-start | bytes 159752 | tf_op jit(solution)/shard_map/ppermute | solution.py:606
  80.7 7.5 %collective-permute-start.12 = (bf16[104,256]{1,0:T(8,128)(2,1)S(1)}, bf16[104,256]{1,0:T(8,128)(2,1)S(1)}, u32[]{:S(2)}, u32[]{:S(2)}) collective-permute-start(bf16[104,256]{1,0:T(8,128)(2,1)S(1)} %get-tuple-element.153), channel_id=1, source_target_pairs={{0,16},{1,17},{2,18},{3,19},{4,20},{5,21},{6,22},{7,23},{8,24},{9,... | collective-permute-start | bytes 159752 | tf_op jit(solution)/shard_map/ppermute | solution.py:606
  84.0 5.9 %collective-permute-start.13 = (bf16[104,256]{1,0:T(8,128)(2,1)S(1)}, bf16[104,256]{1,0:T(8,128)(2,1)S(1)}, u32[]{:S(2)}, u32[]{:S(2)}) collective-permute-start(bf16[104,256]{1,0:T(8,128)(2,1)S(1)} %get-tuple-element.154), channel_id=1, source_target_pairs={{0,24},{1,25},{2,26},{3,27},{4,28},{5,29},{6,30},{7,31},{8,16},{9,... | collective-permute-start | bytes 159752 | tf_op jit(solution)/shard_map/ppermute | solution.py:606
  84.6 8.2 %collective-permute-start.22 = (bf16[416,256]{1,0:T(8,128)(2,1)S(1)}, bf16[416,256]{1,0:T(8,128)(2,1)S(1)}, u32[]{:S(2)}, u32[]{:S(2)}) collective-permute-start(bf16[416,256]{1,0:T(8,128)(2,1)S(1)} %bitcast.48), channel_id=1, source_target_pairs={{0,6},{1,7},{2,4},{3,5},{4,2},{5,3},{6,0},{7,1},{8,14},{9,15},{10,... | collective-permute-start | bytes 638984 | tf_op jit(solution)/shard_map/ppermute | solution.py:606
  86.1 8.8 %collective-permute-start.21 = (bf16[416,256]{1,0:T(8,128)(2,1)S(1)}, bf16[416,256]{1,0:T(8,128)(2,1)S(1)}, u32[]{:S(2)}, u32[]{:S(2)}) collective-permute-start(bf16[416,256]{1,0:T(8,128)(2,1)S(1)} %bitcast.49), channel_id=1, source_target_pairs={{0,4},{1,5},{2,6},{3,7},{4,0},{5,1},{6,2},{7,3},{8,12},{9,13},{10,... | collective-permute-start | bytes 638984 | tf_op jit(solution)/shard_map/ppermute | solution.py:606
  87.3 7.6 %collective-permute-start.20 = (bf16[416,256]{1,0:T(8,128)(2,1)S(1)}, bf16[416,256]{1,0:T(8,128)(2,1)S(1)}, u32[]{:S(2)}, u32[]{:S(2)}) collective-permute-start(bf16[416,256]{1,0:T(8,128)(2,1)S(1)} %bitcast.50), channel_id=1, source_target_pairs={{0,2},{1,3},{2,0},{3,1},{4,6},{5,7},{6,4},{7,5},{8,10},{9,11},{10,... | collective-permute-start | bytes 638984 | tf_op jit(solution)/shard_map/ppermute | solution.py:606
  90.0 6.0 %collective-permute-start.19 = (bf16[104,256]{1,0:T(8,128)(2,1)S(1)}, bf16[104,256]{1,0:T(8,128)(2,1)S(1)}, u32[]{:S(2)}, u32[]{:S(2)}) collective-permute-start(bf16[104,256]{1,0:T(8,128)(2,1)S(1)} %add_convert_fusion), channel_id=1, source_target_pairs={{0,24},{1,25},{2,26},{3,27},{4,28},{5,29},{6,30},{7,31},{8,16},{9,... | collective-permute-start | bytes 159752 | tf_op jit(solution)/shard_map/ppermute | solution.py:606
  91.6 5.6 %collective-permute-start.18 = (bf16[104,256]{1,0:T(8,128)(2,1)S(1)}, bf16[104,256]{1,0:T(8,128)(2,1)S(1)}, u32[]{:S(2)}, u32[]{:S(2)}) collective-permute-start(bf16[104,256]{1,0:T(8,128)(2,1)S(1)} %add_convert_fusion), channel_id=1, source_target_pairs={{0,16},{1,17},{2,18},{3,19},{4,20},{5,21},{6,22},{7,23},{8,24},{9,... | collective-permute-start | bytes 159752 | tf_op jit(solution)/shard_map/ppermute | solution.py:606
  92.8 4.7 %collective-permute-start.17 = (bf16[104,256]{1,0:T(8,128)(2,1)S(1)}, bf16[104,256]{1,0:T(8,128)(2,1)S(1)}, u32[]{:S(2)}, u32[]{:S(2)}) collective-permute-start(bf16[104,256]{1,0:T(8,128)(2,1)S(1)} %add_convert_fusion), channel_id=1, source_target_pairs={{0,8},{1,9},{2,10},{3,11},{4,12},{5,13},{6,14},{7,15},{8,0},{9,1},... | collective-permute-start | bytes 159752 | tf_op jit(solution)/shard_map/ppermute | solution.py:606
  95.1 6.6 %collective-permute-start.26 = (bf16[1664,256]{1,0:T(8,128)(2,1)S(1)}, bf16[1664,256]{1,0:T(8,128)(2,1)S(1)}, u32[]{:S(2)}, u32[]{:S(2)}) collective-permute-start(bf16[1664,256]{1,0:T(8,128)(2,1)S(1)} %bitcast.41), channel_id=1, source_target_pairs={{0,1},{1,0},{2,3},{3,2},{4,5},{5,4},{6,7},{7,6},{8,9},{9,8},{10,11... | collective-permute-start | bytes 2555912 | tf_op jit(solution)/shard_map/ppermute | solution.py:606
  97.6 8.7 %collective-permute-start.25 = (bf16[416,256]{1,0:T(8,128)(2,1)S(1)}, bf16[416,256]{1,0:T(8,128)(2,1)S(1)}, u32[]{:S(2)}, u32[]{:S(2)}) collective-permute-start(bf16[416,256]{1,0:T(8,128)(2,1)S(1)} %bitcast.43), channel_id=1, source_target_pairs={{0,6},{1,7},{2,4},{3,5},{4,2},{5,3},{6,0},{7,1},{8,14},{9,15},{10,... | collective-permute-start | bytes 638984 | tf_op jit(solution)/shard_map/ppermute | solution.py:606
  99.1 9.4 %collective-permute-start.24 = (bf16[416,256]{1,0:T(8,128)(2,1)S(1)}, bf16[416,256]{1,0:T(8,128)(2,1)S(1)}, u32[]{:S(2)}, u32[]{:S(2)}) collective-permute-start(bf16[416,256]{1,0:T(8,128)(2,1)S(1)} %bitcast.44), channel_id=1, source_target_pairs={{0,4},{1,5},{2,6},{3,7},{4,0},{5,1},{6,2},{7,3},{8,12},{9,13},{10,... | collective-permute-start | bytes 638984 | tf_op jit(solution)/shard_map/ppermute | solution.py:606
  100.5 8.0 %collective-permute-start.23 = (bf16[416,256]{1,0:T(8,128)(2,1)S(1)}, bf16[416,256]{1,0:T(8,128)(2,1)S(1)}, u32[]{:S(2)}, u32[]{:S(2)}) collective-permute-start(bf16[416,256]{1,0:T(8,128)(2,1)S(1)} %bitcast.45), channel_id=1, source_target_pairs={{0,2},{1,3},{2,0},{3,1},{4,6},{5,7},{6,4},{7,5},{8,10},{9,11},{10,... | collective-permute-start | bytes 638984 | tf_op jit(solution)/shard_map/ppermute | solution.py:606
  101.7 7.3 %collective-permute-start.27 = (bf16[416,256]{1,0:T(8,128)(2,1)S(1)}, bf16[416,256]{1,0:T(8,128)(2,1)S(1)}, u32[]{:S(2)}, u32[]{:S(2)}) collective-permute-start(bf16[416,256]{1,0:T(8,128)(2,1)S(1)} %bitcast.46), channel_id=1, source_target_pairs={{0,1},{1,0},{2,3},{3,2},{4,5},{5,4},{6,7},{7,6},{8,9},{9,8},{10,11... | collective-permute-start | bytes 638984 | tf_op jit(solution)/shard_map/ppermute | solution.py:606
  108.5 1.5 %collective-permute-start.28 = (bf16[416,256]{1,0:T(8,128)(2,1)S(1)}, bf16[416,256]{1,0:T(8,128)(2,1)S(1)}, u32[]{:S(2)}, u32[]{:S(2)}) collective-permute-start(bf16[416,256]{1,0:T(8,128)(2,1)S(1)} %collective-permute-done.23.refs_1_), channel_id=1, source_target_pairs={{0,1},{1,0},{2,3},{3,2},{4,5},{5,4},{6,7},{7,6},{8,9},{9,8},{10,11... | collective-permute-start | bytes 638984 | tf_op jit(solution)/shard_map/ppermute | solution.py:606
  108.5 1.8 %collective-permute-start.29 = (bf16[416,256]{1,0:T(8,128)(2,1)S(1)}, bf16[416,256]{1,0:T(8,128)(2,1)S(1)}, u32[]{:S(2)}, u32[]{:S(2)}) collective-permute-start(bf16[416,256]{1,0:T(8,128)(2,1)S(1)} %collective-permute-done.24.refs_2_), channel_id=1, source_target_pairs={{0,1},{1,0},{2,3},{3,2},{4,5},{5,4},{6,7},{7,6},{8,9},{9,8},{10,11... | collective-permute-start | bytes 638984 | tf_op jit(solution)/shard_map/ppermute | solution.py:606
  109.0 1.6 %collective-permute-start.30 = (bf16[416,256]{1,0:T(8,128)(2,1)S(1)}, bf16[416,256]{1,0:T(8,128)(2,1)S(1)}, u32[]{:S(2)}, u32[]{:S(2)}) collective-permute-start(bf16[416,256]{1,0:T(8,128)(2,1)S(1)} %collective-permute-done.25.refs_3_), channel_id=1, source_target_pairs={{0,1},{1,0},{2,3},{3,2},{4,5},{5,4},{6,7},{7,6},{8,9},{9,8},{10,11... | collective-permute-start | bytes 638984 | tf_op jit(solution)/shard_map/ppermute | solution.py:606

commit v8 on v7

--- a/solution.py
+++ b/solution.py
@@ -16,8 +16,9 @@
 VECTOR_ROWS = 16
 HALF = 6 * WIDTH + 128
 GROUP_ROWS = 2 * HALF
+LANES = 128
 SOFT = 128
-NORM = 64
+NORM = 32
 GELU = 32
 ln_eps = 1e-06
 score_scale = 0.125
@@ -42,11 +43,8 @@
 
 
 def row_loop(rows, chunk, step):
-    def body(index, carry):
-        step(pl.multiple_of(index * chunk, chunk))
-        return carry
-
-    lax.fori_loop(0, rows // chunk, body, 0, unroll=rows // chunk)
+    for row in range(0, rows, chunk):
+        step(row)
 
 
 def vector(ref, which):
@@ -57,16 +55,12 @@
     return lax.broadcasted_iota(jnp.int32, (rows, WIDTH), 1) // HEAD_DIM
 
 
-def stack_heads(values):
-    head = lane_head(values.shape[0])
-    wide = values.astype(f32)
-    return jnp.concatenate(
-        [jnp.where(head == h, wide, 0.0).astype(bf16) for h in range(HEADS)], axis=0
-    )
-
-
-def one_head(values, h):
-    return jnp.where(lane_head(values.shape[0]) == h, values.astype(f32), 0.0).astype(bf16)
+def one_head(values, h, scale=1.0):
+    return jnp.where(lane_head(values.shape[0]) == h, values.astype(f32) * scale, 0.0).astype(bf16)
+
+
+def some_heads(values, first, last, scale=1.0):
+    return jnp.concatenate([one_head(values, h, scale) for h in range(first, last)], axis=0)
 
 
 def pick_heads(stacked, rows):
@@ -92,8 +86,8 @@
     return centered * inverse, inverse
 
 
-def masked_softmax(scores, size):
-    part = scores * score_scale
+def masked_softmax(scores, size, scale=score_scale):
+    part = scores * scale if scale != 1.0 else scores
     key = lax.broadcasted_iota(jnp.int32, part.shape, 1)
     part = jnp.where(key < size, part, masked_score)
     part = jnp.exp(part - jnp.max(part, axis=1, keepdims=True))
@@ -167,7 +161,36 @@
     lax.fori_loop(0, cls_ref.shape[0], store, 0)
 
 
+def head_groups(length):
+    together = max(1, WIDTH // length)
+    return [(h, h + together, slice(h * length, (h + together) * length)) for h in range(0, HEADS, together)]
+
+
 def attend_kernel(which, seqs, length, len_ref, x_ref, wqkv_ref, qb_ref, vb_ref, qkv_ref, p_ref, ctx_ref, score_ref, prob_ref):
+    step = pl.program_id(0)
+    x = x_ref[...]
+    qkv_ref[:, :WIDTH] = (dot(x, wqkv_ref[:, :WIDTH]) + vector(qb_ref, which)).astype(bf16)
+    qkv_ref[:, WIDTH : 2 * WIDTH] = dot(x, wqkv_ref[:, WIDTH : 2 * WIDTH]).astype(bf16)
+    qkv_ref[:, 2 * WIDTH :] = (dot(x, wqkv_ref[:, 2 * WIDTH :]) + vector(vb_ref, which)).astype(bf16)
+    for s in range(seqs):
+        span = slice(s * length, (s + 1) * length)
+        size = len_ref[step * seqs + s]
+        keys = qkv_ref[span, WIDTH : 2 * WIDTH]
+        for first, last, columns in head_groups(length):
+            score_ref[span, columns] = dot_nt(keys, some_heads(qkv_ref[span, :WIDTH], first, last, score_scale))
+            for lane in range(columns.start, columns.stop, LANES):
+                here = slice(lane, lane + LANES)
+                part = score_ref[span, here]
+                key = lax.broadcasted_iota(jnp.int32, part.shape, 0)
+                part = jnp.where(key < size, part, masked_score)
+                part = jnp.exp(part - jnp.max(part, axis=0, keepdims=True))
+                prob = part * (1.0 / jnp.sum(part, axis=0, keepdims=True))
+                p_ref[span, here] = prob
+                prob_ref[span, here] = prob.astype(bf16)
+        ctx_ref[span, :] = pick_heads(dot_tn(prob_ref[span, :], qkv_ref[span, 2 * WIDTH :]), length).astype(bf16)
+
+
+def attend_long_kernel(which, seqs, length, len_ref, x_ref, wqkv_ref, qb_ref, vb_ref, qkv_ref, p_ref, ctx_ref, score_ref, prob_ref):
     step = pl.program_id(0)
     x = x_ref[...]
     qkv_ref[:, :WIDTH] = (dot(x, wqkv_ref[:, :WIDTH]) + vector(qb_ref, which)).astype(bf16)
@@ -181,24 +204,22 @@
         queries = qkv_ref[span, :WIDTH]
         for h in range(HEADS):
             start = s * stack_rows + h * length
-            score_ref[start : start + length, :] = dot_nt(one_head(queries, h), qkv_ref[span, WIDTH : 2 * WIDTH])
+            score_ref[start : start + length, :] = dot_nt(one_head(queries, h, score_scale), qkv_ref[span, WIDTH : 2 * WIDTH])
 
             def softmax(row):
-                here = pl.ds(start + row, min(SOFT, length))
-                prob = masked_softmax(score_ref[here, :], size)
+                here = pl.ds(start + row, SOFT)
+                prob = masked_softmax(score_ref[here, :], size, 1.0)
                 p_ref[here, :] = prob
                 prob_ref[here, :] = prob.astype(bf16)
 
-            row_loop(length, min(SOFT, length), softmax)
+            row_loop(length, SOFT, softmax)
         ctx_ref[span, :] = pick_heads(dot(prob_ref[stack, :], qkv_ref[span, 2 * WIDTH :]), length).astype(bf16)
 
 
 def forward_phase(
-    which, seqs, length, first,
-    len_ref, x_ref, wo_ref, ob_ref, g1_ref, b1_ref, w1_ref, hb_ref, w2_ref, fb_ref, g2_ref, b2_ref,
-    out_ref, ctx_ref, n1_ref, r1_ref, nb_ref, gp_ref, act_ref, n2_ref, r2_ref, wide_ref,
+    which, rows, x_ref, wo_ref, ob_ref, g1_ref, b1_ref, w1_ref, hb_ref, w2_ref,
+    ctx_ref, n1_ref, r1_ref, nb_ref, gp_ref, act_ref, n2_ref, wide_ref,
 ):
-    rows = seqs * length
     n2_ref[...] = dot(ctx_ref[...], wo_ref[...])
     ob, g1, b1 = vector(ob_ref, which), vector(g1_ref, which), vector(b1_ref, which)
 
@@ -223,41 +244,34 @@
 
         row_loop(rows, GELU, gelu)
     n2_ref[...] = dot(act_ref[...], w2_ref[...])
-    fb, g2, b2 = vector(fb_ref, which), vector(g2_ref, which), vector(b2_ref, which)
-    for s in range(seqs):
-        size = len_ref[first + s]
-
-        def second_norm(row):
-            here = pl.ds(s * length + row, NORM)
-            unit, inverse = normalize((n1_ref[here, :] * g1 + b1) + (n2_ref[here, :] + fb))
-            n2_ref[here, :] = unit
-            r2_ref[here, :] = inverse
-            position = row + lax.broadcasted_iota(jnp.int32, (NORM, WIDTH), 0)
-            out_ref[here, :] = jnp.where(position < size, unit * g2 + b2, 0.0).astype(bf16)
-
-        row_loop(length, NORM, second_norm)
 
 
 def add_row(vec_ref, row, values):
-    vec_ref[row : row + 1, :] = vec_ref[row : row + 1, :] + jnp.sum(values, axis=0, keepdims=True)
-
-
-def ffn_phase(which, seqs, length, first, len_ref, cls_ref, cot_ref, n2_ref, r2_ref, gp_ref, w2_ref, g2_ref, two_ref, gffn_ref, gpre_ref, vec_ref, wide_ref):
-    g2 = vector(g2_ref, which)
+    here = slice(row * PAD, (row + 1) * PAD)
+    vec_ref[here, :] = vec_ref[here, :] + jnp.sum(values.reshape(-1, PAD, WIDTH), axis=0)
+
+
+def ffn_phase(which, seqs, length, first, len_ref, cls_ref, cot_ref, n1_ref, n2_ref, gp_ref, w2_ref, g1_ref, b1_ref, fb_ref, g2_ref, b2_ref, out_ref, two_ref, gffn_ref, gpre_ref, vec_ref, wide_ref):
+    g1, g2, b2 = vector(g1_ref, which), vector(g2_ref, which), vector(b2_ref, which)
+    shift = vector(b1_ref, which) + vector(fb_ref, which)
     for s in range(seqs):
         size = len_ref[first + s]
         cls_row = cls_ref[pl.ds(first + s, 1), :]
 
-        def norm_back(row):
+        def output_norm(row):
             here = pl.ds(s * length + row, NORM)
-            position = row + lax.broadcasted_iota(jnp.int32, (NORM, WIDTH), 0)
-            grad = cot_ref[here, :].astype(f32) + jnp.where(position == 0, cls_row, 0.0)
-            grad = jnp.where(position < size, grad, 0.0)
-            unit = n2_ref[here, :]
+            inside = row + lax.broadcasted_iota(jnp.int32, (NORM, WIDTH), 0) < size
+            unit, inverse = normalize(n1_ref[here, :] * g1 + (n2_ref[here, :] + shift))
+            out_ref[here, :] = jnp.where(inside, unit * g2 + b2, 0.0).astype(bf16)
+            grad = cot_ref[here, :].astype(f32)
+            if row == 0:
+                grad = grad + jnp.where(lax.broadcasted_iota(jnp.int32, (NORM, WIDTH), 0) == 0, cls_row, 0.0)
+            grad = jnp.where(inside, grad, 0.0)
             scaled = grad * g2
+            slope = scaled * unit
             first_mean = jnp.mean(scaled, axis=1, keepdims=True)
-            second_mean = jnp.mean(scaled * unit, axis=1, keepdims=True)
-            two = r2_ref[here, :] * (scaled - first_mean - unit * second_mean)
+            second_mean = jnp.mean(slope, axis=1, keepdims=True)
+            two = inverse * (scaled - first_mean - unit * second_mean)
             low = two.astype(bf16)
             two_ref[here, :] = two
             gffn_ref[here, :] = low
@@ -265,7 +279,7 @@
             add_row(vec_ref, FFN_SHIFT, grad)
             add_row(vec_ref, DOWN_BIAS, low.astype(f32))
 
-        row_loop(length, NORM, norm_back)
+        row_loop(length, NORM, output_norm)
     for j in range(BLOCKS):
         lanes = slice(j * WIDTH, (j + 1) * WIDTH)
         wide_ref[:, lanes] = dot_nt(gffn_ref[...], w2_ref[lanes, :])
@@ -303,6 +317,30 @@
 
 
 def attn_core_phase(seqs, length, dctx_ref, qkv_ref, p_ref, gqkv_ref, vec_ref, dp_ref, ds_ref, pb_ref):
+    for s in range(seqs):
+        span = slice(s * length, (s + 1) * length)
+        values = qkv_ref[span, 2 * WIDTH :]
+        context = some_heads(dctx_ref[span, :], 0, HEADS)
+        for first, last, columns in head_groups(length):
+            dp_ref[span, columns] = dot_nt(values, context[columns])
+            for lane in range(columns.start, columns.stop, LANES):
+                here = slice(lane, lane + LANES)
+                prob = p_ref[span, here]
+                grad = dp_ref[span, here]
+                inner = jnp.sum(prob * grad, axis=0, keepdims=True)
+                ds_ref[span, here] = (prob * (grad - inner)).astype(bf16)
+                pb_ref[span, here] = prob.astype(bf16)
+        queries = some_heads(qkv_ref[span, :WIDTH], 0, HEADS, score_scale)
+        gqkv_ref[span, WIDTH : 2 * WIDTH] = dot(ds_ref[span, :], queries).astype(bf16)
+        grad_v = dot(pb_ref[span, :], context).astype(bf16)
+        gqkv_ref[span, 2 * WIDTH :] = grad_v
+        add_row(vec_ref, VALUE_BIAS, grad_v.astype(f32))
+        grad_q = (pick_heads(dot_tn(ds_ref[span, :], qkv_ref[span, WIDTH : 2 * WIDTH]), length) * score_scale).astype(bf16)
+        gqkv_ref[span, :WIDTH] = grad_q
+        add_row(vec_ref, QUERY_BIAS, grad_q.astype(f32))
+
+
+def attn_core_long(seqs, length, dctx_ref, qkv_ref, p_ref, gqkv_ref, vec_ref, dp_ref, ds_ref, pb_ref):
     stack_rows = HEADS * length
     for s in range(seqs):
         span = slice(s * length, (s + 1) * length)
@@ -313,20 +351,20 @@
             dp_ref[start : start + length, :] = dot_nt(contexts[h], qkv_ref[span, 2 * WIDTH :])
 
             def softmax_back(row):
-                here = pl.ds(start + row, min(SOFT, length))
+                here = pl.ds(start + row, SOFT)
                 prob = p_ref[here, :]
                 grad = dp_ref[here, :]
                 inner = jnp.sum(prob * grad, axis=1, keepdims=True)
                 ds_ref[here, :] = (prob * (grad - inner)).astype(bf16)
                 pb_ref[here, :] = prob.astype(bf16)
 
-            row_loop(length, min(SOFT, length), softmax_back)
+            row_loop(length, SOFT, softmax_back)
         context = jnp.concatenate(contexts, axis=0)
-        queries = stack_heads(qkv_ref[span, :WIDTH])
+        queries = some_heads(qkv_ref[span, :WIDTH], 0, HEADS, score_scale)
         grad_q = (pick_heads(dot(ds_ref[stack, :], qkv_ref[span, WIDTH : 2 * WIDTH]), length) * score_scale).astype(bf16)
         gqkv_ref[span, :WIDTH] = grad_q
         add_row(vec_ref, QUERY_BIAS, grad_q.astype(f32))
-        gqkv_ref[span, WIDTH : 2 * WIDTH] = (dot_tn(ds_ref[stack, :], queries) * score_scale).astype(bf16)
+        gqkv_ref[span, WIDTH : 2 * WIDTH] = dot_tn(ds_ref[stack, :], queries).astype(bf16)
         grad_v = dot_tn(pb_ref[stack, :], context).astype(bf16)
         gqkv_ref[span, 2 * WIDTH :] = grad_v
         add_row(vec_ref, VALUE_BIAS, grad_v.astype(f32))
@@ -337,7 +375,7 @@
     bit_ref, len_ref, cls_ref, x_ref, cot_ref, qkv_ref, p_ref, ctx_ref,
     wqkv_ref, wo_ref, ob_ref, g1_ref, b1_ref, w1_ref, hb_ref, w2_ref, fb_ref, g2_ref, b2_ref,
     out_ref, gx_ref, keep_ref, send_ref,
-    acc_ref, vec_ref, n1_ref, r1_ref, nb_ref, gp_ref, act_ref, n2_ref, r2_ref,
+    acc_ref, vec_ref, n1_ref, r1_ref, nb_ref, gp_ref, act_ref, n2_ref,
     wide_ref, score_ref, prob_ref, two_ref, gffn_ref, gpre_ref, one_ref, gatt_ref, dctx_ref, gqkv_ref, ds_ref,
 ):
     rows = seqs * length
@@ -360,24 +398,26 @@
             acc_ref[block_rows(block), :] = value
 
     forward_phase(
-        which, seqs, length, step * seqs,
-        len_ref, x_ref, wo_ref, ob_ref, g1_ref, b1_ref, w1_ref, hb_ref, w2_ref, fb_ref, g2_ref, b2_ref,
-        out_ref, ctx_ref, n1_ref, r1_ref, nb_ref, gp_ref, act_ref, n2_ref, r2_ref, wide_ref,
+        which, rows, x_ref, wo_ref, ob_ref, g1_ref, b1_ref, w1_ref, hb_ref, w2_ref,
+        ctx_ref, n1_ref, r1_ref, nb_ref, gp_ref, act_ref, n2_ref, wide_ref,
     )
-    ffn_phase(which, seqs, length, step * seqs, len_ref, cls_ref, cot_ref, n2_ref, r2_ref, gp_ref, w2_ref, g2_ref, two_ref, gffn_ref, gpre_ref, vec_ref, wide_ref)
+    ffn_phase(which, seqs, length, step * seqs, len_ref, cls_ref, cot_ref, n1_ref, n2_ref, gp_ref, w2_ref, g1_ref, b1_ref, fb_ref, g2_ref, b2_ref, out_ref, two_ref, gffn_ref, gpre_ref, vec_ref, wide_ref)
+    downs = dot_tn(act_ref[...], gffn_ref[...])
+    ups = dot_tn(nb_ref[...], gpre_ref[...])
     for j in range(BLOCKS):
         lanes = slice(j * WIDTH, (j + 1) * WIDTH)
-        add_block(DOWN_BLOCK + j, dot_tn(act_ref[:, lanes], gffn_ref[...]))
-        add_block(UP_BLOCK + j, dot_tn(nb_ref[...], gpre_ref[:, lanes]))
+        add_block(DOWN_BLOCK + j, downs[lanes])
+        add_block(UP_BLOCK + j, ups[:, lanes])
     attn_norm_phase(which, rows, gpre_ref, w1_ref, two_ref, n1_ref, r1_ref, g1_ref, wo_ref, one_ref, gatt_ref, dctx_ref, vec_ref)
     add_block(PROJ_BLOCK, dot_tn(ctx_ref[...], gatt_ref[...]))
-    attn_core_phase(seqs, length, dctx_ref, qkv_ref, p_ref, gqkv_ref, vec_ref, score_ref, ds_ref, prob_ref)
+    attn_core = attn_core_long if seqs == 1 else attn_core_phase
+    attn_core(seqs, length, dctx_ref, qkv_ref, p_ref, gqkv_ref, vec_ref, score_ref, ds_ref, prob_ref)
     for j in range(3):
         add_block(QKV_BLOCK + j, dot_tn(x_ref[...], gqkv_ref[:, j * WIDTH : (j + 1) * WIDTH]))
     gx_ref[...] = (one_ref[...] + dot_nt(gqkv_ref[...], wqkv_ref[...])).astype(bf16)
 
     def finish():
-        acc_ref[VECTOR_START : VECTOR_START + VECTOR_ROWS, :] = vec_ref[...]
+        acc_ref[VECTOR_START : VECTOR_START + VECTOR_ROWS, :] = jnp.sum(vec_ref[...].reshape(VECTOR_ROWS, PAD, WIDTH), axis=1)
         if steps == 1:
             acc_ref[VECTOR_START + VECTOR_ROWS : HALF, :] = jnp.zeros((HALF - VECTOR_START - VECTOR_ROWS, WIDTH), f32)
             acc_ref[HALF + 6 * WIDTH :, :] = jnp.zeros((HALF - 6 * WIDTH, WIDTH), f32)
@@ -540,16 +580,16 @@
     wqkv, qb, vb, *_ = weights
     rows = seqs * length
     total = steps * rows
-    stack = seqs * HEADS * length
+    block = (HEADS * length, length) if seqs == 1 else (rows, HEADS * length)
     return pl.pallas_call(
-        functools.partial(attend_kernel, which, seqs, length),
+        functools.partial(attend_long_kernel if seqs == 1 else attend_kernel, which, seqs, length),
         out_shape=[
-            pltpu.HBM((total, 3 * WIDTH), bf16), pltpu.HBM((steps * stack, length), f32), pltpu.HBM((total, WIDTH), bf16),
+            pltpu.HBM((total, 3 * WIDTH), bf16), pltpu.HBM((steps * block[0], block[1]), f32), pltpu.HBM((total, WIDTH), bf16),
         ],
         grid=(steps,),
         in_specs=[smem(), rows_of(rows, WIDTH), part_of(which, (WIDTH, 3 * WIDTH)), pair(WIDTH), pair(WIDTH)],
-        out_specs=[rows_of(rows, 3 * WIDTH), rows_of(stack, length), rows_of(rows, WIDTH)],
-        scratch_shapes=[pltpu.VMEM((stack, length), f32), pltpu.VMEM((stack, length), bf16)],
+        out_specs=[rows_of(rows, 3 * WIDTH), rows_of(*block), rows_of(rows, WIDTH)],
+        scratch_shapes=[pltpu.VMEM(block, f32), pltpu.VMEM(block, bf16)],
         compiler_params=params(),
         cost_estimate=cost(total * 2 * 400000, total * 6000),
         name="attend",
@@ -559,7 +599,7 @@
 def layer(which, steps, seqs, length, bit, lengths, cls_grad, x, cot, attended, weights):
     rows = seqs * length
     total = steps * rows
-    stack = seqs * HEADS * length
+    block = (HEADS * length, length) if seqs == 1 else (rows, HEADS * length)
     wqkv, _, _, *rest = weights
     return pl.pallas_call(
         functools.partial(layer_kernel, which, steps, seqs, length),
@@ -567,20 +607,20 @@
         grid=(steps,),
         in_specs=[
             smem(), smem(), whole((PAD, WIDTH)), rows_of(rows, WIDTH), rows_of(rows, WIDTH),
-            rows_of(rows, 3 * WIDTH), rows_of(stack, length), rows_of(rows, WIDTH),
+            rows_of(rows, 3 * WIDTH), rows_of(*block), rows_of(rows, WIDTH),
             part_of(which, (WIDTH, 3 * WIDTH)), part_of(which, (WIDTH, WIDTH)),
             pair(WIDTH), pair(WIDTH), pair(WIDTH), part_of(which, (WIDTH, HIDDEN)), pair(HIDDEN),
             part_of(which, (HIDDEN, WIDTH)), pair(WIDTH), pair(WIDTH), pair(WIDTH),
         ],
         out_specs=[rows_of(rows, WIDTH), rows_of(rows, WIDTH), whole((HALF, WIDTH)), whole((HALF, WIDTH))],
         scratch_shapes=[
-            pltpu.VMEM((GROUP_ROWS, WIDTH), f32), pltpu.VMEM((VECTOR_ROWS, WIDTH), f32),
+            pltpu.VMEM((GROUP_ROWS, WIDTH), f32), pltpu.VMEM((VECTOR_ROWS * PAD, WIDTH), f32),
             pltpu.VMEM((rows, WIDTH), f32), pltpu.VMEM((rows, 1), f32), pltpu.VMEM((rows, WIDTH), bf16),
             pltpu.VMEM((rows, HIDDEN), f32), pltpu.VMEM((rows, HIDDEN), bf16), pltpu.VMEM((rows, WIDTH), f32),
-            pltpu.VMEM((rows, 1), f32), pltpu.VMEM((rows, HIDDEN), f32), pltpu.VMEM((stack, length), f32),
-            pltpu.VMEM((stack, length), bf16), pltpu.VMEM((rows, WIDTH), f32), pltpu.VMEM((rows, WIDTH), bf16),
+            pltpu.VMEM((rows, HIDDEN), f32), pltpu.VMEM(block, f32),
+            pltpu.VMEM(block, bf16), pltpu.VMEM((rows, WIDTH), f32), pltpu.VMEM((rows, WIDTH), bf16),
             pltpu.VMEM((rows, HIDDEN), bf16), pltpu.VMEM((rows, WIDTH), f32), pltpu.VMEM((rows, WIDTH), bf16),
-            pltpu.VMEM((rows, WIDTH), bf16), pltpu.VMEM((rows, 3 * WIDTH), bf16), pltpu.VMEM((stack, length), bf16),
+            pltpu.VMEM((rows, WIDTH), bf16), pltpu.VMEM((rows, 3 * WIDTH), bf16), pltpu.VMEM(block, bf16),
         ],
         compiler_params=params(),
         cost_estimate=cost(total * 6 * 800000, total * 4000),

time: 113 us -> 110 us (0.973)
  Pallas kernels: 51.8 us -> 48.5 us
    pallas_call x2, Pallas kernels: 30.9 us -> 27.8 us  [layer(): pl.pallas_call(functools.partial(layer_kernel, which, steps, seqs, length...]
  transfers between devices with their start and end apart: 32 -> 32, of which waited for: 15 -> 16; matrix products, arithmetic and copies ran while one was open for 1% -> 1% of each run, Pallas kernels for 31% -> 30%
where the time goes in v8:
time: 110 us; the launch traced here: 109 us
  Pallas kernels  48.5 us (44%)
  starting transfers between devices  37.7 us (34%)
  waiting for transfers between devices  20.6 us (19%)
  local copies, waits for them, and re-layouts  1.19 us (1%)
  between operations  1.13 us (1%)
    ppermute x31, starting transfers between devices, partner_send(): return lax.ppermute(values, 'dp', [(i, i ^ mask) for i in range(count)])  30.4 us
    pallas_call x2, Pallas kernels, layer(): pl.pallas_call(functools.partial(layer_kernel, which, steps, seqs, length...  27.8 us
    ppermute x31, waiting for transfers between devices, partner_send(): return lax.ppermute(values, 'dp', [(i, i ^ mask) for i in range(count)])  20.4 us
    pallas_call x2, Pallas kernels, attend(): pl.pallas_call(functools.partial(attend_long_kernel if seqs == 1 else att...  10 us
    all_to_all x1, starting transfers between devices, body(): all_cls = lax.all_to_all(own_cls, 'dp', 0, 0, tiled=True)  7.3 us
    pallas_call x1, Pallas kernels, first_call(): pl.pallas_call(functools.partial(first_kernel, local), out_shape=shape((c...  5.22 us
  transfers between devices with their start and end apart: 32, of which 16 were waited for; matrix products, arithmetic and copies ran while one was open for 1% of the time, Pallas kernels for 30%

profile of v8, /device:TPU:0, one launch (start us, length us, event | category | flops | bytes accessed | tf_op | source)
XLA Modules:
  0.0 109.2 jit_solution(2827198175383340003)
XLA Ops:
  0.7 5.2 %first.1 = bf16[32,16,256]{2,1,0:T(8,128)(2,1)} custom-call(s32[5]{0:T(128)} %len_ref.6, s32[5]{0:T(128)} %len_ref.7, bf16[320,256]{1,0:T(8,128)(2,1)} %bitcast.52, bf16[1280,256]{1,0:T(8,128)(2,1)} %bitcast.55, bf16[2,256,768]{2,1,0:T(8,128)(2,1)} %wqkv_ref.9, bf16[2,256]{1,0:T(2,128)(2,1)} %qb_ref.5, bf16[2,256]{1,0:T(2,128)(2,1)} %vb_ref.5, ...), custom_call_target="tpu_custom_call" | custom-call | tf_op jit(solution)/shard_map/first/pallas_call | solution.py:567
  5.9 7.3 %all-to-all-start = ((bf16[32,16,256]{2,1,0:T(8,128)(2,1)}), bf16[32,16,256]{2,1,0:T(8,128)(2,1)S(1)}, u32[]{:S(2)}, u32[]{:S(2)}) async-start(bf16[32,16,256]{2,1,0:T(8,128)(2,1)} %first.1), calls=%async_computation | async-start | bytes 524288 | tf_op jit(solution)/shard_map/all_to_all | solution.py:731
  13.6 3.1 %attend.3 = (bf16[320,768]{1,0:T(8,128)(2,1)}, f32[320,256]{1,0:T(8,128)}, bf16[320,256]{1,0:T(8,128)(2,1)}) custom-call(s32[5]{0:T(128)S(1)} %copy-done, bf16[320,256]{1,0:T(8,128)(2,1)} %bitcast.53, bf16[2,256,768]{2,1,0:T(8,128)(2,1)} %wqkv_ref.9, bf16[2,256]{1,0:T(2,128)(2,1)} %qb_ref.5, bf16[2,256]{1,0:T(2,128)(2,1)} %vb_ref.5), custom_call_target="tpu_custom_call" | custom-call | flops 256000000 | bytes 1920000 | tf_op jit(solution)/shard_map/attend/pallas_call | solution.py:584
  16.7 6.9 %attend.2 = (bf16[1280,768]{1,0:T(8,128)(2,1)}, f32[5120,256]{1,0:T(8,128)}, bf16[1280,256]{1,0:T(8,128)(2,1)}) custom-call(s32[5]{0:T(128)S(1)} %copy-done.1, bf16[1280,256]{1,0:T(8,128)(2,1)} %bitcast.56, bf16[2,256,768]{2,1,0:T(8,128)(2,1)} %wqkv_ref.9, bf16[2,256]{1,0:T(2,128)(2,1)} %qb_ref.5, bf16[2,256]{1,0:T(2,128)(2,1)} %vb_ref.5), custom_call_target="tpu_custom_call" | custom-call | flops 1024000000 | bytes 7680000 | tf_op jit(solution)/shard_map/attend/pallas_call | solution.py:584
  23.8 0.8 loss.1
  24.6 7.1 %layer.2 = (bf16[320,256]{1,0:T(8,128)(2,1)}, bf16[320,256]{1,0:T(8,128)(2,1)}, bf16[1664,256]{1,0:T(8,128)(2,1)S(1)}, bf16[1664,256]{1,0:T(8,128)(2,1)S(1)}) custom-call(s32[1]{0:T(128)} %bitcast.4.bit_ref, s32[5]{0:T(128)S(1)} %copy-done, f32[8,256]{1,0:T(8,128)S(1)} %get-tuple-element.113.cls_ref, bf16[320,256]{1,0:T(8,128)(2,1)} %bitcast.54, ...), custom_call_target="tpu_custom_call" | custom-call | flops 1536000000 | bytes 1280000 | tf_op jit(solution)/shard_map/layer/pallas_call | solution.py:604
  31.8 2.3 %collective-permute-done.refs_1_ = bf16[1664,256]{1,0:T(8,128)(2,1)S(1)} collective-permute-done((bf16[1664,256]{1,0:T(8,128)(2,1)S(1)}, bf16[1664,256]{1,0:T(8,128)(2,1)S(1)}, u32[]{:S(2)}, u32[]{:S(2)}) %collective-permute-start) | collective-permute-done | bytes 852000 | tf_op jit(solution)/shard_map/ppermute | solution.py:646
  34.1 0.4 combine.4
  34.5 1.6 %collective-permute-start.1 = (bf16[416,256]{1,0:T(8,128)(2,1)S(1)}, bf16[416,256]{1,0:T(8,128)(2,1)S(1)}, u32[]{:S(2)}, u32[]{:S(2)}) collective-permute-start(bf16[416,256]{1,0:T(8,128)(2,1)S(1)} %get-tuple-element.121), channel_id=1, source_target_pairs={{0,2},{1,3},{2,0},{3,1},{4,6},{5,7},{6,4},{7,5},{8,10},{9,11},{10,... | collective-permute-start | bytes 638984 | tf_op jit(solution)/shard_map/ppermute | solution.py:646
  36.1 1.5 %collective-permute-start.2 = (bf16[416,256]{1,0:T(8,128)(2,1)S(1)}, bf16[416,256]{1,0:T(8,128)(2,1)S(1)}, u32[]{:S(2)}, u32[]{:S(2)}) collective-permute-start(bf16[416,256]{1,0:T(8,128)(2,1)S(1)} %get-tuple-element.122), channel_id=1, source_target_pairs={{0,4},{1,5},{2,6},{3,7},{4,0},{5,1},{6,2},{7,3},{8,12},{9,13},{10,... | collective-permute-start | bytes 638984 | tf_op jit(solution)/shard_map/ppermute | solution.py:646
  37.6 0.5 collective-permute-start.3
  38.0 20.6 %layer.3 = (bf16[1280,256]{1,0:T(8,128)(2,1)}, bf16[1280,256]{1,0:T(8,128)(2,1)}, bf16[1664,256]{1,0:T(8,128)(2,1)S(1)}, bf16[1664,256]{1,0:T(8,128)(2,1)S(1)}) custom-call(s32[1]{0:T(128)} %bitcast.4.bit_ref, s32[5]{0:T(128)S(1)} %copy-done.1, f32[8,256]{1,0:T(8,128)S(1)} %get-tuple-element.124.cls_ref, bf16[1280,256]{1,0:T(8,128)(2,1)} %bitcast.57, ...), custom_call_target="tpu_custom_call" | custom-call | flops 6144000000 | bytes 5120000 | tf_op jit(solution)/shard_map/layer/pallas_call | solution.py:604
  59.0 1.6 %collective-permute-start.8 = (bf16[104,256]{1,0:T(8,128)(2,1)S(1)}, bf16[104,256]{1,0:T(8,128)(2,1)S(1)}, u32[]{:S(2)}, u32[]{:S(2)}) collective-permute-start(bf16[104,256]{1,0:T(8,128)(2,1)S(1)} %get-tuple-element.134), channel_id=1, source_target_pairs={{0,8},{1,9},{2,10},{3,11},{4,12},{5,13},{6,14},{7,15},{8,0},{9,1},... | collective-permute-start | bytes 159752 | tf_op jit(solution)/shard_map/ppermute | solution.py:646
  60.6 2.4 %collective-permute-start.9 = (bf16[104,256]{1,0:T(8,128)(2,1)S(1)}, bf16[104,256]{1,0:T(8,128)(2,1)S(1)}, u32[]{:S(2)}, u32[]{:S(2)}) collective-permute-start(bf16[104,256]{1,0:T(8,128)(2,1)S(1)} %get-tuple-element.135), channel_id=1, source_target_pairs={{0,16},{1,17},{2,18},{3,19},{4,20},{5,21},{6,22},{7,23},{8,24},{9,... | collective-permute-start | bytes 159752 | tf_op jit(solution)/shard_map/ppermute | solution.py:646
  63.0 0.4 collective-permute-start.10
  63.5 0.4 combine.6
  63.8 1.6 %collective-permute-start.5 = (bf16[416,256]{1,0:T(8,128)(2,1)S(1)}, bf16[416,256]{1,0:T(8,128)(2,1)S(1)}, u32[]{:S(2)}, u32[]{:S(2)}) collective-permute-start(bf16[416,256]{1,0:T(8,128)(2,1)S(1)} %get-tuple-element.140), channel_id=1, source_target_pairs={{0,2},{1,3},{2,0},{3,1},{4,6},{5,7},{6,4},{7,5},{8,10},{9,11},{10,... | collective-permute-start | bytes 638984 | tf_op jit(solution)/shard_map/ppermute | solution.py:646
  65.4 1.5 %collective-permute-start.6 = (bf16[416,256]{1,0:T(8,128)(2,1)S(1)}, bf16[416,256]{1,0:T(8,128)(2,1)S(1)}, u32[]{:S(2)}, u32[]{:S(2)}) collective-permute-start(bf16[416,256]{1,0:T(8,128)(2,1)S(1)} %get-tuple-element.141), channel_id=1, source_target_pairs={{0,4},{1,5},{2,6},{3,7},{4,0},{5,1},{6,2},{7,3},{8,12},{9,13},{10,... | collective-permute-start | bytes 638984 | tf_op jit(solution)/shard_map/ppermute | solution.py:646
  66.9 0.5 collective-permute-start.7
  67.4 1.6 %collective-permute-done.10 = bf16[104,256]{1,0:T(8,128)(2,1)S(1)} collective-permute-done((bf16[104,256]{1,0:T(8,128)(2,1)S(1)}, bf16[104,256]{1,0:T(8,128)(2,1)S(1)}, u32[]{:S(2)}, u32[]{:S(2)}) %collective-permute-start.10) | collective-permute-done | bytes 53280 | tf_op jit(solution)/shard_map/ppermute | solution.py:646
  69.0 1.9 %collective-permute-start.16 = (bf16[104,256]{1,0:T(8,128)(2,1)S(1)}, bf16[104,256]{1,0:T(8,128)(2,1)S(1)}, u32[]{:S(2)}, u32[]{:S(2)}) collective-permute-start(bf16[104,256]{1,0:T(8,128)(2,1)S(1)} %add_convert_fusion.1), channel_id=1, source_target_pairs={{0,24},{1,25},{2,26},{3,27},{4,28},{5,29},{6,30},{7,31},{8,16},{9,... | collective-permute-start | bytes 159752 | tf_op jit(solution)/shard_map/ppermute | solution.py:646
  70.9 1.1 %collective-permute-done.5.refs_1_ = bf16[416,256]{1,0:T(8,128)(2,1)S(1)} collective-permute-done((bf16[416,256]{1,0:T(8,128)(2,1)S(1)}, bf16[416,256]{1,0:T(8,128)(2,1)S(1)}, u32[]{:S(2)}, u32[]{:S(2)}) %collective-permute-start.5) | collective-permute-done | bytes 213024 | tf_op jit(solution)/shard_map/ppermute | solution.py:646
  72.0 1.4 %collective-permute-start.14 = (bf16[104,256]{1,0:T(8,128)(2,1)S(1)}, bf16[104,256]{1,0:T(8,128)(2,1)S(1)}, u32[]{:S(2)}, u32[]{:S(2)}) collective-permute-start(bf16[104,256]{1,0:T(8,128)(2,1)S(1)} %add_convert_fusion.1), channel_id=1, source_target_pairs={{0,8},{1,9},{2,10},{3,11},{4,12},{5,13},{6,14},{7,15},{8,0},{9,1},... | collective-permute-start | bytes 159752 | tf_op jit(solution)/shard_map/ppermute | solution.py:646
  73.5 3.0 %collective-permute-done.6.refs_2_ = bf16[416,256]{1,0:T(8,128)(2,1)S(1)} collective-permute-done((bf16[416,256]{1,0:T(8,128)(2,1)S(1)}, bf16[416,256]{1,0:T(8,128)(2,1)S(1)}, u32[]{:S(2)}, u32[]{:S(2)}) %collective-permute-start.6) | collective-permute-done | bytes 213024 | tf_op jit(solution)/shard_map/ppermute | solution.py:646
  76.7 0.6 collective-permute-start.11
  77.3 3.3 %collective-permute-start.12 = (bf16[104,256]{1,0:T(8,128)(2,1)S(1)}, bf16[104,256]{1,0:T(8,128)(2,1)S(1)}, u32[]{:S(2)}, u32[]{:S(2)}) collective-permute-start(bf16[104,256]{1,0:T(8,128)(2,1)S(1)} %get-tuple-element.153), channel_id=1, source_target_pairs={{0,16},{1,17},{2,18},{3,19},{4,20},{5,21},{6,22},{7,23},{8,24},{9,... | collective-permute-start | bytes 159752 | tf_op jit(solution)/shard_map/ppermute | solution.py:646
  80.7 0.5 collective-permute-start.13
  81.2 1.5 %collective-permute-start.22 = (bf16[416,256]{1,0:T(8,128)(2,1)S(1)}, bf16[416,256]{1,0:T(8,128)(2,1)S(1)}, u32[]{:S(2)}, u32[]{:S(2)}) collective-permute-start(bf16[416,256]{1,0:T(8,128)(2,1)S(1)} %bitcast.48), channel_id=1, source_target_pairs={{0,6},{1,7},{2,4},{3,5},{4,2},{5,3},{6,0},{7,1},{8,14},{9,15},{10,... | collective-permute-start | bytes 638984 | tf_op jit(solution)/shard_map/ppermute | solution.py:646
  82.8 1.2 %collective-permute-start.21 = (bf16[416,256]{1,0:T(8,128)(2,1)S(1)}, bf16[416,256]{1,0:T(8,128)(2,1)S(1)}, u32[]{:S(2)}, u32[]{:S(2)}) collective-permute-start(bf16[416,256]{1,0:T(8,128)(2,1)S(1)} %bitcast.49), channel_id=1, source_target_pairs={{0,4},{1,5},{2,6},{3,7},{4,0},{5,1},{6,2},{7,3},{8,12},{9,13},{10,... | collective-permute-start | bytes 638984 | tf_op jit(solution)/shard_map/ppermute | solution.py:646
  84.0 0.8 collective-permute-start.20
  84.8 1.8 %collective-permute-done.13 = bf16[104,256]{1,0:T(8,128)(2,1)S(1)} collective-permute-done((bf16[104,256]{1,0:T(8,128)(2,1)S(1)}, bf16[104,256]{1,0:T(8,128)(2,1)S(1)}, u32[]{:S(2)}, u32[]{:S(2)}) %collective-permute-start.13) | collective-permute-done | bytes 53280 | tf_op jit(solution)/shard_map/ppermute | solution.py:646
  86.6 1.6 %collective-permute-start.19 = (bf16[104,256]{1,0:T(8,128)(2,1)S(1)}, bf16[104,256]{1,0:T(8,128)(2,1)S(1)}, u32[]{:S(2)}, u32[]{:S(2)}) collective-permute-start(bf16[104,256]{1,0:T(8,128)(2,1)S(1)} %add_convert_fusion), channel_id=1, source_target_pairs={{0,24},{1,25},{2,26},{3,27},{4,28},{5,29},{6,30},{7,31},{8,16},{9,... | collective-permute-start | bytes 159752 | tf_op jit(solution)/shard_map/ppermute | solution.py:646
  88.3 1.2 %collective-permute-done.22 = bf16[416,256]{1,0:T(8,128)(2,1)S(1)} collective-permute-done((bf16[416,256]{1,0:T(8,128)(2,1)S(1)}, bf16[416,256]{1,0:T(8,128)(2,1)S(1)}, u32[]{:S(2)}, u32[]{:S(2)}) %collective-permute-start.22) | collective-permute-done | bytes 213024 | tf_op jit(solution)/shard_map/ppermute | solution.py:646
  89.5 1.6 %collective-permute-start.17 = (bf16[104,256]{1,0:T(8,128)(2,1)S(1)}, bf16[104,256]{1,0:T(8,128)(2,1)S(1)}, u32[]{:S(2)}, u32[]{:S(2)}) collective-permute-start(bf16[104,256]{1,0:T(8,128)(2,1)S(1)} %add_convert_fusion), channel_id=1, source_target_pairs={{0,8},{1,9},{2,10},{3,11},{4,12},{5,13},{6,14},{7,15},{8,0},{9,1},... | collective-permute-start | bytes 159752 | tf_op jit(solution)/shard_map/ppermute | solution.py:646
  91.1 0.5 collective-permute-done.21
  91.8 0.8 collective-permute-done.19
  92.6 1.2 %collective-permute-done.18 = bf16[104,256]{1,0:T(8,128)(2,1)S(1)} collective-permute-done((bf16[104,256]{1,0:T(8,128)(2,1)S(1)}, bf16[104,256]{1,0:T(8,128)(2,1)S(1)}, u32[]{:S(2)}, u32[]{:S(2)}) %collective-permute-start.18) | collective-permute-done | bytes 53280 | tf_op jit(solution)/shard_map/ppermute | solution.py:646
  94.2 1.5 %collective-permute-start.25 = (bf16[416,256]{1,0:T(8,128)(2,1)S(1)}, bf16[416,256]{1,0:T(8,128)(2,1)S(1)}, u32[]{:S(2)}, u32[]{:S(2)}) collective-permute-start(bf16[416,256]{1,0:T(8,128)(2,1)S(1)} %bitcast.43), channel_id=1, source_target_pairs={{0,6},{1,7},{2,4},{3,5},{4,2},{5,3},{6,0},{7,1},{8,14},{9,15},{10,... | collective-permute-start | bytes 638984 | tf_op jit(solution)/shard_map/ppermute | solution.py:646
  95.7 1.4 %collective-permute-start.24 = (bf16[416,256]{1,0:T(8,128)(2,1)S(1)}, bf16[416,256]{1,0:T(8,128)(2,1)S(1)}, u32[]{:S(2)}, u32[]{:S(2)}) collective-permute-start(bf16[416,256]{1,0:T(8,128)(2,1)S(1)} %bitcast.44), channel_id=1, source_target_pairs={{0,4},{1,5},{2,6},{3,7},{4,0},{5,1},{6,2},{7,3},{8,12},{9,13},{10,... | collective-permute-start | bytes 638984 | tf_op jit(solution)/shard_map/ppermute | solution.py:646
  97.2 0.6 collective-permute-start.23
  97.8 0.6 slice_reduce_fusion
  98.4 1.8 %unpack_q.1 = (f32[2,256,768]{2,1,0:T(8,128)}, f32[2,256,256]{2,1,0:T(8,128)}, f32[2,256,1024]{2,1,0:T(8,128)}, f32[2,1024,256]{2,1,0:T(8,128)}, f32[16,256]{1,0:T(8,128)S(1)}) custom-call(s32[1]{0:T(128)} %bitcast.4.bit_ref, bf16[1664,256]{1,0:T(8,128)(2,1)S(1)} %bitcast.42, bf16[1664,256]{1,0:T(8,128)(2,1)S(1)} %collective-permute-done.26.other_ref), custom_call_target="tpu_custom_call" | custom-call | tf_op jit(solution)/shard_map/unpack_q/pallas_call | solution.py:778
  100.2 2.7 %collective-permute-done.25.refs_3_ = bf16[416,256]{1,0:T(8,128)(2,1)S(1)} collective-permute-done((bf16[416,256]{1,0:T(8,128)(2,1)S(1)}, bf16[416,256]{1,0:T(8,128)(2,1)S(1)}, u32[]{:S(2)}, u32[]{:S(2)}) %collective-permute-start.25) | collective-permute-done | bytes 213024 | tf_op jit(solution)/shard_map/ppermute | solution.py:646
  103.0 2.2 %collective-permute-done.24.refs_2_ = bf16[416,256]{1,0:T(8,128)(2,1)S(1)} collective-permute-done((bf16[416,256]{1,0:T(8,128)(2,1)S(1)}, bf16[416,256]{1,0:T(8,128)(2,1)S(1)}, u32[]{:S(2)}, u32[]{:S(2)}) %collective-permute-start.24) | collective-permute-done | bytes 213024 | tf_op jit(solution)/shard_map/ppermute | solution.py:646
  105.2 0.5 collective-permute-start.29
  105.7 0.9 collective-permute-done.28.refs_5_
  106.6 0.3 collective-permute-done.29.refs_6_
  107.2 1.8 %unpack_p.1 = (f32[2,256,768]{2,1,0:T(8,128)}, f32[2,256,256]{2,1,0:T(8,128)}, f32[2,256,1024]{2,1,0:T(8,128)}, f32[2,1024,256]{2,1,0:T(8,128)}, f32[2,1024]{1,0...) custom-call(s32[1]{0:T(128)} %bitcast.4.bit_ref, ...), custom_call_target="tpu_custom_call", output_to_operand_aliasing={{0}: (11, {}), {1}: (12, {}), {2}: (13, {}), {3}: (14, {})} | custom-call | tf_op jit(solution)/shard_map/unpack_p/pallas_call | solution.py:794
  (58 shorter events, 2.0 us)
Async XLA Ops:
  0.7 12.6 %copy-start.2 = (s32[160]{0:T(256)S(1)}, s32[160]{0:T(256)}, u32[]{:S(2)}) copy-start(s32[160]{0:T(256)} %param.26) | copy-start | bytes 1924
  0.7 12.9 %copy-start = (s32[5]{0:T(128)S(1)}, s32[5]{0:T(128)}, u32[]{:S(2)}) copy-start(s32[5]{0:T(128)} %len_ref.6) | copy-start | bytes 64
  0.7 16.0 %copy-start.1 = (s32[5]{0:T(128)S(1)}, s32[5]{0:T(128)}, u32[]{:S(2)}) copy-start(s32[5]{0:T(128)} %len_ref.7) | copy-start | bytes 64
  5.9 17.9 %all-to-all-start = ((bf16[32,16,256]{2,1,0:T(8,128)(2,1)}), bf16[32,16,256]{2,1,0:T(8,128)(2,1)S(1)}, u32[]{:S(2)}, u32[]{:S(2)}) async-start(bf16[32,16,256]{2,1,0:T(8,128)(2,1)} %first.1), calls=%async_computation | async-start | bytes 524288 | tf_op jit(solution)/shard_map/all_to_all | solution.py:731
  31.8 2.4 %collective-permute-start = (bf16[1664,256]{1,0:T(8,128)(2,1)S(1)}, bf16[1664,256]{1,0:T(8,128)(2,1)S(1)}, u32[]{:S(2)}, u32[]{:S(2)}) collective-permute-start(bf16[1664,256]{1,0:T(8,128)(2,1)S(1)} %get-tuple-element.119), channel_id=1, source_target_pairs={{0,1},{1,0},{2,3},{3,2},{4,5},{5,4},{6,7},{7,6},{8,9},{9,8},{10,11... | collective-permute-start | bytes 2555912 | tf_op jit(solution)/shard_map/ppermute | solution.py:646
  34.5 24.2 %collective-permute-start.1 = (bf16[416,256]{1,0:T(8,128)(2,1)S(1)}, bf16[416,256]{1,0:T(8,128)(2,1)S(1)}, u32[]{:S(2)}, u32[]{:S(2)}) collective-permute-start(bf16[416,256]{1,0:T(8,128)(2,1)S(1)} %get-tuple-element.121), channel_id=1, source_target_pairs={{0,2},{1,3},{2,0},{3,1},{4,6},{5,7},{6,4},{7,5},{8,10},{9,11},{10,... | collective-permute-start | bytes 638984 | tf_op jit(solution)/shard_map/ppermute | solution.py:646
  36.1 22.6 %collective-permute-start.2 = (bf16[416,256]{1,0:T(8,128)(2,1)S(1)}, bf16[416,256]{1,0:T(8,128)(2,1)S(1)}, u32[]{:S(2)}, u32[]{:S(2)}) collective-permute-start(bf16[416,256]{1,0:T(8,128)(2,1)S(1)} %get-tuple-element.122), channel_id=1, source_target_pairs={{0,4},{1,5},{2,6},{3,7},{4,0},{5,1},{6,2},{7,3},{8,12},{9,13},{10,... | collective-permute-start | bytes 638984 | tf_op jit(solution)/shard_map/ppermute | solution.py:646
  37.6 21.1 %collective-permute-start.3 = (bf16[416,256]{1,0:T(8,128)(2,1)S(1)}, bf16[416,256]{1,0:T(8,128)(2,1)S(1)}, u32[]{:S(2)}, u32[]{:S(2)}) collective-permute-start(bf16[416,256]{1,0:T(8,128)(2,1)S(1)} %get-tuple-element.123), channel_id=1, source_target_pairs={{0,6},{1,7},{2,4},{3,5},{4,2},{5,3},{6,0},{7,1},{8,14},{9,15},{10,... | collective-permute-start | bytes 638984 | tf_op jit(solution)/shard_map/ppermute | solution.py:646
  58.7 4.7 %collective-permute-start.4 = (bf16[1664,256]{1,0:T(8,128)(2,1)S(1)}, bf16[1664,256]{1,0:T(8,128)(2,1)S(1)}, u32[]{:S(2)}, u32[]{:S(2)}) collective-permute-start(bf16[1664,256]{1,0:T(8,128)(2,1)S(1)} %get-tuple-element.132), channel_id=1, source_target_pairs={{0,1},{1,0},{2,3},{3,2},{4,5},{5,4},{6,7},{7,6},{8,9},{9,8},{10,11... | collective-permute-start | bytes 2555912 | tf_op jit(solution)/shard_map/ppermute | solution.py:646
  59.0 7.9 %collective-permute-start.8 = (bf16[104,256]{1,0:T(8,128)(2,1)S(1)}, bf16[104,256]{1,0:T(8,128)(2,1)S(1)}, u32[]{:S(2)}, u32[]{:S(2)}) collective-permute-start(bf16[104,256]{1,0:T(8,128)(2,1)S(1)} %get-tuple-element.134), channel_id=1, source_target_pairs={{0,8},{1,9},{2,10},{3,11},{4,12},{5,13},{6,14},{7,15},{8,0},{9,1},... | collective-permute-start | bytes 159752 | tf_op jit(solution)/shard_map/ppermute | solution.py:646
  60.6 6.7 %collective-permute-start.9 = (bf16[104,256]{1,0:T(8,128)(2,1)S(1)}, bf16[104,256]{1,0:T(8,128)(2,1)S(1)}, u32[]{:S(2)}, u32[]{:S(2)}) collective-permute-start(bf16[104,256]{1,0:T(8,128)(2,1)S(1)} %get-tuple-element.135), channel_id=1, source_target_pairs={{0,16},{1,17},{2,18},{3,19},{4,20},{5,21},{6,22},{7,23},{8,24},{9,... | collective-permute-start | bytes 159752 | tf_op jit(solution)/shard_map/ppermute | solution.py:646
  63.0 5.9 %collective-permute-start.10 = (bf16[104,256]{1,0:T(8,128)(2,1)S(1)}, bf16[104,256]{1,0:T(8,128)(2,1)S(1)}, u32[]{:S(2)}, u32[]{:S(2)}) collective-permute-start(bf16[104,256]{1,0:T(8,128)(2,1)S(1)} %get-tuple-element.136), channel_id=1, source_target_pairs={{0,24},{1,25},{2,26},{3,27},{4,28},{5,29},{6,30},{7,31},{8,16},{9,... | collective-permute-start | bytes 159752 | tf_op jit(solution)/shard_map/ppermute | solution.py:646
  63.8 8.2 %collective-permute-start.5 = (bf16[416,256]{1,0:T(8,128)(2,1)S(1)}, bf16[416,256]{1,0:T(8,128)(2,1)S(1)}, u32[]{:S(2)}, u32[]{:S(2)}) collective-permute-start(bf16[416,256]{1,0:T(8,128)(2,1)S(1)} %get-tuple-element.140), channel_id=1, source_target_pairs={{0,2},{1,3},{2,0},{3,1},{4,6},{5,7},{6,4},{7,5},{8,10},{9,11},{10,... | collective-permute-start | bytes 638984 | tf_op jit(solution)/shard_map/ppermute | solution.py:646
  65.4 11.1 %collective-permute-start.6 = (bf16[416,256]{1,0:T(8,128)(2,1)S(1)}, bf16[416,256]{1,0:T(8,128)(2,1)S(1)}, u32[]{:S(2)}, u32[]{:S(2)}) collective-permute-start(bf16[416,256]{1,0:T(8,128)(2,1)S(1)} %get-tuple-element.141), channel_id=1, source_target_pairs={{0,4},{1,5},{2,6},{3,7},{4,0},{5,1},{6,2},{7,3},{8,12},{9,13},{10,... | collective-permute-start | bytes 638984 | tf_op jit(solution)/shard_map/ppermute | solution.py:646
  66.9 9.6 %collective-permute-start.7 = (bf16[416,256]{1,0:T(8,128)(2,1)S(1)}, bf16[416,256]{1,0:T(8,128)(2,1)S(1)}, u32[]{:S(2)}, u32[]{:S(2)}) collective-permute-start(bf16[416,256]{1,0:T(8,128)(2,1)S(1)} %get-tuple-element.142), channel_id=1, source_target_pairs={{0,6},{1,7},{2,4},{3,5},{4,2},{5,3},{6,0},{7,1},{8,14},{9,15},{10,... | collective-permute-start | bytes 638984 | tf_op jit(solution)/shard_map/ppermute | solution.py:646
  69.0 11.6 %collective-permute-start.16 = (bf16[104,256]{1,0:T(8,128)(2,1)S(1)}, bf16[104,256]{1,0:T(8,128)(2,1)S(1)}, u32[]{:S(2)}, u32[]{:S(2)}) collective-permute-start(bf16[104,256]{1,0:T(8,128)(2,1)S(1)} %add_convert_fusion.1), channel_id=1, source_target_pairs={{0,24},{1,25},{2,26},{3,27},{4,28},{5,29},{6,30},{7,31},{8,16},{9,... | collective-permute-start | bytes 159752 | tf_op jit(solution)/shard_map/ppermute | solution.py:646
  70.9 10.2 %collective-permute-start.15 = (bf16[104,256]{1,0:T(8,128)(2,1)S(1)}, bf16[104,256]{1,0:T(8,128)(2,1)S(1)}, u32[]{:S(2)}, u32[]{:S(2)}) collective-permute-start(bf16[104,256]{1,0:T(8,128)(2,1)S(1)} %add_convert_fusion.1), channel_id=1, source_target_pairs={{0,16},{1,17},{2,18},{3,19},{4,20},{5,21},{6,22},{7,23},{8,24},{9,... | collective-permute-start | bytes 159752 | tf_op jit(solution)/shard_map/ppermute | solution.py:646
  72.0 9.1 %collective-permute-start.14 = (bf16[104,256]{1,0:T(8,128)(2,1)S(1)}, bf16[104,256]{1,0:T(8,128)(2,1)S(1)}, u32[]{:S(2)}, u32[]{:S(2)}) collective-permute-start(bf16[104,256]{1,0:T(8,128)(2,1)S(1)} %add_convert_fusion.1), channel_id=1, source_target_pairs={{0,8},{1,9},{2,10},{3,11},{4,12},{5,13},{6,14},{7,15},{8,0},{9,1},... | collective-permute-start | bytes 159752 | tf_op jit(solution)/shard_map/ppermute | solution.py:646
  76.7 7.3 %collective-permute-start.11 = (bf16[104,256]{1,0:T(8,128)(2,1)S(1)}, bf16[104,256]{1,0:T(8,128)(2,1)S(1)}, u32[]{:S(2)}, u32[]{:S(2)}) collective-permute-start(bf16[104,256]{1,0:T(8,128)(2,1)S(1)} %get-tuple-element.152), channel_id=1, source_target_pairs={{0,8},{1,9},{2,10},{3,11},{4,12},{5,13},{6,14},{7,15},{8,0},{9,1},... | collective-permute-start | bytes 159752 | tf_op jit(solution)/shard_map/ppermute | solution.py:646
  77.3 7.5 %collective-permute-start.12 = (bf16[104,256]{1,0:T(8,128)(2,1)S(1)}, bf16[104,256]{1,0:T(8,128)(2,1)S(1)}, u32[]{:S(2)}, u32[]{:S(2)}) collective-permute-start(bf16[104,256]{1,0:T(8,128)(2,1)S(1)} %get-tuple-element.153), channel_id=1, source_target_pairs={{0,16},{1,17},{2,18},{3,19},{4,20},{5,21},{6,22},{7,23},{8,24},{9,... | collective-permute-start | bytes 159752 | tf_op jit(solution)/shard_map/ppermute | solution.py:646
  80.7 5.9 %collective-permute-start.13 = (bf16[104,256]{1,0:T(8,128)(2,1)S(1)}, bf16[104,256]{1,0:T(8,128)(2,1)S(1)}, u32[]{:S(2)}, u32[]{:S(2)}) collective-permute-start(bf16[104,256]{1,0:T(8,128)(2,1)S(1)} %get-tuple-element.154), channel_id=1, source_target_pairs={{0,24},{1,25},{2,26},{3,27},{4,28},{5,29},{6,30},{7,31},{8,16},{9,... | collective-permute-start | bytes 159752 | tf_op jit(solution)/shard_map/ppermute | solution.py:646
  81.2 8.2 %collective-permute-start.22 = (bf16[416,256]{1,0:T(8,128)(2,1)S(1)}, bf16[416,256]{1,0:T(8,128)(2,1)S(1)}, u32[]{:S(2)}, u32[]{:S(2)}) collective-permute-start(bf16[416,256]{1,0:T(8,128)(2,1)S(1)} %bitcast.48), channel_id=1, source_target_pairs={{0,6},{1,7},{2,4},{3,5},{4,2},{5,3},{6,0},{7,1},{8,14},{9,15},{10,... | collective-permute-start | bytes 638984 | tf_op jit(solution)/shard_map/ppermute | solution.py:646
  82.8 8.8 %collective-permute-start.21 = (bf16[416,256]{1,0:T(8,128)(2,1)S(1)}, bf16[416,256]{1,0:T(8,128)(2,1)S(1)}, u32[]{:S(2)}, u32[]{:S(2)}) collective-permute-start(bf16[416,256]{1,0:T(8,128)(2,1)S(1)} %bitcast.49), channel_id=1, source_target_pairs={{0,4},{1,5},{2,6},{3,7},{4,0},{5,1},{6,2},{7,3},{8,12},{9,13},{10,... | collective-permute-start | bytes 638984 | tf_op jit(solution)/shard_map/ppermute | solution.py:646
  84.0 7.6 %collective-permute-start.20 = (bf16[416,256]{1,0:T(8,128)(2,1)S(1)}, bf16[416,256]{1,0:T(8,128)(2,1)S(1)}, u32[]{:S(2)}, u32[]{:S(2)}) collective-permute-start(bf16[416,256]{1,0:T(8,128)(2,1)S(1)} %bitcast.50), channel_id=1, source_target_pairs={{0,2},{1,3},{2,0},{3,1},{4,6},{5,7},{6,4},{7,5},{8,10},{9,11},{10,... | collective-permute-start | bytes 638984 | tf_op jit(solution)/shard_map/ppermute | solution.py:646
  86.6 6.0 %collective-permute-start.19 = (bf16[104,256]{1,0:T(8,128)(2,1)S(1)}, bf16[104,256]{1,0:T(8,128)(2,1)S(1)}, u32[]{:S(2)}, u32[]{:S(2)}) collective-permute-start(bf16[104,256]{1,0:T(8,128)(2,1)S(1)} %add_convert_fusion), channel_id=1, source_target_pairs={{0,24},{1,25},{2,26},{3,27},{4,28},{5,29},{6,30},{7,31},{8,16},{9,... | collective-permute-start | bytes 159752 | tf_op jit(solution)/shard_map/ppermute | solution.py:646
  88.3 5.6 %collective-permute-start.18 = (bf16[104,256]{1,0:T(8,128)(2,1)S(1)}, bf16[104,256]{1,0:T(8,128)(2,1)S(1)}, u32[]{:S(2)}, u32[]{:S(2)}) collective-permute-start(bf16[104,256]{1,0:T(8,128)(2,1)S(1)} %add_convert_fusion), channel_id=1, source_target_pairs={{0,16},{1,17},{2,18},{3,19},{4,20},{5,21},{6,22},{7,23},{8,24},{9,... | collective-permute-start | bytes 159752 | tf_op jit(solution)/shard_map/ppermute | solution.py:646
  89.5 4.7 %collective-permute-start.17 = (bf16[104,256]{1,0:T(8,128)(2,1)S(1)}, bf16[104,256]{1,0:T(8,128)(2,1)S(1)}, u32[]{:S(2)}, u32[]{:S(2)}) collective-permute-start(bf16[104,256]{1,0:T(8,128)(2,1)S(1)} %add_convert_fusion), channel_id=1, source_target_pairs={{0,8},{1,9},{2,10},{3,11},{4,12},{5,13},{6,14},{7,15},{8,0},{9,1},... | collective-permute-start | bytes 159752 | tf_op jit(solution)/shard_map/ppermute | solution.py:646
  91.8 6.6 %collective-permute-start.26 = (bf16[1664,256]{1,0:T(8,128)(2,1)S(1)}, bf16[1664,256]{1,0:T(8,128)(2,1)S(1)}, u32[]{:S(2)}, u32[]{:S(2)}) collective-permute-start(bf16[1664,256]{1,0:T(8,128)(2,1)S(1)} %bitcast.41), channel_id=1, source_target_pairs={{0,1},{1,0},{2,3},{3,2},{4,5},{5,4},{6,7},{7,6},{8,9},{9,8},{10,11... | collective-permute-start | bytes 2555912 | tf_op jit(solution)/shard_map/ppermute | solution.py:646
  94.2 8.7 %collective-permute-start.25 = (bf16[416,256]{1,0:T(8,128)(2,1)S(1)}, bf16[416,256]{1,0:T(8,128)(2,1)S(1)}, u32[]{:S(2)}, u32[]{:S(2)}) collective-permute-start(bf16[416,256]{1,0:T(8,128)(2,1)S(1)} %bitcast.43), channel_id=1, source_target_pairs={{0,6},{1,7},{2,4},{3,5},{4,2},{5,3},{6,0},{7,1},{8,14},{9,15},{10,... | collective-permute-start | bytes 638984 | tf_op jit(solution)/shard_map/ppermute | solution.py:646
  95.7 9.4 %collective-permute-start.24 = (bf16[416,256]{1,0:T(8,128)(2,1)S(1)}, bf16[416,256]{1,0:T(8,128)(2,1)S(1)}, u32[]{:S(2)}, u32[]{:S(2)}) collective-permute-start(bf16[416,256]{1,0:T(8,128)(2,1)S(1)} %bitcast.44), channel_id=1, source_target_pairs={{0,4},{1,5},{2,6},{3,7},{4,0},{5,1},{6,2},{7,3},{8,12},{9,13},{10,... | collective-permute-start | bytes 638984 | tf_op jit(solution)/shard_map/ppermute | solution.py:646
  97.2 8.0 %collective-permute-start.23 = (bf16[416,256]{1,0:T(8,128)(2,1)S(1)}, bf16[416,256]{1,0:T(8,128)(2,1)S(1)}, u32[]{:S(2)}, u32[]{:S(2)}) collective-permute-start(bf16[416,256]{1,0:T(8,128)(2,1)S(1)} %bitcast.45), channel_id=1, source_target_pairs={{0,2},{1,3},{2,0},{3,1},{4,6},{5,7},{6,4},{7,5},{8,10},{9,11},{10,... | collective-permute-start | bytes 638984 | tf_op jit(solution)/shard_map/ppermute | solution.py:646
  98.4 7.3 %collective-permute-start.27 = (bf16[416,256]{1,0:T(8,128)(2,1)S(1)}, bf16[416,256]{1,0:T(8,128)(2,1)S(1)}, u32[]{:S(2)}, u32[]{:S(2)}) collective-permute-start(bf16[416,256]{1,0:T(8,128)(2,1)S(1)} %bitcast.46), channel_id=1, source_target_pairs={{0,1},{1,0},{2,3},{3,2},{4,5},{5,4},{6,7},{7,6},{8,9},{9,8},{10,11... | collective-permute-start | bytes 638984 | tf_op jit(solution)/shard_map/ppermute | solution.py:646
  105.2 1.5 %collective-permute-start.28 = (bf16[416,256]{1,0:T(8,128)(2,1)S(1)}, bf16[416,256]{1,0:T(8,128)(2,1)S(1)}, u32[]{:S(2)}, u32[]{:S(2)}) collective-permute-start(bf16[416,256]{1,0:T(8,128)(2,1)S(1)} %collective-permute-done.23.refs_1_), channel_id=1, source_target_pairs={{0,1},{1,0},{2,3},{3,2},{4,5},{5,4},{6,7},{7,6},{8,9},{9,8},{10,11... | collective-permute-start | bytes 638984 | tf_op jit(solution)/shard_map/ppermute | solution.py:646
  105.2 1.8 %collective-permute-start.29 = (bf16[416,256]{1,0:T(8,128)(2,1)S(1)}, bf16[416,256]{1,0:T(8,128)(2,1)S(1)}, u32[]{:S(2)}, u32[]{:S(2)}) collective-permute-start(bf16[416,256]{1,0:T(8,128)(2,1)S(1)} %collective-permute-done.24.refs_2_), channel_id=1, source_target_pairs={{0,1},{1,0},{2,3},{3,2},{4,5},{5,4},{6,7},{7,6},{8,9},{9,8},{10,11... | collective-permute-start | bytes 638984 | tf_op jit(solution)/shard_map/ppermute | solution.py:646
  105.7 1.6 %collective-permute-start.30 = (bf16[416,256]{1,0:T(8,128)(2,1)S(1)}, bf16[416,256]{1,0:T(8,128)(2,1)S(1)}, u32[]{:S(2)}, u32[]{:S(2)}) collective-permute-start(bf16[416,256]{1,0:T(8,128)(2,1)S(1)} %collective-permute-done.25.refs_3_), channel_id=1, source_target_pairs={{0,1},{1,0},{2,3},{3,2},{4,5},{5,4},{6,7},{7,6},{8,9},{9,8},{10,11... | collective-permute-start | bytes 638984 | tf_op jit(solution)/shard_map/ppermute | solution.py:646

commit v9 on v8

--- a/solution.py
+++ b/solution.py
@@ -373,10 +373,10 @@
 def layer_kernel(
     which, steps, seqs, length,
     bit_ref, len_ref, cls_ref, x_ref, cot_ref, qkv_ref, p_ref, ctx_ref,
-    wqkv_ref, wo_ref, ob_ref, g1_ref, b1_ref, w1_ref, hb_ref, w2_ref, fb_ref, g2_ref, b2_ref,
-    out_ref, gx_ref, keep_ref, send_ref,
+    wo_ref, ob_ref, g1_ref, b1_ref, w1_ref, hb_ref, w2_ref, fb_ref, g2_ref, b2_ref,
+    out_ref, one_ref, gqkv_ref, keep_ref, send_ref,
     acc_ref, vec_ref, n1_ref, r1_ref, nb_ref, gp_ref, act_ref, n2_ref,
-    wide_ref, score_ref, prob_ref, two_ref, gffn_ref, gpre_ref, one_ref, gatt_ref, dctx_ref, gqkv_ref, ds_ref,
+    wide_ref, score_ref, prob_ref, two_ref, gffn_ref, gpre_ref, gatt_ref, dctx_ref, ds_ref,
 ):
     rows = seqs * length
     step = pl.program_id(0)
@@ -414,7 +414,6 @@
     attn_core(seqs, length, dctx_ref, qkv_ref, p_ref, gqkv_ref, vec_ref, score_ref, ds_ref, prob_ref)
     for j in range(3):
         add_block(QKV_BLOCK + j, dot_tn(x_ref[...], gqkv_ref[:, j * WIDTH : (j + 1) * WIDTH]))
-    gx_ref[...] = (one_ref[...] + dot_nt(gqkv_ref[...], wqkv_ref[...])).astype(bf16)
 
     def finish():
         acc_ref[VECTOR_START : VECTOR_START + VECTOR_ROWS, :] = jnp.sum(vec_ref[...].reshape(VECTOR_ROWS, PAD, WIDTH), axis=1)
@@ -432,7 +431,7 @@
         finish()
 
 
-def loss_kernel(local, me_ref, all_ref, hot_ref, own_hot_ref, loss_ref, gq_ref, gp_ref, q_ref, p_ref):
+def loss_phase(local, me_ref, all_ref, hot_ref, own_hot_ref, loss_ref, gq_ref, gp_ref, q_ref, p_ref):
     count = all_ref.shape[0]
     me = me_ref[0]
     wide = all_ref[...].astype(f32)
@@ -453,7 +452,7 @@
     block = 256 if count * PAD % 256 == 0 else count * PAD
 
     def part(index, carry):
-        start = pl.multiple_of(index * block, block)
+        start = index * block if isinstance(index, int) else pl.multiple_of(index * block, block)
         queries = q_ref[pl.ds(start, block), :]
         scores = dot_nt(p_ref[...], queries) * score_scale
         row = lax.broadcasted_iota(jnp.int32, scores.shape, 0)
@@ -468,7 +467,18 @@
         gp_ref[...] += dot(own_grad.astype(bf16), queries) * score_scale
         return carry
 
-    lax.fori_loop(0, count * PAD // block, part, 0)
+    if count * PAD == block:
+        part(0, 0)
+    else:
+        lax.fori_loop(0, count * PAD // block, part, 0)
+
+
+def question_kernel(local, seqs, length, me_ref, all_ref, hot_ref, own_hot_ref, bit_ref, len_ref, *refs):
+    inputs, outputs, scratch = refs[:15], refs[15:22], refs[22:]
+    loss_ref, gp_ref = outputs[5:]
+    gq_ref, q_ref, p_ref = scratch[:3]
+    loss_phase(local, me_ref, all_ref, hot_ref, own_hot_ref, loss_ref, gq_ref, gp_ref, q_ref, p_ref)
+    layer_kernel(0, 1, seqs, length, bit_ref, len_ref, gq_ref, *inputs, *outputs[:5], *scratch[3:])
 
 
 def combine_kernel(radix, digit_ref, *refs):
@@ -596,36 +606,66 @@
     )(lengths, in_hbm(x), in_hbm(wqkv), in_hbm(qb), in_hbm(vb))
 
 
-def layer(which, steps, seqs, length, bit, lengths, cls_grad, x, cot, attended, weights):
+def layer(which, steps, seqs, length, bit, lengths, cls_grad, x, cot, attended, weights, exchange=None):
     rows = seqs * length
     total = steps * rows
     block = (HEADS * length, length) if seqs == 1 else (rows, HEADS * length)
-    wqkv, _, _, *rest = weights
+    _, _, _, *rest = weights
+    kernel = functools.partial(layer_kernel, which, steps, seqs, length)
+    extra_shape, extra_spec, extra_scratch = [], [], []
+    leading, cls_spec = (bit, lengths, cls_grad), [smem(), smem(), whole((PAD, WIDTH))]
+    if exchange:
+        kernel = functools.partial(question_kernel, seqs, seqs, length)
+        count = exchange[1].shape[0]
+        leading = (*exchange, bit, lengths)
+        cls_spec = [smem(), whole(exchange[1].shape), whole((1, count * PAD)), whole((PAD, 1)), smem(), smem()]
+        extra_shape = [shape((PAD, 128), f32), shape((PAD, WIDTH), f32)]
+        extra_spec = [whole((PAD, 128)), whole((PAD, WIDTH))]
+        extra_scratch = [pltpu.VMEM((PAD, WIDTH), f32)] + [pltpu.VMEM((count * PAD, WIDTH), bf16)] * 2
     return pl.pallas_call(
-        functools.partial(layer_kernel, which, steps, seqs, length),
-        out_shape=[shape((total, WIDTH), bf16), shape((total, WIDTH), bf16), shape((HALF, WIDTH), bf16), shape((HALF, WIDTH), bf16)],
+        kernel,
+        out_shape=[shape((total, WIDTH), bf16), pltpu.HBM((total, WIDTH), f32), pltpu.HBM((total, 3 * WIDTH), bf16), shape((HALF, WIDTH), bf16), shape((HALF, WIDTH), bf16)] + extra_shape,
         grid=(steps,),
         in_specs=[
-            smem(), smem(), whole((PAD, WIDTH)), rows_of(rows, WIDTH), rows_of(rows, WIDTH),
+            *cls_spec, rows_of(rows, WIDTH), rows_of(rows, WIDTH),
             rows_of(rows, 3 * WIDTH), rows_of(*block), rows_of(rows, WIDTH),
-            part_of(which, (WIDTH, 3 * WIDTH)), part_of(which, (WIDTH, WIDTH)),
+            part_of(which, (WIDTH, WIDTH)),
             pair(WIDTH), pair(WIDTH), pair(WIDTH), part_of(which, (WIDTH, HIDDEN)), pair(HIDDEN),
             part_of(which, (HIDDEN, WIDTH)), pair(WIDTH), pair(WIDTH), pair(WIDTH),
         ],
-        out_specs=[rows_of(rows, WIDTH), rows_of(rows, WIDTH), whole((HALF, WIDTH)), whole((HALF, WIDTH))],
-        scratch_shapes=[
+        out_specs=[rows_of(rows, WIDTH), rows_of(rows, WIDTH), rows_of(rows, 3 * WIDTH), whole((HALF, WIDTH)), whole((HALF, WIDTH))] + extra_spec,
+        scratch_shapes=extra_scratch + [
             pltpu.VMEM((GROUP_ROWS, WIDTH), f32), pltpu.VMEM((VECTOR_ROWS * PAD, WIDTH), f32),
             pltpu.VMEM((rows, WIDTH), f32), pltpu.VMEM((rows, 1), f32), pltpu.VMEM((rows, WIDTH), bf16),
             pltpu.VMEM((rows, HIDDEN), f32), pltpu.VMEM((rows, HIDDEN), bf16), pltpu.VMEM((rows, WIDTH), f32),
             pltpu.VMEM((rows, HIDDEN), f32), pltpu.VMEM(block, f32),
             pltpu.VMEM(block, bf16), pltpu.VMEM((rows, WIDTH), f32), pltpu.VMEM((rows, WIDTH), bf16),
-            pltpu.VMEM((rows, HIDDEN), bf16), pltpu.VMEM((rows, WIDTH), f32), pltpu.VMEM((rows, WIDTH), bf16),
-            pltpu.VMEM((rows, WIDTH), bf16), pltpu.VMEM((rows, 3 * WIDTH), bf16), pltpu.VMEM(block, bf16),
+            pltpu.VMEM((rows, HIDDEN), bf16), pltpu.VMEM((rows, WIDTH), bf16), pltpu.VMEM((rows, WIDTH), bf16),
+            pltpu.VMEM(block, bf16),
         ],
         compiler_params=params(),
         cost_estimate=cost(total * 6 * 800000, total * 4000),
         name="layer",
-    )(bit, lengths, cls_grad, in_hbm(x), in_hbm(cot), *[in_hbm(member) for member in attended], in_hbm(wqkv), *[in_hbm(member) for member in rest])
+    )(*leading, in_hbm(x), in_hbm(cot), *[in_hbm(member) for member in attended], *[in_hbm(member) for member in rest])
+
+
+def input_grad_kernel(one_ref, gqkv_ref, wqkv_ref, gx_ref):
+    gx_ref[...] = (one_ref[...] + dot_nt(gqkv_ref[...], wqkv_ref[...])).astype(bf16)
+
+
+def input_grad(which, steps, one, gqkv, weights):
+    total = one.shape[0]
+    rows = total // steps
+    return pl.pallas_call(
+        input_grad_kernel,
+        out_shape=shape((total, WIDTH), bf16),
+        grid=(steps,),
+        in_specs=[rows_of(rows, WIDTH), rows_of(rows, 3 * WIDTH), part_of(which, (WIDTH, 3 * WIDTH))],
+        out_specs=rows_of(rows, WIDTH),
+        compiler_params=params(),
+        cost_estimate=cost(total * 2 * 200000, total * 3000),
+        name="input_grad",
+    )(in_hbm(one), in_hbm(gqkv), in_hbm(weights[0]))
 
 
 def stages(count):
@@ -735,27 +775,19 @@
     slots = positive // local * PAD + positive % local
     slots = jnp.pad(slots.reshape(count, local), ((0, 0), (0, PAD - local)), constant_values=-1)
     own_slots = lax.dynamic_slice_in_dim(slots, me, 1, axis=0).reshape(PAD, 1)
-    loss, grad_cls_q, grad_cls_p = pl.pallas_call(
-        functools.partial(loss_kernel, local),
-        out_shape=[shape((PAD, 128), f32), shape((PAD, WIDTH), f32), shape((PAD, WIDTH), f32)],
-        grid=(1,),
-        in_specs=[smem(), whole((count, 2 * PAD, WIDTH)), whole((1, count * PAD)), whole((PAD, 1))],
-        out_specs=[whole((PAD, 128)), whole((PAD, WIDTH)), whole((PAD, WIDTH))],
-        scratch_shapes=[pltpu.VMEM((count * PAD, WIDTH), bf16), pltpu.VMEM((count * PAD, WIDTH), bf16)],
-        compiler_params=params(),
-        name="loss",
-    )(me.reshape(1), all_cls, slots.reshape(1, -1), own_slots)
+    out_q, one_q, gqkv_q, keep_q, send_q, loss, grad_cls_p = layer(
+        0, 1, local, question_length, bit, len_questions, None, x_q, cot_questions.reshape(-1, WIDTH),
+        attended_q, weights, (me.reshape(1), all_cls, slots.reshape(1, -1), own_slots),
+    )
     loss_rows = loss[:local, 0]
-    out_q, grad_q, keep_q, send_q = layer(
-        0, 1, local, question_length, bit, len_questions, grad_cls_q, x_q, cot_questions.reshape(-1, WIDTH),
-        attended_q, weights,
-    )
     groups = stages(count)
     steps = [(True, group) for group in groups] + [(False, group) for group in groups[::-1]]
-    operands_q = prepare([keep_q, partner_send(send_q, groups[0][0], count)], steps[0], steps[1], me)
+    pieces_q = [keep_q, partner_send(send_q, groups[0][0], count)]
+    grad_q = input_grad(0, 1, one_q, gqkv_q, weights)
+    operands_q = prepare(after(pieces_q, grad_q), steps[0], steps[1], me)
     (grad_cls_p,) = after([grad_cls_p], *operands_q)
     pieces_q = launch(operands_q, steps[1], count)
-    out_p, grad_p, keep_p, send_p = layer(
+    out_p, one_p, gqkv_p, keep_p, send_p = layer(
         1, local, 1, passage_length, bit, len_passages, grad_cls_p, x_p, cot_passages.reshape(-1, WIDTH),
         attended_p, weights,
     )
@@ -786,7 +818,8 @@
         name="unpack_q",
     )(bit, own_q, other_q)
     own_piece, *came = pieces_p
-    came = after(came, tail, loss_rows)
+    grad_p = input_grad(1, 1, one_p, gqkv_p, weights)
+    came = after(came, tail, loss_rows, grad_p)
     pieces_p = [own_piece] + came
     other_p = [partner_send(piece, groups[0][0], count) for piece in pieces_p]
     vectors = [(2, HIDDEN)] + [(2, WIDTH)] * len(VECTOR_OUTS)

time: 110 us -> 109 us (level)
  waiting for transfers between devices: 20.6 us -> 11.4 us
  Pallas kernels: 48.5 us -> 52.7 us
  starting transfers between devices: 37.7 us -> 41.6 us
    ppermute x31, waiting for transfers between devices: 20.4 us -> 11.1 us  [partner_send(): return lax.ppermute(values, 'dp', [(i, i ^ mask) for i in range(count)])]
    pallas_call x3 -> x4, Pallas kernels: 28.6 us -> 32.8 us  [the longest x2 27.1 us: layer(): pl.pallas_call(kernel, out_shape=[shape((total, WIDTH), bf16), pltpu.HBM(...]
    ppermute x31, starting transfers between devices: 30.4 us -> 34.4 us  [partner_send(): return lax.ppermute(values, 'dp', [(i, i ^ mask) for i in range(count)])]
  transfers between devices with their start and end apart: 32 -> 32, of which waited for: 16 -> 12; matrix products, arithmetic and copies ran while one was open for 1% -> 1% of each run, Pallas kernels for 30% -> 35%
where the time goes in v9:
time: 109 us; the launch traced here: 108 us
  Pallas kernels  52.7 us (48%)
  starting transfers between devices  41.6 us (38%)
  waiting for transfers between devices  11.4 us (10%)
  local copies, waits for them, and re-layouts  1.19 us (1%)
  between operations  1.15 us (1%)
    ppermute x31, starting transfers between devices, partner_send(): return lax.ppermute(values, 'dp', [(i, i ^ mask) for i in range(count)])  34.4 us
    pallas_call x2, Pallas kernels, layer(): pl.pallas_call(kernel, out_shape=[shape((total, WIDTH), bf16), pltpu.HBM(...  27.1 us
    ppermute x31, waiting for transfers between devices, partner_send(): return lax.ppermute(values, 'dp', [(i, i ^ mask) for i in range(count)])  11.1 us
    pallas_call x2, Pallas kernels, attend(): pl.pallas_call(functools.partial(attend_long_kernel if seqs == 1 else att...  10 us
    all_to_all x1, starting transfers between devices, body(): all_cls = lax.all_to_all(own_cls, 'dp', 0, 0, tiled=True)  7.3 us
    pallas_call x2, Pallas kernels, input_grad(): pl.pallas_call(input_grad_kernel, out_shape=shape((total, WIDTH), bf16),...  5.76 us
    pallas_call x1, Pallas kernels, first_call(): pl.pallas_call(functools.partial(first_kernel, local), out_shape=shape((c...  5.22 us
  transfers between devices with their start and end apart: 32, of which 12 were waited for; matrix products, arithmetic and copies ran while one was open for 1% of the time, Pallas kernels for 35%

profile of v9, /device:TPU:0, one launch (start us, length us, event | category | flops | bytes accessed | tf_op | source)
XLA Modules:
  0.0 108.2 jit_solution(600473911621305813)
XLA Ops:
  0.7 5.2 %first.1 = bf16[32,16,256]{2,1,0:T(8,128)(2,1)} custom-call(s32[5]{0:T(128)} %len_ref.6, s32[5]{0:T(128)} %len_ref.7, bf16[320,256]{1,0:T(8,128)(2,1)} %bitcast.52, bf16[1280,256]{1,0:T(8,128)(2,1)} %bitcast.56, bf16[2,256,768]{2,1,0:T(8,128)(2,1)} %wqkv_ref.9, bf16[2,256]{1,0:T(2,128)(2,1)} %qb_ref.5, bf16[2,256]{1,0:T(2,128)(2,1)} %vb_ref.5, ...), custom_call_target="tpu_custom_call" | custom-call | tf_op jit(solution)/shard_map/first/pallas_call | solution.py:577
  5.9 7.3 %all-to-all-start = ((bf16[32,16,256]{2,1,0:T(8,128)(2,1)}), bf16[32,16,256]{2,1,0:T(8,128)(2,1)S(1)}, u32[]{:S(2)}, u32[]{:S(2)}) async-start(bf16[32,16,256]{2,1,0:T(8,128)(2,1)} %first.1), calls=%async_computation | async-start | bytes 524288 | tf_op jit(solution)/shard_map/all_to_all | solution.py:771
  13.6 3.1 %attend.3 = (bf16[320,768]{1,0:T(8,128)(2,1)}, f32[320,256]{1,0:T(8,128)}, bf16[320,256]{1,0:T(8,128)(2,1)}) custom-call(s32[5]{0:T(128)S(1)} %copy-done, bf16[320,256]{1,0:T(8,128)(2,1)} %bitcast.53, bf16[2,256,768]{2,1,0:T(8,128)(2,1)} %wqkv_ref.9, bf16[2,256]{1,0:T(2,128)(2,1)} %qb_ref.5, bf16[2,256]{1,0:T(2,128)(2,1)} %vb_ref.5), custom_call_target="tpu_custom_call" | custom-call | flops 256000000 | bytes 1920000 | tf_op jit(solution)/shard_map/attend/pallas_call | solution.py:594
  16.7 6.9 %attend.2 = (bf16[1280,768]{1,0:T(8,128)(2,1)}, f32[5120,256]{1,0:T(8,128)}, bf16[1280,256]{1,0:T(8,128)(2,1)}) custom-call(s32[5]{0:T(128)S(1)} %copy-done.1, bf16[1280,256]{1,0:T(8,128)(2,1)} %bitcast.57, bf16[2,256,768]{2,1,0:T(8,128)(2,1)} %wqkv_ref.9, bf16[2,256]{1,0:T(2,128)(2,1)} %qb_ref.5, bf16[2,256]{1,0:T(2,128)(2,1)} %vb_ref.5), custom_call_target="tpu_custom_call" | custom-call | flops 1024000000 | bytes 7680000 | tf_op jit(solution)/shard_map/attend/pallas_call | solution.py:594
  23.6 0.2 all-to-all-done.all_ref
  23.8 7.2 %layer.2 = (bf16[320,256]{1,0:T(8,128)(2,1)}, f32[320,256]{1,0:T(8,128)}, bf16[320,768]{1,0:T(8,128)(2,1)}, bf16[1664,256]{1,0:T(8,128)(2,1)S(1)}, bf16[1664,256...) custom-call(s32[1]{0:T(128)} %bitcast.me_ref, bf16[32,16,256]{2,1,0:T(8,128)(2,1)S(1)} %all-to-all-done.all_ref, ...), custom_call_target="tpu_custom_call" | custom-call | flops 1536000000 | bytes 1280000 | tf_op jit(solution)/shard_map/layer/pallas_call | solution.py:625
  31.1 2.2 %input_grad.2 = bf16[320,256]{1,0:T(8,128)(2,1)} custom-call(f32[320,256]{1,0:T(8,128)} %get-tuple-element.122.one_ref, bf16[320,768]{1,0:T(8,128)(2,1)} %get-tuple-element.123.gqkv_ref, bf16[2,256,768]{2,1,0:T(8,128)(2,1)} %wqkv_ref.9), custom_call_target="tpu_custom_call" | custom-call | flops 128000000 | bytes 960000 | tf_op jit(solution)/shard_map/input_grad/pallas_call | solution.py:659
  33.4 0.4 combine.4
  33.7 1.7 %collective-permute-start.1 = (bf16[416,256]{1,0:T(8,128)(2,1)S(1)}, bf16[416,256]{1,0:T(8,128)(2,1)S(1)}, u32[]{:S(2)}, u32[]{:S(2)}) collective-permute-start(bf16[416,256]{1,0:T(8,128)(2,1)S(1)} %get-tuple-element.127), channel_id=1, source_target_pairs={{0,2},{1,3},{2,0},{3,1},{4,6},{5,7},{6,4},{7,5},{8,10},{9,11},{10,... | collective-permute-start | bytes 638984 | tf_op jit(solution)/shard_map/ppermute | solution.py:686
  35.4 1.5 %collective-permute-start.2 = (bf16[416,256]{1,0:T(8,128)(2,1)S(1)}, bf16[416,256]{1,0:T(8,128)(2,1)S(1)}, u32[]{:S(2)}, u32[]{:S(2)}) collective-permute-start(bf16[416,256]{1,0:T(8,128)(2,1)S(1)} %get-tuple-element.128), channel_id=1, source_target_pairs={{0,4},{1,5},{2,6},{3,7},{4,0},{5,1},{6,2},{7,3},{8,12},{9,13},{10,... | collective-permute-start | bytes 638984 | tf_op jit(solution)/shard_map/ppermute | solution.py:686
  36.8 0.4 collective-permute-start.3
  37.3 19.9 %layer.3 = (bf16[1280,256]{1,0:T(8,128)(2,1)}, f32[1280,256]{1,0:T(8,128)}, bf16[1280,768]{1,0:T(8,128)(2,1)}, bf16[1664,256]{1,0:T(8,128)(2,1)S(1)}, bf16[1664,256]{1,0:T(8,128)(2,1)S(1)}) custom-call(s32[1]{0:T(128)} %bitcast.4.bit_ref, s32[5]{0:T(128)S(1)} %copy-done.1, f32[8,256]{1,0:T(8,128)S(1)} %get-tuple-element.130.cls_ref, ...), custom_call_target="tpu_custom_call" | custom-call | flops 6144000000 | bytes 5120000 | tf_op jit(solution)/shard_map/layer/pallas_call | solution.py:625
  57.3 0.2 combine.5
  57.5 1.6 %collective-permute-start.8 = (bf16[104,256]{1,0:T(8,128)(2,1)S(1)}, bf16[104,256]{1,0:T(8,128)(2,1)S(1)}, u32[]{:S(2)}, u32[]{:S(2)}) collective-permute-start(bf16[104,256]{1,0:T(8,128)(2,1)S(1)} %get-tuple-element.140), channel_id=1, source_target_pairs={{0,8},{1,9},{2,10},{3,11},{4,12},{5,13},{6,14},{7,15},{8,0},{9,1},... | collective-permute-start | bytes 159752 | tf_op jit(solution)/shard_map/ppermute | solution.py:686
  59.1 2.4 %collective-permute-start.9 = (bf16[104,256]{1,0:T(8,128)(2,1)S(1)}, bf16[104,256]{1,0:T(8,128)(2,1)S(1)}, u32[]{:S(2)}, u32[]{:S(2)}) collective-permute-start(bf16[104,256]{1,0:T(8,128)(2,1)S(1)} %get-tuple-element.141), channel_id=1, source_target_pairs={{0,16},{1,17},{2,18},{3,19},{4,20},{5,21},{6,22},{7,23},{8,24},{9,... | collective-permute-start | bytes 159752 | tf_op jit(solution)/shard_map/ppermute | solution.py:686
  61.6 0.4 collective-permute-start.10
  62.0 0.4 combine.6
  62.3 1.7 %collective-permute-start.5 = (bf16[416,256]{1,0:T(8,128)(2,1)S(1)}, bf16[416,256]{1,0:T(8,128)(2,1)S(1)}, u32[]{:S(2)}, u32[]{:S(2)}) collective-permute-start(bf16[416,256]{1,0:T(8,128)(2,1)S(1)} %get-tuple-element.146), channel_id=1, source_target_pairs={{0,2},{1,3},{2,0},{3,1},{4,6},{5,7},{6,4},{7,5},{8,10},{9,11},{10,... | collective-permute-start | bytes 638984 | tf_op jit(solution)/shard_map/ppermute | solution.py:686
  64.0 1.4 %collective-permute-start.6 = (bf16[416,256]{1,0:T(8,128)(2,1)S(1)}, bf16[416,256]{1,0:T(8,128)(2,1)S(1)}, u32[]{:S(2)}, u32[]{:S(2)}) collective-permute-start(bf16[416,256]{1,0:T(8,128)(2,1)S(1)} %get-tuple-element.147), channel_id=1, source_target_pairs={{0,4},{1,5},{2,6},{3,7},{4,0},{5,1},{6,2},{7,3},{8,12},{9,13},{10,... | collective-permute-start | bytes 638984 | tf_op jit(solution)/shard_map/ppermute | solution.py:686
  65.4 0.5 collective-permute-start.7
  65.9 1.6 %collective-permute-done.10 = bf16[104,256]{1,0:T(8,128)(2,1)S(1)} collective-permute-done((bf16[104,256]{1,0:T(8,128)(2,1)S(1)}, bf16[104,256]{1,0:T(8,128)(2,1)S(1)}, u32[]{:S(2)}, u32[]{:S(2)}) %collective-permute-start.10) | collective-permute-done | bytes 53280 | tf_op jit(solution)/shard_map/ppermute | solution.py:686
  67.6 2.4 %collective-permute-start.15 = (bf16[104,256]{1,0:T(8,128)(2,1)S(1)}, bf16[104,256]{1,0:T(8,128)(2,1)S(1)}, u32[]{:S(2)}, u32[]{:S(2)}) collective-permute-start(bf16[104,256]{1,0:T(8,128)(2,1)S(1)} %add_convert_fusion.1), channel_id=1, source_target_pairs={{0,16},{1,17},{2,18},{3,19},{4,20},{5,21},{6,22},{7,23},{8,24},{9,... | collective-permute-start | bytes 159752 | tf_op jit(solution)/shard_map/ppermute | solution.py:686
  70.0 0.6 collective-permute-done.5.refs_1_
  70.6 3.4 %collective-permute-start.16 = (bf16[104,256]{1,0:T(8,128)(2,1)S(1)}, bf16[104,256]{1,0:T(8,128)(2,1)S(1)}, u32[]{:S(2)}, u32[]{:S(2)}) collective-permute-start(bf16[104,256]{1,0:T(8,128)(2,1)S(1)} %add_convert_fusion.1), channel_id=1, source_target_pairs={{0,24},{1,25},{2,26},{3,27},{4,28},{5,29},{6,30},{7,31},{8,16},{9,... | collective-permute-start | bytes 159752 | tf_op jit(solution)/shard_map/ppermute | solution.py:686
  74.0 1.1 collective-permute-done.6.refs_2_
  75.2 0.6 collective-permute-start.11
  75.8 3.3 %collective-permute-start.12 = (bf16[104,256]{1,0:T(8,128)(2,1)S(1)}, bf16[104,256]{1,0:T(8,128)(2,1)S(1)}, u32[]{:S(2)}, u32[]{:S(2)}) collective-permute-start(bf16[104,256]{1,0:T(8,128)(2,1)S(1)} %get-tuple-element.159), channel_id=1, source_target_pairs={{0,16},{1,17},{2,18},{3,19},{4,20},{5,21},{6,22},{7,23},{8,24},{9,... | collective-permute-start | bytes 159752 | tf_op jit(solution)/shard_map/ppermute | solution.py:686
  79.2 0.5 collective-permute-start.13
  79.8 1.2 %collective-permute-start.20 = (bf16[416,256]{1,0:T(8,128)(2,1)S(1)}, bf16[416,256]{1,0:T(8,128)(2,1)S(1)}, u32[]{:S(2)}, u32[]{:S(2)}) collective-permute-start(bf16[416,256]{1,0:T(8,128)(2,1)S(1)} %bitcast.48), channel_id=1, source_target_pairs={{0,2},{1,3},{2,0},{3,1},{4,6},{5,7},{6,4},{7,5},{8,10},{9,11},{10,... | collective-permute-start | bytes 638984 | tf_op jit(solution)/shard_map/ppermute | solution.py:686
  81.0 0.8 collective-permute-start.21
  81.9 1.5 %collective-permute-start.22 = (bf16[416,256]{1,0:T(8,128)(2,1)S(1)}, bf16[416,256]{1,0:T(8,128)(2,1)S(1)}, u32[]{:S(2)}, u32[]{:S(2)}) collective-permute-start(bf16[416,256]{1,0:T(8,128)(2,1)S(1)} %bitcast.50), channel_id=1, source_target_pairs={{0,6},{1,7},{2,4},{3,5},{4,2},{5,3},{6,0},{7,1},{8,14},{9,15},{10,... | collective-permute-start | bytes 638984 | tf_op jit(solution)/shard_map/ppermute | solution.py:686
  83.4 2.3 %collective-permute-done.13 = bf16[104,256]{1,0:T(8,128)(2,1)S(1)} collective-permute-done((bf16[104,256]{1,0:T(8,128)(2,1)S(1)}, bf16[104,256]{1,0:T(8,128)(2,1)S(1)}, u32[]{:S(2)}, u32[]{:S(2)}) %collective-permute-start.13) | collective-permute-done | bytes 53280 | tf_op jit(solution)/shard_map/ppermute | solution.py:686
  85.8 1.5 %collective-permute-start.18 = (bf16[104,256]{1,0:T(8,128)(2,1)S(1)}, bf16[104,256]{1,0:T(8,128)(2,1)S(1)}, u32[]{:S(2)}, u32[]{:S(2)}) collective-permute-start(bf16[104,256]{1,0:T(8,128)(2,1)S(1)} %add_convert_fusion), channel_id=1, source_target_pairs={{0,16},{1,17},{2,18},{3,19},{4,20},{5,21},{6,22},{7,23},{8,24},{9,... | collective-permute-start | bytes 159752 | tf_op jit(solution)/shard_map/ppermute | solution.py:686
  87.3 3.0 %collective-permute-start.19 = (bf16[104,256]{1,0:T(8,128)(2,1)S(1)}, bf16[104,256]{1,0:T(8,128)(2,1)S(1)}, u32[]{:S(2)}, u32[]{:S(2)}) collective-permute-start(bf16[104,256]{1,0:T(8,128)(2,1)S(1)} %add_convert_fusion), channel_id=1, source_target_pairs={{0,24},{1,25},{2,26},{3,27},{4,28},{5,29},{6,30},{7,31},{8,16},{9,... | collective-permute-start | bytes 159752 | tf_op jit(solution)/shard_map/ppermute | solution.py:686
  90.6 0.3 collective-permute-done.18
  90.9 2.4 %collective-permute-done.19 = bf16[104,256]{1,0:T(8,128)(2,1)S(1)} collective-permute-done((bf16[104,256]{1,0:T(8,128)(2,1)S(1)}, bf16[104,256]{1,0:T(8,128)(2,1)S(1)}, u32[]{:S(2)}, u32[]{:S(2)}) %collective-permute-start.19) | collective-permute-done | bytes 53280 | tf_op jit(solution)/shard_map/ppermute | solution.py:686
  93.4 1.3 %collective-permute-start.23 = (bf16[416,256]{1,0:T(8,128)(2,1)S(1)}, bf16[416,256]{1,0:T(8,128)(2,1)S(1)}, u32[]{:S(2)}, u32[]{:S(2)}) collective-permute-start(bf16[416,256]{1,0:T(8,128)(2,1)S(1)} %bitcast.43), channel_id=1, source_target_pairs={{0,2},{1,3},{2,0},{3,1},{4,6},{5,7},{6,4},{7,5},{8,10},{9,11},{10,... | collective-permute-start | bytes 638984 | tf_op jit(solution)/shard_map/ppermute | solution.py:686
  94.7 0.8 collective-permute-start.24
  95.5 1.4 %collective-permute-start.25 = (bf16[416,256]{1,0:T(8,128)(2,1)S(1)}, bf16[416,256]{1,0:T(8,128)(2,1)S(1)}, u32[]{:S(2)}, u32[]{:S(2)}) collective-permute-start(bf16[416,256]{1,0:T(8,128)(2,1)S(1)} %bitcast.45), channel_id=1, source_target_pairs={{0,6},{1,7},{2,4},{3,5},{4,2},{5,3},{6,0},{7,1},{8,14},{9,15},{10,... | collective-permute-start | bytes 638984 | tf_op jit(solution)/shard_map/ppermute | solution.py:686
  96.9 0.6 slice_reduce_fusion
  97.6 3.5 %input_grad.3 = bf16[1280,256]{1,0:T(8,128)(2,1)} custom-call(f32[1280,256]{1,0:T(8,128)} %get-tuple-element.134.one_ref, bf16[1280,768]{1,0:T(8,128)(2,1)} %get-tuple-element.135.gqkv_ref, bf16[2,256,768]{2,1,0:T(8,128)(2,1)} %wqkv_ref.9), custom_call_target="tpu_custom_call" | custom-call | flops 512000000 | bytes 3840000 | tf_op jit(solution)/shard_map/input_grad/pallas_call | solution.py:659
  101.1 1.8 %unpack_q.1 = (f32[2,256,768]{2,1,0:T(8,128)}, f32[2,256,256]{2,1,0:T(8,128)}, f32[2,256,1024]{2,1,0:T(8,128)}, f32[2,1024,256]{2,1,0:T(8,128)}, f32[16,256]{1,0:T(8,128)S(1)}) custom-call(s32[1]{0:T(128)} %bitcast.4.bit_ref, bf16[1664,256]{1,0:T(8,128)(2,1)S(1)} %bitcast.42, bf16[1664,256]{1,0:T(8,128)(2,1)S(1)} %collective-permute-done.26.other_ref), custom_call_target="tpu_custom_call" | custom-call | tf_op jit(solution)/shard_map/unpack_q/pallas_call | solution.py:810
  102.9 1.2 %collective-permute-done.24.refs_2_ = bf16[416,256]{1,0:T(8,128)(2,1)S(1)} collective-permute-done((bf16[416,256]{1,0:T(8,128)(2,1)S(1)}, bf16[416,256]{1,0:T(8,128)(2,1)S(1)}, u32[]{:S(2)}, u32[]{:S(2)}) %collective-permute-start.24) | collective-permute-done | bytes 213024 | tf_op jit(solution)/shard_map/ppermute | solution.py:686
  104.1 0.5 collective-permute-start.29
  104.6 0.9 collective-permute-done.28.refs_5_
  105.6 0.3 collective-permute-done.29.refs_6_
  105.9 0.3 collective-permute-done.30.refs_7_
  106.2 1.8 %unpack_p.1 = (f32[2,256,768]{2,1,0:T(8,128)}, f32[2,256,256]{2,1,0:T(8,128)}, f32[2,256,1024]{2,1,0:T(8,128)}, f32[2,1024,256]{2,1,0:T(8,128)}, f32[2,1024]{1,0...) custom-call(s32[1]{0:T(128)} %bitcast.4.bit_ref, ...), custom_call_target="tpu_custom_call", output_to_operand_aliasing={{0}: (11, {}), {1}: (12, {}), {2}: (13, {}), {3}: (14, {})} | custom-call | tf_op jit(solution)/shard_map/unpack_p/pallas_call | solution.py:827
  (59 shorter events, 1.3 us)
Async XLA Ops:
  0.7 12.6 %copy-start.2 = (s32[160]{0:T(256)S(1)}, s32[160]{0:T(256)}, u32[]{:S(2)}) copy-start(s32[160]{0:T(256)} %param.26) | copy-start | bytes 1924
  0.7 12.9 %copy-start = (s32[5]{0:T(128)S(1)}, s32[5]{0:T(128)}, u32[]{:S(2)}) copy-start(s32[5]{0:T(128)} %len_ref.6) | copy-start | bytes 64
  0.7 16.0 %copy-start.1 = (s32[5]{0:T(128)S(1)}, s32[5]{0:T(128)}, u32[]{:S(2)}) copy-start(s32[5]{0:T(128)} %len_ref.7) | copy-start | bytes 64
  5.9 17.9 %all-to-all-start = ((bf16[32,16,256]{2,1,0:T(8,128)(2,1)}), bf16[32,16,256]{2,1,0:T(8,128)(2,1)S(1)}, u32[]{:S(2)}, u32[]{:S(2)}) async-start(bf16[32,16,256]{2,1,0:T(8,128)(2,1)} %first.1), calls=%async_computation | async-start | bytes 524288 | tf_op jit(solution)/shard_map/all_to_all | solution.py:771
  31.0 2.4 %collective-permute-start = (bf16[1664,256]{1,0:T(8,128)(2,1)S(1)}, bf16[1664,256]{1,0:T(8,128)(2,1)S(1)}, u32[]{:S(2)}, u32[]{:S(2)}) collective-permute-start(bf16[1664,256]{1,0:T(8,128)(2,1)S(1)} %get-tuple-element.121), channel_id=1, source_target_pairs={{0,1},{1,0},{2,3},{3,2},{4,5},{5,4},{6,7},{7,6},{8,9},{9,8},{10,11... | collective-permute-start | bytes 2555912 | tf_op jit(solution)/shard_map/ppermute | solution.py:686
  33.7 23.5 %collective-permute-start.1 = (bf16[416,256]{1,0:T(8,128)(2,1)S(1)}, bf16[416,256]{1,0:T(8,128)(2,1)S(1)}, u32[]{:S(2)}, u32[]{:S(2)}) collective-permute-start(bf16[416,256]{1,0:T(8,128)(2,1)S(1)} %get-tuple-element.127), channel_id=1, source_target_pairs={{0,2},{1,3},{2,0},{3,1},{4,6},{5,7},{6,4},{7,5},{8,10},{9,11},{10,... | collective-permute-start | bytes 638984 | tf_op jit(solution)/shard_map/ppermute | solution.py:686
  35.4 21.8 %collective-permute-start.2 = (bf16[416,256]{1,0:T(8,128)(2,1)S(1)}, bf16[416,256]{1,0:T(8,128)(2,1)S(1)}, u32[]{:S(2)}, u32[]{:S(2)}) collective-permute-start(bf16[416,256]{1,0:T(8,128)(2,1)S(1)} %get-tuple-element.128), channel_id=1, source_target_pairs={{0,4},{1,5},{2,6},{3,7},{4,0},{5,1},{6,2},{7,3},{8,12},{9,13},{10,... | collective-permute-start | bytes 638984 | tf_op jit(solution)/shard_map/ppermute | solution.py:686
  36.8 20.4 %collective-permute-start.3 = (bf16[416,256]{1,0:T(8,128)(2,1)S(1)}, bf16[416,256]{1,0:T(8,128)(2,1)S(1)}, u32[]{:S(2)}, u32[]{:S(2)}) collective-permute-start(bf16[416,256]{1,0:T(8,128)(2,1)S(1)} %get-tuple-element.129), channel_id=1, source_target_pairs={{0,6},{1,7},{2,4},{3,5},{4,2},{5,3},{6,0},{7,1},{8,14},{9,15},{10,... | collective-permute-start | bytes 638984 | tf_op jit(solution)/shard_map/ppermute | solution.py:686
  57.2 4.7 %collective-permute-start.4 = (bf16[1664,256]{1,0:T(8,128)(2,1)S(1)}, bf16[1664,256]{1,0:T(8,128)(2,1)S(1)}, u32[]{:S(2)}, u32[]{:S(2)}) collective-permute-start(bf16[1664,256]{1,0:T(8,128)(2,1)S(1)} %get-tuple-element.138), channel_id=1, source_target_pairs={{0,1},{1,0},{2,3},{3,2},{4,5},{5,4},{6,7},{7,6},{8,9},{9,8},{10,11... | collective-permute-start | bytes 2555912 | tf_op jit(solution)/shard_map/ppermute | solution.py:686
  57.5 7.9 %collective-permute-start.8 = (bf16[104,256]{1,0:T(8,128)(2,1)S(1)}, bf16[104,256]{1,0:T(8,128)(2,1)S(1)}, u32[]{:S(2)}, u32[]{:S(2)}) collective-permute-start(bf16[104,256]{1,0:T(8,128)(2,1)S(1)} %get-tuple-element.140), channel_id=1, source_target_pairs={{0,8},{1,9},{2,10},{3,11},{4,12},{5,13},{6,14},{7,15},{8,0},{9,1},... | collective-permute-start | bytes 159752 | tf_op jit(solution)/shard_map/ppermute | solution.py:686
  59.1 6.7 %collective-permute-start.9 = (bf16[104,256]{1,0:T(8,128)(2,1)S(1)}, bf16[104,256]{1,0:T(8,128)(2,1)S(1)}, u32[]{:S(2)}, u32[]{:S(2)}) collective-permute-start(bf16[104,256]{1,0:T(8,128)(2,1)S(1)} %get-tuple-element.141), channel_id=1, source_target_pairs={{0,16},{1,17},{2,18},{3,19},{4,20},{5,21},{6,22},{7,23},{8,24},{9,... | collective-permute-start | bytes 159752 | tf_op jit(solution)/shard_map/ppermute | solution.py:686
  61.6 5.9 %collective-permute-start.10 = (bf16[104,256]{1,0:T(8,128)(2,1)S(1)}, bf16[104,256]{1,0:T(8,128)(2,1)S(1)}, u32[]{:S(2)}, u32[]{:S(2)}) collective-permute-start(bf16[104,256]{1,0:T(8,128)(2,1)S(1)} %get-tuple-element.142), channel_id=1, source_target_pairs={{0,24},{1,25},{2,26},{3,27},{4,28},{5,29},{6,30},{7,31},{8,16},{9,... | collective-permute-start | bytes 159752 | tf_op jit(solution)/shard_map/ppermute | solution.py:686
  62.3 8.2 %collective-permute-start.5 = (bf16[416,256]{1,0:T(8,128)(2,1)S(1)}, bf16[416,256]{1,0:T(8,128)(2,1)S(1)}, u32[]{:S(2)}, u32[]{:S(2)}) collective-permute-start(bf16[416,256]{1,0:T(8,128)(2,1)S(1)} %get-tuple-element.146), channel_id=1, source_target_pairs={{0,2},{1,3},{2,0},{3,1},{4,6},{5,7},{6,4},{7,5},{8,10},{9,11},{10,... | collective-permute-start | bytes 638984 | tf_op jit(solution)/shard_map/ppermute | solution.py:686
  64.0 11.1 %collective-permute-start.6 = (bf16[416,256]{1,0:T(8,128)(2,1)S(1)}, bf16[416,256]{1,0:T(8,128)(2,1)S(1)}, u32[]{:S(2)}, u32[]{:S(2)}) collective-permute-start(bf16[416,256]{1,0:T(8,128)(2,1)S(1)} %get-tuple-element.147), channel_id=1, source_target_pairs={{0,4},{1,5},{2,6},{3,7},{4,0},{5,1},{6,2},{7,3},{8,12},{9,13},{10,... | collective-permute-start | bytes 638984 | tf_op jit(solution)/shard_map/ppermute | solution.py:686
  65.4 9.6 %collective-permute-start.7 = (bf16[416,256]{1,0:T(8,128)(2,1)S(1)}, bf16[416,256]{1,0:T(8,128)(2,1)S(1)}, u32[]{:S(2)}, u32[]{:S(2)}) collective-permute-start(bf16[416,256]{1,0:T(8,128)(2,1)S(1)} %get-tuple-element.148), channel_id=1, source_target_pairs={{0,6},{1,7},{2,4},{3,5},{4,2},{5,3},{6,0},{7,1},{8,14},{9,15},{10,... | collective-permute-start | bytes 638984 | tf_op jit(solution)/shard_map/ppermute | solution.py:686
  67.5 11.6 %collective-permute-start.14 = (bf16[104,256]{1,0:T(8,128)(2,1)S(1)}, bf16[104,256]{1,0:T(8,128)(2,1)S(1)}, u32[]{:S(2)}, u32[]{:S(2)}) collective-permute-start(bf16[104,256]{1,0:T(8,128)(2,1)S(1)} %add_convert_fusion.1), channel_id=1, source_target_pairs={{0,8},{1,9},{2,10},{3,11},{4,12},{5,13},{6,14},{7,15},{8,0},{9,1},... | collective-permute-start | bytes 159752 | tf_op jit(solution)/shard_map/ppermute | solution.py:686
  67.6 12.1 %collective-permute-start.15 = (bf16[104,256]{1,0:T(8,128)(2,1)S(1)}, bf16[104,256]{1,0:T(8,128)(2,1)S(1)}, u32[]{:S(2)}, u32[]{:S(2)}) collective-permute-start(bf16[104,256]{1,0:T(8,128)(2,1)S(1)} %add_convert_fusion.1), channel_id=1, source_target_pairs={{0,16},{1,17},{2,18},{3,19},{4,20},{5,21},{6,22},{7,23},{8,24},{9,... | collective-permute-start | bytes 159752 | tf_op jit(solution)/shard_map/ppermute | solution.py:686
  70.6 9.1 %collective-permute-start.16 = (bf16[104,256]{1,0:T(8,128)(2,1)S(1)}, bf16[104,256]{1,0:T(8,128)(2,1)S(1)}, u32[]{:S(2)}, u32[]{:S(2)}) collective-permute-start(bf16[104,256]{1,0:T(8,128)(2,1)S(1)} %add_convert_fusion.1), channel_id=1, source_target_pairs={{0,24},{1,25},{2,26},{3,27},{4,28},{5,29},{6,30},{7,31},{8,16},{9,... | collective-permute-start | bytes 159752 | tf_op jit(solution)/shard_map/ppermute | solution.py:686
  75.2 6.6 %collective-permute-start.11 = (bf16[104,256]{1,0:T(8,128)(2,1)S(1)}, bf16[104,256]{1,0:T(8,128)(2,1)S(1)}, u32[]{:S(2)}, u32[]{:S(2)}) collective-permute-start(bf16[104,256]{1,0:T(8,128)(2,1)S(1)} %get-tuple-element.158), channel_id=1, source_target_pairs={{0,8},{1,9},{2,10},{3,11},{4,12},{5,13},{6,14},{7,15},{8,0},{9,1},... | collective-permute-start | bytes 159752 | tf_op jit(solution)/shard_map/ppermute | solution.py:686
  75.8 7.5 %collective-permute-start.12 = (bf16[104,256]{1,0:T(8,128)(2,1)S(1)}, bf16[104,256]{1,0:T(8,128)(2,1)S(1)}, u32[]{:S(2)}, u32[]{:S(2)}) collective-permute-start(bf16[104,256]{1,0:T(8,128)(2,1)S(1)} %get-tuple-element.159), channel_id=1, source_target_pairs={{0,16},{1,17},{2,18},{3,19},{4,20},{5,21},{6,22},{7,23},{8,24},{9,... | collective-permute-start | bytes 159752 | tf_op jit(solution)/shard_map/ppermute | solution.py:686
  79.2 6.5 %collective-permute-start.13 = (bf16[104,256]{1,0:T(8,128)(2,1)S(1)}, bf16[104,256]{1,0:T(8,128)(2,1)S(1)}, u32[]{:S(2)}, u32[]{:S(2)}) collective-permute-start(bf16[104,256]{1,0:T(8,128)(2,1)S(1)} %get-tuple-element.160), channel_id=1, source_target_pairs={{0,24},{1,25},{2,26},{3,27},{4,28},{5,29},{6,30},{7,31},{8,16},{9,... | collective-permute-start | bytes 159752 | tf_op jit(solution)/shard_map/ppermute | solution.py:686
  79.8 7.5 %collective-permute-start.20 = (bf16[416,256]{1,0:T(8,128)(2,1)S(1)}, bf16[416,256]{1,0:T(8,128)(2,1)S(1)}, u32[]{:S(2)}, u32[]{:S(2)}) collective-permute-start(bf16[416,256]{1,0:T(8,128)(2,1)S(1)} %bitcast.48), channel_id=1, source_target_pairs={{0,2},{1,3},{2,0},{3,1},{4,6},{5,7},{6,4},{7,5},{8,10},{9,11},{10,... | collective-permute-start | bytes 638984 | tf_op jit(solution)/shard_map/ppermute | solution.py:686
  81.0 9.4 %collective-permute-start.21 = (bf16[416,256]{1,0:T(8,128)(2,1)S(1)}, bf16[416,256]{1,0:T(8,128)(2,1)S(1)}, u32[]{:S(2)}, u32[]{:S(2)}) collective-permute-start(bf16[416,256]{1,0:T(8,128)(2,1)S(1)} %bitcast.49), channel_id=1, source_target_pairs={{0,4},{1,5},{2,6},{3,7},{4,0},{5,1},{6,2},{7,3},{8,12},{9,13},{10,... | collective-permute-start | bytes 638984 | tf_op jit(solution)/shard_map/ppermute | solution.py:686
  81.9 8.5 %collective-permute-start.22 = (bf16[416,256]{1,0:T(8,128)(2,1)S(1)}, bf16[416,256]{1,0:T(8,128)(2,1)S(1)}, u32[]{:S(2)}, u32[]{:S(2)}) collective-permute-start(bf16[416,256]{1,0:T(8,128)(2,1)S(1)} %bitcast.50), channel_id=1, source_target_pairs={{0,6},{1,7},{2,4},{3,5},{4,2},{5,3},{6,0},{7,1},{8,14},{9,15},{10,... | collective-permute-start | bytes 638984 | tf_op jit(solution)/shard_map/ppermute | solution.py:686
  85.7 4.9 %collective-permute-start.17 = (bf16[104,256]{1,0:T(8,128)(2,1)S(1)}, bf16[104,256]{1,0:T(8,128)(2,1)S(1)}, u32[]{:S(2)}, u32[]{:S(2)}) collective-permute-start(bf16[104,256]{1,0:T(8,128)(2,1)S(1)} %add_convert_fusion), channel_id=1, source_target_pairs={{0,8},{1,9},{2,10},{3,11},{4,12},{5,13},{6,14},{7,15},{8,0},{9,1},... | collective-permute-start | bytes 159752 | tf_op jit(solution)/shard_map/ppermute | solution.py:686
  85.8 5.1 %collective-permute-start.18 = (bf16[104,256]{1,0:T(8,128)(2,1)S(1)}, bf16[104,256]{1,0:T(8,128)(2,1)S(1)}, u32[]{:S(2)}, u32[]{:S(2)}) collective-permute-start(bf16[104,256]{1,0:T(8,128)(2,1)S(1)} %add_convert_fusion), channel_id=1, source_target_pairs={{0,16},{1,17},{2,18},{3,19},{4,20},{5,21},{6,22},{7,23},{8,24},{9,... | collective-permute-start | bytes 159752 | tf_op jit(solution)/shard_map/ppermute | solution.py:686
  87.3 5.9 %collective-permute-start.19 = (bf16[104,256]{1,0:T(8,128)(2,1)S(1)}, bf16[104,256]{1,0:T(8,128)(2,1)S(1)}, u32[]{:S(2)}, u32[]{:S(2)}) collective-permute-start(bf16[104,256]{1,0:T(8,128)(2,1)S(1)} %add_convert_fusion), channel_id=1, source_target_pairs={{0,24},{1,25},{2,26},{3,27},{4,28},{5,29},{6,30},{7,31},{8,16},{9,... | collective-permute-start | bytes 159752 | tf_op jit(solution)/shard_map/ppermute | solution.py:686
  90.5 10.5 %collective-permute-start.26 = (bf16[1664,256]{1,0:T(8,128)(2,1)S(1)}, bf16[1664,256]{1,0:T(8,128)(2,1)S(1)}, u32[]{:S(2)}, u32[]{:S(2)}) collective-permute-start(bf16[1664,256]{1,0:T(8,128)(2,1)S(1)} %bitcast.41), channel_id=1, source_target_pairs={{0,1},{1,0},{2,3},{3,2},{4,5},{5,4},{6,7},{7,6},{8,9},{9,8},{10,11... | collective-permute-start | bytes 2555912 | tf_op jit(solution)/shard_map/ppermute | solution.py:686
  93.4 9.5 %collective-permute-start.23 = (bf16[416,256]{1,0:T(8,128)(2,1)S(1)}, bf16[416,256]{1,0:T(8,128)(2,1)S(1)}, u32[]{:S(2)}, u32[]{:S(2)}) collective-permute-start(bf16[416,256]{1,0:T(8,128)(2,1)S(1)} %bitcast.43), channel_id=1, source_target_pairs={{0,2},{1,3},{2,0},{3,1},{4,6},{5,7},{6,4},{7,5},{8,10},{9,11},{10,... | collective-permute-start | bytes 638984 | tf_op jit(solution)/shard_map/ppermute | solution.py:686
  94.7 9.4 %collective-permute-start.24 = (bf16[416,256]{1,0:T(8,128)(2,1)S(1)}, bf16[416,256]{1,0:T(8,128)(2,1)S(1)}, u32[]{:S(2)}, u32[]{:S(2)}) collective-permute-start(bf16[416,256]{1,0:T(8,128)(2,1)S(1)} %bitcast.44), channel_id=1, source_target_pairs={{0,4},{1,5},{2,6},{3,7},{4,0},{5,1},{6,2},{7,3},{8,12},{9,13},{10,... | collective-permute-start | bytes 638984 | tf_op jit(solution)/shard_map/ppermute | solution.py:686
  95.5 8.6 %collective-permute-start.25 = (bf16[416,256]{1,0:T(8,128)(2,1)S(1)}, bf16[416,256]{1,0:T(8,128)(2,1)S(1)}, u32[]{:S(2)}, u32[]{:S(2)}) collective-permute-start(bf16[416,256]{1,0:T(8,128)(2,1)S(1)} %bitcast.45), channel_id=1, source_target_pairs={{0,6},{1,7},{2,4},{3,5},{4,2},{5,3},{6,0},{7,1},{8,14},{9,15},{10,... | collective-permute-start | bytes 638984 | tf_op jit(solution)/shard_map/ppermute | solution.py:686
  101.1 3.6 %collective-permute-start.27 = (bf16[416,256]{1,0:T(8,128)(2,1)S(1)}, bf16[416,256]{1,0:T(8,128)(2,1)S(1)}, u32[]{:S(2)}, u32[]{:S(2)}) collective-permute-start(bf16[416,256]{1,0:T(8,128)(2,1)S(1)} %bitcast.46), channel_id=1, source_target_pairs={{0,1},{1,0},{2,3},{3,2},{4,5},{5,4},{6,7},{7,6},{8,9},{9,8},{10,11... | collective-permute-start | bytes 638984 | tf_op jit(solution)/shard_map/ppermute | solution.py:686
  104.1 1.5 %collective-permute-start.28 = (bf16[416,256]{1,0:T(8,128)(2,1)S(1)}, bf16[416,256]{1,0:T(8,128)(2,1)S(1)}, u32[]{:S(2)}, u32[]{:S(2)}) collective-permute-start(bf16[416,256]{1,0:T(8,128)(2,1)S(1)} %collective-permute-done.23.refs_1_), channel_id=1, source_target_pairs={{0,1},{1,0},{2,3},{3,2},{4,5},{5,4},{6,7},{7,6},{8,9},{9,8},{10,11... | collective-permute-start | bytes 638984 | tf_op jit(solution)/shard_map/ppermute | solution.py:686
  104.1 1.8 %collective-permute-start.29 = (bf16[416,256]{1,0:T(8,128)(2,1)S(1)}, bf16[416,256]{1,0:T(8,128)(2,1)S(1)}, u32[]{:S(2)}, u32[]{:S(2)}) collective-permute-start(bf16[416,256]{1,0:T(8,128)(2,1)S(1)} %collective-permute-done.24.refs_2_), channel_id=1, source_target_pairs={{0,1},{1,0},{2,3},{3,2},{4,5},{5,4},{6,7},{7,6},{8,9},{9,8},{10,11... | collective-permute-start | bytes 638984 | tf_op jit(solution)/shard_map/ppermute | solution.py:686
  104.6 1.6 %collective-permute-start.30 = (bf16[416,256]{1,0:T(8,128)(2,1)S(1)}, bf16[416,256]{1,0:T(8,128)(2,1)S(1)}, u32[]{:S(2)}, u32[]{:S(2)}) collective-permute-start(bf16[416,256]{1,0:T(8,128)(2,1)S(1)} %collective-permute-done.25.refs_3_), channel_id=1, source_target_pairs={{0,1},{1,0},{2,3},{3,2},{4,5},{5,4},{6,7},{7,6},{8,9},{9,8},{10,11... | collective-permute-start | bytes 638984 | tf_op jit(solution)/shard_map/ppermute | solution.py:686

commit v10 on v9

--- a/solution.py
+++ b/solution.py
@@ -481,7 +481,8 @@
     layer_kernel(0, 1, seqs, length, bit_ref, len_ref, gq_ref, *inputs, *outputs[:5], *scratch[3:])
 
 
-def combine_kernel(radix, digit_ref, *refs):
+def combine_kernel(distances, digit_ref, *refs):
+    radix = len(distances) + 1
     total_ref = refs[-1]
     sends = refs[-1 - (radix - 1) : -1]
     keep_ref = refs[-1 - radix]
@@ -497,8 +498,8 @@
         return total_ref[pl.ds(pl.multiple_of(which * part, part), part), :].astype(bf16)
 
     keep_ref[...] = section(digit)
-    for step, ref in enumerate(sends, start=1):
-        ref[...] = section(digit ^ step)
+    for distance, ref in zip(distances, sends):
+        ref[...] = section(digit ^ distance)
 
 
 VECTOR_OUTS = (QUERY_BIAS, VALUE_BIAS, PROJ_BIAS, ATTN_GAIN, ATTN_SHIFT, DOWN_BIAS, FFN_GAIN, FFN_SHIFT)
@@ -686,8 +687,13 @@
     return lax.ppermute(values, "dp", [(i, i ^ mask) for i in range(count)])
 
 
+def visits(group):
+    distances = list(range(1, 2 ** len(group)))
+    return distances[::-1] if group[0] >= 8 else distances
+
+
 def combos(group):
-    return [index * group[0] for index in range(1, 2 ** len(group))]
+    return [distance * group[0] for distance in visits(group)]
 
 
 def combine(pieces, group, me):
@@ -697,7 +703,7 @@
     part = rows // radix
     if part % 8 == 0:
         return pl.pallas_call(
-            functools.partial(combine_kernel, radix),
+            functools.partial(combine_kernel, tuple(visits(group))),
             out_shape=[shape((part, WIDTH), bf16)] * radix,
             grid=(1,),
             in_specs=[smem()] + [whole((rows, WIDTH))] * len(pieces),
@@ -710,7 +716,7 @@
     for piece in pieces[1:]:
         total = total + piece.astype(f32)
     split = total.astype(bf16).reshape(radix, part, WIDTH)
-    return [lax.dynamic_index_in_dim(split, digit ^ step, 0, keepdims=False) for step in range(radix)]
+    return [lax.dynamic_index_in_dim(split, digit ^ distance, 0, keepdims=False) for distance in [0] + visits(group)]
 
 
 def send_parts(cut, group, count):
@@ -733,8 +739,8 @@
     radix = 2 ** len(group)
     digit = (me // group[0]) % radix
     joined = jnp.zeros((radix,) + pieces[0].shape, pieces[0].dtype)
-    for step, piece in enumerate(pieces):
-        joined = lax.dynamic_update_index_in_dim(joined, piece, digit ^ step, 0)
+    for distance, piece in zip([0] + visits(group), pieces):
+        joined = lax.dynamic_update_index_in_dim(joined, piece, digit ^ distance, 0)
     return joined.reshape((radix * pieces[0].shape[0],) + pieces[0].shape[1:])
 
 

time: 109 us -> 108 us (level)
  transfers between devices with their start and end apart: 32 -> 32, of which waited for: 12 -> 13; matrix products, arithmetic and copies ran while one was open for 1% -> 1% of each run, Pallas kernels for 35% -> 36%
where the time goes in v10:
time: 108 us; the launch traced here: 107 us
  Pallas kernels  52.7 us (49%)
  starting transfers between devices  40.6 us (38%)
  waiting for transfers between devices  11.7 us (11%)
  local copies, waits for them, and re-layouts  1.19 us (1%)
  between operations  1.14 us (1%)
    ppermute x31, starting transfers between devices, partner_send(): return lax.ppermute(values, 'dp', [(i, i ^ mask) for i in range(count)])  33.3 us
    pallas_call x2, Pallas kernels, layer(): pl.pallas_call(kernel, out_shape=[shape((total, WIDTH), bf16), pltpu.HBM(...  27.1 us
    ppermute x31, waiting for transfers between devices, partner_send(): return lax.ppermute(values, 'dp', [(i, i ^ mask) for i in range(count)])  11.5 us
    pallas_call x2, Pallas kernels, attend(): pl.pallas_call(functools.partial(attend_long_kernel if seqs == 1 else att...  10 us
    all_to_all x1, starting transfers between devices, body(): all_cls = lax.all_to_all(own_cls, 'dp', 0, 0, tiled=True)  7.3 us
    pallas_call x2, Pallas kernels, input_grad(): pl.pallas_call(input_grad_kernel, out_shape=shape((total, WIDTH), bf16),...  5.76 us
    pallas_call x1, Pallas kernels, first_call(): pl.pallas_call(functools.partial(first_kernel, local), out_shape=shape((c...  5.22 us
  transfers between devices with their start and end apart: 32, of which 13 were waited for; matrix products, arithmetic and copies ran while one was open for 1% of the time, Pallas kernels for 36%

profile of v10, /device:TPU:0, one launch (start us, length us, event | category | flops | bytes accessed | tf_op | source)
XLA Modules:
  0.0 107.4 jit_solution(12578881099768622482)
XLA Ops:
  0.7 5.2 %first.1 = bf16[32,16,256]{2,1,0:T(8,128)(2,1)} custom-call(s32[5]{0:T(128)} %len_ref.6, s32[5]{0:T(128)} %len_ref.7, bf16[320,256]{1,0:T(8,128)(2,1)} %bitcast.52, bf16[1280,256]{1,0:T(8,128)(2,1)} %bitcast.56, bf16[2,256,768]{2,1,0:T(8,128)(2,1)} %wqkv_ref.9, bf16[2,256]{1,0:T(2,128)(2,1)} %qb_ref.5, bf16[2,256]{1,0:T(2,128)(2,1)} %vb_ref.5, ...), custom_call_target="tpu_custom_call" | custom-call | tf_op jit(solution)/shard_map/first/pallas_call | solution.py:578
  5.9 7.3 %all-to-all-start = ((bf16[32,16,256]{2,1,0:T(8,128)(2,1)}), bf16[32,16,256]{2,1,0:T(8,128)(2,1)S(1)}, u32[]{:S(2)}, u32[]{:S(2)}) async-start(bf16[32,16,256]{2,1,0:T(8,128)(2,1)} %first.1), calls=%async_computation | async-start | bytes 524288 | tf_op jit(solution)/shard_map/all_to_all | solution.py:777
  13.6 3.1 %attend.3 = (bf16[320,768]{1,0:T(8,128)(2,1)}, f32[320,256]{1,0:T(8,128)}, bf16[320,256]{1,0:T(8,128)(2,1)}) custom-call(s32[5]{0:T(128)S(1)} %copy-done, bf16[320,256]{1,0:T(8,128)(2,1)} %bitcast.53, bf16[2,256,768]{2,1,0:T(8,128)(2,1)} %wqkv_ref.9, bf16[2,256]{1,0:T(2,128)(2,1)} %qb_ref.5, bf16[2,256]{1,0:T(2,128)(2,1)} %vb_ref.5), custom_call_target="tpu_custom_call" | custom-call | flops 256000000 | bytes 1920000 | tf_op jit(solution)/shard_map/attend/pallas_call | solution.py:595
  16.7 6.9 %attend.2 = (bf16[1280,768]{1,0:T(8,128)(2,1)}, f32[5120,256]{1,0:T(8,128)}, bf16[1280,256]{1,0:T(8,128)(2,1)}) custom-call(s32[5]{0:T(128)S(1)} %copy-done.1, bf16[1280,256]{1,0:T(8,128)(2,1)} %bitcast.57, bf16[2,256,768]{2,1,0:T(8,128)(2,1)} %wqkv_ref.9, bf16[2,256]{1,0:T(2,128)(2,1)} %qb_ref.5, bf16[2,256]{1,0:T(2,128)(2,1)} %vb_ref.5), custom_call_target="tpu_custom_call" | custom-call | flops 1024000000 | bytes 7680000 | tf_op jit(solution)/shard_map/attend/pallas_call | solution.py:595
  23.6 0.2 all-to-all-done.all_ref
  23.8 7.2 %layer.2 = (bf16[320,256]{1,0:T(8,128)(2,1)}, f32[320,256]{1,0:T(8,128)}, bf16[320,768]{1,0:T(8,128)(2,1)}, bf16[1664,256]{1,0:T(8,128)(2,1)S(1)}, bf16[1664,256...) custom-call(s32[1]{0:T(128)} %bitcast.me_ref, bf16[32,16,256]{2,1,0:T(8,128)(2,1)S(1)} %all-to-all-done.all_ref, ...), custom_call_target="tpu_custom_call" | custom-call | flops 1536000000 | bytes 1280000 | tf_op jit(solution)/shard_map/layer/pallas_call | solution.py:626
  31.1 2.2 %input_grad.2 = bf16[320,256]{1,0:T(8,128)(2,1)} custom-call(f32[320,256]{1,0:T(8,128)} %get-tuple-element.122.one_ref, bf16[320,768]{1,0:T(8,128)(2,1)} %get-tuple-element.123.gqkv_ref, bf16[2,256,768]{2,1,0:T(8,128)(2,1)} %wqkv_ref.9), custom_call_target="tpu_custom_call" | custom-call | flops 128000000 | bytes 960000 | tf_op jit(solution)/shard_map/input_grad/pallas_call | solution.py:660
  33.4 0.4 combine.4
  33.7 1.7 %collective-permute-start.1 = (bf16[416,256]{1,0:T(8,128)(2,1)S(1)}, bf16[416,256]{1,0:T(8,128)(2,1)S(1)}, u32[]{:S(2)}, u32[]{:S(2)}) collective-permute-start(bf16[416,256]{1,0:T(8,128)(2,1)S(1)} %get-tuple-element.127), channel_id=1, source_target_pairs={{0,2},{1,3},{2,0},{3,1},{4,6},{5,7},{6,4},{7,5},{8,10},{9,11},{10,... | collective-permute-start | bytes 638984 | tf_op jit(solution)/shard_map/ppermute | solution.py:687
  35.4 1.5 %collective-permute-start.2 = (bf16[416,256]{1,0:T(8,128)(2,1)S(1)}, bf16[416,256]{1,0:T(8,128)(2,1)S(1)}, u32[]{:S(2)}, u32[]{:S(2)}) collective-permute-start(bf16[416,256]{1,0:T(8,128)(2,1)S(1)} %get-tuple-element.128), channel_id=1, source_target_pairs={{0,4},{1,5},{2,6},{3,7},{4,0},{5,1},{6,2},{7,3},{8,12},{9,13},{10,... | collective-permute-start | bytes 638984 | tf_op jit(solution)/shard_map/ppermute | solution.py:687
  36.8 0.4 collective-permute-start.3
  37.3 19.9 %layer.3 = (bf16[1280,256]{1,0:T(8,128)(2,1)}, f32[1280,256]{1,0:T(8,128)}, bf16[1280,768]{1,0:T(8,128)(2,1)}, bf16[1664,256]{1,0:T(8,128)(2,1)S(1)}, bf16[1664,256]{1,0:T(8,128)(2,1)S(1)}) custom-call(s32[1]{0:T(128)} %bitcast.4.bit_ref, s32[5]{0:T(128)S(1)} %copy-done.1, f32[8,256]{1,0:T(8,128)S(1)} %get-tuple-element.130.cls_ref, ...), custom_call_target="tpu_custom_call" | custom-call | flops 6144000000 | bytes 5120000 | tf_op jit(solution)/shard_map/layer/pallas_call | solution.py:626
  57.3 0.2 combine.5
  57.5 3.5 %collective-permute-start.8 = (bf16[104,256]{1,0:T(8,128)(2,1)S(1)}, bf16[104,256]{1,0:T(8,128)(2,1)S(1)}, u32[]{:S(2)}, u32[]{:S(2)}) collective-permute-start(bf16[104,256]{1,0:T(8,128)(2,1)S(1)} %get-tuple-element.140), channel_id=1, source_target_pairs={{0,24},{1,25},{2,26},{3,27},{4,28},{5,29},{6,30},{7,31},{8,16},{9,... | collective-permute-start | bytes 159752 | tf_op jit(solution)/shard_map/ppermute | solution.py:687
  61.0 1.0 collective-permute-start.10
  62.0 0.4 combine.6
  62.3 1.7 %collective-permute-start.5 = (bf16[416,256]{1,0:T(8,128)(2,1)S(1)}, bf16[416,256]{1,0:T(8,128)(2,1)S(1)}, u32[]{:S(2)}, u32[]{:S(2)}) collective-permute-start(bf16[416,256]{1,0:T(8,128)(2,1)S(1)} %get-tuple-element.146), channel_id=1, source_target_pairs={{0,2},{1,3},{2,0},{3,1},{4,6},{5,7},{6,4},{7,5},{8,10},{9,11},{10,... | collective-permute-start | bytes 638984 | tf_op jit(solution)/shard_map/ppermute | solution.py:687
  64.0 1.4 %collective-permute-start.6 = (bf16[416,256]{1,0:T(8,128)(2,1)S(1)}, bf16[416,256]{1,0:T(8,128)(2,1)S(1)}, u32[]{:S(2)}, u32[]{:S(2)}) collective-permute-start(bf16[416,256]{1,0:T(8,128)(2,1)S(1)} %get-tuple-element.147), channel_id=1, source_target_pairs={{0,4},{1,5},{2,6},{3,7},{4,0},{5,1},{6,2},{7,3},{8,12},{9,13},{10,... | collective-permute-start | bytes 638984 | tf_op jit(solution)/shard_map/ppermute | solution.py:687
  65.4 0.7 collective-permute-start.7
  66.1 0.1 collective-permute-done.9
  66.3 3.8 %collective-permute-start.14 = (bf16[104,256]{1,0:T(8,128)(2,1)S(1)}, bf16[104,256]{1,0:T(8,128)(2,1)S(1)}, u32[]{:S(2)}, u32[]{:S(2)}) collective-permute-start(bf16[104,256]{1,0:T(8,128)(2,1)S(1)} %add_convert_fusion.1), channel_id=1, source_target_pairs={{0,24},{1,25},{2,26},{3,27},{4,28},{5,29},{6,30},{7,31},{8,16},{9,... | collective-permute-start | bytes 159752 | tf_op jit(solution)/shard_map/ppermute | solution.py:687
  70.1 0.5 collective-permute-done.5.refs_1_
  70.6 1.0 collective-permute-start.16
  71.6 3.5 %collective-permute-done.6.refs_2_ = bf16[416,256]{1,0:T(8,128)(2,1)S(1)} collective-permute-done((bf16[416,256]{1,0:T(8,128)(2,1)S(1)}, bf16[416,256]{1,0:T(8,128)(2,1)S(1)}, u32[]{:S(2)}, u32[]{:S(2)}) %collective-permute-start.6) | collective-permute-done | bytes 213024 | tf_op jit(solution)/shard_map/ppermute | solution.py:687
  75.0 0.2 combine.7
  75.2 3.4 %collective-permute-start.11 = (bf16[104,256]{1,0:T(8,128)(2,1)S(1)}, bf16[104,256]{1,0:T(8,128)(2,1)S(1)}, u32[]{:S(2)}, u32[]{:S(2)}) collective-permute-start(bf16[104,256]{1,0:T(8,128)(2,1)S(1)} %get-tuple-element.158), channel_id=1, source_target_pairs={{0,24},{1,25},{2,26},{3,27},{4,28},{5,29},{6,30},{7,31},{8,16},{9,... | collective-permute-start | bytes 159752 | tf_op jit(solution)/shard_map/ppermute | solution.py:687
  78.6 1.1 collective-permute-start.13
  79.8 1.2 %collective-permute-start.20 = (bf16[416,256]{1,0:T(8,128)(2,1)S(1)}, bf16[416,256]{1,0:T(8,128)(2,1)S(1)}, u32[]{:S(2)}, u32[]{:S(2)}) collective-permute-start(bf16[416,256]{1,0:T(8,128)(2,1)S(1)} %bitcast.48), channel_id=1, source_target_pairs={{0,2},{1,3},{2,0},{3,1},{4,6},{5,7},{6,4},{7,5},{8,10},{9,11},{10,... | collective-permute-start | bytes 638984 | tf_op jit(solution)/shard_map/ppermute | solution.py:687
  81.0 0.8 collective-permute-start.21
  81.9 1.5 %collective-permute-start.22 = (bf16[416,256]{1,0:T(8,128)(2,1)S(1)}, bf16[416,256]{1,0:T(8,128)(2,1)S(1)}, u32[]{:S(2)}, u32[]{:S(2)}) collective-permute-start(bf16[416,256]{1,0:T(8,128)(2,1)S(1)} %bitcast.50), channel_id=1, source_target_pairs={{0,6},{1,7},{2,4},{3,5},{4,2},{5,3},{6,0},{7,1},{8,14},{9,15},{10,... | collective-permute-start | bytes 638984 | tf_op jit(solution)/shard_map/ppermute | solution.py:687
  83.3 0.3 collective-permute-done.12
  83.7 3.1 %collective-permute-start.17 = (bf16[104,256]{1,0:T(8,128)(2,1)S(1)}, bf16[104,256]{1,0:T(8,128)(2,1)S(1)}, u32[]{:S(2)}, u32[]{:S(2)}) collective-permute-start(bf16[104,256]{1,0:T(8,128)(2,1)S(1)} %add_convert_fusion), channel_id=1, source_target_pairs={{0,24},{1,25},{2,26},{3,27},{4,28},{5,29},{6,30},{7,31},{8,16},{9,... | collective-permute-start | bytes 159752 | tf_op jit(solution)/shard_map/ppermute | solution.py:687
  86.8 0.2 collective-permute-done.20
  87.0 1.3 %collective-permute-start.19 = (bf16[104,256]{1,0:T(8,128)(2,1)S(1)}, bf16[104,256]{1,0:T(8,128)(2,1)S(1)}, u32[]{:S(2)}, u32[]{:S(2)}) collective-permute-start(bf16[104,256]{1,0:T(8,128)(2,1)S(1)} %add_convert_fusion), channel_id=1, source_target_pairs={{0,8},{1,9},{2,10},{3,11},{4,12},{5,13},{6,14},{7,15},{8,0},{9,1},... | collective-permute-start | bytes 159752 | tf_op jit(solution)/shard_map/ppermute | solution.py:687
  88.3 2.1 %collective-permute-done.21 = bf16[416,256]{1,0:T(8,128)(2,1)S(1)} collective-permute-done((bf16[416,256]{1,0:T(8,128)(2,1)S(1)}, bf16[416,256]{1,0:T(8,128)(2,1)S(1)}, u32[]{:S(2)}, u32[]{:S(2)}) %collective-permute-start.21) | collective-permute-done | bytes 213024 | tf_op jit(solution)/shard_map/ppermute | solution.py:687
  90.6 1.2 %collective-permute-done.18 = bf16[104,256]{1,0:T(8,128)(2,1)S(1)} collective-permute-done((bf16[104,256]{1,0:T(8,128)(2,1)S(1)}, bf16[104,256]{1,0:T(8,128)(2,1)S(1)}, u32[]{:S(2)}, u32[]{:S(2)}) %collective-permute-start.18) | collective-permute-done | bytes 53280 | tf_op jit(solution)/shard_map/ppermute | solution.py:687
  91.9 1.3 %collective-permute-start.23 = (bf16[416,256]{1,0:T(8,128)(2,1)S(1)}, bf16[416,256]{1,0:T(8,128)(2,1)S(1)}, u32[]{:S(2)}, u32[]{:S(2)}) collective-permute-start(bf16[416,256]{1,0:T(8,128)(2,1)S(1)} %bitcast.43), channel_id=1, source_target_pairs={{0,2},{1,3},{2,0},{3,1},{4,6},{5,7},{6,4},{7,5},{8,10},{9,11},{10,... | collective-permute-start | bytes 638984 | tf_op jit(solution)/shard_map/ppermute | solution.py:687
  93.2 0.8 collective-permute-start.24
  94.0 1.4 %collective-permute-start.25 = (bf16[416,256]{1,0:T(8,128)(2,1)S(1)}, bf16[416,256]{1,0:T(8,128)(2,1)S(1)}, u32[]{:S(2)}, u32[]{:S(2)}) collective-permute-start(bf16[416,256]{1,0:T(8,128)(2,1)S(1)} %bitcast.45), channel_id=1, source_target_pairs={{0,6},{1,7},{2,4},{3,5},{4,2},{5,3},{6,0},{7,1},{8,14},{9,15},{10,... | collective-permute-start | bytes 638984 | tf_op jit(solution)/shard_map/ppermute | solution.py:687
  95.5 0.6 slice_reduce_fusion
  96.1 3.5 %input_grad.3 = bf16[1280,256]{1,0:T(8,128)(2,1)} custom-call(f32[1280,256]{1,0:T(8,128)} %get-tuple-element.134.one_ref, bf16[1280,768]{1,0:T(8,128)(2,1)} %get-tuple-element.135.gqkv_ref, bf16[2,256,768]{2,1,0:T(8,128)(2,1)} %wqkv_ref.9), custom_call_target="tpu_custom_call" | custom-call | flops 512000000 | bytes 3840000 | tf_op jit(solution)/shard_map/input_grad/pallas_call | solution.py:660
  99.6 1.8 %unpack_q.1 = (f32[2,256,768]{2,1,0:T(8,128)}, f32[2,256,256]{2,1,0:T(8,128)}, f32[2,256,1024]{2,1,0:T(8,128)}, f32[2,1024,256]{2,1,0:T(8,128)}, f32[16,256]{1,0:T(8,128)S(1)}) custom-call(s32[1]{0:T(128)} %bitcast.4.bit_ref, bf16[1664,256]{1,0:T(8,128)(2,1)S(1)} %bitcast.42, bf16[1664,256]{1,0:T(8,128)(2,1)S(1)} %collective-permute-done.26.other_ref), custom_call_target="tpu_custom_call" | custom-call | tf_op jit(solution)/shard_map/unpack_q/pallas_call | solution.py:816
  101.4 1.9 %collective-permute-done.24.refs_2_ = bf16[416,256]{1,0:T(8,128)(2,1)S(1)} collective-permute-done((bf16[416,256]{1,0:T(8,128)(2,1)S(1)}, bf16[416,256]{1,0:T(8,128)(2,1)S(1)}, u32[]{:S(2)}, u32[]{:S(2)}) %collective-permute-start.24) | collective-permute-done | bytes 213024 | tf_op jit(solution)/shard_map/ppermute | solution.py:687
  103.4 0.5 collective-permute-start.29
  103.9 0.9 collective-permute-done.28.refs_5_
  104.8 0.3 collective-permute-done.29.refs_6_
  105.1 0.3 collective-permute-done.30.refs_7_
  105.4 1.8 %unpack_p.1 = (f32[2,256,768]{2,1,0:T(8,128)}, f32[2,256,256]{2,1,0:T(8,128)}, f32[2,256,1024]{2,1,0:T(8,128)}, f32[2,1024,256]{2,1,0:T(8,128)}, f32[2,1024]{1,0...) custom-call(s32[1]{0:T(128)} %bitcast.4.bit_ref, ...), custom_call_target="tpu_custom_call", output_to_operand_aliasing={{0}: (11, {}), {1}: (12, {}), {2}: (13, {}), {3}: (14, {})} | custom-call | tf_op jit(solution)/shard_map/unpack_p/pallas_call | solution.py:833
  (59 shorter events, 1.0 us)
Async XLA Ops:
  0.7 12.6 %copy-start.2 = (s32[160]{0:T(256)S(1)}, s32[160]{0:T(256)}, u32[]{:S(2)}) copy-start(s32[160]{0:T(256)} %param.26) | copy-start | bytes 1924
  0.7 12.9 %copy-start = (s32[5]{0:T(128)S(1)}, s32[5]{0:T(128)}, u32[]{:S(2)}) copy-start(s32[5]{0:T(128)} %len_ref.6) | copy-start | bytes 64
  0.7 16.0 %copy-start.1 = (s32[5]{0:T(128)S(1)}, s32[5]{0:T(128)}, u32[]{:S(2)}) copy-start(s32[5]{0:T(128)} %len_ref.7) | copy-start | bytes 64
  5.9 17.9 %all-to-all-start = ((bf16[32,16,256]{2,1,0:T(8,128)(2,1)}), bf16[32,16,256]{2,1,0:T(8,128)(2,1)S(1)}, u32[]{:S(2)}, u32[]{:S(2)}) async-start(bf16[32,16,256]{2,1,0:T(8,128)(2,1)} %first.1), calls=%async_computation | async-start | bytes 524288 | tf_op jit(solution)/shard_map/all_to_all | solution.py:777
  31.0 2.4 %collective-permute-start = (bf16[1664,256]{1,0:T(8,128)(2,1)S(1)}, bf16[1664,256]{1,0:T(8,128)(2,1)S(1)}, u32[]{:S(2)}, u32[]{:S(2)}) collective-permute-start(bf16[1664,256]{1,0:T(8,128)(2,1)S(1)} %get-tuple-element.121), channel_id=1, source_target_pairs={{0,1},{1,0},{2,3},{3,2},{4,5},{5,4},{6,7},{7,6},{8,9},{9,8},{10,11... | collective-permute-start | bytes 2555912 | tf_op jit(solution)/shard_map/ppermute | solution.py:687
  33.7 23.5 %collective-permute-start.1 = (bf16[416,256]{1,0:T(8,128)(2,1)S(1)}, bf16[416,256]{1,0:T(8,128)(2,1)S(1)}, u32[]{:S(2)}, u32[]{:S(2)}) collective-permute-start(bf16[416,256]{1,0:T(8,128)(2,1)S(1)} %get-tuple-element.127), channel_id=1, source_target_pairs={{0,2},{1,3},{2,0},{3,1},{4,6},{5,7},{6,4},{7,5},{8,10},{9,11},{10,... | collective-permute-start | bytes 638984 | tf_op jit(solution)/shard_map/ppermute | solution.py:687
  35.4 21.8 %collective-permute-start.2 = (bf16[416,256]{1,0:T(8,128)(2,1)S(1)}, bf16[416,256]{1,0:T(8,128)(2,1)S(1)}, u32[]{:S(2)}, u32[]{:S(2)}) collective-permute-start(bf16[416,256]{1,0:T(8,128)(2,1)S(1)} %get-tuple-element.128), channel_id=1, source_target_pairs={{0,4},{1,5},{2,6},{3,7},{4,0},{5,1},{6,2},{7,3},{8,12},{9,13},{10,... | collective-permute-start | bytes 638984 | tf_op jit(solution)/shard_map/ppermute | solution.py:687
  36.8 20.4 %collective-permute-start.3 = (bf16[416,256]{1,0:T(8,128)(2,1)S(1)}, bf16[416,256]{1,0:T(8,128)(2,1)S(1)}, u32[]{:S(2)}, u32[]{:S(2)}) collective-permute-start(bf16[416,256]{1,0:T(8,128)(2,1)S(1)} %get-tuple-element.129), channel_id=1, source_target_pairs={{0,6},{1,7},{2,4},{3,5},{4,2},{5,3},{6,0},{7,1},{8,14},{9,15},{10,... | collective-permute-start | bytes 638984 | tf_op jit(solution)/shard_map/ppermute | solution.py:687
  57.2 4.7 %collective-permute-start.4 = (bf16[1664,256]{1,0:T(8,128)(2,1)S(1)}, bf16[1664,256]{1,0:T(8,128)(2,1)S(1)}, u32[]{:S(2)}, u32[]{:S(2)}) collective-permute-start(bf16[1664,256]{1,0:T(8,128)(2,1)S(1)} %get-tuple-element.138), channel_id=1, source_target_pairs={{0,1},{1,0},{2,3},{3,2},{4,5},{5,4},{6,7},{7,6},{8,9},{9,8},{10,11... | collective-permute-start | bytes 2555912 | tf_op jit(solution)/shard_map/ppermute | solution.py:687
  57.5 7.9 %collective-permute-start.8 = (bf16[104,256]{1,0:T(8,128)(2,1)S(1)}, bf16[104,256]{1,0:T(8,128)(2,1)S(1)}, u32[]{:S(2)}, u32[]{:S(2)}) collective-permute-start(bf16[104,256]{1,0:T(8,128)(2,1)S(1)} %get-tuple-element.140), channel_id=1, source_target_pairs={{0,24},{1,25},{2,26},{3,27},{4,28},{5,29},{6,30},{7,31},{8,16},{9,... | collective-permute-start | bytes 159752 | tf_op jit(solution)/shard_map/ppermute | solution.py:687
  61.0 5.3 %collective-permute-start.9 = (bf16[104,256]{1,0:T(8,128)(2,1)S(1)}, bf16[104,256]{1,0:T(8,128)(2,1)S(1)}, u32[]{:S(2)}, u32[]{:S(2)}) collective-permute-start(bf16[104,256]{1,0:T(8,128)(2,1)S(1)} %get-tuple-element.141), channel_id=1, source_target_pairs={{0,16},{1,17},{2,18},{3,19},{4,20},{5,21},{6,22},{7,23},{8,24},{9,... | collective-permute-start | bytes 159752 | tf_op jit(solution)/shard_map/ppermute | solution.py:687
  61.0 5.3 %collective-permute-start.10 = (bf16[104,256]{1,0:T(8,128)(2,1)S(1)}, bf16[104,256]{1,0:T(8,128)(2,1)S(1)}, u32[]{:S(2)}, u32[]{:S(2)}) collective-permute-start(bf16[104,256]{1,0:T(8,128)(2,1)S(1)} %get-tuple-element.142), channel_id=1, source_target_pairs={{0,8},{1,9},{2,10},{3,11},{4,12},{5,13},{6,14},{7,15},{8,0},{9,1},... | collective-permute-start | bytes 159752 | tf_op jit(solution)/shard_map/ppermute | solution.py:687
  62.3 8.2 %collective-permute-start.5 = (bf16[416,256]{1,0:T(8,128)(2,1)S(1)}, bf16[416,256]{1,0:T(8,128)(2,1)S(1)}, u32[]{:S(2)}, u32[]{:S(2)}) collective-permute-start(bf16[416,256]{1,0:T(8,128)(2,1)S(1)} %get-tuple-element.146), channel_id=1, source_target_pairs={{0,2},{1,3},{2,0},{3,1},{4,6},{5,7},{6,4},{7,5},{8,10},{9,11},{10,... | collective-permute-start | bytes 638984 | tf_op jit(solution)/shard_map/ppermute | solution.py:687
  64.0 11.1 %collective-permute-start.6 = (bf16[416,256]{1,0:T(8,128)(2,1)S(1)}, bf16[416,256]{1,0:T(8,128)(2,1)S(1)}, u32[]{:S(2)}, u32[]{:S(2)}) collective-permute-start(bf16[416,256]{1,0:T(8,128)(2,1)S(1)} %get-tuple-element.147), channel_id=1, source_target_pairs={{0,4},{1,5},{2,6},{3,7},{4,0},{5,1},{6,2},{7,3},{8,12},{9,13},{10,... | collective-permute-start | bytes 638984 | tf_op jit(solution)/shard_map/ppermute | solution.py:687
  65.4 9.6 %collective-permute-start.7 = (bf16[416,256]{1,0:T(8,128)(2,1)S(1)}, bf16[416,256]{1,0:T(8,128)(2,1)S(1)}, u32[]{:S(2)}, u32[]{:S(2)}) collective-permute-start(bf16[416,256]{1,0:T(8,128)(2,1)S(1)} %get-tuple-element.148), channel_id=1, source_target_pairs={{0,6},{1,7},{2,4},{3,5},{4,2},{5,3},{6,0},{7,1},{8,14},{9,15},{10,... | collective-permute-start | bytes 638984 | tf_op jit(solution)/shard_map/ppermute | solution.py:687
  66.3 12.3 %collective-permute-start.14 = (bf16[104,256]{1,0:T(8,128)(2,1)S(1)}, bf16[104,256]{1,0:T(8,128)(2,1)S(1)}, u32[]{:S(2)}, u32[]{:S(2)}) collective-permute-start(bf16[104,256]{1,0:T(8,128)(2,1)S(1)} %add_convert_fusion.1), channel_id=1, source_target_pairs={{0,24},{1,25},{2,26},{3,27},{4,28},{5,29},{6,30},{7,31},{8,16},{9,... | collective-permute-start | bytes 159752 | tf_op jit(solution)/shard_map/ppermute | solution.py:687
  70.1 9.6 %collective-permute-start.15 = (bf16[104,256]{1,0:T(8,128)(2,1)S(1)}, bf16[104,256]{1,0:T(8,128)(2,1)S(1)}, u32[]{:S(2)}, u32[]{:S(2)}) collective-permute-start(bf16[104,256]{1,0:T(8,128)(2,1)S(1)} %add_convert_fusion.1), channel_id=1, source_target_pairs={{0,16},{1,17},{2,18},{3,19},{4,20},{5,21},{6,22},{7,23},{8,24},{9,... | collective-permute-start | bytes 159752 | tf_op jit(solution)/shard_map/ppermute | solution.py:687
  70.6 9.1 %collective-permute-start.16 = (bf16[104,256]{1,0:T(8,128)(2,1)S(1)}, bf16[104,256]{1,0:T(8,128)(2,1)S(1)}, u32[]{:S(2)}, u32[]{:S(2)}) collective-permute-start(bf16[104,256]{1,0:T(8,128)(2,1)S(1)} %add_convert_fusion.1), channel_id=1, source_target_pairs={{0,8},{1,9},{2,10},{3,11},{4,12},{5,13},{6,14},{7,15},{8,0},{9,1},... | collective-permute-start | bytes 159752 | tf_op jit(solution)/shard_map/ppermute | solution.py:687
  75.2 6.6 %collective-permute-start.11 = (bf16[104,256]{1,0:T(8,128)(2,1)S(1)}, bf16[104,256]{1,0:T(8,128)(2,1)S(1)}, u32[]{:S(2)}, u32[]{:S(2)}) collective-permute-start(bf16[104,256]{1,0:T(8,128)(2,1)S(1)} %get-tuple-element.158), channel_id=1, source_target_pairs={{0,24},{1,25},{2,26},{3,27},{4,28},{5,29},{6,30},{7,31},{8,16},{9,... | collective-permute-start | bytes 159752 | tf_op jit(solution)/shard_map/ppermute | solution.py:687
  78.6 5.0 %collective-permute-start.12 = (bf16[104,256]{1,0:T(8,128)(2,1)S(1)}, bf16[104,256]{1,0:T(8,128)(2,1)S(1)}, u32[]{:S(2)}, u32[]{:S(2)}) collective-permute-start(bf16[104,256]{1,0:T(8,128)(2,1)S(1)} %get-tuple-element.159), channel_id=1, source_target_pairs={{0,16},{1,17},{2,18},{3,19},{4,20},{5,21},{6,22},{7,23},{8,24},{9,... | collective-permute-start | bytes 159752 | tf_op jit(solution)/shard_map/ppermute | solution.py:687
  78.6 5.0 %collective-permute-start.13 = (bf16[104,256]{1,0:T(8,128)(2,1)S(1)}, bf16[104,256]{1,0:T(8,128)(2,1)S(1)}, u32[]{:S(2)}, u32[]{:S(2)}) collective-permute-start(bf16[104,256]{1,0:T(8,128)(2,1)S(1)} %get-tuple-element.160), channel_id=1, source_target_pairs={{0,8},{1,9},{2,10},{3,11},{4,12},{5,13},{6,14},{7,15},{8,0},{9,1},... | collective-permute-start | bytes 159752 | tf_op jit(solution)/shard_map/ppermute | solution.py:687
  79.8 7.2 %collective-permute-start.20 = (bf16[416,256]{1,0:T(8,128)(2,1)S(1)}, bf16[416,256]{1,0:T(8,128)(2,1)S(1)}, u32[]{:S(2)}, u32[]{:S(2)}) collective-permute-start(bf16[416,256]{1,0:T(8,128)(2,1)S(1)} %bitcast.48), channel_id=1, source_target_pairs={{0,2},{1,3},{2,0},{3,1},{4,6},{5,7},{6,4},{7,5},{8,10},{9,11},{10,... | collective-permute-start | bytes 638984 | tf_op jit(solution)/shard_map/ppermute | solution.py:687
  81.0 9.3 %collective-permute-start.21 = (bf16[416,256]{1,0:T(8,128)(2,1)S(1)}, bf16[416,256]{1,0:T(8,128)(2,1)S(1)}, u32[]{:S(2)}, u32[]{:S(2)}) collective-permute-start(bf16[416,256]{1,0:T(8,128)(2,1)S(1)} %bitcast.49), channel_id=1, source_target_pairs={{0,4},{1,5},{2,6},{3,7},{4,0},{5,1},{6,2},{7,3},{8,12},{9,13},{10,... | collective-permute-start | bytes 638984 | tf_op jit(solution)/shard_map/ppermute | solution.py:687
  81.9 8.5 %collective-permute-start.22 = (bf16[416,256]{1,0:T(8,128)(2,1)S(1)}, bf16[416,256]{1,0:T(8,128)(2,1)S(1)}, u32[]{:S(2)}, u32[]{:S(2)}) collective-permute-start(bf16[416,256]{1,0:T(8,128)(2,1)S(1)} %bitcast.50), channel_id=1, source_target_pairs={{0,6},{1,7},{2,4},{3,5},{4,2},{5,3},{6,0},{7,1},{8,14},{9,15},{10,... | collective-permute-start | bytes 638984 | tf_op jit(solution)/shard_map/ppermute | solution.py:687
  83.7 6.9 %collective-permute-start.17 = (bf16[104,256]{1,0:T(8,128)(2,1)S(1)}, bf16[104,256]{1,0:T(8,128)(2,1)S(1)}, u32[]{:S(2)}, u32[]{:S(2)}) collective-permute-start(bf16[104,256]{1,0:T(8,128)(2,1)S(1)} %add_convert_fusion), channel_id=1, source_target_pairs={{0,24},{1,25},{2,26},{3,27},{4,28},{5,29},{6,30},{7,31},{8,16},{9,... | collective-permute-start | bytes 159752 | tf_op jit(solution)/shard_map/ppermute | solution.py:687
  86.8 5.0 %collective-permute-start.18 = (bf16[104,256]{1,0:T(8,128)(2,1)S(1)}, bf16[104,256]{1,0:T(8,128)(2,1)S(1)}, u32[]{:S(2)}, u32[]{:S(2)}) collective-permute-start(bf16[104,256]{1,0:T(8,128)(2,1)S(1)} %add_convert_fusion), channel_id=1, source_target_pairs={{0,16},{1,17},{2,18},{3,19},{4,20},{5,21},{6,22},{7,23},{8,24},{9,... | collective-permute-start | bytes 159752 | tf_op jit(solution)/shard_map/ppermute | solution.py:687
  87.0 4.8 %collective-permute-start.19 = (bf16[104,256]{1,0:T(8,128)(2,1)S(1)}, bf16[104,256]{1,0:T(8,128)(2,1)S(1)}, u32[]{:S(2)}, u32[]{:S(2)}) collective-permute-start(bf16[104,256]{1,0:T(8,128)(2,1)S(1)} %add_convert_fusion), channel_id=1, source_target_pairs={{0,8},{1,9},{2,10},{3,11},{4,12},{5,13},{6,14},{7,15},{8,0},{9,1},... | collective-permute-start | bytes 159752 | tf_op jit(solution)/shard_map/ppermute | solution.py:687
  90.5 9.1 %collective-permute-start.26 = (bf16[1664,256]{1,0:T(8,128)(2,1)S(1)}, bf16[1664,256]{1,0:T(8,128)(2,1)S(1)}, u32[]{:S(2)}, u32[]{:S(2)}) collective-permute-start(bf16[1664,256]{1,0:T(8,128)(2,1)S(1)} %bitcast.41), channel_id=1, source_target_pairs={{0,1},{1,0},{2,3},{3,2},{4,5},{5,4},{6,7},{7,6},{8,9},{9,8},{10,11... | collective-permute-start | bytes 2555912 | tf_op jit(solution)/shard_map/ppermute | solution.py:687
  91.9 9.5 %collective-permute-start.23 = (bf16[416,256]{1,0:T(8,128)(2,1)S(1)}, bf16[416,256]{1,0:T(8,128)(2,1)S(1)}, u32[]{:S(2)}, u32[]{:S(2)}) collective-permute-start(bf16[416,256]{1,0:T(8,128)(2,1)S(1)} %bitcast.43), channel_id=1, source_target_pairs={{0,2},{1,3},{2,0},{3,1},{4,6},{5,7},{6,4},{7,5},{8,10},{9,11},{10,... | collective-permute-start | bytes 638984 | tf_op jit(solution)/shard_map/ppermute | solution.py:687
  93.2 10.2 %collective-permute-start.24 = (bf16[416,256]{1,0:T(8,128)(2,1)S(1)}, bf16[416,256]{1,0:T(8,128)(2,1)S(1)}, u32[]{:S(2)}, u32[]{:S(2)}) collective-permute-start(bf16[416,256]{1,0:T(8,128)(2,1)S(1)} %bitcast.44), channel_id=1, source_target_pairs={{0,4},{1,5},{2,6},{3,7},{4,0},{5,1},{6,2},{7,3},{8,12},{9,13},{10,... | collective-permute-start | bytes 638984 | tf_op jit(solution)/shard_map/ppermute | solution.py:687
  94.0 9.3 %collective-permute-start.25 = (bf16[416,256]{1,0:T(8,128)(2,1)S(1)}, bf16[416,256]{1,0:T(8,128)(2,1)S(1)}, u32[]{:S(2)}, u32[]{:S(2)}) collective-permute-start(bf16[416,256]{1,0:T(8,128)(2,1)S(1)} %bitcast.45), channel_id=1, source_target_pairs={{0,6},{1,7},{2,4},{3,5},{4,2},{5,3},{6,0},{7,1},{8,14},{9,15},{10,... | collective-permute-start | bytes 638984 | tf_op jit(solution)/shard_map/ppermute | solution.py:687
  99.6 4.3 %collective-permute-start.27 = (bf16[416,256]{1,0:T(8,128)(2,1)S(1)}, bf16[416,256]{1,0:T(8,128)(2,1)S(1)}, u32[]{:S(2)}, u32[]{:S(2)}) collective-permute-start(bf16[416,256]{1,0:T(8,128)(2,1)S(1)} %bitcast.46), channel_id=1, source_target_pairs={{0,1},{1,0},{2,3},{3,2},{4,5},{5,4},{6,7},{7,6},{8,9},{9,8},{10,11... | collective-permute-start | bytes 638984 | tf_op jit(solution)/shard_map/ppermute | solution.py:687
  103.4 1.5 %collective-permute-start.28 = (bf16[416,256]{1,0:T(8,128)(2,1)S(1)}, bf16[416,256]{1,0:T(8,128)(2,1)S(1)}, u32[]{:S(2)}, u32[]{:S(2)}) collective-permute-start(bf16[416,256]{1,0:T(8,128)(2,1)S(1)} %collective-permute-done.23.refs_1_), channel_id=1, source_target_pairs={{0,1},{1,0},{2,3},{3,2},{4,5},{5,4},{6,7},{7,6},{8,9},{9,8},{10,11... | collective-permute-start | bytes 638984 | tf_op jit(solution)/shard_map/ppermute | solution.py:687
  103.4 1.8 %collective-permute-start.29 = (bf16[416,256]{1,0:T(8,128)(2,1)S(1)}, bf16[416,256]{1,0:T(8,128)(2,1)S(1)}, u32[]{:S(2)}, u32[]{:S(2)}) collective-permute-start(bf16[416,256]{1,0:T(8,128)(2,1)S(1)} %collective-permute-done.24.refs_2_), channel_id=1, source_target_pairs={{0,1},{1,0},{2,3},{3,2},{4,5},{5,4},{6,7},{7,6},{8,9},{9,8},{10,11... | collective-permute-start | bytes 638984 | tf_op jit(solution)/shard_map/ppermute | solution.py:687
  103.9 1.6 %collective-permute-start.30 = (bf16[416,256]{1,0:T(8,128)(2,1)S(1)}, bf16[416,256]{1,0:T(8,128)(2,1)S(1)}, u32[]{:S(2)}, u32[]{:S(2)}) collective-permute-start(bf16[416,256]{1,0:T(8,128)(2,1)S(1)} %collective-permute-done.25.refs_3_), channel_id=1, source_target_pairs={{0,1},{1,0},{2,3},{3,2},{4,5},{5,4},{6,7},{7,6},{8,9},{9,8},{10,11... | collective-permute-start | bytes 638984 | tf_op jit(solution)/shard_map/ppermute | solution.py:687

commit v11 on v10

--- a/solution.py
+++ b/solution.py
@@ -16,10 +16,10 @@
 VECTOR_ROWS = 16
 HALF = 6 * WIDTH + 128
 GROUP_ROWS = 2 * HALF
-LANES = 128
-SOFT = 128
+LANES = 256
+SOFT = 256
 NORM = 32
-GELU = 32
+GELU = 16
 ln_eps = 1e-06
 score_scale = 0.125
 masked_score = -1e30

time: 108 us -> 108 us (level)
  no operation moved by 1% of the time
where the time goes in v11:
time: 108 us; the launch traced here: 107 us
  Pallas kernels  52.7 us (49%)
  starting transfers between devices  40.4 us (37%)
  waiting for transfers between devices  11.8 us (11%)
  local copies, waits for them, and re-layouts  1.19 us (1%)
  between operations  1.14 us (1%)
    ppermute x31, starting transfers between devices, partner_send(): return lax.ppermute(values, 'dp', [(i, i ^ mask) for i in range(count)])  33.1 us
    pallas_call x2, Pallas kernels, layer(): pl.pallas_call(kernel, out_shape=[shape((total, WIDTH), bf16), pltpu.HBM(...  27 us
    ppermute x31, waiting for transfers between devices, partner_send(): return lax.ppermute(values, 'dp', [(i, i ^ mask) for i in range(count)])  11.6 us
    pallas_call x2, Pallas kernels, attend(): pl.pallas_call(functools.partial(attend_long_kernel if seqs == 1 else att...  10 us
    all_to_all x1, starting transfers between devices, body(): all_cls = lax.all_to_all(own_cls, 'dp', 0, 0, tiled=True)  7.3 us
    pallas_call x2, Pallas kernels, input_grad(): pl.pallas_call(input_grad_kernel, out_shape=shape((total, WIDTH), bf16),...  5.76 us
    pallas_call x1, Pallas kernels, first_call(): pl.pallas_call(functools.partial(first_kernel, local), out_shape=shape((c...  5.22 us
  transfers between devices with their start and end apart: 32, of which 13 were waited for; matrix products, arithmetic and copies ran while one was open for 1% of the time, Pallas kernels for 36%

profile of v11, /device:TPU:0, one launch (start us, length us, event | category | flops | bytes accessed | tf_op | source)
XLA Modules:
  0.0 107.3 jit_solution(2357184342548116063)
XLA Ops:
  0.7 5.2 %first.1 = bf16[32,16,256]{2,1,0:T(8,128)(2,1)} custom-call(s32[5]{0:T(128)} %len_ref.6, s32[5]{0:T(128)} %len_ref.7, bf16[320,256]{1,0:T(8,128)(2,1)} %bitcast.52, bf16[1280,256]{1,0:T(8,128)(2,1)} %bitcast.56, bf16[2,256,768]{2,1,0:T(8,128)(2,1)} %wqkv_ref.9, bf16[2,256]{1,0:T(2,128)(2,1)} %qb_ref.5, bf16[2,256]{1,0:T(2,128)(2,1)} %vb_ref.5, ...), custom_call_target="tpu_custom_call" | custom-call | tf_op jit(solution)/shard_map/first/pallas_call | solution.py:578
  5.9 7.3 %all-to-all-start = ((bf16[32,16,256]{2,1,0:T(8,128)(2,1)}), bf16[32,16,256]{2,1,0:T(8,128)(2,1)S(1)}, u32[]{:S(2)}, u32[]{:S(2)}) async-start(bf16[32,16,256]{2,1,0:T(8,128)(2,1)} %first.1), calls=%async_computation | async-start | bytes 524288 | tf_op jit(solution)/shard_map/all_to_all | solution.py:777
  13.6 3.1 %attend.3 = (bf16[320,768]{1,0:T(8,128)(2,1)}, f32[320,256]{1,0:T(8,128)}, bf16[320,256]{1,0:T(8,128)(2,1)}) custom-call(s32[5]{0:T(128)S(1)} %copy-done, bf16[320,256]{1,0:T(8,128)(2,1)} %bitcast.53, bf16[2,256,768]{2,1,0:T(8,128)(2,1)} %wqkv_ref.9, bf16[2,256]{1,0:T(2,128)(2,1)} %qb_ref.5, bf16[2,256]{1,0:T(2,128)(2,1)} %vb_ref.5), custom_call_target="tpu_custom_call" | custom-call | flops 256000000 | bytes 1920000 | tf_op jit(solution)/shard_map/attend/pallas_call | solution.py:595
  16.6 6.9 %attend.2 = (bf16[1280,768]{1,0:T(8,128)(2,1)}, f32[5120,256]{1,0:T(8,128)}, bf16[1280,256]{1,0:T(8,128)(2,1)}) custom-call(s32[5]{0:T(128)S(1)} %copy-done.1, bf16[1280,256]{1,0:T(8,128)(2,1)} %bitcast.57, bf16[2,256,768]{2,1,0:T(8,128)(2,1)} %wqkv_ref.9, bf16[2,256]{1,0:T(2,128)(2,1)} %qb_ref.5, bf16[2,256]{1,0:T(2,128)(2,1)} %vb_ref.5), custom_call_target="tpu_custom_call" | custom-call | flops 1024000000 | bytes 7680000 | tf_op jit(solution)/shard_map/attend/pallas_call | solution.py:595
  23.6 0.2 all-to-all-done.all_ref
  23.8 7.1 %layer.2 = (bf16[320,256]{1,0:T(8,128)(2,1)}, f32[320,256]{1,0:T(8,128)}, bf16[320,768]{1,0:T(8,128)(2,1)}, bf16[1664,256]{1,0:T(8,128)(2,1)S(1)}, bf16[1664,256...) custom-call(s32[1]{0:T(128)} %bitcast.me_ref, bf16[32,16,256]{2,1,0:T(8,128)(2,1)S(1)} %all-to-all-done.all_ref, ...), custom_call_target="tpu_custom_call" | custom-call | flops 1536000000 | bytes 1280000 | tf_op jit(solution)/shard_map/layer/pallas_call | solution.py:626
  31.0 2.2 %input_grad.2 = bf16[320,256]{1,0:T(8,128)(2,1)} custom-call(f32[320,256]{1,0:T(8,128)} %get-tuple-element.122.one_ref, bf16[320,768]{1,0:T(8,128)(2,1)} %get-tuple-element.123.gqkv_ref, bf16[2,256,768]{2,1,0:T(8,128)(2,1)} %wqkv_ref.9), custom_call_target="tpu_custom_call" | custom-call | flops 128000000 | bytes 960000 | tf_op jit(solution)/shard_map/input_grad/pallas_call | solution.py:660
  33.3 0.4 combine.4
  33.7 1.6 %collective-permute-start.1 = (bf16[416,256]{1,0:T(8,128)(2,1)S(1)}, bf16[416,256]{1,0:T(8,128)(2,1)S(1)}, u32[]{:S(2)}, u32[]{:S(2)}) collective-permute-start(bf16[416,256]{1,0:T(8,128)(2,1)S(1)} %get-tuple-element.127), channel_id=1, source_target_pairs={{0,2},{1,3},{2,0},{3,1},{4,6},{5,7},{6,4},{7,5},{8,10},{9,11},{10,... | collective-permute-start | bytes 638984 | tf_op jit(solution)/shard_map/ppermute | solution.py:687
  35.3 1.5 %collective-permute-start.2 = (bf16[416,256]{1,0:T(8,128)(2,1)S(1)}, bf16[416,256]{1,0:T(8,128)(2,1)S(1)}, u32[]{:S(2)}, u32[]{:S(2)}) collective-permute-start(bf16[416,256]{1,0:T(8,128)(2,1)S(1)} %get-tuple-element.128), channel_id=1, source_target_pairs={{0,4},{1,5},{2,6},{3,7},{4,0},{5,1},{6,2},{7,3},{8,12},{9,13},{10,... | collective-permute-start | bytes 638984 | tf_op jit(solution)/shard_map/ppermute | solution.py:687
  36.8 0.5 collective-permute-start.3
  37.2 19.9 %layer.3 = (bf16[1280,256]{1,0:T(8,128)(2,1)}, f32[1280,256]{1,0:T(8,128)}, bf16[1280,768]{1,0:T(8,128)(2,1)}, bf16[1664,256]{1,0:T(8,128)(2,1)S(1)}, bf16[1664,256]{1,0:T(8,128)(2,1)S(1)}) custom-call(s32[1]{0:T(128)} %bitcast.4.bit_ref, s32[5]{0:T(128)S(1)} %copy-done.1, f32[8,256]{1,0:T(8,128)S(1)} %get-tuple-element.130.cls_ref, ...), custom_call_target="tpu_custom_call" | custom-call | flops 6144000000 | bytes 5120000 | tf_op jit(solution)/shard_map/layer/pallas_call | solution.py:626
  57.3 0.2 combine.5
  57.4 3.4 %collective-permute-start.8 = (bf16[104,256]{1,0:T(8,128)(2,1)S(1)}, bf16[104,256]{1,0:T(8,128)(2,1)S(1)}, u32[]{:S(2)}, u32[]{:S(2)}) collective-permute-start(bf16[104,256]{1,0:T(8,128)(2,1)S(1)} %get-tuple-element.140), channel_id=1, source_target_pairs={{0,24},{1,25},{2,26},{3,27},{4,28},{5,29},{6,30},{7,31},{8,16},{9,... | collective-permute-start | bytes 159752 | tf_op jit(solution)/shard_map/ppermute | solution.py:687
  60.9 1.0 collective-permute-start.10
  61.9 0.4 combine.6
  62.3 1.6 %collective-permute-start.5 = (bf16[416,256]{1,0:T(8,128)(2,1)S(1)}, bf16[416,256]{1,0:T(8,128)(2,1)S(1)}, u32[]{:S(2)}, u32[]{:S(2)}) collective-permute-start(bf16[416,256]{1,0:T(8,128)(2,1)S(1)} %get-tuple-element.146), channel_id=1, source_target_pairs={{0,2},{1,3},{2,0},{3,1},{4,6},{5,7},{6,4},{7,5},{8,10},{9,11},{10,... | collective-permute-start | bytes 638984 | tf_op jit(solution)/shard_map/ppermute | solution.py:687
  63.9 1.5 %collective-permute-start.6 = (bf16[416,256]{1,0:T(8,128)(2,1)S(1)}, bf16[416,256]{1,0:T(8,128)(2,1)S(1)}, u32[]{:S(2)}, u32[]{:S(2)}) collective-permute-start(bf16[416,256]{1,0:T(8,128)(2,1)S(1)} %get-tuple-element.147), channel_id=1, source_target_pairs={{0,4},{1,5},{2,6},{3,7},{4,0},{5,1},{6,2},{7,3},{8,12},{9,13},{10,... | collective-permute-start | bytes 638984 | tf_op jit(solution)/shard_map/ppermute | solution.py:687
  65.3 0.7 collective-permute-start.7
  66.0 0.1 collective-permute-done.9
  66.2 3.7 %collective-permute-start.14 = (bf16[104,256]{1,0:T(8,128)(2,1)S(1)}, bf16[104,256]{1,0:T(8,128)(2,1)S(1)}, u32[]{:S(2)}, u32[]{:S(2)}) collective-permute-start(bf16[104,256]{1,0:T(8,128)(2,1)S(1)} %add_convert_fusion.1), channel_id=1, source_target_pairs={{0,24},{1,25},{2,26},{3,27},{4,28},{5,29},{6,30},{7,31},{8,16},{9,... | collective-permute-start | bytes 159752 | tf_op jit(solution)/shard_map/ppermute | solution.py:687
  70.0 0.5 collective-permute-done.5.refs_1_
  70.5 1.0 collective-permute-start.16
  71.5 3.5 %collective-permute-done.6.refs_2_ = bf16[416,256]{1,0:T(8,128)(2,1)S(1)} collective-permute-done((bf16[416,256]{1,0:T(8,128)(2,1)S(1)}, bf16[416,256]{1,0:T(8,128)(2,1)S(1)}, u32[]{:S(2)}, u32[]{:S(2)}) %collective-permute-start.6) | collective-permute-done | bytes 213024 | tf_op jit(solution)/shard_map/ppermute | solution.py:687
  74.9 0.2 combine.7
  75.1 3.4 %collective-permute-start.11 = (bf16[104,256]{1,0:T(8,128)(2,1)S(1)}, bf16[104,256]{1,0:T(8,128)(2,1)S(1)}, u32[]{:S(2)}, u32[]{:S(2)}) collective-permute-start(bf16[104,256]{1,0:T(8,128)(2,1)S(1)} %get-tuple-element.158), channel_id=1, source_target_pairs={{0,24},{1,25},{2,26},{3,27},{4,28},{5,29},{6,30},{7,31},{8,16},{9,... | collective-permute-start | bytes 159752 | tf_op jit(solution)/shard_map/ppermute | solution.py:687
  78.5 1.1 collective-permute-start.13
  79.7 1.2 %collective-permute-start.20 = (bf16[416,256]{1,0:T(8,128)(2,1)S(1)}, bf16[416,256]{1,0:T(8,128)(2,1)S(1)}, u32[]{:S(2)}, u32[]{:S(2)}) collective-permute-start(bf16[416,256]{1,0:T(8,128)(2,1)S(1)} %bitcast.48), channel_id=1, source_target_pairs={{0,2},{1,3},{2,0},{3,1},{4,6},{5,7},{6,4},{7,5},{8,10},{9,11},{10,... | collective-permute-start | bytes 638984 | tf_op jit(solution)/shard_map/ppermute | solution.py:687
  80.9 0.8 collective-permute-start.21
  81.8 1.5 %collective-permute-start.22 = (bf16[416,256]{1,0:T(8,128)(2,1)S(1)}, bf16[416,256]{1,0:T(8,128)(2,1)S(1)}, u32[]{:S(2)}, u32[]{:S(2)}) collective-permute-start(bf16[416,256]{1,0:T(8,128)(2,1)S(1)} %bitcast.50), channel_id=1, source_target_pairs={{0,6},{1,7},{2,4},{3,5},{4,2},{5,3},{6,0},{7,1},{8,14},{9,15},{10,... | collective-permute-start | bytes 638984 | tf_op jit(solution)/shard_map/ppermute | solution.py:687
  83.2 0.3 collective-permute-done.12
  83.6 3.1 %collective-permute-start.17 = (bf16[104,256]{1,0:T(8,128)(2,1)S(1)}, bf16[104,256]{1,0:T(8,128)(2,1)S(1)}, u32[]{:S(2)}, u32[]{:S(2)}) collective-permute-start(bf16[104,256]{1,0:T(8,128)(2,1)S(1)} %add_convert_fusion), channel_id=1, source_target_pairs={{0,24},{1,25},{2,26},{3,27},{4,28},{5,29},{6,30},{7,31},{8,16},{9,... | collective-permute-start | bytes 159752 | tf_op jit(solution)/shard_map/ppermute | solution.py:687
  86.7 0.2 collective-permute-done.20
  86.9 1.3 %collective-permute-start.19 = (bf16[104,256]{1,0:T(8,128)(2,1)S(1)}, bf16[104,256]{1,0:T(8,128)(2,1)S(1)}, u32[]{:S(2)}, u32[]{:S(2)}) collective-permute-start(bf16[104,256]{1,0:T(8,128)(2,1)S(1)} %add_convert_fusion), channel_id=1, source_target_pairs={{0,8},{1,9},{2,10},{3,11},{4,12},{5,13},{6,14},{7,15},{8,0},{9,1},... | collective-permute-start | bytes 159752 | tf_op jit(solution)/shard_map/ppermute | solution.py:687
  88.2 2.1 %collective-permute-done.21 = bf16[416,256]{1,0:T(8,128)(2,1)S(1)} collective-permute-done((bf16[416,256]{1,0:T(8,128)(2,1)S(1)}, bf16[416,256]{1,0:T(8,128)(2,1)S(1)}, u32[]{:S(2)}, u32[]{:S(2)}) %collective-permute-start.21) | collective-permute-done | bytes 213024 | tf_op jit(solution)/shard_map/ppermute | solution.py:687
  90.5 1.2 %collective-permute-done.18 = bf16[104,256]{1,0:T(8,128)(2,1)S(1)} collective-permute-done((bf16[104,256]{1,0:T(8,128)(2,1)S(1)}, bf16[104,256]{1,0:T(8,128)(2,1)S(1)}, u32[]{:S(2)}, u32[]{:S(2)}) %collective-permute-start.18) | collective-permute-done | bytes 53280 | tf_op jit(solution)/shard_map/ppermute | solution.py:687
  91.8 1.3 %collective-permute-start.23 = (bf16[416,256]{1,0:T(8,128)(2,1)S(1)}, bf16[416,256]{1,0:T(8,128)(2,1)S(1)}, u32[]{:S(2)}, u32[]{:S(2)}) collective-permute-start(bf16[416,256]{1,0:T(8,128)(2,1)S(1)} %bitcast.43), channel_id=1, source_target_pairs={{0,2},{1,3},{2,0},{3,1},{4,6},{5,7},{6,4},{7,5},{8,10},{9,11},{10,... | collective-permute-start | bytes 638984 | tf_op jit(solution)/shard_map/ppermute | solution.py:687
  93.1 0.8 collective-permute-start.24
  93.9 1.4 %collective-permute-start.25 = (bf16[416,256]{1,0:T(8,128)(2,1)S(1)}, bf16[416,256]{1,0:T(8,128)(2,1)S(1)}, u32[]{:S(2)}, u32[]{:S(2)}) collective-permute-start(bf16[416,256]{1,0:T(8,128)(2,1)S(1)} %bitcast.45), channel_id=1, source_target_pairs={{0,6},{1,7},{2,4},{3,5},{4,2},{5,3},{6,0},{7,1},{8,14},{9,15},{10,... | collective-permute-start | bytes 638984 | tf_op jit(solution)/shard_map/ppermute | solution.py:687
  95.4 0.6 slice_reduce_fusion
  96.0 3.5 %input_grad.3 = bf16[1280,256]{1,0:T(8,128)(2,1)} custom-call(f32[1280,256]{1,0:T(8,128)} %get-tuple-element.134.one_ref, bf16[1280,768]{1,0:T(8,128)(2,1)} %get-tuple-element.135.gqkv_ref, bf16[2,256,768]{2,1,0:T(8,128)(2,1)} %wqkv_ref.9), custom_call_target="tpu_custom_call" | custom-call | flops 512000000 | bytes 3840000 | tf_op jit(solution)/shard_map/input_grad/pallas_call | solution.py:660
  99.5 1.8 %unpack_q.1 = (f32[2,256,768]{2,1,0:T(8,128)}, f32[2,256,256]{2,1,0:T(8,128)}, f32[2,256,1024]{2,1,0:T(8,128)}, f32[2,1024,256]{2,1,0:T(8,128)}, f32[16,256]{1,0:T(8,128)S(1)}) custom-call(s32[1]{0:T(128)} %bitcast.4.bit_ref, bf16[1664,256]{1,0:T(8,128)(2,1)S(1)} %bitcast.42, bf16[1664,256]{1,0:T(8,128)(2,1)S(1)} %collective-permute-done.26.other_ref), custom_call_target="tpu_custom_call" | custom-call | tf_op jit(solution)/shard_map/unpack_q/pallas_call | solution.py:816
  101.3 1.9 %collective-permute-done.24.refs_2_ = bf16[416,256]{1,0:T(8,128)(2,1)S(1)} collective-permute-done((bf16[416,256]{1,0:T(8,128)(2,1)S(1)}, bf16[416,256]{1,0:T(8,128)(2,1)S(1)}, u32[]{:S(2)}, u32[]{:S(2)}) %collective-permute-start.24) | collective-permute-done | bytes 213024 | tf_op jit(solution)/shard_map/ppermute | solution.py:687
  103.3 0.5 collective-permute-start.29
  103.8 0.9 collective-permute-done.28.refs_5_
  104.7 0.3 collective-permute-done.29.refs_6_
  105.0 0.3 collective-permute-done.30.refs_7_
  105.3 1.8 %unpack_p.1 = (f32[2,256,768]{2,1,0:T(8,128)}, f32[2,256,256]{2,1,0:T(8,128)}, f32[2,256,1024]{2,1,0:T(8,128)}, f32[2,1024,256]{2,1,0:T(8,128)}, f32[2,1024]{1,0...) custom-call(s32[1]{0:T(128)} %bitcast.4.bit_ref, ...), custom_call_target="tpu_custom_call", output_to_operand_aliasing={{0}: (11, {}), {1}: (12, {}), {2}: (13, {}), {3}: (14, {})} | custom-call | tf_op jit(solution)/shard_map/unpack_p/pallas_call | solution.py:833
  (59 shorter events, 1.0 us)
Async XLA Ops:
  0.7 12.6 %copy-start.2 = (s32[160]{0:T(256)S(1)}, s32[160]{0:T(256)}, u32[]{:S(2)}) copy-start(s32[160]{0:T(256)} %param.26) | copy-start | bytes 1924
  0.7 12.9 %copy-start = (s32[5]{0:T(128)S(1)}, s32[5]{0:T(128)}, u32[]{:S(2)}) copy-start(s32[5]{0:T(128)} %len_ref.6) | copy-start | bytes 64
  0.7 16.0 %copy-start.1 = (s32[5]{0:T(128)S(1)}, s32[5]{0:T(128)}, u32[]{:S(2)}) copy-start(s32[5]{0:T(128)} %len_ref.7) | copy-start | bytes 64
  5.9 17.9 %all-to-all-start = ((bf16[32,16,256]{2,1,0:T(8,128)(2,1)}), bf16[32,16,256]{2,1,0:T(8,128)(2,1)S(1)}, u32[]{:S(2)}, u32[]{:S(2)}) async-start(bf16[32,16,256]{2,1,0:T(8,128)(2,1)} %first.1), calls=%async_computation | async-start | bytes 524288 | tf_op jit(solution)/shard_map/all_to_all | solution.py:777
  30.9 2.4 %collective-permute-start = (bf16[1664,256]{1,0:T(8,128)(2,1)S(1)}, bf16[1664,256]{1,0:T(8,128)(2,1)S(1)}, u32[]{:S(2)}, u32[]{:S(2)}) collective-permute-start(bf16[1664,256]{1,0:T(8,128)(2,1)S(1)} %get-tuple-element.121), channel_id=1, source_target_pairs={{0,1},{1,0},{2,3},{3,2},{4,5},{5,4},{6,7},{7,6},{8,9},{9,8},{10,11... | collective-permute-start | bytes 2555912 | tf_op jit(solution)/shard_map/ppermute | solution.py:687
  33.7 23.5 %collective-permute-start.1 = (bf16[416,256]{1,0:T(8,128)(2,1)S(1)}, bf16[416,256]{1,0:T(8,128)(2,1)S(1)}, u32[]{:S(2)}, u32[]{:S(2)}) collective-permute-start(bf16[416,256]{1,0:T(8,128)(2,1)S(1)} %get-tuple-element.127), channel_id=1, source_target_pairs={{0,2},{1,3},{2,0},{3,1},{4,6},{5,7},{6,4},{7,5},{8,10},{9,11},{10,... | collective-permute-start | bytes 638984 | tf_op jit(solution)/shard_map/ppermute | solution.py:687
  35.3 21.8 %collective-permute-start.2 = (bf16[416,256]{1,0:T(8,128)(2,1)S(1)}, bf16[416,256]{1,0:T(8,128)(2,1)S(1)}, u32[]{:S(2)}, u32[]{:S(2)}) collective-permute-start(bf16[416,256]{1,0:T(8,128)(2,1)S(1)} %get-tuple-element.128), channel_id=1, source_target_pairs={{0,4},{1,5},{2,6},{3,7},{4,0},{5,1},{6,2},{7,3},{8,12},{9,13},{10,... | collective-permute-start | bytes 638984 | tf_op jit(solution)/shard_map/ppermute | solution.py:687
  36.8 20.4 %collective-permute-start.3 = (bf16[416,256]{1,0:T(8,128)(2,1)S(1)}, bf16[416,256]{1,0:T(8,128)(2,1)S(1)}, u32[]{:S(2)}, u32[]{:S(2)}) collective-permute-start(bf16[416,256]{1,0:T(8,128)(2,1)S(1)} %get-tuple-element.129), channel_id=1, source_target_pairs={{0,6},{1,7},{2,4},{3,5},{4,2},{5,3},{6,0},{7,1},{8,14},{9,15},{10,... | collective-permute-start | bytes 638984 | tf_op jit(solution)/shard_map/ppermute | solution.py:687
  57.2 4.7 %collective-permute-start.4 = (bf16[1664,256]{1,0:T(8,128)(2,1)S(1)}, bf16[1664,256]{1,0:T(8,128)(2,1)S(1)}, u32[]{:S(2)}, u32[]{:S(2)}) collective-permute-start(bf16[1664,256]{1,0:T(8,128)(2,1)S(1)} %get-tuple-element.138), channel_id=1, source_target_pairs={{0,1},{1,0},{2,3},{3,2},{4,5},{5,4},{6,7},{7,6},{8,9},{9,8},{10,11... | collective-permute-start | bytes 2555912 | tf_op jit(solution)/shard_map/ppermute | solution.py:687
  57.4 7.9 %collective-permute-start.8 = (bf16[104,256]{1,0:T(8,128)(2,1)S(1)}, bf16[104,256]{1,0:T(8,128)(2,1)S(1)}, u32[]{:S(2)}, u32[]{:S(2)}) collective-permute-start(bf16[104,256]{1,0:T(8,128)(2,1)S(1)} %get-tuple-element.140), channel_id=1, source_target_pairs={{0,24},{1,25},{2,26},{3,27},{4,28},{5,29},{6,30},{7,31},{8,16},{9,... | collective-permute-start | bytes 159752 | tf_op jit(solution)/shard_map/ppermute | solution.py:687
  60.9 5.3 %collective-permute-start.9 = (bf16[104,256]{1,0:T(8,128)(2,1)S(1)}, bf16[104,256]{1,0:T(8,128)(2,1)S(1)}, u32[]{:S(2)}, u32[]{:S(2)}) collective-permute-start(bf16[104,256]{1,0:T(8,128)(2,1)S(1)} %get-tuple-element.141), channel_id=1, source_target_pairs={{0,16},{1,17},{2,18},{3,19},{4,20},{5,21},{6,22},{7,23},{8,24},{9,... | collective-permute-start | bytes 159752 | tf_op jit(solution)/shard_map/ppermute | solution.py:687
  60.9 5.3 %collective-permute-start.10 = (bf16[104,256]{1,0:T(8,128)(2,1)S(1)}, bf16[104,256]{1,0:T(8,128)(2,1)S(1)}, u32[]{:S(2)}, u32[]{:S(2)}) collective-permute-start(bf16[104,256]{1,0:T(8,128)(2,1)S(1)} %get-tuple-element.142), channel_id=1, source_target_pairs={{0,8},{1,9},{2,10},{3,11},{4,12},{5,13},{6,14},{7,15},{8,0},{9,1},... | collective-permute-start | bytes 159752 | tf_op jit(solution)/shard_map/ppermute | solution.py:687
  62.3 8.2 %collective-permute-start.5 = (bf16[416,256]{1,0:T(8,128)(2,1)S(1)}, bf16[416,256]{1,0:T(8,128)(2,1)S(1)}, u32[]{:S(2)}, u32[]{:S(2)}) collective-permute-start(bf16[416,256]{1,0:T(8,128)(2,1)S(1)} %get-tuple-element.146), channel_id=1, source_target_pairs={{0,2},{1,3},{2,0},{3,1},{4,6},{5,7},{6,4},{7,5},{8,10},{9,11},{10,... | collective-permute-start | bytes 638984 | tf_op jit(solution)/shard_map/ppermute | solution.py:687
  63.9 11.1 %collective-permute-start.6 = (bf16[416,256]{1,0:T(8,128)(2,1)S(1)}, bf16[416,256]{1,0:T(8,128)(2,1)S(1)}, u32[]{:S(2)}, u32[]{:S(2)}) collective-permute-start(bf16[416,256]{1,0:T(8,128)(2,1)S(1)} %get-tuple-element.147), channel_id=1, source_target_pairs={{0,4},{1,5},{2,6},{3,7},{4,0},{5,1},{6,2},{7,3},{8,12},{9,13},{10,... | collective-permute-start | bytes 638984 | tf_op jit(solution)/shard_map/ppermute | solution.py:687
  65.3 9.6 %collective-permute-start.7 = (bf16[416,256]{1,0:T(8,128)(2,1)S(1)}, bf16[416,256]{1,0:T(8,128)(2,1)S(1)}, u32[]{:S(2)}, u32[]{:S(2)}) collective-permute-start(bf16[416,256]{1,0:T(8,128)(2,1)S(1)} %get-tuple-element.148), channel_id=1, source_target_pairs={{0,6},{1,7},{2,4},{3,5},{4,2},{5,3},{6,0},{7,1},{8,14},{9,15},{10,... | collective-permute-start | bytes 638984 | tf_op jit(solution)/shard_map/ppermute | solution.py:687
  66.2 12.3 %collective-permute-start.14 = (bf16[104,256]{1,0:T(8,128)(2,1)S(1)}, bf16[104,256]{1,0:T(8,128)(2,1)S(1)}, u32[]{:S(2)}, u32[]{:S(2)}) collective-permute-start(bf16[104,256]{1,0:T(8,128)(2,1)S(1)} %add_convert_fusion.1), channel_id=1, source_target_pairs={{0,24},{1,25},{2,26},{3,27},{4,28},{5,29},{6,30},{7,31},{8,16},{9,... | collective-permute-start | bytes 159752 | tf_op jit(solution)/shard_map/ppermute | solution.py:687
  70.0 9.6 %collective-permute-start.15 = (bf16[104,256]{1,0:T(8,128)(2,1)S(1)}, bf16[104,256]{1,0:T(8,128)(2,1)S(1)}, u32[]{:S(2)}, u32[]{:S(2)}) collective-permute-start(bf16[104,256]{1,0:T(8,128)(2,1)S(1)} %add_convert_fusion.1), channel_id=1, source_target_pairs={{0,16},{1,17},{2,18},{3,19},{4,20},{5,21},{6,22},{7,23},{8,24},{9,... | collective-permute-start | bytes 159752 | tf_op jit(solution)/shard_map/ppermute | solution.py:687
  70.5 9.1 %collective-permute-start.16 = (bf16[104,256]{1,0:T(8,128)(2,1)S(1)}, bf16[104,256]{1,0:T(8,128)(2,1)S(1)}, u32[]{:S(2)}, u32[]{:S(2)}) collective-permute-start(bf16[104,256]{1,0:T(8,128)(2,1)S(1)} %add_convert_fusion.1), channel_id=1, source_target_pairs={{0,8},{1,9},{2,10},{3,11},{4,12},{5,13},{6,14},{7,15},{8,0},{9,1},... | collective-permute-start | bytes 159752 | tf_op jit(solution)/shard_map/ppermute | solution.py:687
  75.1 6.6 %collective-permute-start.11 = (bf16[104,256]{1,0:T(8,128)(2,1)S(1)}, bf16[104,256]{1,0:T(8,128)(2,1)S(1)}, u32[]{:S(2)}, u32[]{:S(2)}) collective-permute-start(bf16[104,256]{1,0:T(8,128)(2,1)S(1)} %get-tuple-element.158), channel_id=1, source_target_pairs={{0,24},{1,25},{2,26},{3,27},{4,28},{5,29},{6,30},{7,31},{8,16},{9,... | collective-permute-start | bytes 159752 | tf_op jit(solution)/shard_map/ppermute | solution.py:687
  78.5 5.0 %collective-permute-start.12 = (bf16[104,256]{1,0:T(8,128)(2,1)S(1)}, bf16[104,256]{1,0:T(8,128)(2,1)S(1)}, u32[]{:S(2)}, u32[]{:S(2)}) collective-permute-start(bf16[104,256]{1,0:T(8,128)(2,1)S(1)} %get-tuple-element.159), channel_id=1, source_target_pairs={{0,16},{1,17},{2,18},{3,19},{4,20},{5,21},{6,22},{7,23},{8,24},{9,... | collective-permute-start | bytes 159752 | tf_op jit(solution)/shard_map/ppermute | solution.py:687
  78.5 5.0 %collective-permute-start.13 = (bf16[104,256]{1,0:T(8,128)(2,1)S(1)}, bf16[104,256]{1,0:T(8,128)(2,1)S(1)}, u32[]{:S(2)}, u32[]{:S(2)}) collective-permute-start(bf16[104,256]{1,0:T(8,128)(2,1)S(1)} %get-tuple-element.160), channel_id=1, source_target_pairs={{0,8},{1,9},{2,10},{3,11},{4,12},{5,13},{6,14},{7,15},{8,0},{9,1},... | collective-permute-start | bytes 159752 | tf_op jit(solution)/shard_map/ppermute | solution.py:687
  79.7 7.2 %collective-permute-start.20 = (bf16[416,256]{1,0:T(8,128)(2,1)S(1)}, bf16[416,256]{1,0:T(8,128)(2,1)S(1)}, u32[]{:S(2)}, u32[]{:S(2)}) collective-permute-start(bf16[416,256]{1,0:T(8,128)(2,1)S(1)} %bitcast.48), channel_id=1, source_target_pairs={{0,2},{1,3},{2,0},{3,1},{4,6},{5,7},{6,4},{7,5},{8,10},{9,11},{10,... | collective-permute-start | bytes 638984 | tf_op jit(solution)/shard_map/ppermute | solution.py:687
  80.9 9.3 %collective-permute-start.21 = (bf16[416,256]{1,0:T(8,128)(2,1)S(1)}, bf16[416,256]{1,0:T(8,128)(2,1)S(1)}, u32[]{:S(2)}, u32[]{:S(2)}) collective-permute-start(bf16[416,256]{1,0:T(8,128)(2,1)S(1)} %bitcast.49), channel_id=1, source_target_pairs={{0,4},{1,5},{2,6},{3,7},{4,0},{5,1},{6,2},{7,3},{8,12},{9,13},{10,... | collective-permute-start | bytes 638984 | tf_op jit(solution)/shard_map/ppermute | solution.py:687
  81.8 8.5 %collective-permute-start.22 = (bf16[416,256]{1,0:T(8,128)(2,1)S(1)}, bf16[416,256]{1,0:T(8,128)(2,1)S(1)}, u32[]{:S(2)}, u32[]{:S(2)}) collective-permute-start(bf16[416,256]{1,0:T(8,128)(2,1)S(1)} %bitcast.50), channel_id=1, source_target_pairs={{0,6},{1,7},{2,4},{3,5},{4,2},{5,3},{6,0},{7,1},{8,14},{9,15},{10,... | collective-permute-start | bytes 638984 | tf_op jit(solution)/shard_map/ppermute | solution.py:687
  83.6 6.9 %collective-permute-start.17 = (bf16[104,256]{1,0:T(8,128)(2,1)S(1)}, bf16[104,256]{1,0:T(8,128)(2,1)S(1)}, u32[]{:S(2)}, u32[]{:S(2)}) collective-permute-start(bf16[104,256]{1,0:T(8,128)(2,1)S(1)} %add_convert_fusion), channel_id=1, source_target_pairs={{0,24},{1,25},{2,26},{3,27},{4,28},{5,29},{6,30},{7,31},{8,16},{9,... | collective-permute-start | bytes 159752 | tf_op jit(solution)/shard_map/ppermute | solution.py:687
  86.7 5.0 %collective-permute-start.18 = (bf16[104,256]{1,0:T(8,128)(2,1)S(1)}, bf16[104,256]{1,0:T(8,128)(2,1)S(1)}, u32[]{:S(2)}, u32[]{:S(2)}) collective-permute-start(bf16[104,256]{1,0:T(8,128)(2,1)S(1)} %add_convert_fusion), channel_id=1, source_target_pairs={{0,16},{1,17},{2,18},{3,19},{4,20},{5,21},{6,22},{7,23},{8,24},{9,... | collective-permute-start | bytes 159752 | tf_op jit(solution)/shard_map/ppermute | solution.py:687
  86.9 4.8 %collective-permute-start.19 = (bf16[104,256]{1,0:T(8,128)(2,1)S(1)}, bf16[104,256]{1,0:T(8,128)(2,1)S(1)}, u32[]{:S(2)}, u32[]{:S(2)}) collective-permute-start(bf16[104,256]{1,0:T(8,128)(2,1)S(1)} %add_convert_fusion), channel_id=1, source_target_pairs={{0,8},{1,9},{2,10},{3,11},{4,12},{5,13},{6,14},{7,15},{8,0},{9,1},... | collective-permute-start | bytes 159752 | tf_op jit(solution)/shard_map/ppermute | solution.py:687
  90.4 9.1 %collective-permute-start.26 = (bf16[1664,256]{1,0:T(8,128)(2,1)S(1)}, bf16[1664,256]{1,0:T(8,128)(2,1)S(1)}, u32[]{:S(2)}, u32[]{:S(2)}) collective-permute-start(bf16[1664,256]{1,0:T(8,128)(2,1)S(1)} %bitcast.41), channel_id=1, source_target_pairs={{0,1},{1,0},{2,3},{3,2},{4,5},{5,4},{6,7},{7,6},{8,9},{9,8},{10,11... | collective-permute-start | bytes 2555912 | tf_op jit(solution)/shard_map/ppermute | solution.py:687
  91.8 9.5 %collective-permute-start.23 = (bf16[416,256]{1,0:T(8,128)(2,1)S(1)}, bf16[416,256]{1,0:T(8,128)(2,1)S(1)}, u32[]{:S(2)}, u32[]{:S(2)}) collective-permute-start(bf16[416,256]{1,0:T(8,128)(2,1)S(1)} %bitcast.43), channel_id=1, source_target_pairs={{0,2},{1,3},{2,0},{3,1},{4,6},{5,7},{6,4},{7,5},{8,10},{9,11},{10,... | collective-permute-start | bytes 638984 | tf_op jit(solution)/shard_map/ppermute | solution.py:687
  93.1 10.1 %collective-permute-start.24 = (bf16[416,256]{1,0:T(8,128)(2,1)S(1)}, bf16[416,256]{1,0:T(8,128)(2,1)S(1)}, u32[]{:S(2)}, u32[]{:S(2)}) collective-permute-start(bf16[416,256]{1,0:T(8,128)(2,1)S(1)} %bitcast.44), channel_id=1, source_target_pairs={{0,4},{1,5},{2,6},{3,7},{4,0},{5,1},{6,2},{7,3},{8,12},{9,13},{10,... | collective-permute-start | bytes 638984 | tf_op jit(solution)/shard_map/ppermute | solution.py:687
  93.9 9.3 %collective-permute-start.25 = (bf16[416,256]{1,0:T(8,128)(2,1)S(1)}, bf16[416,256]{1,0:T(8,128)(2,1)S(1)}, u32[]{:S(2)}, u32[]{:S(2)}) collective-permute-start(bf16[416,256]{1,0:T(8,128)(2,1)S(1)} %bitcast.45), channel_id=1, source_target_pairs={{0,6},{1,7},{2,4},{3,5},{4,2},{5,3},{6,0},{7,1},{8,14},{9,15},{10,... | collective-permute-start | bytes 638984 | tf_op jit(solution)/shard_map/ppermute | solution.py:687
  99.5 4.3 %collective-permute-start.27 = (bf16[416,256]{1,0:T(8,128)(2,1)S(1)}, bf16[416,256]{1,0:T(8,128)(2,1)S(1)}, u32[]{:S(2)}, u32[]{:S(2)}) collective-permute-start(bf16[416,256]{1,0:T(8,128)(2,1)S(1)} %bitcast.46), channel_id=1, source_target_pairs={{0,1},{1,0},{2,3},{3,2},{4,5},{5,4},{6,7},{7,6},{8,9},{9,8},{10,11... | collective-permute-start | bytes 638984 | tf_op jit(solution)/shard_map/ppermute | solution.py:687
  103.3 1.5 %collective-permute-start.28 = (bf16[416,256]{1,0:T(8,128)(2,1)S(1)}, bf16[416,256]{1,0:T(8,128)(2,1)S(1)}, u32[]{:S(2)}, u32[]{:S(2)}) collective-permute-start(bf16[416,256]{1,0:T(8,128)(2,1)S(1)} %collective-permute-done.23.refs_1_), channel_id=1, source_target_pairs={{0,1},{1,0},{2,3},{3,2},{4,5},{5,4},{6,7},{7,6},{8,9},{9,8},{10,11... | collective-permute-start | bytes 638984 | tf_op jit(solution)/shard_map/ppermute | solution.py:687
  103.3 1.8 %collective-permute-start.29 = (bf16[416,256]{1,0:T(8,128)(2,1)S(1)}, bf16[416,256]{1,0:T(8,128)(2,1)S(1)}, u32[]{:S(2)}, u32[]{:S(2)}) collective-permute-start(bf16[416,256]{1,0:T(8,128)(2,1)S(1)} %collective-permute-done.24.refs_2_), channel_id=1, source_target_pairs={{0,1},{1,0},{2,3},{3,2},{4,5},{5,4},{6,7},{7,6},{8,9},{9,8},{10,11... | collective-permute-start | bytes 638984 | tf_op jit(solution)/shard_map/ppermute | solution.py:687
  103.8 1.6 %collective-permute-start.30 = (bf16[416,256]{1,0:T(8,128)(2,1)S(1)}, bf16[416,256]{1,0:T(8,128)(2,1)S(1)}, u32[]{:S(2)}, u32[]{:S(2)}) collective-permute-start(bf16[416,256]{1,0:T(8,128)(2,1)S(1)} %collective-permute-done.25.refs_3_), channel_id=1, source_target_pairs={{0,1},{1,0},{2,3},{3,2},{4,5},{5,4},{6,7},{7,6},{8,9},{9,8},{10,11... | collective-permute-start | bytes 638984 | tf_op jit(solution)/shard_map/ppermute | solution.py:687
